TPU v7x, 256 devices: a whole 4x4x8 slice. The times are simulated.
256 devices in a mesh: lon: 64 (over z, x, y_hi), probe: 4 (over y_lo, core).
Axes of the slice: x: 4, y: 4 (y_hi: 2, y_lo: 2; y = y_hi * 2 + y_lo), z: 8, core: 2. Of those that a mesh axis runs over, the one named last changes fastest.
Arguments:
- increments: float32 [64, 1536, 8, 256], P('probe', 'lon'), may hold values from -6 to 6
- winds: float32 [2, 1536, 8, 256], P(None, 'lon'), may hold values from -0.2 to 0.2
- obs_weight: float32 [1536, 8, 256], P('lon'), may hold values from 0.1 to 10
Outputs:
- basis: float32 [64, 384, 512], P('probe', 'lon')
- upper: float32 [64, 64], replicated
All inputs are finite; a program needn't handle non-finite values.
Results may differ from a plain program's by a relative error of at most 0.00011.
Values sent between devices are 32-bit elements; how exact they have to be, the bound alone decides.
A program may use at most 128 MiB of HBM per device.

v0:
```python
import jax
import jax.numpy as jnp
from jax import lax
from jax.sharding import PartitionSpec as P


def from_behind(block, axis, distance):
    devices = range(lax.axis_size(axis))
    route = [((i - distance) % len(devices), i) for i in devices]
    return lax.ppermute(block, axis, route)


def padded(block, sides, width):
    for axis, dim in sides:
        count = lax.axis_size(axis)
        forward = [(i, i + 1) for i in range(count - 1)]
        forward.append((count - 1, 0))
        backward = [(target, source) for source, target in forward]
        low = lax.ppermute(
            lax.slice_in_dim(block, block.shape[dim] - width, None, axis=dim), axis, forward
        )
        high = lax.ppermute(lax.slice_in_dim(block, 0, width, axis=dim), axis, backward)
        block = jnp.concatenate([low, block, high], axis=dim)
    return block


def lat_mask(field):
    rows = lax.broadcasted_iota(jnp.int32, field.shape, field.ndim - 1)
    return jnp.where(rows > 0, field, jnp.zeros_like(field))


def below(field):
    return jnp.concatenate([jnp.zeros_like(field[..., :1]), field[..., :-1]], axis=-1)


def above(field):
    return jnp.concatenate([field[..., 1:], jnp.zeros_like(field[..., :1])], axis=-1)


def forward_core(widened, east, north):
    a_pos = jnp.maximum(east, 0.0)
    b_neg = jnp.minimum(east, 0.0)
    c_pos = jnp.maximum(north[1:-1], 0.0)
    d_neg = jnp.minimum(north[1:-1], 0.0)
    flux_w = a_pos[1:] * widened[:, :-1] + b_neg[1:] * widened[:, 1:]
    inner = widened[:, 1:-1]
    flux_s = c_pos * below(inner) + d_neg * inner
    flux_n = above(flux_s)
    return inner - (flux_w[:, 1:] - flux_w[:, :-1]) - (flux_n - flux_s)


def adjoint_core(widened, east, north):
    a_pos = jnp.maximum(east, 0.0)
    b_neg = jnp.minimum(east, 0.0)[1:-1]
    c_pos = jnp.maximum(north[1:-1], 0.0)
    d_neg = jnp.minimum(north[1:-1], 0.0)
    a_east = a_pos[2:]
    c_north = above(c_pos)
    inner = widened[:, 1:-1]
    west_val = widened[:, :-2]
    east_val = widened[:, 2:]
    return (
        inner * (1.0 - a_east + b_neg - c_north + d_neg)
        - b_neg * west_val
        + a_east * east_val
        - d_neg * below(inner)
        + c_north * above(inner)
    )


def body(increments, winds, obs_weight):
    east_local = winds[0]
    north_local = lat_mask(winds[1])
    next_first = from_behind(east_local[:1], "lon", -1)
    near_east = jnp.concatenate([jnp.zeros_like(next_first), east_local, next_first], axis=0)
    edge_zero = jnp.zeros_like(north_local[:1])
    near_north = jnp.concatenate([edge_zero, north_local, edge_zero], axis=0)

    def widen(field):
        return padded(field, (("lon", 1),), 1)

    state = increments
    for step in range(2):
        state = forward_core(widen(state), near_east, near_north)
    state = obs_weight * state
    for step in range(2):
        state = adjoint_core(widen(state), near_east, near_north)
    sketch = increments + state
    probe_count, lon_count, level_count, lat_count = sketch.shape
    coarse = jnp.mean(
        sketch.reshape(probe_count, lon_count // 4, 4, level_count, lat_count // 4, 4), axis=(2, 5)
    )
    coarse = coarse.reshape(probe_count, -1)
    all_probes = probe_count * lax.axis_size("probe")
    ident = jnp.eye(all_probes, dtype=jnp.float32)
    full_panel = lax.all_gather(coarse, "probe", axis=0, tiled=True)
    local_gram = jnp.dot(
        full_panel,
        full_panel.T,
        precision=lax.Precision.HIGHEST,
        preferred_element_type=jnp.float32,
    )
    gram = lax.psum(local_gram, "lon")
    lower = jnp.linalg.cholesky(gram)
    inverse = lax.linalg.triangular_solve(lower, ident, left_side=True, lower=True)
    own_rows = lax.dynamic_slice_in_dim(
        inverse, lax.axis_index("probe") * probe_count, probe_count, 0
    )
    basis = jnp.dot(
        own_rows, full_panel, precision=lax.Precision.HIGHEST, preferred_element_type=jnp.float32
    )
    return (basis.reshape(probe_count, lon_count // 4, -1), lower.T)


def solution(mesh):
    in_specs = (P("probe", "lon", None, None), P(None, "lon", None, None), P("lon", None, None))
    out_specs = (P("probe", "lon", None), P())
    return jax.shard_map(body, mesh=mesh, in_specs=in_specs, out_specs=out_specs, check_vma=False)
```

profile of v0, /device:TPU:8, one launch (start us, length us, event | category | flops | bytes accessed | tf_op | source)
XLA Modules:
  0.0 485.5 jit_solution(4162303472473665741)
XLA Ops:
  1.3 9.8 %collective-permute-start = (f32[1,8,256]{2,1,0:T(8,128)S(1)}, f32[1,8,256]{2,1,0:T(8,128)S(1)}, u32[]{:S(2)}, u32[]{:S(2)}) collective-permute-start(f32[1,8,256]{2,1,0:T(8,128)S(1)} %slice_bitcast_fusion.1), channel_id=1, source_target_pairs={{4,0},{8,4},{12,8},{16,12},{20,16},{24,20},{28,24},{32,28},{36,32}... | collective-permute-start | bytes 24584 | tf_op jit(solution)/shard_map/ppermute | solution.py:10
  11.1 1.7 fusion.34
  12.8 7.7 %collective-permute-start.2 = (f32[16,1,8,256]{3,2,1,0:T(8,128)}, f32[16,1,8,256]{3,2,1,0:T(8,128)}, u32[]{:S(2)}, u32[]{:S(2)}) collective-permute-start(f32[16,1,8,256]{3,2,1,0:T(8,128)} %get-tuple-element.22), channel_id=1, source_target_pairs={{4,0},{8,4},{12,8},{16,12},{20,16},{24,20},{28,24},{32,28},{36,32}... | collective-permute-start | bytes 393224 | tf_op jit(solution)/shard_map/ppermute | solution.py:22
  20.6 1.1 maximum_bitcast_fusion
  21.6 1.0 bitcast_select_fusion
  22.7 3.8 multiply_add_fusion.1
  26.5 0.9 slice_maximum_fusion
  27.4 0.8 copy-done.1
  28.2 2.6 slice.164
  32.1 1.1 minimum_add_fusion
  33.2 1.5 fusion
  35.2 1.0 copy-done.3
  36.1 0.9 fusion.19
  37.1 7.7 %collective-permute-start.4 = (f32[16,1,8,256]{3,2,1,0:T(8,128)S(1)}, f32[16,1,8,256]{3,2,1,0:T(8,128)S(1)}, u32[]{:S(2)}, u32[]{:S(2)}) collective-permute-start(f32[16,1,8,256]{3,2,1,0:T(8,128)S(1)} %get-tuple-element.20), channel_id=1, source_target_pairs={{4,0},{8,4},{12,8},{16,12},{20,16},{24,20},{28,24},{32,28},{36,32}... | collective-permute-start | bytes 393224 | tf_op jit(solution)/shard_map/ppermute | solution.py:22
  44.9 1.0 multiply_add_fusion
  45.9 2.5 slice.170
  49.3 2.8 fusion.17
  52.3 7.7 %collective-permute-start.6 = (f32[16,1,8,256]{3,2,1,0:T(8,128)S(1)}, f32[16,1,8,256]{3,2,1,0:T(8,128)S(1)}, u32[]{:S(2)}, u32[]{:S(2)}) collective-permute-start(f32[16,1,8,256]{3,2,1,0:T(8,128)S(1)} %get-tuple-element.19), channel_id=1, source_target_pairs={{4,0},{8,4},{12,8},{16,12},{20,16},{24,20},{28,24},{32,28},{36,32}... | collective-permute-start | bytes 393224 | tf_op jit(solution)/shard_map/ppermute | solution.py:22
  60.0 1.1 fusion.31
  61.1 1.8 collective-permute-done.5
  63.0 2.2 fusion.12
  65.3 7.8 %collective-permute-start.8 = (f32[16,1,8,256]{3,2,1,0:T(8,128)S(1)}, f32[16,1,8,256]{3,2,1,0:T(8,128)S(1)}, u32[]{:S(2)}, u32[]{:S(2)}) collective-permute-start(f32[16,1,8,256]{3,2,1,0:T(8,128)S(1)} %get-tuple-element.15), channel_id=1, source_target_pairs={{4,0},{8,4},{12,8},{16,12},{20,16},{24,20},{28,24},{32,28},{36,32}... | collective-permute-start | bytes 393224 | tf_op jit(solution)/shard_map/ppermute | solution.py:22
  73.1 1.2 fusion.29
  74.3 1.7 collective-permute-done.7
  76.0 3.7 fusion.6
  79.6 13.4 %copy.25 = f32[16,24,8,256]{0,2,3,1:T(8,128)} copy(f32[16,24,8,256]{3,2,1,0:T(8,128)} %fusion.6) | data formatting | bytes 6291456 | tf_op jit(solution)/shard_map/add | solution.py:88
  93.0 10.1 %reduce_sum.9 = f32[16,6,8,64]{0,2,3,1:T(8,128)S(1)} reduce(f32[16,6,4,8,64,4]{0,3,5,4,2,1:T(8,128)} %bitcast.36, f32[]{:T(128)} %constant.53.clone.1), dimensions={2,5}, to_apply=%region_0.1 | reduce | flops 737280 | bytes 3342340 | tf_op jit(solution)/shard_map/reduce_sum | solution.py:90
  103.9 8.5 %all_gather.3 = f32[64,3072]{1,0:T(8,128)S(1)} all-gather(f32[16,3072]{1,0:T(8,128)S(1)} %div.18), channel_id=1, replica_groups=mesh['lon'=64,'probe'=4] {'probe'}, dimensions={0}, use_global_device_ids=true | all-gather | bytes 983040 | tf_op jit(solution)/shard_map/all_gather | solution.py:96
  112.3 0.8 fusion.35
  113.1 358.1 %psum.7 = f32[64,64]{0,1:T(8,128)S(1)} all-reduce(f32[64,64]{0,1:T(8,128)S(1)} %fusion.35), channel_id=1, replica_groups=mesh['lon'=64,'probe'=4] {'lon'}, use_global_device_ids=true, to_apply=%region_1.2 | all-reduce | flops 4096 | bytes 32768 | tf_op jit(solution)/shard_map/psum | solution.py:103
  471.2 5.8 %cholesky.17 = f32[64,64]{1,0:T(8,128)S(1)} custom-call(f32[64,64]{1,0:T(8,128)S(1)} %fusion.24), custom_call_target="Cholesky" | custom-call | tf_op jit(solution)/shard_map/jit(cholesky)/cholesky | solution.py:104
  478.4 4.9 %custom-call.6 = f32[1,64,64]{1,2,0:T(8,128)S(1)} custom-call(f32[1,64,64]{2,1,0:T(8,128)S(1)} %get-tuple-element.34), custom_call_target="InvertDiagBlocksLowerTriangular" | custom-call | tf_op jit(solution)/shard_map/triangular_solve | solution.py:105
  (47 shorter events, 8.0 us)
Async XLA Ops:
  1.3 29.9 %collective-permute-start = (f32[1,8,256]{2,1,0:T(8,128)S(1)}, f32[1,8,256]{2,1,0:T(8,128)S(1)}, u32[]{:S(2)}, u32[]{:S(2)}) collective-permute-start(f32[1,8,256]{2,1,0:T(8,128)S(1)} %slice_bitcast_fusion.1), channel_id=1, source_target_pairs={{4,0},{8,4},{12,8},{16,12},{20,16},{24,20},{28,24},{32,28},{36,32}... | collective-permute-start | bytes 24584 | tf_op jit(solution)/shard_map/ppermute | solution.py:10
  12.8 20.4 %collective-permute-start.1 = (f32[16,1,8,256]{3,2,1,0:T(8,128)}, f32[16,1,8,256]{3,2,1,0:T(8,128)}, u32[]{:S(2)}, u32[]{:S(2)}) collective-permute-start(f32[16,1,8,256]{3,2,1,0:T(8,128)} %get-tuple-element.23), channel_id=1, source_target_pairs={{0,4},{4,8},{8,12},{12,16},{16,20},{20,24},{24,28},{28,32},{32,36}... | collective-permute-start | bytes 393224 | tf_op jit(solution)/shard_map/ppermute | solution.py:19
  12.8 20.4 %collective-permute-start.2 = (f32[16,1,8,256]{3,2,1,0:T(8,128)}, f32[16,1,8,256]{3,2,1,0:T(8,128)}, u32[]{:S(2)}, u32[]{:S(2)}) collective-permute-start(f32[16,1,8,256]{3,2,1,0:T(8,128)} %get-tuple-element.22), channel_id=1, source_target_pairs={{4,0},{8,4},{12,8},{16,12},{20,16},{24,20},{28,24},{32,28},{36,32}... | collective-permute-start | bytes 393224 | tf_op jit(solution)/shard_map/ppermute | solution.py:22
  20.6 5.9 %copy-start.7 = (pred[256]{0:T(512)(128)(4,1)}, pred[256]{0:T(512)(128)(4,1)S(1)}, u32[]{:S(2)}) copy-start(pred[256]{0:T(512)(128)(4,1)S(1)} %iota_compare_fusion.3) | copy-start | bytes 772
  21.6 4.8 copy-start.4
  26.5 1.7 copy-start.1
  28.2 5.0 %copy-start = (f32[16,24,8,256]{3,2,1,0:T(8,128)S(1)}, f32[16,24,8,256]{3,2,1,0:T(8,128)}, u32[]{:S(2)}) copy-start(f32[16,24,8,256]{3,2,1,0:T(8,128)} %param.3) | copy-start | bytes 9437188
  33.2 2.0 copy-start.2
  33.2 3.0 copy-start.3
  36.1 8.8 %copy-start.5 = (f32[24,8,256]{2,1,0:T(8,128)S(1)}, f32[24,8,256]{2,1,0:T(8,128)}, u32[]{:S(2)}) copy-start(f32[24,8,256]{2,1,0:T(8,128)} %copy-done.4) | copy-start | bytes 589828
  37.1 11.3 %collective-permute-start.3 = (f32[16,1,8,256]{3,2,1,0:T(8,128)S(1)}, f32[16,1,8,256]{3,2,1,0:T(8,128)S(1)}, u32[]{:S(2)}, u32[]{:S(2)}) collective-permute-start(f32[16,1,8,256]{3,2,1,0:T(8,128)S(1)} %get-tuple-element.21), channel_id=1, source_target_pairs={{0,4},{4,8},{8,12},{12,16},{16,20},{20,24},{24,28},{28,32},{32,36}... | collective-permute-start | bytes 393224 | tf_op jit(solution)/shard_map/ppermute | solution.py:19
  37.1 11.2 %collective-permute-start.4 = (f32[16,1,8,256]{3,2,1,0:T(8,128)S(1)}, f32[16,1,8,256]{3,2,1,0:T(8,128)S(1)}, u32[]{:S(2)}, u32[]{:S(2)}) collective-permute-start(f32[16,1,8,256]{3,2,1,0:T(8,128)S(1)} %get-tuple-element.20), channel_id=1, source_target_pairs={{4,0},{8,4},{12,8},{16,12},{20,16},{24,20},{28,24},{32,28},{36,32}... | collective-permute-start | bytes 393224 | tf_op jit(solution)/shard_map/ppermute | solution.py:22
  48.4 0.9 copy-start.6
  52.2 10.8 %collective-permute-start.5 = (f32[16,1,8,256]{3,2,1,0:T(8,128)S(1)}, f32[16,1,8,256]{3,2,1,0:T(8,128)S(1)}, u32[]{:S(2)}, u32[]{:S(2)}) collective-permute-start(f32[16,1,8,256]{3,2,1,0:T(8,128)S(1)} %get-tuple-element.18), channel_id=1, source_target_pairs={{0,4},{4,8},{8,12},{12,16},{16,20},{20,24},{24,28},{28,32},{32,36}... | collective-permute-start | bytes 393224 | tf_op jit(solution)/shard_map/ppermute | solution.py:19
  52.3 10.7 %collective-permute-start.6 = (f32[16,1,8,256]{3,2,1,0:T(8,128)S(1)}, f32[16,1,8,256]{3,2,1,0:T(8,128)S(1)}, u32[]{:S(2)}, u32[]{:S(2)}) collective-permute-start(f32[16,1,8,256]{3,2,1,0:T(8,128)S(1)} %get-tuple-element.19), channel_id=1, source_target_pairs={{4,0},{8,4},{12,8},{16,12},{20,16},{24,20},{28,24},{32,28},{36,32}... | collective-permute-start | bytes 393224 | tf_op jit(solution)/shard_map/ppermute | solution.py:22
  65.2 10.8 %collective-permute-start.7 = (f32[16,1,8,256]{3,2,1,0:T(8,128)S(1)}, f32[16,1,8,256]{3,2,1,0:T(8,128)S(1)}, u32[]{:S(2)}, u32[]{:S(2)}) collective-permute-start(f32[16,1,8,256]{3,2,1,0:T(8,128)S(1)} %get-tuple-element.14), channel_id=1, source_target_pairs={{0,4},{4,8},{8,12},{12,16},{16,20},{20,24},{24,28},{28,32},{32,36}... | collective-permute-start | bytes 393224 | tf_op jit(solution)/shard_map/ppermute | solution.py:19
  65.3 10.7 %collective-permute-start.8 = (f32[16,1,8,256]{3,2,1,0:T(8,128)S(1)}, f32[16,1,8,256]{3,2,1,0:T(8,128)S(1)}, u32[]{:S(2)}, u32[]{:S(2)}) collective-permute-start(f32[16,1,8,256]{3,2,1,0:T(8,128)S(1)} %get-tuple-element.15), channel_id=1, source_target_pairs={{4,0},{8,4},{12,8},{16,12},{20,16},{24,20},{28,24},{32,28},{36,32}... | collective-permute-start | bytes 393224 | tf_op jit(solution)/shard_map/ppermute | solution.py:22
where the time goes:
time: 486 us; the launch traced here: 485 us
  blocking collectives  367 us (76%)
  other arithmetic  43.3 us (9%)
  starting transfers between devices  41.1 us (8%)
  local copies, waits for them, and re-layouts  28.6 us (6%)
    psum x1, blocking collectives, body(): gram = lax.psum(local_gram, 'lon')  358 us
    ppermute x4, starting transfers between devices, padded(): lax.ppermute(lax.slice_in_dim(block, 0, width, axis=dim), axis, backward)  31 us
    add x1, local copies, waits for them, and re-layouts, body(): sketch = increments + state  13.4 us
    reduce_sum x1, other arithmetic, body(): jnp.mean(sketch.reshape(probe_count, lon_count // 4, 4, level_count, lat_...  10.1 us
    ppermute x1, starting transfers between devices, from_behind(): return lax.ppermute(block, axis, route)  9.78 us
  transfers between devices with their start and end apart: 9, of which 2 were waited for; matrix products, arithmetic and copies ran while one was open for 4% of the time, Pallas kernels for 0%

commit v1 on v0

--- a/solution.py
+++ b/solution.py
@@ -8,6 +8,18 @@
     devices = range(lax.axis_size(axis))
     route = [((i - distance) % len(devices), i) for i in devices]
     return lax.ppermute(block, axis, route)
+
+
+def butterfly_sum(block, axis):
+    count = lax.axis_size(axis)
+    if count & (count - 1):
+        return lax.psum(block, axis)
+    distance = 1
+    while distance < count:
+        route = [(i, i ^ distance) for i in range(count)]
+        block = block + lax.ppermute(block, axis, route)
+        distance *= 2
+    return block
 
 
 def padded(block, sides, width):
@@ -100,7 +112,7 @@
         precision=lax.Precision.HIGHEST,
         preferred_element_type=jnp.float32,
     )
-    gram = lax.psum(local_gram, "lon")
+    gram = butterfly_sum(local_gram, "lon")
     lower = jnp.linalg.cholesky(gram)
     inverse = lax.linalg.triangular_solve(lower, ident, left_side=True, lower=True)
     own_rows = lax.dynamic_slice_in_dim(

time: 486 us -> 149 us (0.31)
  blocking collectives: 367 us -> 8.45 us
  waiting for transfers between devices: 3.54 us -> 33.5 us
  local copies, waits for them, and re-layouts: 28.6 us -> 23 us
    psum x1 -> x0, blocking collectives: 358 us -> none  [body(): gram = lax.psum(local_gram, 'lon')]
    ppermute x0 -> x6, waiting for transfers between devices: none -> 30 us  [butterfly_sum(): block = block + lax.ppermute(block, axis, route)]
  transfers between devices with their start and end apart: 9 -> 15, of which waited for: 2 -> 8; matrix products, arithmetic and copies ran while one was open for 4% -> 9% of each run, Pallas kernels for 0% -> 0%
where the time goes in v1:
time: 149 us
  starting transfers between devices  42.7 us (29%)
  other arithmetic  38.7 us (26%)
  waiting for transfers between devices  33.5 us (22%)
  local copies, waits for them, and re-layouts  23 us (15%)
  blocking collectives  8.45 us (6%)
    ppermute x4, starting transfers between devices, padded(): lax.ppermute(lax.slice_in_dim(block, 0, width, axis=dim), axis, backward)  31 us
    ppermute x6, waiting for transfers between devices, butterfly_sum(): block = block + lax.ppermute(block, axis, route)  30 us
    add x1, local copies, waits for them, and re-layouts, body(): sketch = increments + state  12 us
    reduce_sum x1, other arithmetic, body(): jnp.mean(sketch.reshape(probe_count, lon_count // 4, 4, level_count, lat_...  10.1 us
    ppermute x1, starting transfers between devices, from_behind(): return lax.ppermute(block, axis, route)  9.78 us
    all_gather x1, blocking collectives, body(): full_panel = lax.all_gather(coarse, 'probe', axis=0, tiled=True)  8.45 us
    another operation x3, other arithmetic, body(): lower = jnp.linalg.cholesky(gram)  6.52 us
    another operation x1, other arithmetic, body(): lax.linalg.triangular_solve(lower, ident, left_side=True, lower=True)  4.9 us
  transfers between devices with their start and end apart: 15, of which 8 were waited for; matrix products, arithmetic and copies ran while one was open for 9% of the time, Pallas kernels for 0%

profile of v1, /device:TPU:8, one launch (start us, length us, event | category | flops | bytes accessed | tf_op | source)
XLA Modules:
  0.0 148.9 jit_solution(1681838737861612050)
XLA Ops:
  1.3 9.8 %collective-permute-start = (f32[1,8,256]{2,1,0:T(8,128)S(1)}, f32[1,8,256]{2,1,0:T(8,128)S(1)}, u32[]{:S(2)}, u32[]{:S(2)}) collective-permute-start(f32[1,8,256]{2,1,0:T(8,128)S(1)} %slice_bitcast_fusion.1), channel_id=1, source_target_pairs={{4,0},{8,4},{12,8},{16,12},{20,16},{24,20},{28,24},{32,28},{36,32}... | collective-permute-start | bytes 24584 | tf_op jit(solution)/shard_map/ppermute | solution.py:10
  11.1 1.0 fusion.34
  12.2 7.7 %collective-permute-start.2 = (f32[16,1,8,256]{3,2,1,0:T(8,128)S(1)}, f32[16,1,8,256]{3,2,1,0:T(8,128)S(1)}, u32[]{:S(2)}, u32[]{:S(2)}) collective-permute-start(f32[16,1,8,256]{3,2,1,0:T(8,128)S(1)} %get-tuple-element.22), channel_id=1, source_target_pairs={{4,0},{8,4},{12,8},{16,12},{20,16},{24,20},{28,24},{32,28},{36,32}... | collective-permute-start | bytes 393224 | tf_op jit(solution)/shard_map/ppermute | solution.py:34
  19.9 1.1 maximum_bitcast_fusion
  21.0 0.9 bitcast_select_fusion
  21.9 3.7 %multiply_add_fusion.1 = f32[16,24,8,256]{3,2,1,0:T(8,128)S(1)} fusion(f32[16,24,8,256]{3,2,1,0:T(8,128)} %param.3, f32[16,24,8,255]{3,2,1,0:T(8,128)} %bitcast.37, f32[24,8,256]{2,1,0:T(8,128)S(1)} %get-tuple-element.25, f32[24,8,256]{2,1,0:T(8,128)S(1)} %get-tuple-element.24), kind=kLoop, calls=%fused_computation.31 | loop fusion | flops 2359296 | bytes 9818112 | tf_op jit(solution)/shard_map/add | solution.py:59
  25.8 0.9 slice.164
  28.2 1.0 fusion.19
  29.3 7.7 %collective-permute-start.4 = (f32[16,1,8,256]{3,2,1,0:T(8,128)S(1)}, f32[16,1,8,256]{3,2,1,0:T(8,128)S(1)}, u32[]{:S(2)}, u32[]{:S(2)}) collective-permute-start(f32[16,1,8,256]{3,2,1,0:T(8,128)S(1)} %get-tuple-element.20), channel_id=1, source_target_pairs={{4,0},{8,4},{12,8},{16,12},{20,16},{24,20},{28,24},{32,28},{36,32}... | collective-permute-start | bytes 393224 | tf_op jit(solution)/shard_map/ppermute | solution.py:34
  37.1 1.0 multiply_add_fusion
  38.1 2.5 %slice.170 = f32[16,24,8,255]{3,2,1,0:T(8,128)} slice(f32[16,24,8,256]{3,2,1,0:T(8,128)S(1)} %multiply_add_fusion), slice={[0:16], [0:24], [0:8], [1:256]} | slice | bytes 6266880 | tf_op jit(solution)/shard_map/slice | solution.py:49
  41.5 2.8 %fusion.17 = f32[16,24,8,256]{3,2,1,0:T(8,128)S(1)} fusion(f32[16,24,8,256]{3,2,1,0:T(8,128)S(1)} %fusion.19, f32[16,25,8,256]{3,2,1,0:T(8,128)S(1)} %fusion.1, f32[16,24,8,256]{3,2,1,0:T(8,128)S(1)} %multiply_add_fusion, f32[16,24,8,255]{3,2,1,0:T(8,128)} %slice.170, f32[24,8,256]{2,1,0:T(8,128)S(1)} %copy-done.8), kind=kLoop, calls=%fused_computation.26 | loop fusion | flops 3932160 | bytes 19058688 | tf_op jit(solution)/shard_map/mul | solution.py:97
  44.5 7.7 %collective-permute-start.6 = (f32[16,1,8,256]{3,2,1,0:T(8,128)S(1)}, f32[16,1,8,256]{3,2,1,0:T(8,128)S(1)}, u32[]{:S(2)}, u32[]{:S(2)}) collective-permute-start(f32[16,1,8,256]{3,2,1,0:T(8,128)S(1)} %get-tuple-element.19), channel_id=1, source_target_pairs={{4,0},{8,4},{12,8},{16,12},{20,16},{24,20},{28,24},{32,28},{36,32}... | collective-permute-start | bytes 393224 | tf_op jit(solution)/shard_map/ppermute | solution.py:34
  52.2 1.1 fusion.31
  53.3 1.8 %collective-permute-done.5 = f32[16,1,8,256]{3,2,1,0:T(8,128)S(1)} collective-permute-done((f32[16,1,8,256]{3,2,1,0:T(8,128)S(1)}, f32[16,1,8,256]{3,2,1,0:T(8,128)S(1)}, u32[]{:S(2)}, u32[]{:S(2)}) %collective-permute-start.5) | collective-permute-done | bytes 131104 | tf_op jit(solution)/shard_map/ppermute | solution.py:31
  55.2 2.2 %fusion.12 = f32[16,24,8,256]{3,2,1,0:T(8,128)S(1)} fusion(f32[16,1,8,256]{3,2,1,0:T(8,128)S(1)} %collective-permute-done.6, f32[16,24,8,256]{3,2,1,0:T(8,128)S(1)} %fusion.17, f32[16,1,8,256]{3,2,1,0:T(8,128)S(1)} %collective-permute-done.5, f32[16,24,8,255]{3,2,1,0:T(8,128)S(1)} %get-tuple-element.17, f32[16,24,8,255]{3,2,1,0:T(8,128)S(1)} %get-tuple-element.16, ...), kind=kLoop, calls=%fused_computation.19 | loop fusion | flops 8650752 | bytes 13803520 | tf_op jit(solution)/shard_map/add | solution.py:75
  57.5 7.8 %collective-permute-start.8 = (f32[16,1,8,256]{3,2,1,0:T(8,128)S(1)}, f32[16,1,8,256]{3,2,1,0:T(8,128)S(1)}, u32[]{:S(2)}, u32[]{:S(2)}) collective-permute-start(f32[16,1,8,256]{3,2,1,0:T(8,128)S(1)} %get-tuple-element.15), channel_id=1, source_target_pairs={{4,0},{8,4},{12,8},{16,12},{20,16},{24,20},{28,24},{32,28},{36,32}... | collective-permute-start | bytes 393224 | tf_op jit(solution)/shard_map/ppermute | solution.py:34
  65.3 1.2 fusion.29
  66.5 1.7 %collective-permute-done.7 = f32[16,1,8,256]{3,2,1,0:T(8,128)S(1)} collective-permute-done((f32[16,1,8,256]{3,2,1,0:T(8,128)S(1)}, f32[16,1,8,256]{3,2,1,0:T(8,128)S(1)}, u32[]{:S(2)}, u32[]{:S(2)}) %collective-permute-start.7) | collective-permute-done | bytes 131104 | tf_op jit(solution)/shard_map/ppermute | solution.py:31
  68.2 2.6 %fusion.6 = f32[16,24,8,256]{3,2,1,0:T(8,128)S(1)} fusion(f32[16,24,8,256]{3,2,1,0:T(8,128)S(1)} %copy-done, f32[16,1,8,256]{3,2,1,0:T(8,128)S(1)} %collective-permute-done.8, f32[16,24,8,256]{3,2,1,0:T(8,128)S(1)} %fusion.12, f32[16,1,8,256]{3,2,1,0:T(8,128)S(1)} %collective-permute-done.7, f32[16,24,8,255]{3,2,1,0:T(8,128)S(1)} %get-tuple-element.13, ...), kind=kLoop, calls=%fused_computation.11 | loop fusion | flops 9437184 | bytes 16949248 | tf_op jit(solution)/shard_map/add | solution.py:100
  70.8 12.0 %copy.29 = f32[16,24,8,256]{0,2,3,1:T(8,128)} copy(f32[16,24,8,256]{3,2,1,0:T(8,128)S(1)} %fusion.6) | data formatting | bytes 6291456 | tf_op jit(solution)/shard_map/add | solution.py:100
  82.9 10.1 %reduce_sum.9 = f32[16,6,8,64]{0,2,3,1:T(8,128)S(1)} reduce(f32[16,6,4,8,64,4]{0,3,5,4,2,1:T(8,128)} %bitcast.36, f32[]{:T(128)} %constant.53.clone.1), dimensions={2,5}, to_apply=%region_0.1 | reduce | flops 737280 | bytes 3342340 | tf_op jit(solution)/shard_map/reduce_sum | solution.py:102
  93.7 8.5 %all_gather.3 = f32[64,3072]{1,0:T(8,128)S(1)} all-gather(f32[16,3072]{1,0:T(8,128)S(1)} %div.18), channel_id=1, replica_groups=mesh['lon'=64,'probe'=4] {'probe'}, dimensions={0}, use_global_device_ids=true | all-gather | bytes 983040 | tf_op jit(solution)/shard_map/all_gather | solution.py:108
  103.1 5.4 %collective-permute-done.9 = f32[64,64]{0,1:T(8,128)S(1)} collective-permute-done((f32[64,64]{0,1:T(8,128)S(1)}, f32[64,64]{0,1:T(8,128)S(1)}, u32[]{:S(2)}, u32[]{:S(2)}) %collective-permute-start.9) | collective-permute-done | bytes 16416 | tf_op jit(solution)/shard_map/ppermute | solution.py:20
  108.5 3.9 %collective-permute-done.10 = f32[64,64]{0,1:T(8,128)S(1)} collective-permute-done((f32[64,64]{0,1:T(8,128)S(1)}, f32[64,64]{0,1:T(8,128)S(1)}, u32[]{:S(2)}, u32[]{:S(2)}) %collective-permute-start.10) | collective-permute-done | bytes 16416 | tf_op jit(solution)/shard_map/ppermute | solution.py:20
  112.4 5.4 %collective-permute-done.11 = f32[64,64]{0,1:T(8,128)S(1)} collective-permute-done((f32[64,64]{0,1:T(8,128)S(1)}, f32[64,64]{0,1:T(8,128)S(1)}, u32[]{:S(2)}, u32[]{:S(2)}) %collective-permute-start.11) | collective-permute-done | bytes 16416 | tf_op jit(solution)/shard_map/ppermute | solution.py:20
  117.8 4.2 %collective-permute-done.12 = f32[64,64]{0,1:T(8,128)S(1)} collective-permute-done((f32[64,64]{0,1:T(8,128)S(1)}, f32[64,64]{0,1:T(8,128)S(1)}, u32[]{:S(2)}, u32[]{:S(2)}) %collective-permute-start.12) | collective-permute-done | bytes 16416 | tf_op jit(solution)/shard_map/ppermute | solution.py:20
  122.0 4.8 %collective-permute-done.13 = f32[64,64]{0,1:T(8,128)S(1)} collective-permute-done((f32[64,64]{0,1:T(8,128)S(1)}, f32[64,64]{0,1:T(8,128)S(1)}, u32[]{:S(2)}, u32[]{:S(2)}) %collective-permute-start.13) | collective-permute-done | bytes 16416 | tf_op jit(solution)/shard_map/ppermute | solution.py:20
  126.8 1.5 collective-permute-start.14
  128.3 6.3 %collective-permute-done.14 = f32[64,64]{0,1:T(8,128)S(1)} collective-permute-done((f32[64,64]{0,1:T(8,128)S(1)}, f32[64,64]{0,1:T(8,128)S(1)}, u32[]{:S(2)}, u32[]{:S(2)}) %collective-permute-start.14) | collective-permute-done | bytes 16416 | tf_op jit(solution)/shard_map/ppermute | solution.py:20
  134.7 5.8 %cholesky.17 = f32[64,64]{1,0:T(8,128)S(1)} custom-call(f32[64,64]{1,0:T(8,128)S(1)} %fusion.24), custom_call_target="Cholesky" | custom-call | tf_op jit(solution)/shard_map/jit(cholesky)/cholesky | solution.py:116
  141.9 4.9 %custom-call.6 = f32[1,64,64]{1,2,0:T(8,128)S(1)} custom-call(f32[1,64,64]{2,1,0:T(8,128)S(1)} %get-tuple-element.34), custom_call_target="InvertDiagBlocksLowerTriangular" | custom-call | tf_op jit(solution)/shard_map/triangular_solve | solution.py:117
  (66 shorter events, 8.7 us)
Async XLA Ops:
  1.3 25.4 %collective-permute-start = (f32[1,8,256]{2,1,0:T(8,128)S(1)}, f32[1,8,256]{2,1,0:T(8,128)S(1)}, u32[]{:S(2)}, u32[]{:S(2)}) collective-permute-start(f32[1,8,256]{2,1,0:T(8,128)S(1)} %slice_bitcast_fusion.1), channel_id=1, source_target_pairs={{4,0},{8,4},{12,8},{16,12},{20,16},{24,20},{28,24},{32,28},{36,32}... | collective-permute-start | bytes 24584 | tf_op jit(solution)/shard_map/ppermute | solution.py:10
  12.1 14.9 %collective-permute-start.1 = (f32[16,1,8,256]{3,2,1,0:T(8,128)S(1)}, f32[16,1,8,256]{3,2,1,0:T(8,128)S(1)}, u32[]{:S(2)}, u32[]{:S(2)}) collective-permute-start(f32[16,1,8,256]{3,2,1,0:T(8,128)S(1)} %get-tuple-element.23), channel_id=1, source_target_pairs={{0,4},{4,8},{8,12},{12,16},{16,20},{20,24},{24,28},{28,32},{32,36}... | collective-permute-start | bytes 393224 | tf_op jit(solution)/shard_map/ppermute | solution.py:31
  12.2 14.8 %collective-permute-start.2 = (f32[16,1,8,256]{3,2,1,0:T(8,128)S(1)}, f32[16,1,8,256]{3,2,1,0:T(8,128)S(1)}, u32[]{:S(2)}, u32[]{:S(2)}) collective-permute-start(f32[16,1,8,256]{3,2,1,0:T(8,128)S(1)} %get-tuple-element.22), channel_id=1, source_target_pairs={{4,0},{8,4},{12,8},{16,12},{20,16},{24,20},{28,24},{32,28},{36,32}... | collective-permute-start | bytes 393224 | tf_op jit(solution)/shard_map/ppermute | solution.py:34
  25.8 1.1 copy-start.7
  25.8 2.0 %copy-start = (f32[16,24,8,256]{3,2,1,0:T(8,128)S(1)}, f32[16,24,8,256]{3,2,1,0:T(8,128)}, u32[]{:S(2)}) copy-start(f32[16,24,8,256]{3,2,1,0:T(8,128)} %param.3) | copy-start | bytes 9437188
  27.0 28.2 %copy-start.1 = (f32[24,8,256]{2,1,0:T(8,128)}, f32[24,8,256]{2,1,0:T(8,128)S(1)}, u32[]{:S(2)}) copy-start(f32[24,8,256]{2,1,0:T(8,128)S(1)} %get-tuple-element.28) | copy-start | bytes 589828
  27.0 28.2 %copy-start.3 = (f32[24,8,256]{2,1,0:T(8,128)}, f32[24,8,256]{2,1,0:T(8,128)S(1)}, u32[]{:S(2)}) copy-start(f32[24,8,256]{2,1,0:T(8,128)S(1)} %get-tuple-element.29) | copy-start | bytes 589828
  27.0 28.2 %copy-start.5 = (f32[24,8,256]{2,1,0:T(8,128)}, f32[24,8,256]{2,1,0:T(8,128)S(1)}, u32[]{:S(2)}) copy-start(f32[24,8,256]{2,1,0:T(8,128)S(1)} %get-tuple-element.32) | copy-start | bytes 589828
  29.3 11.3 %collective-permute-start.3 = (f32[16,1,8,256]{3,2,1,0:T(8,128)S(1)}, f32[16,1,8,256]{3,2,1,0:T(8,128)S(1)}, u32[]{:S(2)}, u32[]{:S(2)}) collective-permute-start(f32[16,1,8,256]{3,2,1,0:T(8,128)S(1)} %get-tuple-element.21), channel_id=1, source_target_pairs={{0,4},{4,8},{8,12},{12,16},{16,20},{20,24},{24,28},{28,32},{32,36}... | collective-permute-start | bytes 393224 | tf_op jit(solution)/shard_map/ppermute | solution.py:31
  29.3 11.2 %collective-permute-start.4 = (f32[16,1,8,256]{3,2,1,0:T(8,128)S(1)}, f32[16,1,8,256]{3,2,1,0:T(8,128)S(1)}, u32[]{:S(2)}, u32[]{:S(2)}) collective-permute-start(f32[16,1,8,256]{3,2,1,0:T(8,128)S(1)} %get-tuple-element.20), channel_id=1, source_target_pairs={{4,0},{8,4},{12,8},{16,12},{20,16},{24,20},{28,24},{32,28},{36,32}... | collective-permute-start | bytes 393224 | tf_op jit(solution)/shard_map/ppermute | solution.py:34
  40.6 0.9 copy-start.8
  44.4 10.8 %collective-permute-start.5 = (f32[16,1,8,256]{3,2,1,0:T(8,128)S(1)}, f32[16,1,8,256]{3,2,1,0:T(8,128)S(1)}, u32[]{:S(2)}, u32[]{:S(2)}) collective-permute-start(f32[16,1,8,256]{3,2,1,0:T(8,128)S(1)} %get-tuple-element.18), channel_id=1, source_target_pairs={{0,4},{4,8},{8,12},{12,16},{16,20},{20,24},{24,28},{28,32},{32,36}... | collective-permute-start | bytes 393224 | tf_op jit(solution)/shard_map/ppermute | solution.py:31
  44.5 10.7 %collective-permute-start.6 = (f32[16,1,8,256]{3,2,1,0:T(8,128)S(1)}, f32[16,1,8,256]{3,2,1,0:T(8,128)S(1)}, u32[]{:S(2)}, u32[]{:S(2)}) collective-permute-start(f32[16,1,8,256]{3,2,1,0:T(8,128)S(1)} %get-tuple-element.19), channel_id=1, source_target_pairs={{4,0},{8,4},{12,8},{16,12},{20,16},{24,20},{28,24},{32,28},{36,32}... | collective-permute-start | bytes 393224 | tf_op jit(solution)/shard_map/ppermute | solution.py:34
  57.4 10.8 %collective-permute-start.7 = (f32[16,1,8,256]{3,2,1,0:T(8,128)S(1)}, f32[16,1,8,256]{3,2,1,0:T(8,128)S(1)}, u32[]{:S(2)}, u32[]{:S(2)}) collective-permute-start(f32[16,1,8,256]{3,2,1,0:T(8,128)S(1)} %get-tuple-element.14), channel_id=1, source_target_pairs={{0,4},{4,8},{8,12},{12,16},{16,20},{20,24},{24,28},{28,32},{32,36}... | collective-permute-start | bytes 393224 | tf_op jit(solution)/shard_map/ppermute | solution.py:31
  57.5 10.7 %copy-start.2 = (f32[24,8,256]{2,1,0:T(8,128)S(1)}, f32[24,8,256]{2,1,0:T(8,128)}, u32[]{:S(2)}) copy-start(f32[24,8,256]{2,1,0:T(8,128)} %copy-done.1) | copy-start | bytes 589828
  57.5 10.7 %copy-start.4 = (f32[24,8,256]{2,1,0:T(8,128)S(1)}, f32[24,8,256]{2,1,0:T(8,128)}, u32[]{:S(2)}) copy-start(f32[24,8,256]{2,1,0:T(8,128)} %copy-done.3) | copy-start | bytes 589828
  57.5 10.7 %copy-start.6 = (f32[24,8,256]{2,1,0:T(8,128)S(1)}, f32[24,8,256]{2,1,0:T(8,128)}, u32[]{:S(2)}) copy-start(f32[24,8,256]{2,1,0:T(8,128)} %copy-done.5) | copy-start | bytes 589828
  57.5 10.6 %collective-permute-start.8 = (f32[16,1,8,256]{3,2,1,0:T(8,128)S(1)}, f32[16,1,8,256]{3,2,1,0:T(8,128)S(1)}, u32[]{:S(2)}, u32[]{:S(2)}) collective-permute-start(f32[16,1,8,256]{3,2,1,0:T(8,128)S(1)} %get-tuple-element.15), channel_id=1, source_target_pairs={{4,0},{8,4},{12,8},{16,12},{20,16},{24,20},{28,24},{32,28},{36,32}... | collective-permute-start | bytes 393224 | tf_op jit(solution)/shard_map/ppermute | solution.py:34
  103.0 5.5 %collective-permute-start.9 = (f32[64,64]{0,1:T(8,128)S(1)}, f32[64,64]{0,1:T(8,128)S(1)}, u32[]{:S(2)}, u32[]{:S(2)}) collective-permute-start(f32[64,64]{0,1:T(8,128)S(1)} %fusion.35), channel_id=1, source_target_pairs={{0,4},{4,0},{8,12},{12,8},{16,20},{20,16},{24,28},{28,24},{32,36},... | collective-permute-start | bytes 49160 | tf_op jit(solution)/shard_map/ppermute | solution.py:20
  108.5 3.9 %collective-permute-start.10 = (f32[64,64]{0,1:T(8,128)S(1)}, f32[64,64]{0,1:T(8,128)S(1)}, u32[]{:S(2)}, u32[]{:S(2)}) collective-permute-start(f32[64,64]{0,1:T(8,128)S(1)} %add.96), channel_id=1, source_target_pairs={{0,8},{4,12},{8,0},{12,4},{16,24},{20,28},{24,16},{28,20},{32,40},... | collective-permute-start | bytes 49160 | tf_op jit(solution)/shard_map/ppermute | solution.py:20
  112.4 5.4 %collective-permute-start.11 = (f32[64,64]{0,1:T(8,128)S(1)}, f32[64,64]{0,1:T(8,128)S(1)}, u32[]{:S(2)}, u32[]{:S(2)}) collective-permute-start(f32[64,64]{0,1:T(8,128)S(1)} %add.97), channel_id=1, source_target_pairs={{0,16},{4,20},{8,24},{12,28},{16,0},{20,4},{24,8},{28,12},{32,48},... | collective-permute-start | bytes 49160 | tf_op jit(solution)/shard_map/ppermute | solution.py:20
  117.8 4.2 %collective-permute-start.12 = (f32[64,64]{0,1:T(8,128)S(1)}, f32[64,64]{0,1:T(8,128)S(1)}, u32[]{:S(2)}, u32[]{:S(2)}) collective-permute-start(f32[64,64]{0,1:T(8,128)S(1)} %add.98), channel_id=1, source_target_pairs={{0,32},{4,36},{8,40},{12,44},{16,48},{20,52},{24,56},{28,60},{32,0... | collective-permute-start | bytes 49160 | tf_op jit(solution)/shard_map/ppermute | solution.py:20
  122.0 4.8 %collective-permute-start.13 = (f32[64,64]{0,1:T(8,128)S(1)}, f32[64,64]{0,1:T(8,128)S(1)}, u32[]{:S(2)}, u32[]{:S(2)}) collective-permute-start(f32[64,64]{0,1:T(8,128)S(1)} %add.99), channel_id=1, source_target_pairs={{0,64},{4,68},{8,72},{12,76},{16,80},{20,84},{24,88},{28,92},{32,9... | collective-permute-start | bytes 49160 | tf_op jit(solution)/shard_map/ppermute | solution.py:20
  126.8 7.8 %collective-permute-start.14 = (f32[64,64]{0,1:T(8,128)S(1)}, f32[64,64]{0,1:T(8,128)S(1)}, u32[]{:S(2)}, u32[]{:S(2)}) collective-permute-start(f32[64,64]{0,1:T(8,128)S(1)} %add.100), channel_id=1, source_target_pairs={{0,128},{4,132},{8,136},{12,140},{16,144},{20,148},{24,152},{28,15... | collective-permute-start | bytes 49160 | tf_op jit(solution)/shard_map/ppermute | solution.py:20

commit v2 on v1

--- a/solution.py
+++ b/solution.py
@@ -10,15 +10,21 @@
     return lax.ppermute(block, axis, route)
 
 
-def butterfly_sum(block, axis):
+def butterfly_sum(block, axis, radix=8):
     count = lax.axis_size(axis)
     if count & (count - 1):
         return lax.psum(block, axis)
-    distance = 1
-    while distance < count:
-        route = [(i, i ^ distance) for i in range(count)]
-        block = block + lax.ppermute(block, axis, route)
-        distance *= 2
+    stride = 1
+    while stride < count:
+        width = min(radix, count // stride)
+        terms = [block]
+        for j in range(1, width):
+            route = [(i, i ^ (j * stride)) for i in range(count)]
+            terms.append(lax.ppermute(block, axis, route))
+        while len(terms) > 1:
+            terms = [terms[k] + terms[k + 1] for k in range(0, len(terms), 2)]
+        block = terms[0]
+        stride *= width
     return block
 
 

time: 149 us -> 157 us (1.054); the launches traced: 149 us -> 154 us
  starting transfers between devices: 42.7 us -> 70.9 us
  waiting for transfers between devices: 33.5 us -> 10.5 us
    ppermute x6 -> x14, starting transfers between devices: 1.58 us -> 29.8 us  [butterfly_sum(): terms.append(lax.ppermute(block, axis, route))]
    ppermute x6 -> x14, waiting for transfers between devices: 30 us -> 7.01 us  [butterfly_sum(): terms.append(lax.ppermute(block, axis, route))]
  transfers between devices with their start and end apart: 15 -> 23, of which waited for: 8 -> 7; matrix products, arithmetic and copies ran while one was open for 9% -> 9% of each run, Pallas kernels for 0% -> 0%
where the time goes in v2:
time: 157 us; the launch traced here: 154 us
  starting transfers between devices  70.9 us (45%)
  other arithmetic  38.7 us (25%)
  local copies, waits for them, and re-layouts  23.2 us (15%)
  waiting for transfers between devices  10.5 us (7%)
  blocking collectives  8.45 us (5%)
    ppermute x4, starting transfers between devices, padded(): lax.ppermute(lax.slice_in_dim(block, 0, width, axis=dim), axis, backward)  31 us
    ppermute x14, starting transfers between devices, butterfly_sum(): terms.append(lax.ppermute(block, axis, route))  29.8 us
    add x1, local copies, waits for them, and re-layouts, body(): sketch = increments + state  12.2 us
    reduce_sum x1, other arithmetic, body(): jnp.mean(sketch.reshape(probe_count, lon_count // 4, 4, level_count, lat_...  10.1 us
    ppermute x1, starting transfers between devices, from_behind(): return lax.ppermute(block, axis, route)  9.78 us
    all_gather x1, blocking collectives, body(): full_panel = lax.all_gather(coarse, 'probe', axis=0, tiled=True)  8.45 us
    ppermute x14, waiting for transfers between devices, butterfly_sum(): terms.append(lax.ppermute(block, axis, route))  7.01 us
    another operation x3, other arithmetic, body(): lower = jnp.linalg.cholesky(gram)  6.52 us
  transfers between devices with their start and end apart: 23, of which 7 were waited for; matrix products, arithmetic and copies ran while one was open for 9% of the time, Pallas kernels for 0%

profile of v2, /device:TPU:8, one launch (start us, length us, event | category | flops | bytes accessed | tf_op | source)
XLA Modules:
  0.0 154.3 jit_solution(6683204837433735403)
XLA Ops:
  1.3 9.8 %collective-permute-start = (f32[1,8,256]{2,1,0:T(8,128)S(1)}, f32[1,8,256]{2,1,0:T(8,128)S(1)}, u32[]{:S(2)}, u32[]{:S(2)}) collective-permute-start(f32[1,8,256]{2,1,0:T(8,128)S(1)} %slice_bitcast_fusion.1), channel_id=1, source_target_pairs={{4,0},{8,4},{12,8},{16,12},{20,16},{24,20},{28,24},{32,28},{36,32}... | collective-permute-start | bytes 24584 | tf_op jit(solution)/shard_map/ppermute | solution.py:10
  11.1 1.0 fusion.34
  12.2 7.7 %collective-permute-start.2 = (f32[16,1,8,256]{3,2,1,0:T(8,128)S(1)}, f32[16,1,8,256]{3,2,1,0:T(8,128)S(1)}, u32[]{:S(2)}, u32[]{:S(2)}) collective-permute-start(f32[16,1,8,256]{3,2,1,0:T(8,128)S(1)} %get-tuple-element.22), channel_id=1, source_target_pairs={{4,0},{8,4},{12,8},{16,12},{20,16},{24,20},{28,24},{32,28},{36,32}... | collective-permute-start | bytes 393224 | tf_op jit(solution)/shard_map/ppermute | solution.py:40
  19.9 1.1 maximum_bitcast_fusion
  21.9 3.7 %multiply_add_fusion.1 = f32[16,24,8,256]{3,2,1,0:T(8,128)S(1)} fusion(f32[16,24,8,256]{3,2,1,0:T(8,128)} %param.3, f32[16,24,8,255]{3,2,1,0:T(8,128)} %bitcast.37, f32[24,8,256]{2,1,0:T(8,128)S(1)} %get-tuple-element.25, f32[24,8,256]{2,1,0:T(8,128)S(1)} %get-tuple-element.24), kind=kLoop, calls=%fused_computation.31 | loop fusion | flops 2359296 | bytes 9818112 | tf_op jit(solution)/shard_map/add | solution.py:65
  28.2 1.0 fusion.19
  29.3 7.7 %collective-permute-start.4 = (f32[16,1,8,256]{3,2,1,0:T(8,128)S(1)}, f32[16,1,8,256]{3,2,1,0:T(8,128)S(1)}, u32[]{:S(2)}, u32[]{:S(2)}) collective-permute-start(f32[16,1,8,256]{3,2,1,0:T(8,128)S(1)} %get-tuple-element.20), channel_id=1, source_target_pairs={{4,0},{8,4},{12,8},{16,12},{20,16},{24,20},{28,24},{32,28},{36,32}... | collective-permute-start | bytes 393224 | tf_op jit(solution)/shard_map/ppermute | solution.py:40
  37.1 1.0 multiply_add_fusion
  38.1 2.5 %slice.170 = f32[16,24,8,255]{3,2,1,0:T(8,128)} slice(f32[16,24,8,256]{3,2,1,0:T(8,128)S(1)} %multiply_add_fusion), slice={[0:16], [0:24], [0:8], [1:256]} | slice | bytes 6266880 | tf_op jit(solution)/shard_map/slice | solution.py:55
  41.5 2.8 %fusion.17 = f32[16,24,8,256]{3,2,1,0:T(8,128)S(1)} fusion(f32[16,24,8,256]{3,2,1,0:T(8,128)S(1)} %fusion.19, f32[16,25,8,256]{3,2,1,0:T(8,128)S(1)} %fusion.1, f32[16,24,8,256]{3,2,1,0:T(8,128)S(1)} %multiply_add_fusion, f32[16,24,8,255]{3,2,1,0:T(8,128)} %slice.170, f32[24,8,256]{2,1,0:T(8,128)S(1)} %copy-done.8), kind=kLoop, calls=%fused_computation.26 | loop fusion | flops 3932160 | bytes 19058688 | tf_op jit(solution)/shard_map/mul | solution.py:103
  44.5 7.7 %collective-permute-start.6 = (f32[16,1,8,256]{3,2,1,0:T(8,128)S(1)}, f32[16,1,8,256]{3,2,1,0:T(8,128)S(1)}, u32[]{:S(2)}, u32[]{:S(2)}) collective-permute-start(f32[16,1,8,256]{3,2,1,0:T(8,128)S(1)} %get-tuple-element.19), channel_id=1, source_target_pairs={{4,0},{8,4},{12,8},{16,12},{20,16},{24,20},{28,24},{32,28},{36,32}... | collective-permute-start | bytes 393224 | tf_op jit(solution)/shard_map/ppermute | solution.py:40
  52.2 1.1 fusion.31
  53.3 1.8 %collective-permute-done.5 = f32[16,1,8,256]{3,2,1,0:T(8,128)S(1)} collective-permute-done((f32[16,1,8,256]{3,2,1,0:T(8,128)S(1)}, f32[16,1,8,256]{3,2,1,0:T(8,128)S(1)}, u32[]{:S(2)}, u32[]{:S(2)}) %collective-permute-start.5) | collective-permute-done | bytes 131104 | tf_op jit(solution)/shard_map/ppermute | solution.py:37
  55.2 2.2 %fusion.12 = f32[16,24,8,256]{3,2,1,0:T(8,128)S(1)} fusion(f32[16,1,8,256]{3,2,1,0:T(8,128)S(1)} %collective-permute-done.6, f32[16,24,8,256]{3,2,1,0:T(8,128)S(1)} %fusion.17, f32[16,1,8,256]{3,2,1,0:T(8,128)S(1)} %collective-permute-done.5, f32[16,24,8,255]{3,2,1,0:T(8,128)S(1)} %get-tuple-element.17, f32[16,24,8,255]{3,2,1,0:T(8,128)S(1)} %get-tuple-element.16, ...), kind=kLoop, calls=%fused_computation.19 | loop fusion | flops 8650752 | bytes 13803520 | tf_op jit(solution)/shard_map/add | solution.py:81
  57.5 7.8 %collective-permute-start.8 = (f32[16,1,8,256]{3,2,1,0:T(8,128)S(1)}, f32[16,1,8,256]{3,2,1,0:T(8,128)S(1)}, u32[]{:S(2)}, u32[]{:S(2)}) collective-permute-start(f32[16,1,8,256]{3,2,1,0:T(8,128)S(1)} %get-tuple-element.15), channel_id=1, source_target_pairs={{4,0},{8,4},{12,8},{16,12},{20,16},{24,20},{28,24},{32,28},{36,32}... | collective-permute-start | bytes 393224 | tf_op jit(solution)/shard_map/ppermute | solution.py:40
  65.3 1.2 fusion.29
  66.5 1.7 %collective-permute-done.7 = f32[16,1,8,256]{3,2,1,0:T(8,128)S(1)} collective-permute-done((f32[16,1,8,256]{3,2,1,0:T(8,128)S(1)}, f32[16,1,8,256]{3,2,1,0:T(8,128)S(1)}, u32[]{:S(2)}, u32[]{:S(2)}) %collective-permute-start.7) | collective-permute-done | bytes 131104 | tf_op jit(solution)/shard_map/ppermute | solution.py:37
  68.2 2.6 %fusion.6 = f32[16,24,8,256]{3,2,1,0:T(8,128)S(1)} fusion(f32[16,24,8,256]{3,2,1,0:T(8,128)S(1)} %copy-done, f32[16,1,8,256]{3,2,1,0:T(8,128)S(1)} %collective-permute-done.8, f32[16,24,8,256]{3,2,1,0:T(8,128)S(1)} %fusion.12, f32[16,1,8,256]{3,2,1,0:T(8,128)S(1)} %collective-permute-done.7, f32[16,24,8,255]{3,2,1,0:T(8,128)S(1)} %get-tuple-element.13, ...), kind=kLoop, calls=%fused_computation.11 | loop fusion | flops 9437184 | bytes 16949248 | tf_op jit(solution)/shard_map/add | solution.py:106
  70.8 12.2 %copy.53 = f32[16,24,8,256]{0,2,3,1:T(8,128)} copy(f32[16,24,8,256]{3,2,1,0:T(8,128)S(1)} %fusion.6) | data formatting | bytes 6291456 | tf_op jit(solution)/shard_map/add | solution.py:106
  83.1 10.1 %reduce_sum.9 = f32[16,6,8,64]{0,2,3,1:T(8,128)S(1)} reduce(f32[16,6,4,8,64,4]{0,3,5,4,2,1:T(8,128)} %bitcast.36, f32[]{:T(128)} %constant.53.clone.1), dimensions={2,5}, to_apply=%region_0.1 | reduce | flops 737280 | bytes 3342340 | tf_op jit(solution)/shard_map/reduce_sum | solution.py:108
  93.9 8.5 %all_gather.3 = f32[64,3072]{1,0:T(8,128)S(1)} all-gather(f32[16,3072]{1,0:T(8,128)S(1)} %div.18), channel_id=1, replica_groups=mesh['lon'=64,'probe'=4] {'probe'}, dimensions={0}, use_global_device_ids=true | all-gather | bytes 983040 | tf_op jit(solution)/shard_map/all_gather | solution.py:114
  103.5 7.7 %collective-permute-start.13 = (f32[64,64]{0,1:T(8,128)S(1)}, f32[64,64]{0,1:T(8,128)S(1)}, u32[]{:S(2)}, u32[]{:S(2)}) collective-permute-start(f32[64,64]{0,1:T(8,128)S(1)} %fusion.35), channel_id=1, source_target_pairs={{0,20},{4,16},{8,28},{12,24},{16,4},{20,0},{24,12},{28,8},{32,52},... | collective-permute-start | bytes 49160 | tf_op jit(solution)/shard_map/ppermute | solution.py:23
  111.2 1.4 collective-permute-start.15
  112.6 4.8 %collective-permute-start.9 = (f32[64,64]{0,1:T(8,128)S(1)}, f32[64,64]{0,1:T(8,128)S(1)}, u32[]{:S(2)}, u32[]{:S(2)}) collective-permute-start(f32[64,64]{0,1:T(8,128)S(1)} %fusion.35), channel_id=1, source_target_pairs={{0,4},{4,0},{8,12},{12,8},{16,20},{20,16},{24,28},{28,24},{32,36},... | collective-permute-start | bytes 49160 | tf_op jit(solution)/shard_map/ppermute | solution.py:23
  117.4 1.3 collective-permute-done.15
  119.4 4.5 %collective-permute-start.17 = (f32[64,64]{0,1:T(8,128)S(1)}, f32[64,64]{0,1:T(8,128)S(1)}, u32[]{:S(2)}, u32[]{:S(2)}) collective-permute-start(f32[64,64]{0,1:T(8,128)S(1)} %add_add_fusion.1), channel_id=1, source_target_pairs={{0,64},{4,68},{8,72},{12,76},{16,80},{20,84},{24,88},{28,92},{32,9... | collective-permute-start | bytes 49160 | tf_op jit(solution)/shard_map/ppermute | solution.py:23
  123.9 4.5 %collective-permute-start.19 = (f32[64,64]{0,1:T(8,128)S(1)}, f32[64,64]{0,1:T(8,128)S(1)}, u32[]{:S(2)}, u32[]{:S(2)}) collective-permute-start(f32[64,64]{0,1:T(8,128)S(1)} %add_add_fusion.1), channel_id=1, source_target_pairs={{0,128},{4,132},{8,136},{12,140},{16,144},{20,148},{24,152},{28,15... | collective-permute-start | bytes 49160 | tf_op jit(solution)/shard_map/ppermute | solution.py:23
  128.9 6.0 %collective-permute-start.21 = (f32[64,64]{0,1:T(8,128)S(1)}, f32[64,64]{0,1:T(8,128)S(1)}, u32[]{:S(2)}, u32[]{:S(2)}) collective-permute-start(f32[64,64]{0,1:T(8,128)S(1)} %add_add_fusion.1), channel_id=1, source_target_pairs={{0,192},{4,196},{8,200},{12,204},{16,208},{20,212},{24,216},{28,22... | collective-permute-start | bytes 49160 | tf_op jit(solution)/shard_map/ppermute | solution.py:23
  135.5 1.3 collective-permute-done.21
  136.8 3.2 %collective-permute-done.22 = f32[64,64]{0,1:T(8,128)S(1)} collective-permute-done((f32[64,64]{0,1:T(8,128)S(1)}, f32[64,64]{0,1:T(8,128)S(1)}, u32[]{:S(2)}, u32[]{:S(2)}) %collective-permute-start.22) | collective-permute-done | bytes 16416 | tf_op jit(solution)/shard_map/ppermute | solution.py:23
  140.1 5.8 %cholesky.17 = f32[64,64]{1,0:T(8,128)S(1)} custom-call(f32[64,64]{1,0:T(8,128)S(1)} %fusion.24), custom_call_target="Cholesky" | custom-call | tf_op jit(solution)/shard_map/jit(cholesky)/cholesky | solution.py:122
  147.3 4.9 %custom-call.6 = f32[1,64,64]{1,2,0:T(8,128)S(1)} custom-call(f32[1,64,64]{2,1,0:T(8,128)S(1)} %get-tuple-element.34), custom_call_target="InvertDiagBlocksLowerTriangular" | custom-call | tf_op jit(solution)/shard_map/triangular_solve | solution.py:123
  (78 shorter events, 12.5 us)
Async XLA Ops:
  1.3 25.4 %collective-permute-start = (f32[1,8,256]{2,1,0:T(8,128)S(1)}, f32[1,8,256]{2,1,0:T(8,128)S(1)}, u32[]{:S(2)}, u32[]{:S(2)}) collective-permute-start(f32[1,8,256]{2,1,0:T(8,128)S(1)} %slice_bitcast_fusion.1), channel_id=1, source_target_pairs={{4,0},{8,4},{12,8},{16,12},{20,16},{24,20},{28,24},{32,28},{36,32}... | collective-permute-start | bytes 24584 | tf_op jit(solution)/shard_map/ppermute | solution.py:10
  12.1 14.9 %collective-permute-start.1 = (f32[16,1,8,256]{3,2,1,0:T(8,128)S(1)}, f32[16,1,8,256]{3,2,1,0:T(8,128)S(1)}, u32[]{:S(2)}, u32[]{:S(2)}) collective-permute-start(f32[16,1,8,256]{3,2,1,0:T(8,128)S(1)} %get-tuple-element.23), channel_id=1, source_target_pairs={{0,4},{4,8},{8,12},{12,16},{16,20},{20,24},{24,28},{28,32},{32,36}... | collective-permute-start | bytes 393224 | tf_op jit(solution)/shard_map/ppermute | solution.py:37
  12.2 14.8 %collective-permute-start.2 = (f32[16,1,8,256]{3,2,1,0:T(8,128)S(1)}, f32[16,1,8,256]{3,2,1,0:T(8,128)S(1)}, u32[]{:S(2)}, u32[]{:S(2)}) collective-permute-start(f32[16,1,8,256]{3,2,1,0:T(8,128)S(1)} %get-tuple-element.22), channel_id=1, source_target_pairs={{4,0},{8,4},{12,8},{16,12},{20,16},{24,20},{28,24},{32,28},{36,32}... | collective-permute-start | bytes 393224 | tf_op jit(solution)/shard_map/ppermute | solution.py:40
  25.8 1.1 copy-start.7
  25.8 2.0 %copy-start = (f32[16,24,8,256]{3,2,1,0:T(8,128)S(1)}, f32[16,24,8,256]{3,2,1,0:T(8,128)}, u32[]{:S(2)}) copy-start(f32[16,24,8,256]{3,2,1,0:T(8,128)} %param.3) | copy-start | bytes 9437188
  27.0 28.2 %copy-start.1 = (f32[24,8,256]{2,1,0:T(8,128)}, f32[24,8,256]{2,1,0:T(8,128)S(1)}, u32[]{:S(2)}) copy-start(f32[24,8,256]{2,1,0:T(8,128)S(1)} %get-tuple-element.28) | copy-start | bytes 589828
  27.0 28.2 %copy-start.3 = (f32[24,8,256]{2,1,0:T(8,128)}, f32[24,8,256]{2,1,0:T(8,128)S(1)}, u32[]{:S(2)}) copy-start(f32[24,8,256]{2,1,0:T(8,128)S(1)} %get-tuple-element.29) | copy-start | bytes 589828
  27.0 28.2 %copy-start.5 = (f32[24,8,256]{2,1,0:T(8,128)}, f32[24,8,256]{2,1,0:T(8,128)S(1)}, u32[]{:S(2)}) copy-start(f32[24,8,256]{2,1,0:T(8,128)S(1)} %get-tuple-element.32) | copy-start | bytes 589828
  29.3 11.3 %collective-permute-start.3 = (f32[16,1,8,256]{3,2,1,0:T(8,128)S(1)}, f32[16,1,8,256]{3,2,1,0:T(8,128)S(1)}, u32[]{:S(2)}, u32[]{:S(2)}) collective-permute-start(f32[16,1,8,256]{3,2,1,0:T(8,128)S(1)} %get-tuple-element.21), channel_id=1, source_target_pairs={{0,4},{4,8},{8,12},{12,16},{16,20},{20,24},{24,28},{28,32},{32,36}... | collective-permute-start | bytes 393224 | tf_op jit(solution)/shard_map/ppermute | solution.py:37
  29.3 11.2 %collective-permute-start.4 = (f32[16,1,8,256]{3,2,1,0:T(8,128)S(1)}, f32[16,1,8,256]{3,2,1,0:T(8,128)S(1)}, u32[]{:S(2)}, u32[]{:S(2)}) collective-permute-start(f32[16,1,8,256]{3,2,1,0:T(8,128)S(1)} %get-tuple-element.20), channel_id=1, source_target_pairs={{4,0},{8,4},{12,8},{16,12},{20,16},{24,20},{28,24},{32,28},{36,32}... | collective-permute-start | bytes 393224 | tf_op jit(solution)/shard_map/ppermute | solution.py:40
  40.6 0.9 copy-start.8
  44.4 10.8 %collective-permute-start.5 = (f32[16,1,8,256]{3,2,1,0:T(8,128)S(1)}, f32[16,1,8,256]{3,2,1,0:T(8,128)S(1)}, u32[]{:S(2)}, u32[]{:S(2)}) collective-permute-start(f32[16,1,8,256]{3,2,1,0:T(8,128)S(1)} %get-tuple-element.18), channel_id=1, source_target_pairs={{0,4},{4,8},{8,12},{12,16},{16,20},{20,24},{24,28},{28,32},{32,36}... | collective-permute-start | bytes 393224 | tf_op jit(solution)/shard_map/ppermute | solution.py:37
  44.5 10.7 %collective-permute-start.6 = (f32[16,1,8,256]{3,2,1,0:T(8,128)S(1)}, f32[16,1,8,256]{3,2,1,0:T(8,128)S(1)}, u32[]{:S(2)}, u32[]{:S(2)}) collective-permute-start(f32[16,1,8,256]{3,2,1,0:T(8,128)S(1)} %get-tuple-element.19), channel_id=1, source_target_pairs={{4,0},{8,4},{12,8},{16,12},{20,16},{24,20},{28,24},{32,28},{36,32}... | collective-permute-start | bytes 393224 | tf_op jit(solution)/shard_map/ppermute | solution.py:40
  57.4 10.8 %collective-permute-start.7 = (f32[16,1,8,256]{3,2,1,0:T(8,128)S(1)}, f32[16,1,8,256]{3,2,1,0:T(8,128)S(1)}, u32[]{:S(2)}, u32[]{:S(2)}) collective-permute-start(f32[16,1,8,256]{3,2,1,0:T(8,128)S(1)} %get-tuple-element.14), channel_id=1, source_target_pairs={{0,4},{4,8},{8,12},{12,16},{16,20},{20,24},{24,28},{28,32},{32,36}... | collective-permute-start | bytes 393224 | tf_op jit(solution)/shard_map/ppermute | solution.py:37
  57.5 10.7 %copy-start.2 = (f32[24,8,256]{2,1,0:T(8,128)S(1)}, f32[24,8,256]{2,1,0:T(8,128)}, u32[]{:S(2)}) copy-start(f32[24,8,256]{2,1,0:T(8,128)} %copy-done.1) | copy-start | bytes 589828
  57.5 10.7 %copy-start.4 = (f32[24,8,256]{2,1,0:T(8,128)S(1)}, f32[24,8,256]{2,1,0:T(8,128)}, u32[]{:S(2)}) copy-start(f32[24,8,256]{2,1,0:T(8,128)} %copy-done.3) | copy-start | bytes 589828
  57.5 10.7 %copy-start.6 = (f32[24,8,256]{2,1,0:T(8,128)S(1)}, f32[24,8,256]{2,1,0:T(8,128)}, u32[]{:S(2)}) copy-start(f32[24,8,256]{2,1,0:T(8,128)} %copy-done.5) | copy-start | bytes 589828
  57.5 10.6 %collective-permute-start.8 = (f32[16,1,8,256]{3,2,1,0:T(8,128)S(1)}, f32[16,1,8,256]{3,2,1,0:T(8,128)S(1)}, u32[]{:S(2)}, u32[]{:S(2)}) collective-permute-start(f32[16,1,8,256]{3,2,1,0:T(8,128)S(1)} %get-tuple-element.15), channel_id=1, source_target_pairs={{4,0},{8,4},{12,8},{16,12},{20,16},{24,20},{28,24},{32,28},{36,32}... | collective-permute-start | bytes 393224 | tf_op jit(solution)/shard_map/ppermute | solution.py:40
  103.2 8.1 %collective-permute-start.10 = (f32[64,64]{0,1:T(8,128)S(1)}, f32[64,64]{0,1:T(8,128)S(1)}, u32[]{:S(2)}, u32[]{:S(2)}) collective-permute-start(f32[64,64]{0,1:T(8,128)S(1)} %fusion.35), channel_id=1, source_target_pairs={{0,8},{4,12},{8,0},{12,4},{16,24},{20,28},{24,16},{28,20},{32,40},... | collective-permute-start | bytes 49160 | tf_op jit(solution)/shard_map/ppermute | solution.py:23
  103.3 9.4 %collective-permute-start.11 = (f32[64,64]{0,1:T(8,128)S(1)}, f32[64,64]{0,1:T(8,128)S(1)}, u32[]{:S(2)}, u32[]{:S(2)}) collective-permute-start(f32[64,64]{0,1:T(8,128)S(1)} %fusion.35), channel_id=1, source_target_pairs={{0,12},{4,8},{8,4},{12,0},{16,28},{20,24},{24,20},{28,16},{32,44},... | collective-permute-start | bytes 49160 | tf_op jit(solution)/shard_map/ppermute | solution.py:23
  103.4 14.1 %collective-permute-start.12 = (f32[64,64]{0,1:T(8,128)S(1)}, f32[64,64]{0,1:T(8,128)S(1)}, u32[]{:S(2)}, u32[]{:S(2)}) collective-permute-start(f32[64,64]{0,1:T(8,128)S(1)} %fusion.35), channel_id=1, source_target_pairs={{0,16},{4,20},{8,24},{12,28},{16,0},{20,4},{24,8},{28,12},{32,48},... | collective-permute-start | bytes 49160 | tf_op jit(solution)/shard_map/ppermute | solution.py:23
  103.5 14.0 %collective-permute-start.13 = (f32[64,64]{0,1:T(8,128)S(1)}, f32[64,64]{0,1:T(8,128)S(1)}, u32[]{:S(2)}, u32[]{:S(2)}) collective-permute-start(f32[64,64]{0,1:T(8,128)S(1)} %fusion.35), channel_id=1, source_target_pairs={{0,20},{4,16},{8,28},{12,24},{16,4},{20,0},{24,12},{28,8},{32,52},... | collective-permute-start | bytes 49160 | tf_op jit(solution)/shard_map/ppermute | solution.py:23
  111.2 6.2 %collective-permute-start.14 = (f32[64,64]{0,1:T(8,128)S(1)}, f32[64,64]{0,1:T(8,128)S(1)}, u32[]{:S(2)}, u32[]{:S(2)}) collective-permute-start(f32[64,64]{0,1:T(8,128)S(1)} %fusion.35), channel_id=1, source_target_pairs={{0,24},{4,28},{8,16},{12,20},{16,8},{20,12},{24,0},{28,4},{32,56},... | collective-permute-start | bytes 49160 | tf_op jit(solution)/shard_map/ppermute | solution.py:23
  111.2 7.5 %collective-permute-start.15 = (f32[64,64]{0,1:T(8,128)S(1)}, f32[64,64]{0,1:T(8,128)S(1)}, u32[]{:S(2)}, u32[]{:S(2)}) collective-permute-start(f32[64,64]{0,1:T(8,128)S(1)} %fusion.35), channel_id=1, source_target_pairs={{0,28},{4,24},{8,20},{12,16},{16,12},{20,8},{24,4},{28,0},{32,60},... | collective-permute-start | bytes 49160 | tf_op jit(solution)/shard_map/ppermute | solution.py:23
  112.6 6.7 %collective-permute-start.9 = (f32[64,64]{0,1:T(8,128)S(1)}, f32[64,64]{0,1:T(8,128)S(1)}, u32[]{:S(2)}, u32[]{:S(2)}) collective-permute-start(f32[64,64]{0,1:T(8,128)S(1)} %fusion.35), channel_id=1, source_target_pairs={{0,4},{4,0},{8,12},{12,8},{16,20},{20,16},{24,28},{28,24},{32,36},... | collective-permute-start | bytes 49160 | tf_op jit(solution)/shard_map/ppermute | solution.py:23
  119.3 9.6 %collective-permute-start.16 = (f32[64,64]{0,1:T(8,128)S(1)}, f32[64,64]{0,1:T(8,128)S(1)}, u32[]{:S(2)}, u32[]{:S(2)}) collective-permute-start(f32[64,64]{0,1:T(8,128)S(1)} %add_add_fusion.1), channel_id=1, source_target_pairs={{0,32},{4,36},{8,40},{12,44},{16,48},{20,52},{24,56},{28,60},{32,0... | collective-permute-start | bytes 49160 | tf_op jit(solution)/shard_map/ppermute | solution.py:23
  119.4 15.5 %collective-permute-start.17 = (f32[64,64]{0,1:T(8,128)S(1)}, f32[64,64]{0,1:T(8,128)S(1)}, u32[]{:S(2)}, u32[]{:S(2)}) collective-permute-start(f32[64,64]{0,1:T(8,128)S(1)} %add_add_fusion.1), channel_id=1, source_target_pairs={{0,64},{4,68},{8,72},{12,76},{16,80},{20,84},{24,88},{28,92},{32,9... | collective-permute-start | bytes 49160 | tf_op jit(solution)/shard_map/ppermute | solution.py:23
  123.9 11.0 %collective-permute-start.18 = (f32[64,64]{0,1:T(8,128)S(1)}, f32[64,64]{0,1:T(8,128)S(1)}, u32[]{:S(2)}, u32[]{:S(2)}) collective-permute-start(f32[64,64]{0,1:T(8,128)S(1)} %add_add_fusion.1), channel_id=1, source_target_pairs={{0,96},{4,100},{8,104},{12,108},{16,112},{20,116},{24,120},{28,124... | collective-permute-start | bytes 49160 | tf_op jit(solution)/shard_map/ppermute | solution.py:23
  123.9 11.0 %collective-permute-start.19 = (f32[64,64]{0,1:T(8,128)S(1)}, f32[64,64]{0,1:T(8,128)S(1)}, u32[]{:S(2)}, u32[]{:S(2)}) collective-permute-start(f32[64,64]{0,1:T(8,128)S(1)} %add_add_fusion.1), channel_id=1, source_target_pairs={{0,128},{4,132},{8,136},{12,140},{16,144},{20,148},{24,152},{28,15... | collective-permute-start | bytes 49160 | tf_op jit(solution)/shard_map/ppermute | solution.py:23
  128.4 7.1 %collective-permute-start.20 = (f32[64,64]{0,1:T(8,128)S(1)}, f32[64,64]{0,1:T(8,128)S(1)}, u32[]{:S(2)}, u32[]{:S(2)}) collective-permute-start(f32[64,64]{0,1:T(8,128)S(1)} %add_add_fusion.1), channel_id=1, source_target_pairs={{0,160},{4,164},{8,168},{12,172},{16,176},{20,180},{24,184},{28,18... | collective-permute-start | bytes 49160 | tf_op jit(solution)/shard_map/ppermute | solution.py:23
  128.9 7.8 %collective-permute-start.21 = (f32[64,64]{0,1:T(8,128)S(1)}, f32[64,64]{0,1:T(8,128)S(1)}, u32[]{:S(2)}, u32[]{:S(2)}) collective-permute-start(f32[64,64]{0,1:T(8,128)S(1)} %add_add_fusion.1), channel_id=1, source_target_pairs={{0,192},{4,196},{8,200},{12,204},{16,208},{20,212},{24,216},{28,22... | collective-permute-start | bytes 49160 | tf_op jit(solution)/shard_map/ppermute | solution.py:23
  134.9 5.1 %collective-permute-start.22 = (f32[64,64]{0,1:T(8,128)S(1)}, f32[64,64]{0,1:T(8,128)S(1)}, u32[]{:S(2)}, u32[]{:S(2)}) collective-permute-start(f32[64,64]{0,1:T(8,128)S(1)} %add_add_fusion.1), channel_id=1, source_target_pairs={{0,224},{4,228},{8,232},{12,236},{16,240},{20,244},{24,248},{28,25... | collective-permute-start | bytes 49160 | tf_op jit(solution)/shard_map/ppermute | solution.py:23

commit v3 on v2

--- a/solution.py
+++ b/solution.py
@@ -1,7 +1,13 @@
+import functools
+
 import jax
 import jax.numpy as jnp
 from jax import lax
+from jax.experimental import pallas as pl
+from jax.experimental.pallas import tpu as pltpu
 from jax.sharding import PartitionSpec as P
+
+MESH = pl.DeviceIdType.MESH
 
 
 def from_behind(block, axis, distance):
@@ -10,22 +16,71 @@
     return lax.ppermute(block, axis, route)
 
 
-def butterfly_sum(block, axis, radix=8):
-    count = lax.axis_size(axis)
-    if count & (count - 1):
-        return lax.psum(block, axis)
+def exchange_kernel(count, radix, block_ref, out_ref, held, current, send_sem, recv_sem):
+    me = lax.axis_index("lon")
+    rounds = []
     stride = 1
     while stride < count:
         width = min(radix, count // stride)
-        terms = [block]
+        rounds.append((stride, width))
+        stride *= width
+    partners = [me ^ (j * stride) for stride, width in rounds for j in range(1, width)]
+
+    barrier = pltpu.get_barrier_semaphore()
+    for partner in partners:
+        pl.semaphore_signal(barrier, inc=1, device_id={"lon": partner}, device_id_type=MESH)
+    pl.semaphore_wait(barrier, len(partners))
+
+    current[0] = block_ref[...]
+    slot = 0
+    for step, (stride, width) in enumerate(rounds):
+        copies = []
         for j in range(1, width):
-            route = [(i, i ^ (j * stride)) for i in range(count)]
-            terms.append(lax.ppermute(block, axis, route))
+            copy = pltpu.make_async_remote_copy(
+                src_ref=current.at[step],
+                dst_ref=held.at[slot + j - 1],
+                send_sem=send_sem.at[slot + j - 1],
+                recv_sem=recv_sem.at[slot + j - 1],
+                device_id={"lon": me ^ (j * stride)},
+                device_id_type=MESH,
+            )
+            copy.start()
+            copies.append(copy)
+        for copy in copies:
+            copy.wait()
+        terms = [current[step]] + [held[slot + j - 1] for j in range(1, width)]
         while len(terms) > 1:
             terms = [terms[k] + terms[k + 1] for k in range(0, len(terms), 2)]
-        block = terms[0]
+        current[step + 1] = terms[0]
+        slot += width - 1
+    out_ref[...] = current[len(rounds)]
+
+
+def butterfly_sum(block, axis, radix=4):
+    count = lax.axis_size(axis)
+    if count & (count - 1) or count < 2:
+        return lax.psum(block, axis)
+    rounds = 0
+    slots = 0
+    stride = 1
+    while stride < count:
+        width = min(radix, count // stride)
+        rounds += 1
+        slots += width - 1
         stride *= width
-    return block
+    return pl.pallas_call(
+        functools.partial(exchange_kernel, count, radix),
+        out_shape=jax.ShapeDtypeStruct(block.shape, block.dtype),
+        in_specs=[pl.BlockSpec(memory_space=pltpu.VMEM)],
+        out_specs=pl.BlockSpec(memory_space=pltpu.VMEM),
+        scratch_shapes=[
+            pltpu.VMEM((slots,) + block.shape, block.dtype),
+            pltpu.VMEM((rounds + 1,) + block.shape, block.dtype),
+            pltpu.SemaphoreType.DMA((slots,)),
+            pltpu.SemaphoreType.DMA((slots,)),
+        ],
+        compiler_params=pltpu.CompilerParams(collective_id=0, has_side_effects=True),
+    )(block)
 
 
 def padded(block, sides, width):

time: 157 us -> 152 us (0.968); the launches traced: 154 us -> 152 us
  starting transfers between devices: 70.9 us -> 41.1 us
  Pallas kernels: 0 us -> 21.9 us
  waiting for transfers between devices: 10.5 us -> 3.54 us
  local copies, waits for them, and re-layouts: 23.2 us -> 29.3 us
  other arithmetic: 38.7 us -> 44.3 us
    ppermute x14 -> x0, starting transfers between devices: 29.8 us -> none  [butterfly_sum(): terms.append(lax.ppermute(block, axis, route))]
    pallas_call x0 -> x1, Pallas kernels: none -> 21.9 us  [butterfly_sum(): pl.pallas_call(functools.partial(exchange_kernel, count, radix), out_shap...]
    ppermute x14 -> x0, waiting for transfers between devices: 7.01 us -> none  [butterfly_sum(): terms.append(lax.ppermute(block, axis, route))]
    slice x2, local copies, waits for them, and re-layouts: 3.38 us -> 5.08 us  [above(): field[..., 1:]]
    unnamed x19 -> x17, local copies, waits for them, and re-layouts: 2.09 us -> 3.4 us
  transfers between devices with their start and end apart: 23 -> 9, of which waited for: 7 -> 2; matrix products, arithmetic and copies ran while one was open for 9% -> 13% of each run, Pallas kernels for 0% -> 0%
where the time goes in v3:
time: 152 us
  other arithmetic  44.3 us (29%)
  starting transfers between devices  41.1 us (27%)
  local copies, waits for them, and re-layouts  29.3 us (19%)
  Pallas kernels  21.9 us (14%)
  blocking collectives  8.45 us (6%)
  waiting for transfers between devices  3.54 us (2%)
  matrix products  2.1 us (1%)
    ppermute x4, starting transfers between devices, padded(): lax.ppermute(lax.slice_in_dim(block, 0, width, axis=dim), axis, backward)  31 us
    pallas_call x1, Pallas kernels, butterfly_sum(): pl.pallas_call(functools.partial(exchange_kernel, count, radix), out_shap...  21.9 us
    add x1, local copies, waits for them, and re-layouts, body(): sketch = increments + state  13.4 us
    reduce_sum x1, other arithmetic, body(): jnp.mean(sketch.reshape(probe_count, lon_count // 4, 4, level_count, lat_...  10.1 us
    ppermute x1, starting transfers between devices, from_behind(): return lax.ppermute(block, axis, route)  9.78 us
    all_gather x1, blocking collectives, body(): full_panel = lax.all_gather(coarse, 'probe', axis=0, tiled=True)  8.45 us
    another operation x3, other arithmetic, body(): lower = jnp.linalg.cholesky(gram)  6.52 us
    slice x2, local copies, waits for them, and re-layouts, above(): field[..., 1:]  5.08 us
  transfers between devices with their start and end apart: 9, of which 2 were waited for; matrix products, arithmetic and copies ran while one was open for 13% of the time, Pallas kernels for 0%

profile of v3, /device:TPU:8, one launch (start us, length us, event | category | flops | bytes accessed | tf_op | source)
XLA Modules:
  0.0 151.6 jit_solution(6578818134545801361)
XLA Ops:
  1.3 9.8 %collective-permute-start = (f32[1,8,256]{2,1,0:T(8,128)S(1)}, f32[1,8,256]{2,1,0:T(8,128)S(1)}, u32[]{:S(2)}, u32[]{:S(2)}) collective-permute-start(f32[1,8,256]{2,1,0:T(8,128)S(1)} %slice_bitcast_fusion.1), channel_id=1, source_target_pairs={{4,0},{8,4},{12,8},{16,12},{20,16},{24,20},{28,24},{32,28},{36,32}... | collective-permute-start | bytes 24584 | tf_op jit(solution)/shard_map/ppermute | solution.py:16
  11.1 1.7 %fusion.34 = (f32[16,1,8,256]{3,2,1,0:T(8,128)}, f32[16,1,8,256]{3,2,1,0:T(8,128)}) fusion(f32[16,24,8,256]{3,2,1,0:T(8,128)} %param.3), kind=kLoop, calls=%fused_computation.64 | loop fusion | bytes 524288 | tf_op jit(solution)/shard_map/slice | solution.py:95
  12.8 7.7 %collective-permute-start.2 = (f32[16,1,8,256]{3,2,1,0:T(8,128)}, f32[16,1,8,256]{3,2,1,0:T(8,128)}, u32[]{:S(2)}, u32[]{:S(2)}) collective-permute-start(f32[16,1,8,256]{3,2,1,0:T(8,128)} %get-tuple-element.22), channel_id=1, source_target_pairs={{4,0},{8,4},{12,8},{16,12},{20,16},{24,20},{28,24},{32,28},{36,32}... | collective-permute-start | bytes 393224 | tf_op jit(solution)/shard_map/ppermute | solution.py:95
  20.6 1.1 maximum_bitcast_fusion
  21.6 1.0 bitcast_select_fusion
  22.7 3.8 %multiply_add_fusion.1 = f32[16,24,8,256]{3,2,1,0:T(8,128)S(1)} fusion(f32[16,24,8,256]{3,2,1,0:T(8,128)} %param.3, f32[16,24,8,255]{3,2,1,0:T(8,128)} %bitcast.37, f32[24,8,256]{2,1,0:T(8,128)S(1)} %get-tuple-element.25, f32[24,8,256]{2,1,0:T(8,128)S(1)} %get-tuple-element.24), kind=kLoop, calls=%fused_computation.31 | loop fusion | flops 2359296 | bytes 9818112 | tf_op jit(solution)/shard_map/add | solution.py:120
  26.5 1.0 slice_maximum_fusion
  28.2 2.6 %slice.164 = f32[16,24,8,255]{3,2,1,0:T(8,128)} slice(f32[16,24,8,256]{3,2,1,0:T(8,128)S(1)} %multiply_add_fusion.1), slice={[0:16], [0:24], [0:8], [1:256]} | slice | bytes 6266880 | tf_op jit(solution)/shard_map/slice | solution.py:110
  32.1 1.1 minimum_add_fusion
  33.2 1.5 fusion
  35.2 1.0 copy-done.3
  36.1 0.9 fusion.19
  37.2 7.7 %collective-permute-start.4 = (f32[16,1,8,256]{3,2,1,0:T(8,128)S(1)}, f32[16,1,8,256]{3,2,1,0:T(8,128)S(1)}, u32[]{:S(2)}, u32[]{:S(2)}) collective-permute-start(f32[16,1,8,256]{3,2,1,0:T(8,128)S(1)} %get-tuple-element.20), channel_id=1, source_target_pairs={{4,0},{8,4},{12,8},{16,12},{20,16},{24,20},{28,24},{32,28},{36,32}... | collective-permute-start | bytes 393224 | tf_op jit(solution)/shard_map/ppermute | solution.py:95
  44.9 1.0 multiply_add_fusion
  45.9 2.5 %slice.170 = f32[16,24,8,255]{3,2,1,0:T(8,128)} slice(f32[16,24,8,256]{3,2,1,0:T(8,128)S(1)} %multiply_add_fusion), slice={[0:16], [0:24], [0:8], [1:256]} | slice | bytes 6266880 | tf_op jit(solution)/shard_map/slice | solution.py:110
  49.3 2.8 %fusion.17 = f32[16,24,8,256]{3,2,1,0:T(8,128)S(1)} fusion(f32[16,24,8,256]{3,2,1,0:T(8,128)S(1)} %fusion.19, f32[16,25,8,256]{3,2,1,0:T(8,128)S(1)} %fusion.1, f32[16,24,8,256]{3,2,1,0:T(8,128)S(1)} %multiply_add_fusion, f32[16,24,8,255]{3,2,1,0:T(8,128)} %slice.170, f32[24,8,256]{2,1,0:T(8,128)S(1)} %copy-done.6), kind=kLoop, calls=%fused_computation.26 | loop fusion | flops 3932160 | bytes 19058688 | tf_op jit(solution)/shard_map/mul | solution.py:158
  52.3 7.7 %collective-permute-start.6 = (f32[16,1,8,256]{3,2,1,0:T(8,128)S(1)}, f32[16,1,8,256]{3,2,1,0:T(8,128)S(1)}, u32[]{:S(2)}, u32[]{:S(2)}) collective-permute-start(f32[16,1,8,256]{3,2,1,0:T(8,128)S(1)} %get-tuple-element.19), channel_id=1, source_target_pairs={{4,0},{8,4},{12,8},{16,12},{20,16},{24,20},{28,24},{32,28},{36,32}... | collective-permute-start | bytes 393224 | tf_op jit(solution)/shard_map/ppermute | solution.py:95
  60.0 1.1 fusion.31
  61.1 1.8 %collective-permute-done.5 = f32[16,1,8,256]{3,2,1,0:T(8,128)S(1)} collective-permute-done((f32[16,1,8,256]{3,2,1,0:T(8,128)S(1)}, f32[16,1,8,256]{3,2,1,0:T(8,128)S(1)}, u32[]{:S(2)}, u32[]{:S(2)}) %collective-permute-start.5) | collective-permute-done | bytes 131104 | tf_op jit(solution)/shard_map/ppermute | solution.py:92
  63.0 2.2 %fusion.12 = f32[16,24,8,256]{3,2,1,0:T(8,128)S(1)} fusion(f32[16,1,8,256]{3,2,1,0:T(8,128)S(1)} %collective-permute-done.6, f32[16,24,8,256]{3,2,1,0:T(8,128)S(1)} %fusion.17, f32[16,1,8,256]{3,2,1,0:T(8,128)S(1)} %collective-permute-done.5, f32[16,24,8,255]{3,2,1,0:T(8,128)S(1)} %get-tuple-element.17, f32[16,24,8,255]{3,2,1,0:T(8,128)S(1)} %get-tuple-element.16, ...), kind=kLoop, calls=%fused_computation.19 | loop fusion | flops 8650752 | bytes 13803520 | tf_op jit(solution)/shard_map/add | solution.py:136
  65.3 7.8 %collective-permute-start.8 = (f32[16,1,8,256]{3,2,1,0:T(8,128)S(1)}, f32[16,1,8,256]{3,2,1,0:T(8,128)S(1)}, u32[]{:S(2)}, u32[]{:S(2)}) collective-permute-start(f32[16,1,8,256]{3,2,1,0:T(8,128)S(1)} %get-tuple-element.15), channel_id=1, source_target_pairs={{4,0},{8,4},{12,8},{16,12},{20,16},{24,20},{28,24},{32,28},{36,32}... | collective-permute-start | bytes 393224 | tf_op jit(solution)/shard_map/ppermute | solution.py:95
  73.1 1.2 fusion.29
  74.3 1.7 %collective-permute-done.7 = f32[16,1,8,256]{3,2,1,0:T(8,128)S(1)} collective-permute-done((f32[16,1,8,256]{3,2,1,0:T(8,128)S(1)}, f32[16,1,8,256]{3,2,1,0:T(8,128)S(1)}, u32[]{:S(2)}, u32[]{:S(2)}) %collective-permute-start.7) | collective-permute-done | bytes 131104 | tf_op jit(solution)/shard_map/ppermute | solution.py:92
  76.0 3.8 %fusion.6 = f32[16,24,8,256]{3,2,1,0:T(8,128)} fusion(f32[16,24,8,256]{3,2,1,0:T(8,128)S(1)} %copy-done, f32[16,1,8,256]{3,2,1,0:T(8,128)S(1)} %collective-permute-done.8, f32[16,24,8,256]{3,2,1,0:T(8,128)S(1)} %fusion.12, f32[16,1,8,256]{3,2,1,0:T(8,128)S(1)} %collective-permute-done.7, f32[16,24,8,255]{3,2,1,0:T(8,128)S(1)} %get-tuple-element.13, ...), kind=kLoop, calls=%fused_computation.11 | loop fusion | flops 9437184 | bytes 16949248 | tf_op jit(solution)/shard_map/add | solution.py:161
  79.8 13.4 %copy.21 = f32[16,24,8,256]{0,2,3,1:T(8,128)} copy(f32[16,24,8,256]{3,2,1,0:T(8,128)} %fusion.6) | data formatting | bytes 6291456 | tf_op jit(solution)/shard_map/add | solution.py:161
  93.2 10.1 %reduce_sum.9 = f32[16,6,8,64]{0,2,3,1:T(8,128)S(1)} reduce(f32[16,6,4,8,64,4]{0,3,5,4,2,1:T(8,128)} %bitcast.36, f32[]{:T(128)} %constant.53.clone.1), dimensions={2,5}, to_apply=%region_0.1 | reduce | flops 737280 | bytes 3342340 | tf_op jit(solution)/shard_map/reduce_sum | solution.py:163
  104.0 8.5 %all_gather.3 = f32[64,3072]{1,0:T(8,128)S(1)} all-gather(f32[16,3072]{1,0:T(8,128)S(1)} %div.18), channel_id=1, replica_groups=mesh['lon'=64,'probe'=4] {'probe'}, dimensions={0}, use_global_device_ids=true | all-gather | bytes 983040 | tf_op jit(solution)/shard_map/all_gather | solution.py:169
  112.5 1.4 fusion.35.block_ref
  113.9 21.9 %shard_map.50 = f32[64,64]{1,0:T(8,128)} custom-call(f32[64,64]{1,0:T(8,128)} %fusion.35.block_ref), custom_call_target="tpu_custom_call" | custom-call | tf_op jit(solution)/shard_map/pallas_call | solution.py:71
  135.7 0.8 copy.23
  137.3 5.8 %cholesky.17 = f32[64,64]{1,0:T(8,128)S(1)} custom-call(f32[64,64]{1,0:T(8,128)S(1)} %fusion.24), custom_call_target="Cholesky" | custom-call | tf_op jit(solution)/shard_map/jit(cholesky)/cholesky | solution.py:177
  144.5 4.9 %custom-call.6 = f32[1,64,64]{1,2,0:T(8,128)S(1)} custom-call(f32[1,64,64]{2,1,0:T(8,128)S(1)} %get-tuple-element.34), custom_call_target="InvertDiagBlocksLowerTriangular" | custom-call | tf_op jit(solution)/shard_map/triangular_solve | solution.py:178
  (47 shorter events, 9.4 us)
Async XLA Ops:
  1.3 29.9 %collective-permute-start = (f32[1,8,256]{2,1,0:T(8,128)S(1)}, f32[1,8,256]{2,1,0:T(8,128)S(1)}, u32[]{:S(2)}, u32[]{:S(2)}) collective-permute-start(f32[1,8,256]{2,1,0:T(8,128)S(1)} %slice_bitcast_fusion.1), channel_id=1, source_target_pairs={{4,0},{8,4},{12,8},{16,12},{20,16},{24,20},{28,24},{32,28},{36,32}... | collective-permute-start | bytes 24584 | tf_op jit(solution)/shard_map/ppermute | solution.py:16
  12.8 20.4 %collective-permute-start.1 = (f32[16,1,8,256]{3,2,1,0:T(8,128)}, f32[16,1,8,256]{3,2,1,0:T(8,128)}, u32[]{:S(2)}, u32[]{:S(2)}) collective-permute-start(f32[16,1,8,256]{3,2,1,0:T(8,128)} %get-tuple-element.23), channel_id=1, source_target_pairs={{0,4},{4,8},{8,12},{12,16},{16,20},{20,24},{24,28},{28,32},{32,36}... | collective-permute-start | bytes 393224 | tf_op jit(solution)/shard_map/ppermute | solution.py:92
  12.8 20.4 %collective-permute-start.2 = (f32[16,1,8,256]{3,2,1,0:T(8,128)}, f32[16,1,8,256]{3,2,1,0:T(8,128)}, u32[]{:S(2)}, u32[]{:S(2)}) collective-permute-start(f32[16,1,8,256]{3,2,1,0:T(8,128)} %get-tuple-element.22), channel_id=1, source_target_pairs={{4,0},{8,4},{12,8},{16,12},{20,16},{24,20},{28,24},{32,28},{36,32}... | collective-permute-start | bytes 393224 | tf_op jit(solution)/shard_map/ppermute | solution.py:95
  20.6 5.9 %copy-start.7 = (pred[256]{0:T(512)(128)(4,1)}, pred[256]{0:T(512)(128)(4,1)S(1)}, u32[]{:S(2)}) copy-start(pred[256]{0:T(512)(128)(4,1)S(1)} %iota_compare_fusion.3) | copy-start | bytes 772
  21.6 4.8 %copy-start.4 = (f32[24,8,256]{2,1,0:T(8,128)}, f32[24,8,256]{2,1,0:T(8,128)S(1)}, u32[]{:S(2)}) copy-start(f32[24,8,256]{2,1,0:T(8,128)S(1)} %get-tuple-element.24) | copy-start | bytes 589828
  26.5 1.7 %copy-start.1 = (f32[16,24,8,256]{3,2,1,0:T(8,128)}, f32[16,24,8,256]{3,2,1,0:T(8,128)S(1)}, u32[]{:S(2)}) copy-start(f32[16,24,8,256]{3,2,1,0:T(8,128)S(1)} %multiply_add_fusion.1) | copy-start | bytes 9437188
  28.2 5.0 %copy-start = (f32[16,24,8,256]{3,2,1,0:T(8,128)S(1)}, f32[16,24,8,256]{3,2,1,0:T(8,128)}, u32[]{:S(2)}) copy-start(f32[16,24,8,256]{3,2,1,0:T(8,128)} %param.3) | copy-start | bytes 9437188
  33.2 2.0 %copy-start.2 = (f32[16,24,8,256]{3,2,1,0:T(8,128)S(1)}, f32[16,24,8,256]{3,2,1,0:T(8,128)}, u32[]{:S(2)}) copy-start(f32[16,24,8,256]{3,2,1,0:T(8,128)} %copy-done.1) | copy-start | bytes 9437188
  33.2 3.0 %copy-start.3 = (f32[16,24,8,255]{3,2,1,0:T(8,128)S(1)}, f32[16,24,8,255]{3,2,1,0:T(8,128)}, u32[]{:S(2)}) copy-start(f32[16,24,8,255]{3,2,1,0:T(8,128)} %slice.164) | copy-start | bytes 9400324
  36.1 8.8 %copy-start.5 = (f32[24,8,256]{2,1,0:T(8,128)S(1)}, f32[24,8,256]{2,1,0:T(8,128)}, u32[]{:S(2)}) copy-start(f32[24,8,256]{2,1,0:T(8,128)} %copy-done.4) | copy-start | bytes 589828
  37.1 11.3 %collective-permute-start.3 = (f32[16,1,8,256]{3,2,1,0:T(8,128)S(1)}, f32[16,1,8,256]{3,2,1,0:T(8,128)S(1)}, u32[]{:S(2)}, u32[]{:S(2)}) collective-permute-start(f32[16,1,8,256]{3,2,1,0:T(8,128)S(1)} %get-tuple-element.21), channel_id=1, source_target_pairs={{0,4},{4,8},{8,12},{12,16},{16,20},{20,24},{24,28},{28,32},{32,36}... | collective-permute-start | bytes 393224 | tf_op jit(solution)/shard_map/ppermute | solution.py:92
  37.2 11.2 %collective-permute-start.4 = (f32[16,1,8,256]{3,2,1,0:T(8,128)S(1)}, f32[16,1,8,256]{3,2,1,0:T(8,128)S(1)}, u32[]{:S(2)}, u32[]{:S(2)}) collective-permute-start(f32[16,1,8,256]{3,2,1,0:T(8,128)S(1)} %get-tuple-element.20), channel_id=1, source_target_pairs={{4,0},{8,4},{12,8},{16,12},{20,16},{24,20},{28,24},{32,28},{36,32}... | collective-permute-start | bytes 393224 | tf_op jit(solution)/shard_map/ppermute | solution.py:95
  48.4 0.9 copy-start.6
  52.2 10.8 %collective-permute-start.5 = (f32[16,1,8,256]{3,2,1,0:T(8,128)S(1)}, f32[16,1,8,256]{3,2,1,0:T(8,128)S(1)}, u32[]{:S(2)}, u32[]{:S(2)}) collective-permute-start(f32[16,1,8,256]{3,2,1,0:T(8,128)S(1)} %get-tuple-element.18), channel_id=1, source_target_pairs={{0,4},{4,8},{8,12},{12,16},{16,20},{20,24},{24,28},{28,32},{32,36}... | collective-permute-start | bytes 393224 | tf_op jit(solution)/shard_map/ppermute | solution.py:92
  52.3 10.7 %collective-permute-start.6 = (f32[16,1,8,256]{3,2,1,0:T(8,128)S(1)}, f32[16,1,8,256]{3,2,1,0:T(8,128)S(1)}, u32[]{:S(2)}, u32[]{:S(2)}) collective-permute-start(f32[16,1,8,256]{3,2,1,0:T(8,128)S(1)} %get-tuple-element.19), channel_id=1, source_target_pairs={{4,0},{8,4},{12,8},{16,12},{20,16},{24,20},{28,24},{32,28},{36,32}... | collective-permute-start | bytes 393224 | tf_op jit(solution)/shard_map/ppermute | solution.py:95
  65.2 10.8 %collective-permute-start.7 = (f32[16,1,8,256]{3,2,1,0:T(8,128)S(1)}, f32[16,1,8,256]{3,2,1,0:T(8,128)S(1)}, u32[]{:S(2)}, u32[]{:S(2)}) collective-permute-start(f32[16,1,8,256]{3,2,1,0:T(8,128)S(1)} %get-tuple-element.14), channel_id=1, source_target_pairs={{0,4},{4,8},{8,12},{12,16},{16,20},{20,24},{24,28},{28,32},{32,36}... | collective-permute-start | bytes 393224 | tf_op jit(solution)/shard_map/ppermute | solution.py:92
  65.3 10.7 %collective-permute-start.8 = (f32[16,1,8,256]{3,2,1,0:T(8,128)S(1)}, f32[16,1,8,256]{3,2,1,0:T(8,128)S(1)}, u32[]{:S(2)}, u32[]{:S(2)}) collective-permute-start(f32[16,1,8,256]{3,2,1,0:T(8,128)S(1)} %get-tuple-element.15), channel_id=1, source_target_pairs={{4,0},{8,4},{12,8},{16,12},{20,16},{24,20},{28,24},{32,28},{36,32}... | collective-permute-start | bytes 393224 | tf_op jit(solution)/shard_map/ppermute | solution.py:95

commit v4 on v3

--- a/solution.py
+++ b/solution.py
@@ -142,27 +142,35 @@
 
 
 def body(increments, winds, obs_weight):
-    east_local = winds[0]
-    north_local = lat_mask(winds[1])
-    next_first = from_behind(east_local[:1], "lon", -1)
-    near_east = jnp.concatenate([jnp.zeros_like(next_first), east_local, next_first], axis=0)
-    edge_zero = jnp.zeros_like(north_local[:1])
-    near_north = jnp.concatenate([edge_zero, north_local, edge_zero], axis=0)
-
-    def widen(field):
-        return padded(field, (("lon", 1),), 1)
-
-    state = increments
+    probe_count, lon_count, level_count, lat_count = increments.shape
+    halo = 4
+    pack = (increments, winds[0][None], lat_mask(winds[1])[None], obs_weight[None])
+    count = lax.axis_size("lon")
+    forward = [(i, (i + 1) % count) for i in range(count)]
+    backward = [((i + 1) % count, i) for i in range(count)]
+    west_edge = jnp.concatenate([part[:, lon_count - halo:] for part in pack], axis=0)
+    east_edge = jnp.concatenate([part[:, :halo] for part in pack], axis=0)
+    from_west = lax.ppermute(west_edge, "lon", forward)
+    from_east = lax.ppermute(east_edge, "lon", backward)
+    wide = [
+        jnp.concatenate([from_west[lo:hi], part, from_east[lo:hi]], axis=1)
+        for part, (lo, hi) in zip(
+            pack,
+            ((0, probe_count), (probe_count, probe_count + 1),
+             (probe_count + 1, probe_count + 2), (probe_count + 2, probe_count + 3)),
+        )
+    ]
+    state, east, north, weight = wide[0], wide[1][0], wide[2][0], wide[3][0]
+    span = lon_count + 2 * halo
     for step in range(2):
-        state = forward_core(widen(state), near_east, near_north)
-    state = obs_weight * state
-    for step in range(2):
-        state = adjoint_core(widen(state), near_east, near_north)
+        state = forward_core(state, east[step:span - step], north[step:span - step])
+    state = weight[2:span - 2] * state
+    for step in range(2, 4):
+        state = adjoint_core(state, east[step:span - step], north[step:span - step])
     sketch = increments + state
-    probe_count, lon_count, level_count, lat_count = sketch.shape
-    coarse = jnp.mean(
-        sketch.reshape(probe_count, lon_count // 4, 4, level_count, lat_count // 4, 4), axis=(2, 5)
-    )
+    coarse = sketch.reshape(probe_count, lon_count // 4, 4, level_count, lat_count).sum(axis=2)
+    coarse = coarse.reshape(probe_count, lon_count // 4, level_count, lat_count // 4, 4).sum(axis=4)
+    coarse = coarse * (1.0 / 16.0)
     coarse = coarse.reshape(probe_count, -1)
     all_probes = probe_count * lax.axis_size("probe")
     ident = jnp.eye(all_probes, dtype=jnp.float32)

time: 152 us -> 137 us (0.901)
  starting transfers between devices: 41.1 us -> 9.94 us
  waiting for transfers between devices: 3.54 us -> 20.3 us
  local copies, waits for them, and re-layouts: 29.3 us -> 22.5 us
  other arithmetic: 44.3 us -> 47.3 us
  Pallas kernels: 21.9 us -> 24.7 us
    ppermute x9 -> x2, starting transfers between devices: 41.1 us -> 9.94 us  [the longest x1 9.86 us: body(): from_east = lax.ppermute(east_edge, 'lon', backward)]
    ppermute x9 -> x2, waiting for transfers between devices: 3.54 us -> 20.3 us  [the longest x1 12.3 us: body(): from_east = lax.ppermute(east_edge, 'lon', backward)]
    add x1 -> x0, local copies, waits for them, and re-layouts: 13.4 us -> none  [body(): sketch = increments + state]
    sub x1, other arithmetic: 0.9 us -> 6.83 us  [forward_core(): return inner - (flux_w[:, 1:] - flux_w[:, :-1]) - (flux_n - flux_s)]
    reduce_sum x1 -> x2, local copies, waits for them, and re-layouts: 0.53 us -> 5.53 us  [the longest x1 4.99 us: body(): sketch.reshape(probe_count, lon_count // 4, 4, level_count, lat_count)]
    reduce_sum x1 -> x2, other arithmetic: 10.1 us -> 5.5 us  [the longest x1 4.2 us: body(): coarse.reshape(probe_count, lon_count // 4, level_count, lat_count // 4, 4)]
    mul x1 -> x3, other arithmetic: 2.84 us -> 6.54 us  [the longest x2 6.51 us: body(): state = weight[2:span - 2] * state]
    pallas_call x1, Pallas kernels: 21.9 us -> 24.7 us  [butterfly_sum(): pl.pallas_call(functools.partial(exchange_kernel, count, radix), out_shap...]
  transfers between devices with their start and end apart: 9 -> 2, of which waited for: 2 -> 2; matrix products, arithmetic and copies ran while one was open for 13% -> 1% of each run, Pallas kernels for 0% -> 0%
where the time goes in v4:
time: 137 us; the launch traced here: 136 us
  other arithmetic  47.3 us (35%)
  Pallas kernels  24.7 us (18%)
  local copies, waits for them, and re-layouts  22.5 us (16%)
  waiting for transfers between devices  20.3 us (15%)
  starting transfers between devices  9.94 us (7%)
  blocking collectives  8.45 us (6%)
  matrix products  2.1 us (2%)
    pallas_call x1, Pallas kernels, butterfly_sum(): pl.pallas_call(functools.partial(exchange_kernel, count, radix), out_shap...  24.7 us
    ppermute x1, waiting for transfers between devices, body(): from_east = lax.ppermute(east_edge, 'lon', backward)  12.3 us
    ppermute x1, starting transfers between devices, body(): from_east = lax.ppermute(east_edge, 'lon', backward)  9.86 us
    all_gather x1, blocking collectives, body(): full_panel = lax.all_gather(coarse, 'probe', axis=0, tiled=True)  8.45 us
    ppermute x1, waiting for transfers between devices, body(): from_west = lax.ppermute(west_edge, 'lon', forward)  8.04 us
    slice x4, local copies, waits for them, and re-layouts, above(): field[..., 1:]  7.05 us
    sub x1, other arithmetic, forward_core(): return inner - (flux_w[:, 1:] - flux_w[:, :-1]) - (flux_n - flux_s)  6.83 us
    another operation x3, other arithmetic, body(): lower = jnp.linalg.cholesky(gram)  6.52 us
  transfers between devices with their start and end apart: 2, of which 2 were waited for; matrix products, arithmetic and copies ran while one was open for 1% of the time, Pallas kernels for 0%

profile of v4, /device:TPU:8, one launch (start us, length us, event | category | flops | bytes accessed | tf_op | source)
XLA Modules:
  0.0 136.4 jit_solution(16672792243334035644)
XLA Ops:
  0.6 0.8 fusion.35
  1.4 0.8 fusion.33
  2.2 1.7 %minimum_bitcast_fusion.5 = (f32[24,8,256]{2,1,0:T(8,128)}, f32[1,24,8,256]{3,2,1,0:T(8,128)S(1)}, f32[1,24,8,256]{3,2,1,0:T(8,128)S(1)}) fusion(f32[2,24,8,256]{3,2,1,0:T(8,128)} %param.4, pred[256]{0:T(512)(128)(4,1)S(1)} %iota_compare_fusion.3), kind=kLoop, calls=%fused_computation.59 | loop fusion | flops 98304 | bytes 983296 | tf_op jit(solution)/shard_map/min | solution.py:129
  3.9 1.3 fusion.30
  5.3 9.9 %collective-permute-start.1 = (f32[19,4,8,256]{3,2,1,0:T(8,128)S(1)}, f32[19,4,8,256]{3,2,1,0:T(8,128)S(1)}, u32[]{:S(2)}, u32[]{:S(2)}) collective-permute-start(f32[19,4,8,256]{3,2,1,0:T(8,128)S(1)} %pad_maximum_fusion.2), channel_id=1, source_target_pairs={{4,0},{8,4},{12,8},{16,12},{20,16},{24,20},{28,24},{32,28},{36,32}... | collective-permute-start | bytes 1867784 | tf_op jit(solution)/shard_map/ppermute | solution.py:154
  15.3 0.8 slice.354
  16.2 12.3 %collective-permute-done.1 = f32[19,4,8,256]{3,2,1,0:T(8,128)S(1)} collective-permute-done((f32[19,4,8,256]{3,2,1,0:T(8,128)S(1)}, f32[19,4,8,256]{3,2,1,0:T(8,128)S(1)}, u32[]{:S(2)}, u32[]{:S(2)}) %collective-permute-start.1) | collective-permute-done | bytes 622624 | tf_op jit(solution)/shard_map/ppermute | solution.py:154
  28.5 8.0 %collective-permute-done = f32[19,4,8,256]{3,2,1,0:T(8,128)S(1)} collective-permute-done((f32[19,4,8,256]{3,2,1,0:T(8,128)S(1)}, f32[19,4,8,256]{3,2,1,0:T(8,128)S(1)}, u32[]{:S(2)}, u32[]{:S(2)}) %collective-permute-start) | collective-permute-done | bytes 622624 | tf_op jit(solution)/shard_map/ppermute | solution.py:153
  37.4 0.8 minimum_bitcast_fusion.4
  39.2 1.1 multiply_add_fusion
  40.4 3.1 %slice.328 = f32[16,30,8,255]{3,2,1,0:T(8,128)} slice(f32[16,30,8,256]{3,2,1,0:T(8,128)S(1)} %multiply_add_fusion), slice={[0:16], [0:30], [0:8], [1:256]} | slice | bytes 7833600 | tf_op jit(solution)/shard_map/slice | solution.py:110
  43.5 2.4 %fusion = f32[16,31,8,256]{3,2,1,0:T(8,128)} fusion(f32[16,32,8,256]{3,2,1,0:T(8,128)S(1)} %pad_maximum_fusion, f32[31,8,256]{2,1,0:T(8,128)S(1)} %get-tuple-element.36, f32[31,8,256]{2,1,0:T(8,128)S(1)} %get-tuple-element.35), kind=kLoop, calls=%fused_computation.2 | loop fusion | flops 3047424 | bytes 12697600 | tf_op jit(solution)/shard_map/add | solution.py:118
  45.9 6.8 %fusion.2 = f32[16,30,8,256]{3,2,1,0:T(8,128)S(1)} fusion(f32[16,31,8,256]{3,2,1,0:T(8,128)} %fusion, f32[16,30,8,256]{3,2,1,0:T(8,128)} %copy-done, f32[16,30,8,255]{3,2,1,0:T(8,128)} %slice.328, f32[16,32,8,256]{3,2,1,0:T(8,128)S(1)} %pad_maximum_fusion), kind=kLoop, calls=%fused_computation.6 | loop fusion | flops 3932160 | bytes 23577600 | tf_op jit(solution)/shard_map/sub | solution.py:122
  53.7 1.2 multiply_add_fusion.1
  54.9 3.0 %slice.339 = f32[16,28,8,255]{3,2,1,0:T(8,128)} slice(f32[16,28,8,256]{3,2,1,0:T(8,128)S(1)} %multiply_add_fusion.1), slice={[0:16], [0:28], [0:8], [1:256]} | slice | bytes 7311360 | tf_op jit(solution)/shard_map/slice | solution.py:110
  57.9 2.2 %fusion.3 = f32[16,29,8,256]{3,2,1,0:T(8,128)} fusion(f32[16,30,8,256]{3,2,1,0:T(8,128)S(1)} %fusion.2, f32[29,8,256]{2,1,0:T(8,128)S(1)} %get-tuple-element.38, f32[29,8,256]{2,1,0:T(8,128)S(1)} %get-tuple-element.37), kind=kLoop, calls=%fused_computation.9 | loop fusion | flops 2850816 | bytes 11878400 | tf_op jit(solution)/shard_map/add | solution.py:118
  60.2 6.5 %fusion.6 = f32[16,28,8,256]{3,2,1,0:T(8,128)S(1)} fusion(f32[16,29,8,256]{3,2,1,0:T(8,128)} %fusion.3, f32[16,28,8,256]{3,2,1,0:T(8,128)} %copy-done.1, f32[16,28,8,255]{3,2,1,0:T(8,128)} %slice.339, f32[16,30,8,256]{3,2,1,0:T(8,128)S(1)} %fusion.2, f32[28,8,256]{2,1,0:T(8,128)S(1)} %fusion.16), kind=kLoop, calls=%fused_computation.14 | loop fusion | flops 4587520 | bytes 22235136 | tf_op jit(solution)/shard_map/mul | solution.py:167
  66.7 1.2 fusion.28
  68.1 2.3 %fusion.9 = f32[16,26,8,256]{3,2,1,0:T(8,128)S(1)} fusion(f32[16,28,8,256]{3,2,1,0:T(8,128)S(1)} %fusion.6, f32[16,26,8,255]{3,2,1,0:T(8,128)S(1)} %get-tuple-element.15, f32[16,26,8,255]{3,2,1,0:T(8,128)S(1)} %get-tuple-element.14, f32[26,8,256]{2,1,0:T(8,128)S(1)} %get-tuple-element.44, f32[26,8,256]{2,1,0:T(8,128)S(1)} %copy-done.5, ...), kind=kLoop, calls=%fused_computation.19 | loop fusion | flops 7667712 | bytes 21485568 | tf_op jit(solution)/shard_map/add | solution.py:136
  70.5 1.1 fusion.29
  71.7 0.8 copy-done.3
  72.4 2.4 %fusion.14 = f32[16,24,8,256]{3,2,1,0:T(8,128)S(1)} fusion(f32[16,24,8,256]{3,2,1,0:T(8,128)S(1)} %copy-done.3, f32[16,26,8,256]{3,2,1,0:T(8,128)S(1)} %fusion.9, f32[16,24,8,255]{3,2,1,0:T(8,128)S(1)} %get-tuple-element.17, f32[16,24,8,255]{3,2,1,0:T(8,128)S(1)} %get-tuple-element.16, f32[24,8,256]{2,1,0:T(8,128)S(1)} %get-tuple-element.46, ...), kind=kLoop, calls=%fused_computation.27 | loop fusion | flops 7864320 | bytes 22978560 | tf_op jit(solution)/shard_map/add | solution.py:170
  74.8 1.3 reduce_sum.18
  76.1 5.0 %copy.20 = f32[16,6,8,256]{0,2,3,1:T(8,128)} copy(f32[16,6,8,256]{3,2,1,0:T(8,128)} %reduce_sum.18) | data formatting | bytes 1572864 | tf_op jit(solution)/shard_map/reduce_sum | solution.py:171
  81.1 4.2 %reduce_sum.19 = f32[16,6,8,64]{0,2,3,1:T(8,128)S(1)} reduce(f32[16,6,8,64,4]{0,2,4,3,1:T(8,128)} %bitcast.69, f32[]{:T(128)} %constant.60.clone.1), dimensions={4}, to_apply=%region_1.2 | reduce | flops 147456 | bytes 983044 | tf_op jit(solution)/shard_map/reduce_sum | solution.py:172
  86.1 8.5 %all_gather.3 = f32[64,3072]{1,0:T(8,128)S(1)} all-gather(f32[16,3072]{1,0:T(8,128)S(1)} %mul.220), channel_id=1, replica_groups=mesh['lon'=64,'probe'=4] {'probe'}, dimensions={0}, use_global_device_ids=true | all-gather | bytes 983040 | tf_op jit(solution)/shard_map/all_gather | solution.py:177
  94.5 1.4 %fusion.36.block_ref = f32[64,64]{1,0:T(8,128)} fusion(f32[64,3072]{1,0:T(8,128)S(1)} %all_gather.3), kind=kOutput, calls=%fused_computation.86 | convolution fusion | flops 150994944 | bytes 802816 | tf_op jit(solution)/shard_map/dot_general | solution.py:178
  95.9 24.7 %shard_map.50 = f32[64,64]{1,0:T(8,128)} custom-call(f32[64,64]{1,0:T(8,128)} %fusion.36.block_ref), custom_call_target="tpu_custom_call" | custom-call | tf_op jit(solution)/shard_map/pallas_call | solution.py:71
  120.6 0.8 copy.22
  121.4 0.8 fusion.23
  122.2 5.8 %cholesky.17 = f32[64,64]{1,0:T(8,128)S(1)} custom-call(f32[64,64]{1,0:T(8,128)S(1)} %fusion.23), custom_call_target="Cholesky" | custom-call | tf_op jit(solution)/shard_map/jit(cholesky)/cholesky | solution.py:185
  129.4 4.9 %custom-call.6 = f32[1,64,64]{1,2,0:T(8,128)S(1)} custom-call(f32[1,64,64]{2,1,0:T(8,128)S(1)} %get-tuple-element.52), custom_call_target="InvertDiagBlocksLowerTriangular" | custom-call | tf_op jit(solution)/shard_map/triangular_solve | solution.py:186
  (56 shorter events, 7.5 us)
Async XLA Ops:
  5.3 23.1 %collective-permute-start.1 = (f32[19,4,8,256]{3,2,1,0:T(8,128)S(1)}, f32[19,4,8,256]{3,2,1,0:T(8,128)S(1)}, u32[]{:S(2)}, u32[]{:S(2)}) collective-permute-start(f32[19,4,8,256]{3,2,1,0:T(8,128)S(1)} %pad_maximum_fusion.2), channel_id=1, source_target_pairs={{4,0},{8,4},{12,8},{16,12},{20,16},{24,20},{28,24},{32,28},{36,32}... | collective-permute-start | bytes 1867784 | tf_op jit(solution)/shard_map/ppermute | solution.py:154
  15.2 21.3 %collective-permute-start = (f32[19,4,8,256]{3,2,1,0:T(8,128)S(1)}, f32[19,4,8,256]{3,2,1,0:T(8,128)S(1)}, u32[]{:S(2)}, u32[]{:S(2)}) collective-permute-start(f32[19,4,8,256]{3,2,1,0:T(8,128)S(1)} %pad_maximum_fusion.1), channel_id=1, source_target_pairs={{0,4},{4,8},{8,12},{12,16},{16,20},{20,24},{24,28},{28,32},{32,36}... | collective-permute-start | bytes 1867784 | tf_op jit(solution)/shard_map/ppermute | solution.py:153
  36.5 2.1 %copy-start.2 = (f32[16,24,8,256]{3,2,1,0:T(8,128)S(1)}, f32[16,24,8,256]{3,2,1,0:T(8,128)}, u32[]{:S(2)}) copy-start(f32[16,24,8,256]{3,2,1,0:T(8,128)} %param.3) | copy-start | bytes 9437188
  40.4 3.1 %copy-start = (f32[16,30,8,256]{3,2,1,0:T(8,128)}, f32[16,30,8,256]{3,2,1,0:T(8,128)S(1)}, u32[]{:S(2)}) copy-start(f32[16,30,8,256]{3,2,1,0:T(8,128)S(1)} %multiply_add_fusion) | copy-start | bytes 11796484
  52.7 0.9 copy-start.4
  54.9 5.3 %copy-start.1 = (f32[16,28,8,256]{3,2,1,0:T(8,128)}, f32[16,28,8,256]{3,2,1,0:T(8,128)S(1)}, u32[]{:S(2)}) copy-start(f32[16,28,8,256]{3,2,1,0:T(8,128)S(1)} %multiply_add_fusion.1) | copy-start | bytes 11010052
  57.9 2.3 %copy-start.9 = (f32[24,8,256]{2,1,0:T(8,128)S(1)}, f32[24,8,256]{2,1,0:T(8,128)}, u32[]{:S(2)}) copy-start(f32[24,8,256]{2,1,0:T(8,128)} %param.5) | copy-start | bytes 589828
  66.7 1.2 copy-start.6
  66.7 1.4 %copy-start.5 = (f32[26,8,256]{2,1,0:T(8,128)S(1)}, f32[26,8,256]{2,1,0:T(8,128)}, u32[]{:S(2)}) copy-start(f32[26,8,256]{2,1,0:T(8,128)} %get-tuple-element.29) | copy-start | bytes 638980
  70.4 1.2 copy-start.8
  70.4 2.0 %copy-start.3 = (f32[16,24,8,256]{3,2,1,0:T(8,128)S(1)}, f32[16,24,8,256]{3,2,1,0:T(8,128)}, u32[]{:S(2)}) copy-start(f32[16,24,8,256]{3,2,1,0:T(8,128)} %param.3) | copy-start | bytes 9437188
  70.5 2.0 %copy-start.7 = (f32[24,8,256]{2,1,0:T(8,128)S(1)}, f32[24,8,256]{2,1,0:T(8,128)}, u32[]{:S(2)}) copy-start(f32[24,8,256]{2,1,0:T(8,128)} %get-tuple-element.12) | copy-start | bytes 589828

commit v5 on v4

--- a/solution.py
+++ b/solution.py
@@ -141,6 +141,23 @@
     )
 
 
+def four_steps(state, east, north, weight):
+    span = state.shape[1]
+    for step in range(2):
+        state = forward_core(state, east[step:span - step], north[step:span - step])
+    state = weight[2:span - 2] * state
+    for step in range(2, 4):
+        state = adjoint_core(state, east[step:span - step], north[step:span - step])
+    return state
+
+
+def coarsen(sketch):
+    probe_count, lon_count, level_count, lat_count = sketch.shape
+    coarse = sketch.reshape(probe_count, lon_count // 4, 4, level_count, lat_count).sum(axis=2)
+    coarse = coarse.reshape(probe_count, lon_count // 4, level_count, lat_count // 4, 4).sum(axis=4)
+    return coarse * (1.0 / 16.0)
+
+
 def body(increments, winds, obs_weight):
     probe_count, lon_count, level_count, lat_count = increments.shape
     halo = 4
@@ -152,25 +169,21 @@
     east_edge = jnp.concatenate([part[:, :halo] for part in pack], axis=0)
     from_west = lax.ppermute(west_edge, "lon", forward)
     from_east = lax.ppermute(east_edge, "lon", backward)
-    wide = [
-        jnp.concatenate([from_west[lo:hi], part, from_east[lo:hi]], axis=1)
-        for part, (lo, hi) in zip(
-            pack,
-            ((0, probe_count), (probe_count, probe_count + 1),
-             (probe_count + 1, probe_count + 2), (probe_count + 2, probe_count + 3)),
-        )
-    ]
-    state, east, north, weight = wide[0], wide[1][0], wide[2][0], wide[3][0]
-    span = lon_count + 2 * halo
-    for step in range(2):
-        state = forward_core(state, east[step:span - step], north[step:span - step])
-    state = weight[2:span - 2] * state
-    for step in range(2, 4):
-        state = adjoint_core(state, east[step:span - step], north[step:span - step])
-    sketch = increments + state
-    coarse = sketch.reshape(probe_count, lon_count // 4, 4, level_count, lat_count).sum(axis=2)
-    coarse = coarse.reshape(probe_count, lon_count // 4, level_count, lat_count // 4, 4).sum(axis=4)
-    coarse = coarse * (1.0 / 16.0)
+    bounds = ((0, probe_count), (probe_count, probe_count + 1),
+              (probe_count + 1, probe_count + 2), (probe_count + 2, probe_count + 3))
+
+    def fields(parts):
+        return parts[0], parts[1][0], parts[2][0], parts[3][0]
+
+    inner = four_steps(*fields(pack))
+    inner = coarsen(increments[:, halo:lon_count - halo] + inner)
+    west = [jnp.concatenate([from_west[lo:hi], part[:, :2 * halo]], axis=1)
+            for part, (lo, hi) in zip(pack, bounds)]
+    west = coarsen(increments[:, :halo] + four_steps(*fields(west)))
+    east = [jnp.concatenate([part[:, lon_count - 2 * halo:], from_east[lo:hi]], axis=1)
+            for part, (lo, hi) in zip(pack, bounds)]
+    east = coarsen(increments[:, lon_count - halo:] + four_steps(*fields(east)))
+    coarse = jnp.concatenate([west, inner, east], axis=1)
     coarse = coarse.reshape(probe_count, -1)
     all_probes = probe_count * lax.axis_size("probe")
     ident = jnp.eye(all_probes, dtype=jnp.float32)

time: 137 us -> 125 us (0.912); the launches traced: 136 us -> 122 us
  waiting for transfers between devices: 20.3 us -> 7.57 us
  other arithmetic: 47.3 us -> 38.1 us
  local copies, waits for them, and re-layouts: 22.5 us -> 30.4 us
    ppermute x1, waiting for transfers between devices: 8.04 us -> 0.01 us  [body(): from_west = lax.ppermute(west_edge, 'lon', forward)]
    sub x1 -> x3, other arithmetic: 6.83 us -> 1.45 us  [forward_core(): return inner - (flux_w[:, 1:] - flux_w[:, :-1]) - (flux_n - flux_s)]
    ppermute x1, waiting for transfers between devices: 12.3 us -> 7.57 us  [body(): from_east = lax.ppermute(east_edge, 'lon', backward)]
    mul x3 -> x8, other arithmetic: 6.54 us -> 2.1 us  [the longest x5 1.34 us: four_steps(): state = weight[2:span - 2] * state]
    slice x3 -> x12, local copies, waits for them, and re-layouts: 0.05 us -> 3.84 us  [the longest x4 3.56 us: body(): part[:, :2 * halo]]
    add x2 -> x6, other arithmetic: 4.62 us -> 1.27 us  [forward_core(): flux_w = a_pos[1:] * widened[:, :-1] + b_neg[1:] * widened[:, 1:]]
    slice x4 -> x10, local copies, waits for them, and re-layouts: 7.05 us -> 3.93 us  [above(): field[..., 1:]]
    ppermute x1, starting transfers between devices: 9.86 us -> 7.49 us  [body(): from_east = lax.ppermute(east_edge, 'lon', backward)]
  transfers between devices with their start and end apart: 2 -> 2, of which waited for: 2 -> 1; matrix products, arithmetic and copies ran while one was open for 1% -> 25% of each run, Pallas kernels for 0% -> 0%
where the time goes in v5:
time: 125 us; the launch traced here: 122 us
  other arithmetic  38.1 us (30%)
  local copies, waits for them, and re-layouts  30.4 us (24%)
  Pallas kernels  24.5 us (20%)
  starting transfers between devices  9.79 us (8%)
  blocking collectives  8.45 us (7%)
  waiting for transfers between devices  7.57 us (6%)
  matrix products  2.1 us (2%)
  between operations  1.4 us (1%)
    pallas_call x1, Pallas kernels, butterfly_sum(): pl.pallas_call(functools.partial(exchange_kernel, count, radix), out_shap...  24.5 us
    all_gather x1, blocking collectives, body(): full_panel = lax.all_gather(coarse, 'probe', axis=0, tiled=True)  8.45 us
    ppermute x1, waiting for transfers between devices, body(): from_east = lax.ppermute(east_edge, 'lon', backward)  7.57 us
    ppermute x1, starting transfers between devices, body(): from_east = lax.ppermute(east_edge, 'lon', backward)  7.49 us
    another operation x3, other arithmetic, body(): lower = jnp.linalg.cholesky(gram)  6.52 us
    reduce_sum x3, other arithmetic, coarsen(): coarse.reshape(probe_count, lon_count // 4, level_count, lat_count // 4, 4)  5.71 us
    reduce_sum x3, local copies, waits for them, and re-layouts, coarsen(): sketch.reshape(probe_count, lon_count // 4, 4, level_count, lat_count)  5.58 us
    another operation x1, other arithmetic, body(): lax.linalg.triangular_solve(lower, ident, left_side=True, lower=True)  4.9 us
  transfers between devices with their start and end apart: 2, of which 1 were waited for; matrix products, arithmetic and copies ran while one was open for 25% of the time, Pallas kernels for 0%

profile of v5, /device:TPU:8, one launch (start us, length us, event | category | flops | bytes accessed | tf_op | source)
XLA Modules:
  0.0 122.2 jit_solution(4487017046563899631)
XLA Ops:
  0.7 1.5 %fusion.118 = (f32[1,4,8,256]{3,2,1,0:T(8,128)S(1)}, f32[1,4,8,256]{3,2,1,0:T(8,128)}) fusion(f32[1,24,8,256]{3,2,1,0:T(8,128)} %bitcast.146), kind=kLoop, calls=%fused_computation.263 | loop fusion | bytes 131072 | tf_op jit(solution)/shard_map/slice | solution.py:168
  2.2 1.0 fusion.115
  3.3 1.5 %minimum_bitcast_fusion.13 = (f32[4,8,256]{2,1,0:T(8,128)S(1)}, f32[4,8,256]{2,1,0:T(8,128)S(1)}, f32[4,8,256]{2,1,0:T(8,128)}, f32[4,8,256]{2,1,0:T(8,128)S(1)}...) fusion(f32[1,24,8,256]{3,2,1,0:T(8,128)S(1)} %get-tuple-element, ...), kind=kLoop, calls=%fused_computation.238 | loop fusion | flops 32768 | bytes 393216 | tf_op jit(solution)/shard_map/min | solution.py:129
  4.8 0.9 pad_maximum_fusion
  5.6 2.3 %collective-permute-start = (f32[19,4,8,256]{3,2,1,0:T(8,128)}, f32[19,4,8,256]{3,2,1,0:T(8,128)}, u32[]{:S(2)}, u32[]{:S(2)}) collective-permute-start(f32[19,4,8,256]{3,2,1,0:T(8,128)} %pad_maximum_fusion), channel_id=1, source_target_pairs={{0,4},{4,8},{8,12},{12,16},{16,20},{20,24},{24,28},{28,32},{32,36}... | collective-permute-start | bytes 1867784 | tf_op jit(solution)/shard_map/ppermute | solution.py:170
  7.9 0.9 fusion.113
  10.0 0.8 multiply_add_fusion.1
  10.9 0.8 slice.856
  15.7 0.8 fusion.105
  16.8 1.2 %fusion.8 = f32[16,18,8,256]{3,2,1,0:T(8,128)S(1)} fusion(f32[16,20,8,256]{3,2,1,0:T(8,128)S(1)} %fusion.5, f32[16,18,8,255]{3,2,1,0:T(8,128)S(1)} %get-tuple-element.29, f32[16,18,8,255]{3,2,1,0:T(8,128)S(1)} %get-tuple-element.28, f32[18,8,256]{2,1,0:T(8,128)S(1)} %get-tuple-element.80, f32[18,8,256]{2,1,0:T(8,128)S(1)} %get-tuple-element.67, ...), kind=kLoop, calls=%fused_computation.22 | loop fusion | flops 5308416 | bytes 14874624 | tf_op jit(solution)/shard_map/add | solution.py:136
  19.1 1.3 %fusion.13 = f32[16,16,8,256]{3,2,1,0:T(8,128)S(1)} fusion(f32[16,18,8,256]{3,2,1,0:T(8,128)S(1)} %fusion.8, f32[16,16,8,255]{3,2,1,0:T(8,128)S(1)} %get-tuple-element.31, f32[16,16,8,255]{3,2,1,0:T(8,128)S(1)} %get-tuple-element.30, f32[16,24,8,256]{3,2,1,0:T(8,128)S(1)} %copy-done, f32[16,8,256]{2,1,0:T(8,128)S(1)} %get-tuple-element.81, ...), kind=kLoop, calls=%fused_computation.30 | loop fusion | flops 5242880 | bytes 15319040 | tf_op jit(solution)/shard_map/add | solution.py:179
  21.4 2.9 %copy.38 = f32[16,4,8,256]{0,2,3,1:T(8,128)} copy(f32[16,4,8,256]{3,2,1,0:T(8,128)S(1)} %reduce_sum.56) | data formatting | bytes 1048576 | tf_op jit(solution)/shard_map/reduce_sum | solution.py:156
  24.3 4.2 %reduce_sum.57 = f32[16,4,8,64]{0,2,3,1:T(8,128)} reduce(f32[16,4,8,64,4]{0,2,4,3,1:T(8,128)} %bitcast.143, f32[]{:T(128)} %constant.74.clone.1), dimensions={4}, to_apply=%region_3.4 | reduce | flops 98304 | bytes 655364 | tf_op jit(solution)/shard_map/reduce_sum | solution.py:157
  28.5 2.3 %copy.39 = f32[16,4,8,64]{3,2,1,0:T(8,128)} copy(f32[16,4,8,64]{0,2,3,1:T(8,128)} %reduce_sum.57) | data formatting | bytes 262144 | tf_op jit(solution)/shard_map/reduce_sum | solution.py:157
  30.8 1.5 %fusion.116 = (f32[1,8,8,256]{3,2,1,0:T(8,128)S(1)}, f32[1,8,8,256]{3,2,1,0:T(8,128)}) fusion(f32[1,24,8,256]{3,2,1,0:T(8,128)} %bitcast.147), kind=kLoop, calls=%fused_computation.261 | loop fusion | bytes 262144 | tf_op jit(solution)/shard_map/slice | solution.py:180
  32.3 1.2 fusion.104
  33.5 0.8 fusion.111
  34.4 1.1 slice.800
  40.0 1.0 fusion.61
  41.0 0.9 pad_maximum_fusion.1
  41.9 7.5 %collective-permute-start.1 = (f32[19,4,8,256]{3,2,1,0:T(8,128)}, f32[19,4,8,256]{3,2,1,0:T(8,128)}, u32[]{:S(2)}, u32[]{:S(2)}) collective-permute-start(f32[19,4,8,256]{3,2,1,0:T(8,128)} %pad_maximum_fusion.1), channel_id=1, source_target_pairs={{4,0},{8,4},{12,8},{16,12},{20,16},{24,20},{28,24},{32,28},{36,32}... | collective-permute-start | bytes 1867784 | tf_op jit(solution)/shard_map/ppermute | solution.py:171
  49.4 2.2 %copy.37 = f32[16,8,256]{0,1,2:T(8,128)} copy(f32[16,8,256]{2,1,0:T(8,128)} %get-tuple-element.24) | data formatting | bytes 262144 | tf_op jit(solution)/shard_map/reduce_sum | solution.py:156
  51.7 1.4 %bitcast_reduce_fusion.1 = f32[16,8,64]{0,1,2:T(8,128)S(1)} fusion(f32[16,8,256]{0,1,2:T(8,128)} %copy.37), kind=kLoop, calls=%fused_computation.80 | loop fusion | flops 24576 | bytes 163840 | tf_op jit(solution)/shard_map/reduce_sum | solution.py:157
  53.8 1.7 %copy.41 = f32[16,1,8,64]{3,2,1,0:T(8,128)} copy(f32[16,1,8,64]{0,2,3,1:T(8,128)} %multiply_bitcast_fusion.1) | data formatting | bytes 65536 | tf_op jit(solution)/shard_map/mul | solution.py:158
  55.4 7.6 %collective-permute-done.1 = f32[19,4,8,256]{3,2,1,0:T(8,128)} collective-permute-done((f32[19,4,8,256]{3,2,1,0:T(8,128)}, f32[19,4,8,256]{3,2,1,0:T(8,128)}, u32[]{:S(2)}, u32[]{:S(2)}) %collective-permute-start.1) | collective-permute-done | bytes 622624 | tf_op jit(solution)/shard_map/ppermute | solution.py:171
  63.9 1.1 slice.888
  72.1 8.5 %all_gather.3 = f32[64,3072]{1,0:T(8,128)S(1)} all-gather(f32[16,3072]{1,0:T(8,128)S(1)} %reshape.219), channel_id=1, replica_groups=mesh['lon'=64,'probe'=4] {'probe'}, dimensions={0}, use_global_device_ids=true | all-gather | bytes 983040 | tf_op jit(solution)/shard_map/all_gather | solution.py:190
  80.6 1.4 %fusion.119.block_ref = f32[64,64]{1,0:T(8,128)} fusion(f32[64,3072]{1,0:T(8,128)S(1)} %all_gather.3), kind=kOutput, calls=%fused_computation.264 | convolution fusion | flops 150994944 | bytes 802816 | tf_op jit(solution)/shard_map/dot_general | solution.py:191
  82.0 24.5 %shard_map.50 = f32[64,64]{1,0:T(8,128)} custom-call(f32[64,64]{1,0:T(8,128)} %fusion.119.block_ref), custom_call_target="tpu_custom_call" | custom-call | tf_op jit(solution)/shard_map/pallas_call | solution.py:71
  106.4 0.8 copy.43
  108.0 5.8 %cholesky.17 = f32[64,64]{1,0:T(8,128)S(1)} custom-call(f32[64,64]{1,0:T(8,128)S(1)} %fusion.95), custom_call_target="Cholesky" | custom-call | tf_op jit(solution)/shard_map/jit(cholesky)/cholesky | solution.py:198
  115.2 4.9 %custom-call.6 = f32[1,64,64]{1,2,0:T(8,128)S(1)} custom-call(f32[1,64,64]{2,1,0:T(8,128)S(1)} %get-tuple-element.105), custom_call_target="InvertDiagBlocksLowerTriangular" | custom-call | tf_op jit(solution)/shard_map/triangular_solve | solution.py:199
  (130 shorter events, 24.6 us)
Async XLA Ops:
  0.6 4.1 %slice-start = ((f32[16,24,8,256]{3,2,1,0:T(8,128)}), f32[16,4,8,256]{3,2,1,0:T(8,128)S(1)}, s32[]{:S(2)}) async-start(f32[16,24,8,256]{3,2,1,0:T(8,128)} %param.3), calls=%async_computation | async-start | bytes 1048576 | tf_op jit(solution)/shard_map/slice | solution.py:168
  0.6 8.2 %copy-start = (f32[16,24,8,256]{3,2,1,0:T(8,128)S(1)}, f32[16,24,8,256]{3,2,1,0:T(8,128)}, u32[]{:S(2)}) copy-start(f32[16,24,8,256]{3,2,1,0:T(8,128)} %param.3) | copy-start | bytes 9437188
  3.3 17.1 %copy-start.6 = (f32[1,24,8,256]{3,2,1,0:T(8,128)}, f32[1,24,8,256]{3,2,1,0:T(8,128)S(1)}, u32[]{:S(2)}) copy-start(f32[1,24,8,256]{3,2,1,0:T(8,128)S(1)} %get-tuple-element.51) | copy-start | bytes 589828
  5.6 27.9 %collective-permute-start = (f32[19,4,8,256]{3,2,1,0:T(8,128)}, f32[19,4,8,256]{3,2,1,0:T(8,128)}, u32[]{:S(2)}, u32[]{:S(2)}) collective-permute-start(f32[19,4,8,256]{3,2,1,0:T(8,128)} %pad_maximum_fusion), channel_id=1, source_target_pairs={{0,4},{4,8},{8,12},{12,16},{16,20},{20,24},{24,28},{28,32},{32,36}... | collective-permute-start | bytes 1867784 | tf_op jit(solution)/shard_map/ppermute | solution.py:170
  8.8 1.0 copy-start.5
  8.8 1.1 copy-start.8
  9.8 1.1 copy-start.3
  15.7 0.9 slice-start.1
  15.7 1.0 copy-start.4
  18.0 0.9 slice-start.2
  24.3 8.0 %copy-start.1 = (f32[16,24,8,256]{3,2,1,0:T(8,128)S(1)}, f32[16,24,8,256]{3,2,1,0:T(8,128)}, u32[]{:S(2)}) copy-start(f32[16,24,8,256]{3,2,1,0:T(8,128)} %param.3) | copy-start | bytes 9437188
  39.2 1.8 %copy-start.13 = (f32[1,4,8,256]{3,2,1,0:T(8,128)S(1)}, f32[1,4,8,256]{3,2,1,0:T(8,128)}, u32[]{:S(2)}) copy-start(f32[1,4,8,256]{3,2,1,0:T(8,128)} %get-tuple-element.63) | copy-start | bytes 98308
  40.0 9.4 %copy-start.7 = (f32[16,4,8,64]{3,2,1,0:T(8,128)S(1)}, f32[16,4,8,64]{3,2,1,0:T(8,128)}, u32[]{:S(2)}) copy-start(f32[16,4,8,64]{3,2,1,0:T(8,128)} %copy.39) | copy-start | bytes 393220
  41.9 21.1 %collective-permute-start.1 = (f32[19,4,8,256]{3,2,1,0:T(8,128)}, f32[19,4,8,256]{3,2,1,0:T(8,128)}, u32[]{:S(2)}, u32[]{:S(2)}) collective-permute-start(f32[19,4,8,256]{3,2,1,0:T(8,128)} %pad_maximum_fusion.1), channel_id=1, source_target_pairs={{4,0},{8,4},{12,8},{16,12},{20,16},{24,20},{28,24},{32,28},{36,32}... | collective-permute-start | bytes 1867784 | tf_op jit(solution)/shard_map/ppermute | solution.py:171
  55.4 9.6 %copy-start.2 = (f32[16,8,8,256]{3,2,1,0:T(8,128)S(1)}, f32[16,8,8,256]{3,2,1,0:T(8,128)}, u32[]{:S(2)}) copy-start(f32[16,8,8,256]{3,2,1,0:T(8,128)} %get-tuple-element.27) | copy-start | bytes 3145732
  67.2 0.8 copy-start.10
  69.2 0.8 copy-start.12
  69.2 1.5 %copy-start.11 = (f32[4,8,256]{2,1,0:T(8,128)S(1)}, f32[4,8,256]{2,1,0:T(8,128)}, u32[]{:S(2)}) copy-start(f32[4,8,256]{2,1,0:T(8,128)} %get-tuple-element.54) | copy-start | bytes 98308
  71.1 0.8 copy-start.9

commit v6 on v5

--- a/solution.py
+++ b/solution.py
@@ -177,12 +177,16 @@
 
     inner = four_steps(*fields(pack))
     inner = coarsen(increments[:, halo:lon_count - halo] + inner)
-    west = [jnp.concatenate([from_west[lo:hi], part[:, :2 * halo]], axis=1)
-            for part, (lo, hi) in zip(pack, bounds)]
-    west = coarsen(increments[:, :halo] + four_steps(*fields(west)))
-    east = [jnp.concatenate([part[:, lon_count - 2 * halo:], from_east[lo:hi]], axis=1)
-            for part, (lo, hi) in zip(pack, bounds)]
-    east = coarsen(increments[:, lon_count - halo:] + four_steps(*fields(east)))
+    rim = [
+        jnp.concatenate(
+            [from_west[lo:hi], part[:, :2 * halo], part[:, lon_count - 2 * halo:], from_east[lo:hi]],
+            axis=1,
+        )
+        for part, (lo, hi) in zip(pack, bounds)
+    ]
+    rim = four_steps(*fields(rim))
+    west = coarsen(increments[:, :halo] + rim[:, :halo])
+    east = coarsen(increments[:, lon_count - halo:] + rim[:, rim.shape[1] - halo:])
     coarse = jnp.concatenate([west, inner, east], axis=1)
     coarse = coarse.reshape(probe_count, -1)
     all_probes = probe_count * lax.axis_size("probe")

time: 125 us -> 114 us (0.912); the launches traced: 122 us -> 113 us
  waiting for transfers between devices: 7.57 us -> 0.01 us
  Pallas kernels: 24.5 us -> 21.8 us
  other arithmetic: 38.1 us -> 40.2 us
  local copies, waits for them, and re-layouts: 30.4 us -> 29 us
    ppermute x1, waiting for transfers between devices: 7.57 us -> 0.01 us  [body(): from_east = lax.ppermute(east_edge, 'lon', backward)]
    pallas_call x1, Pallas kernels: 24.5 us -> 21.8 us  [butterfly_sum(): pl.pallas_call(functools.partial(exchange_kernel, count, radix), out_shap...]
    ppermute x1, starting transfers between devices: 2.3 us -> 0.01 us  [body(): from_west = lax.ppermute(west_edge, 'lon', forward)]
    ppermute x1, starting transfers between devices: 7.49 us -> 9.78 us  [body(): from_east = lax.ppermute(east_edge, 'lon', backward)]
    reduce_sum x3 -> x2, other arithmetic: 1.6 us -> 3.48 us  [coarsen(): sketch.reshape(probe_count, lon_count // 4, 4, level_count, lat_count)]
    slice x4 -> x3, local copies, waits for them, and re-layouts: 3.56 us -> 1.73 us  [body(): part[:, :2 * halo]]
    mul x2, local copies, waits for them, and re-layouts: 1.82 us -> 0.26 us  [coarsen(): return coarse * (1.0 / 16.0)]
    slice x3, local copies, waits for them, and re-layouts: 1.56 us -> 3.08 us  [body(): part[:, lon_count - halo:]]
  transfers between devices with their start and end apart: 2 -> 2, of which waited for: 1 -> 0; matrix products, arithmetic and copies ran while one was open for 25% -> 27% of each run, Pallas kernels for 0% -> 0%
where the time goes in v6:
time: 114 us; the launch traced here: 113 us
  other arithmetic  40.2 us (35%)
  local copies, waits for them, and re-layouts  29 us (25%)
  Pallas kernels  21.8 us (19%)
  starting transfers between devices  9.79 us (9%)
  blocking collectives  8.45 us (7%)
  matrix products  2.1 us (2%)
  between operations  1.31 us (1%)
    pallas_call x1, Pallas kernels, butterfly_sum(): pl.pallas_call(functools.partial(exchange_kernel, count, radix), out_shap...  21.8 us
    ppermute x1, starting transfers between devices, body(): from_east = lax.ppermute(east_edge, 'lon', backward)  9.78 us
    all_gather x1, blocking collectives, body(): full_panel = lax.all_gather(coarse, 'probe', axis=0, tiled=True)  8.45 us
    another operation x3, other arithmetic, body(): lower = jnp.linalg.cholesky(gram)  6.52 us
    reduce_sum x3, local copies, waits for them, and re-layouts, coarsen(): sketch.reshape(probe_count, lon_count // 4, 4, level_count, lat_count)  5.59 us
    another operation x1, other arithmetic, body(): lax.linalg.triangular_solve(lower, ident, left_side=True, lower=True)  4.9 us
    reduce_sum x3, other arithmetic, coarsen(): coarse.reshape(probe_count, lon_count // 4, level_count, lat_count // 4, 4)  4.29 us
    slice x8, local copies, waits for them, and re-layouts, below(): field[..., :-1]  4.02 us
  transfers between devices with their start and end apart: 2, of which 0 were waited for; matrix products, arithmetic and copies ran while one was open for 27% of the time, Pallas kernels for 0%

profile of v6, /device:TPU:8, one launch (start us, length us, event | category | flops | bytes accessed | tf_op | source)
XLA Modules:
  0.0 112.6 jit_solution(11222737068656156246)
XLA Ops:
  1.4 1.0 fusion.56
  2.5 0.8 fusion.58
  3.3 1.5 %fusion.48 = (f32[16,4,8,256]{3,2,1,0:T(8,128)S(1)}, f32[16,4,8,256]{3,2,1,0:T(8,128)S(1)}) fusion(f32[16,24,8,256]{3,2,1,0:T(8,128)} %param.3), kind=kLoop, calls=%fused_computation.141 | loop fusion | bytes 2097152 | tf_op jit(solution)/shard_map/slice | solution.py:168
  4.8 0.9 pad_maximum_fusion.2
  5.7 9.8 %collective-permute-start.1 = (f32[19,4,8,256]{3,2,1,0:T(8,128)}, f32[19,4,8,256]{3,2,1,0:T(8,128)}, u32[]{:S(2)}, u32[]{:S(2)}) collective-permute-start(f32[19,4,8,256]{3,2,1,0:T(8,128)} %pad_maximum_fusion.2), channel_id=1, source_target_pairs={{4,0},{8,4},{12,8},{16,12},{20,16},{24,20},{28,24},{32,28},{36,32}... | collective-permute-start | bytes 1867784 | tf_op jit(solution)/shard_map/ppermute | solution.py:171
  15.5 0.9 pad_maximum_fusion.1
  19.5 0.9 multiply_add_fusion.1
  20.5 0.8 slice.640
  25.2 0.8 fusion.50
  26.3 1.2 %fusion.15 = f32[16,18,8,256]{3,2,1,0:T(8,128)S(1)} fusion(f32[16,20,8,256]{3,2,1,0:T(8,128)S(1)} %fusion.9, f32[16,18,8,255]{3,2,1,0:T(8,128)S(1)} %get-tuple-element.21, f32[16,18,8,255]{3,2,1,0:T(8,128)S(1)} %get-tuple-element.20, f32[18,8,256]{2,1,0:T(8,128)S(1)} %get-tuple-element.78, f32[18,8,256]{2,1,0:T(8,128)S(1)} %get-tuple-element.43, ...), kind=kLoop, calls=%fused_computation.32 | loop fusion | flops 5308416 | bytes 14874624 | tf_op jit(solution)/shard_map/add | solution.py:136
  28.6 2.6 %fusion.24 = f32[16,16,8,256]{3,2,1,0:T(8,128)} fusion(f32[16,18,8,256]{3,2,1,0:T(8,128)S(1)} %fusion.15, f32[16,16,8,255]{3,2,1,0:T(8,128)S(1)} %get-tuple-element.25, f32[16,16,8,255]{3,2,1,0:T(8,128)S(1)} %get-tuple-element.24, f32[16,24,8,256]{3,2,1,0:T(8,128)S(1)} %copy-done, f32[16,8,256]{2,1,0:T(8,128)S(1)} %get-tuple-element.83, ...), kind=kLoop, calls=%fused_computation.47 | loop fusion | flops 5242880 | bytes 15319040 | tf_op jit(solution)/shard_map/add | solution.py:179
  31.2 2.6 %reduce_sum.56 = f32[16,4,8,256]{3,2,1,0:T(8,128)} reduce(f32[16,4,4,8,256]{4,3,2,1,0:T(8,128)} %bitcast.106, f32[]{:T(128)} %constant.61.clone.1), dimensions={2}, to_apply=%region_2.3 | reduce | flops 393216 | bytes 2621444 | tf_op jit(solution)/shard_map/reduce_sum | solution.py:156
  33.9 3.6 %copy.38 = f32[16,4,8,256]{0,2,3,1:T(8,128)} copy(f32[16,4,8,256]{3,2,1,0:T(8,128)} %reduce_sum.56) | data formatting | bytes 1048576 | tf_op jit(solution)/shard_map/reduce_sum | solution.py:156
  37.5 4.0 %reduce_sum.57 = f32[16,4,8,64]{0,2,3,1:T(8,128)} reduce(f32[16,4,8,64,4]{0,2,4,3,1:T(8,128)} %bitcast.105, f32[]{:T(128)} %constant.61.clone.1), dimensions={4}, to_apply=%region_3.4 | reduce | flops 98304 | bytes 655364 | tf_op jit(solution)/shard_map/reduce_sum | solution.py:157
  41.5 2.3 %copy.39 = f32[16,4,8,64]{3,2,1,0:T(8,128)} copy(f32[16,4,8,64]{0,2,3,1:T(8,128)} %reduce_sum.57) | data formatting | bytes 262144 | tf_op jit(solution)/shard_map/reduce_sum | solution.py:157
  43.8 1.0 broadcast_multiply_fusion
  44.8 0.9 fusion.59
  45.7 0.9 maximum_minimum_fusion
  48.6 1.1 slice.587
  49.7 1.1 slice.586
  51.4 0.8 multiply_add_fusion.2
  57.2 0.8 fusion.51
  58.2 1.2 %fusion.19 = f32[16,18,8,256]{3,2,1,0:T(8,128)S(1)} fusion(f32[16,20,8,256]{3,2,1,0:T(8,128)S(1)} %fusion.12, f32[16,18,8,255]{3,2,1,0:T(8,128)S(1)} %get-tuple-element.23, f32[16,18,8,255]{3,2,1,0:T(8,128)S(1)} %get-tuple-element.22, f32[18,8,256]{2,1,0:T(8,128)S(1)} %get-tuple-element.82, f32[18,8,256]{2,1,0:T(8,128)S(1)} %get-tuple-element.54, ...), kind=kLoop, calls=%fused_computation.39 | loop fusion | flops 5308416 | bytes 14874624 | tf_op jit(solution)/shard_map/add | solution.py:136
  60.4 1.1 fusion.28
  61.5 0.8 fusion.31
  62.3 1.5 %copy.40 = f32[16,8,256]{0,1,2:T(8,128)S(1)} copy(f32[16,8,256]{2,1,0:T(8,128)} %get-tuple-element.15) | data formatting | bytes 262144 | tf_op jit(solution)/shard_map/reduce_sum | solution.py:156
  65.1 8.5 %all_gather.3 = f32[64,3072]{1,0:T(8,128)S(1)} all-gather(f32[16,3072]{1,0:T(8,128)S(1)} %reshape.175), channel_id=1, replica_groups=mesh['lon'=64,'probe'=4] {'probe'}, dimensions={0}, use_global_device_ids=true | all-gather | bytes 983040 | tf_op jit(solution)/shard_map/all_gather | solution.py:194
  73.6 1.4 %fusion.62.block_ref = f32[64,64]{1,0:T(8,128)} fusion(f32[64,3072]{1,0:T(8,128)S(1)} %all_gather.3), kind=kOutput, calls=%fused_computation.155 | convolution fusion | flops 150994944 | bytes 802816 | tf_op jit(solution)/shard_map/dot_general | solution.py:195
  75.0 21.8 %shard_map.50 = f32[64,64]{1,0:T(8,128)} custom-call(f32[64,64]{1,0:T(8,128)} %fusion.62.block_ref), custom_call_target="tpu_custom_call" | custom-call | tf_op jit(solution)/shard_map/pallas_call | solution.py:71
  96.8 0.8 copy.43
  98.4 5.8 %cholesky.17 = f32[64,64]{1,0:T(8,128)S(1)} custom-call(f32[64,64]{1,0:T(8,128)S(1)} %fusion.43), custom_call_target="Cholesky" | custom-call | tf_op jit(solution)/shard_map/jit(cholesky)/cholesky | solution.py:202
  105.6 4.9 %custom-call.6 = f32[1,64,64]{1,2,0:T(8,128)S(1)} custom-call(f32[1,64,64]{2,1,0:T(8,128)S(1)} %get-tuple-element.87), custom_call_target="InvertDiagBlocksLowerTriangular" | custom-call | tf_op jit(solution)/shard_map/triangular_solve | solution.py:203
  (103 shorter events, 22.9 us)
Async XLA Ops:
  2.5 13.9 %copy-start.3 = (f32[2,24,8,256]{3,2,1,0:T(8,128)S(1)}, f32[2,24,8,256]{3,2,1,0:T(8,128)}, u32[]{:S(2)}) copy-start(f32[2,24,8,256]{3,2,1,0:T(8,128)} %param.4) | copy-start | bytes 1179652
  3.3 14.4 %copy-start = (f32[16,24,8,256]{3,2,1,0:T(8,128)S(1)}, f32[16,24,8,256]{3,2,1,0:T(8,128)}, u32[]{:S(2)}) copy-start(f32[16,24,8,256]{3,2,1,0:T(8,128)} %param.3) | copy-start | bytes 9437188
  5.7 41.0 %collective-permute-start.1 = (f32[19,4,8,256]{3,2,1,0:T(8,128)}, f32[19,4,8,256]{3,2,1,0:T(8,128)}, u32[]{:S(2)}, u32[]{:S(2)}) collective-permute-start(f32[19,4,8,256]{3,2,1,0:T(8,128)} %pad_maximum_fusion.2), channel_id=1, source_target_pairs={{4,0},{8,4},{12,8},{16,12},{20,16},{24,20},{28,24},{32,28},{36,32}... | collective-permute-start | bytes 1867784 | tf_op jit(solution)/shard_map/ppermute | solution.py:171
  16.4 31.2 %collective-permute-start = (f32[19,4,8,256]{3,2,1,0:T(8,128)}, f32[19,4,8,256]{3,2,1,0:T(8,128)}, u32[]{:S(2)}, u32[]{:S(2)}) collective-permute-start(f32[19,4,8,256]{3,2,1,0:T(8,128)} %pad_maximum_fusion.1), channel_id=1, source_target_pairs={{0,4},{4,8},{8,12},{12,16},{16,20},{20,24},{24,28},{28,32},{32,36}... | collective-permute-start | bytes 1867784 | tf_op jit(solution)/shard_map/ppermute | solution.py:170
  17.7 0.9 copy-start.5
  18.0 2.5 %copy-start.1 = (f32[24,8,256]{2,1,0:T(8,128)}, f32[24,8,256]{2,1,0:T(8,128)S(1)}, u32[]{:S(2)}) copy-start(f32[24,8,256]{2,1,0:T(8,128)S(1)} %bitcast_select_fusion) | copy-start | bytes 589828
  25.2 0.9 slice-start
  25.2 1.0 copy-start.2
  27.5 0.9 slice-start.1
  44.8 3.6 %copy-start.7 = (f32[1,8,8,256]{3,2,1,0:T(8,128)S(1)}, f32[1,8,8,256]{3,2,1,0:T(8,128)}, u32[]{:S(2)}) copy-start(f32[1,8,8,256]{3,2,1,0:T(8,128)} %get-tuple-element.36) | copy-start | bytes 196612
  44.8 3.6 %copy-start.8 = (f32[1,8,8,256]{3,2,1,0:T(8,128)S(1)}, f32[1,8,8,256]{3,2,1,0:T(8,128)}, u32[]{:S(2)}) copy-start(f32[1,8,8,256]{3,2,1,0:T(8,128)} %get-tuple-element.37) | copy-start | bytes 196612
  48.4 2.4 %copy-start.4 = (f32[1,24,8,256]{3,2,1,0:T(8,128)}, f32[1,24,8,256]{3,2,1,0:T(8,128)S(1)}, u32[]{:S(2)}) copy-start(f32[1,24,8,256]{3,2,1,0:T(8,128)S(1)} %pad_maximum_fusion.4) | copy-start | bytes 589828
  52.2 0.9 slice-start.2
  59.4 0.9 copy-start.6

commit v7 on v6

--- a/solution.py
+++ b/solution.py
@@ -153,9 +153,17 @@
 
 def coarsen(sketch):
     probe_count, lon_count, level_count, lat_count = sketch.shape
-    coarse = sketch.reshape(probe_count, lon_count // 4, 4, level_count, lat_count).sum(axis=2)
-    coarse = coarse.reshape(probe_count, lon_count // 4, level_count, lat_count // 4, 4).sum(axis=4)
-    return coarse * (1.0 / 16.0)
+    summed = sketch.reshape(probe_count, lon_count // 4, 4, level_count, lat_count).sum(axis=2)
+    rows = lax.broadcasted_iota(jnp.int32, (lat_count, lat_count // 4), 0) // 4
+    cols = lax.broadcasted_iota(jnp.int32, (lat_count, lat_count // 4), 1)
+    average = jnp.where(rows == cols, 1.0 / 16.0, 0.0).astype(jnp.float32)
+    coarse = jnp.dot(
+        summed.reshape(-1, lat_count),
+        average,
+        precision=lax.Precision.HIGHEST,
+        preferred_element_type=jnp.float32,
+    )
+    return coarse.reshape(probe_count, lon_count // 4, level_count, lat_count // 4)
 
 
 def body(increments, winds, obs_weight):

time: 114 us -> 108 us (0.947)
  local copies, waits for them, and re-layouts: 29 us -> 21.8 us
  matrix products: 2.1 us -> 4.25 us
    reduce_sum x4 -> x0, local copies, waits for them, and re-layouts: 7.9 us -> none  [the longest x3 5.59 us: coarsen(): sketch.reshape(probe_count, lon_count // 4, 4, level_count, lat_count)]
    reduce_sum x3 -> x0, other arithmetic: 4.29 us -> none  [coarsen(): coarse.reshape(probe_count, lon_count // 4, level_count, lat_count // 4, 4)]
    add x1, other arithmetic: 2.6 us -> 6.86 us  [body(): inner = coarsen(increments[:, halo:lon_count - halo] + inner)]
    slice x8, local copies, waits for them, and re-layouts: 4.02 us -> 6.21 us  [below(): field[..., :-1]]
    dot_general x0 -> x3, matrix products: none -> 2.15 us  [coarsen(): jnp.dot(summed.reshape(-1, lat_count), average, precision=lax.Precision.H...]
  transfers between devices with their start and end apart: 2 -> 2, of which waited for: 0 -> 0; matrix products, arithmetic and copies ran while one was open for 27% -> 26% of each run, Pallas kernels for 0% -> 0%
where the time goes in v7:
time: 108 us
  other arithmetic  39.9 us (37%)
  local copies, waits for them, and re-layouts  21.8 us (20%)
  Pallas kernels  21.8 us (20%)
  starting transfers between devices  9.79 us (9%)
  blocking collectives  8.67 us (8%)
  matrix products  4.25 us (4%)
  between operations  1.27 us (1%)
    pallas_call x1, Pallas kernels, butterfly_sum(): pl.pallas_call(functools.partial(exchange_kernel, count, radix), out_shap...  21.8 us
    ppermute x1, starting transfers between devices, body(): from_east = lax.ppermute(east_edge, 'lon', backward)  9.78 us
    all_gather x1, blocking collectives, body(): full_panel = lax.all_gather(coarse, 'probe', axis=0, tiled=True)  8.67 us
    add x1, other arithmetic, body(): inner = coarsen(increments[:, halo:lon_count - halo] + inner)  6.86 us
    another operation x3, other arithmetic, body(): lower = jnp.linalg.cholesky(gram)  6.52 us
    slice x8, local copies, waits for them, and re-layouts, below(): field[..., :-1]  6.21 us
    another operation x1, other arithmetic, body(): lax.linalg.triangular_solve(lower, ident, left_side=True, lower=True)  4.9 us
    slice x6, local copies, waits for them, and re-layouts, above(): field[..., 1:]  3.93 us
  transfers between devices with their start and end apart: 2, of which 0 were waited for; matrix products, arithmetic and copies ran while one was open for 26% of the time, Pallas kernels for 0%

profile of v7, /device:TPU:8, one launch (start us, length us, event | category | flops | bytes accessed | tf_op | source)
XLA Modules:
  0.0 107.6 jit_solution(8761668478826832046)
XLA Ops:
  0.6 0.8 fusion.83
  1.4 1.0 fusion.78
  2.5 0.8 fusion.80
  3.3 1.5 %fusion.70 = (f32[16,4,8,256]{3,2,1,0:T(8,128)S(1)}, f32[16,4,8,256]{3,2,1,0:T(8,128)S(1)}) fusion(f32[16,24,8,256]{3,2,1,0:T(8,128)} %param.3), kind=kLoop, calls=%fused_computation.168 | loop fusion | bytes 2097152 | tf_op jit(solution)/shard_map/slice | solution.py:176
  4.8 0.9 pad_maximum_fusion.2
  5.7 9.8 %collective-permute-start.1 = (f32[19,4,8,256]{3,2,1,0:T(8,128)}, f32[19,4,8,256]{3,2,1,0:T(8,128)}, u32[]{:S(2)}, u32[]{:S(2)}) collective-permute-start(f32[19,4,8,256]{3,2,1,0:T(8,128)} %pad_maximum_fusion.2), channel_id=1, source_target_pairs={{4,0},{8,4},{12,8},{16,12},{20,16},{24,20},{28,24},{32,28},{36,32}... | collective-permute-start | bytes 1867784 | tf_op jit(solution)/shard_map/ppermute | solution.py:179
  15.5 0.9 pad_maximum_fusion.1
  19.5 0.9 multiply_add_fusion.1
  20.4 0.8 slice.640
  25.2 0.8 fusion.72
  26.3 1.2 %fusion.15 = f32[16,18,8,256]{3,2,1,0:T(8,128)S(1)} fusion(f32[16,20,8,256]{3,2,1,0:T(8,128)S(1)} %fusion.9, f32[16,18,8,255]{3,2,1,0:T(8,128)S(1)} %get-tuple-element.13, f32[16,18,8,255]{3,2,1,0:T(8,128)S(1)} %get-tuple-element.12, f32[18,8,256]{2,1,0:T(8,128)S(1)} %get-tuple-element.70, f32[18,8,256]{2,1,0:T(8,128)S(1)} %get-tuple-element.35, ...), kind=kLoop, calls=%fused_computation.32 | loop fusion | flops 5308416 | bytes 14874624 | tf_op jit(solution)/shard_map/add | solution.py:136
  27.5 2.8 %fusion.74 = (f32[16,16,8,255]{3,2,1,0:T(8,128)}, f32[16,16,8,255]{3,2,1,0:T(8,128)}) fusion(f32[16,18,8,256]{3,2,1,0:T(8,128)S(1)} %fusion.15), kind=kLoop, calls=%fused_computation.172 | loop fusion | bytes 8355840 | tf_op jit(solution)/shard_map/slice | solution.py:106
  31.8 6.9 %fusion.24 = f32[16,16,8,256]{3,2,1,0:T(8,128)} fusion(f32[16,18,8,256]{3,2,1,0:T(8,128)} %copy-done.1, f32[16,16,8,255]{3,2,1,0:T(8,128)} %get-tuple-element.17, f32[16,16,8,255]{3,2,1,0:T(8,128)} %get-tuple-element.16, f32[16,24,8,256]{3,2,1,0:T(8,128)S(1)} %copy-done, f32[16,8,256]{2,1,0:T(8,128)} %get-tuple-element.75, ...), kind=kLoop, calls=%fused_computation.47 | loop fusion | flops 5242880 | bytes 15319040 | tf_op jit(solution)/shard_map/add | solution.py:187
  38.7 2.6 %reduce_sum.28 = f32[16,4,8,256]{3,2,1,0:T(8,128)} reduce(f32[16,4,4,8,256]{4,3,2,1,0:T(8,128)} %bitcast.114, f32[]{:T(128)} %constant.79.clone.1), dimensions={2}, to_apply=%region_1.2 | reduce | flops 393216 | bytes 2621444 | tf_op jit(solution)/shard_map/reduce_sum | solution.py:156
  41.3 1.6 %fusion.41 = f32[16,4,8,64]{3,2,1,0:T(8,128)S(1)} fusion(f32[16,4,8,256]{3,2,1,0:T(8,128)} %reduce_sum.28, s32[256]{0:T(256)S(1)} %get-tuple-element.82, s32[256]{0:T(256)S(1)} %get-tuple-element.83, pred[256]{0:T(512)(128)(4,1)S(1)} %compare_and_fusion), kind=kOutput, calls=%fused_computation.122 | convolution fusion | flops 100712448 | bytes 657664 | tf_op jit(solution)/shard_map/dot_general | solution.py:160
  43.0 0.9 maximum_minimum_fusion
  44.0 0.8 fusion.77
  44.8 0.8 fusion.76
  45.9 1.1 %slice.587 = f32[16,4,8,256]{3,2,1,0:T(8,128)S(1)} slice(f32[19,4,8,256]{3,2,1,0:T(8,128)} %collective-permute-done.1), slice={[0:16], [0:4], [0:8], [0:256]} | slice | bytes 1048576 | tf_op jit(solution)/shard_map/slice | solution.py:190
  46.9 1.1 %slice.586 = f32[16,4,8,256]{3,2,1,0:T(8,128)S(1)} slice(f32[19,4,8,256]{3,2,1,0:T(8,128)} %collective-permute-done), slice={[0:16], [0:4], [0:8], [0:256]} | slice | bytes 1048576 | tf_op jit(solution)/shard_map/slice | solution.py:190
  48.8 0.8 multiply_add_fusion.2
  49.7 0.8 slice.603
  54.6 0.8 fusion.73
  55.6 1.2 %fusion.19 = f32[16,18,8,256]{3,2,1,0:T(8,128)S(1)} fusion(f32[16,20,8,256]{3,2,1,0:T(8,128)S(1)} %fusion.12, f32[16,18,8,255]{3,2,1,0:T(8,128)S(1)} %get-tuple-element.15, f32[16,18,8,255]{3,2,1,0:T(8,128)S(1)} %get-tuple-element.14, f32[18,8,256]{2,1,0:T(8,128)S(1)} %get-tuple-element.74, f32[18,8,256]{2,1,0:T(8,128)S(1)} %get-tuple-element.46, ...), kind=kLoop, calls=%fused_computation.39 | loop fusion | flops 5308416 | bytes 14874624 | tf_op jit(solution)/shard_map/add | solution.py:136
  57.8 1.1 %fusion.28 = f32[16,16,8,256]{3,2,1,0:T(8,128)S(1)} fusion(f32[16,18,8,256]{3,2,1,0:T(8,128)S(1)} %fusion.19, f32[16,16,8,255]{3,2,1,0:T(8,128)S(1)} %get-tuple-element.19, f32[16,16,8,255]{3,2,1,0:T(8,128)S(1)} %get-tuple-element.18, f32[16,8,256]{2,1,0:T(8,128)S(1)} %get-tuple-element.77, f32[16,8,256]{2,1,0:T(8,128)S(1)} %maximum_minimum_fusion, ...), kind=kLoop, calls=%fused_computation.54 | loop fusion | flops 4718592 | bytes 13221888 | tf_op jit(solution)/shard_map/add | solution.py:136
  59.8 8.7 %all_gather.3 = f32[64,3072]{1,0:T(8,128)S(1)} all-gather(f32[16,3072]{1,0:T(8,128)S(1)} %reshape.159), channel_id=1, replica_groups=mesh['lon'=64,'probe'=4] {'probe'}, dimensions={0}, use_global_device_ids=true | all-gather | bytes 983040 | tf_op jit(solution)/shard_map/all_gather | solution.py:202
  68.5 1.4 %fusion.84.block_ref = f32[64,64]{1,0:T(8,128)} fusion(f32[64,3072]{1,0:T(8,128)S(1)} %all_gather.3), kind=kOutput, calls=%fused_computation.182 | convolution fusion | flops 150994944 | bytes 802816 | tf_op jit(solution)/shard_map/dot_general | solution.py:203
  69.9 21.8 %shard_map.50 = f32[64,64]{1,0:T(8,128)} custom-call(f32[64,64]{1,0:T(8,128)} %fusion.84.block_ref), custom_call_target="tpu_custom_call" | custom-call | tf_op jit(solution)/shard_map/pallas_call | solution.py:71
  91.8 0.8 copy.10
  92.6 0.8 fusion.44
  93.4 5.8 %cholesky.17 = f32[64,64]{1,0:T(8,128)S(1)} custom-call(f32[64,64]{1,0:T(8,128)S(1)} %fusion.44), custom_call_target="Cholesky" | custom-call | tf_op jit(solution)/shard_map/jit(cholesky)/cholesky | solution.py:210
  100.5 4.9 %custom-call.6 = f32[1,64,64]{1,2,0:T(8,128)S(1)} custom-call(f32[1,64,64]{2,1,0:T(8,128)S(1)} %get-tuple-element.79), custom_call_target="InvertDiagBlocksLowerTriangular" | custom-call | tf_op jit(solution)/shard_map/triangular_solve | solution.py:211
  (96 shorter events, 19.3 us)
Async XLA Ops:
  2.5 13.9 %copy-start.4 = (f32[2,24,8,256]{3,2,1,0:T(8,128)S(1)}, f32[2,24,8,256]{3,2,1,0:T(8,128)}, u32[]{:S(2)}) copy-start(f32[2,24,8,256]{3,2,1,0:T(8,128)} %param.4) | copy-start | bytes 1179652
  3.3 14.4 %copy-start = (f32[16,24,8,256]{3,2,1,0:T(8,128)S(1)}, f32[16,24,8,256]{3,2,1,0:T(8,128)}, u32[]{:S(2)}) copy-start(f32[16,24,8,256]{3,2,1,0:T(8,128)} %param.3) | copy-start | bytes 9437188
  5.7 38.3 %collective-permute-start.1 = (f32[19,4,8,256]{3,2,1,0:T(8,128)}, f32[19,4,8,256]{3,2,1,0:T(8,128)}, u32[]{:S(2)}, u32[]{:S(2)}) collective-permute-start(f32[19,4,8,256]{3,2,1,0:T(8,128)} %pad_maximum_fusion.2), channel_id=1, source_target_pairs={{4,0},{8,4},{12,8},{16,12},{20,16},{24,20},{28,24},{32,28},{36,32}... | collective-permute-start | bytes 1867784 | tf_op jit(solution)/shard_map/ppermute | solution.py:179
  16.4 28.4 %collective-permute-start = (f32[19,4,8,256]{3,2,1,0:T(8,128)}, f32[19,4,8,256]{3,2,1,0:T(8,128)}, u32[]{:S(2)}, u32[]{:S(2)}) collective-permute-start(f32[19,4,8,256]{3,2,1,0:T(8,128)} %pad_maximum_fusion.1), channel_id=1, source_target_pairs={{0,4},{4,8},{8,12},{12,16},{16,20},{20,24},{24,28},{28,32},{32,36}... | collective-permute-start | bytes 1867784 | tf_op jit(solution)/shard_map/ppermute | solution.py:178
  17.7 0.9 copy-start.6
  18.0 2.5 %copy-start.2 = (f32[24,8,256]{2,1,0:T(8,128)}, f32[24,8,256]{2,1,0:T(8,128)S(1)}, u32[]{:S(2)}) copy-start(f32[24,8,256]{2,1,0:T(8,128)S(1)} %bitcast_select_fusion) | copy-start | bytes 589828
  25.2 0.9 slice-start
  25.2 1.0 copy-start.3
  27.5 2.8 %copy-start.1 = (f32[16,18,8,256]{3,2,1,0:T(8,128)}, f32[16,18,8,256]{3,2,1,0:T(8,128)S(1)}, u32[]{:S(2)}) copy-start(f32[16,18,8,256]{3,2,1,0:T(8,128)S(1)} %fusion.15) | copy-start | bytes 7077892
  27.5 2.8 %slice-start.1 = ((f32[24,8,256]{2,1,0:T(8,128)}), f32[16,8,256]{2,1,0:T(8,128)S(1)}, s32[]{:S(2)}) async-start(f32[24,8,256]{2,1,0:T(8,128)} %copy-done.2), calls=%async_computation.1 | async-start | bytes 262144 | tf_op jit(solution)/shard_map/slice | solution.py:128
  43.0 2.7 %copy-start.8 = (f32[1,8,8,256]{3,2,1,0:T(8,128)S(1)}, f32[1,8,8,256]{3,2,1,0:T(8,128)}, u32[]{:S(2)}) copy-start(f32[1,8,8,256]{3,2,1,0:T(8,128)} %get-tuple-element.29) | copy-start | bytes 196612
  45.7 2.4 %copy-start.5 = (f32[1,24,8,256]{3,2,1,0:T(8,128)}, f32[1,24,8,256]{3,2,1,0:T(8,128)S(1)}, u32[]{:S(2)}) copy-start(f32[1,24,8,256]{3,2,1,0:T(8,128)S(1)} %pad_maximum_fusion.4) | copy-start | bytes 589828
  49.6 0.9 slice-start.2
  56.8 0.9 copy-start.7

commit v8 on v7

--- a/solution.py
+++ b/solution.py
@@ -166,6 +166,92 @@
     return coarse.reshape(probe_count, lon_count // 4, level_count, lat_count // 4)
 
 
+def lat_below(x, lanes):
+    rolled = pltpu.roll(x, 1, x.ndim - 1)
+    return jnp.where(lanes > 0, rolled, 0.0)
+
+
+def lat_above(x, lanes):
+    rolled = pltpu.roll(x, x.shape[-1] - 1, x.ndim - 1)
+    return jnp.where(lanes < x.shape[-1] - 1, rolled, 0.0)
+
+
+def stencil_kernel(q_ref, a_ref, b_ref, c_ref, d_ref, w_ref, o_ref):
+    span = q_ref.shape[1]
+    field = q_ref[0]
+    lanes = lax.broadcasted_iota(jnp.int32, field.shape[1:], 1)[None]
+    state = field
+    for step in range(2):
+        lo, hi = step, span - step
+        east_a = a_ref[lo:hi]
+        east_b = b_ref[lo:hi]
+        north_c = c_ref[lo + 1:hi - 1]
+        north_d = d_ref[lo + 1:hi - 1]
+        flux_w = east_a[1:] * state[:-1] + east_b[1:] * state[1:]
+        inner = state[1:-1]
+        flux_s = north_c * lat_below(inner, lanes) + north_d * inner
+        flux_n = lat_above(flux_s, lanes)
+        state = inner - (flux_w[1:] - flux_w[:-1]) - (flux_n - flux_s)
+    state = w_ref[2:span - 2] * state
+    for step in range(2, 4):
+        lo, hi = step, span - step
+        west_b = b_ref[lo + 1:hi - 1]
+        east_a = a_ref[lo + 2:hi]
+        north_c = c_ref[lo + 1:hi - 1]
+        north_d = d_ref[lo + 1:hi - 1]
+        north_up = lat_above(north_c, lanes)
+        inner = state[1:-1]
+        state = (
+            inner * (1.0 - east_a + west_b - north_up + north_d)
+            - west_b * state[:-2]
+            + east_a * state[2:]
+            - north_d * lat_below(inner, lanes)
+            + north_up * lat_above(inner, lanes)
+        )
+    sketch = field[4:span - 4] + state
+    groups = sketch.shape[0] // 4
+    for g in range(groups):
+        o_ref[0, g] = ((sketch[4 * g] + sketch[4 * g + 1]) + sketch[4 * g + 2]) + sketch[4 * g + 3]
+
+
+def stencil_sums(slab, east, north, weight):
+    probe_count, span, level_count, lat_count = slab.shape
+    groups = (span - 8) // 4
+    winds = (
+        jnp.maximum(east, 0.0),
+        jnp.minimum(east, 0.0),
+        jnp.maximum(north, 0.0),
+        jnp.minimum(north, 0.0),
+        weight,
+    )
+    full = pl.BlockSpec((span, level_count, lat_count), lambda i: (0, 0, 0))
+    elements = probe_count * span * level_count * lat_count
+    return pl.pallas_call(
+        stencil_kernel,
+        out_shape=jax.ShapeDtypeStruct((probe_count, groups, level_count, lat_count), slab.dtype),
+        grid=(probe_count,),
+        in_specs=[pl.BlockSpec((1, span, level_count, lat_count), lambda i: (i, 0, 0, 0))] + [full] * 5,
+        out_specs=pl.BlockSpec((1, groups, level_count, lat_count), lambda i: (i, 0, 0, 0)),
+        cost_estimate=pl.CostEstimate(
+            flops=80 * elements, transcendentals=0, bytes_accessed=4 * elements + 20 * span * level_count * lat_count
+        ),
+    )(slab, *winds)
+
+
+def lat_average(summed):
+    probe_count, groups, level_count, lat_count = summed.shape
+    rows = lax.broadcasted_iota(jnp.int32, (lat_count, lat_count // 4), 0) // 4
+    cols = lax.broadcasted_iota(jnp.int32, (lat_count, lat_count // 4), 1)
+    average = jnp.where(rows == cols, 1.0 / 16.0, 0.0).astype(jnp.float32)
+    coarse = jnp.dot(
+        summed.reshape(-1, lat_count),
+        average,
+        precision=lax.Precision.HIGHEST,
+        preferred_element_type=jnp.float32,
+    )
+    return coarse.reshape(probe_count, groups, level_count, lat_count // 4)
+
+
 def body(increments, winds, obs_weight):
     probe_count, lon_count, level_count, lat_count = increments.shape
     halo = 4
@@ -183,8 +269,7 @@
     def fields(parts):
         return parts[0], parts[1][0], parts[2][0], parts[3][0]
 
-    inner = four_steps(*fields(pack))
-    inner = coarsen(increments[:, halo:lon_count - halo] + inner)
+    inner = stencil_sums(*fields(pack))
     rim = [
         jnp.concatenate(
             [from_west[lo:hi], part[:, :2 * halo], part[:, lon_count - 2 * halo:], from_east[lo:hi]],
@@ -192,10 +277,9 @@
         )
         for part, (lo, hi) in zip(pack, bounds)
     ]
-    rim = four_steps(*fields(rim))
-    west = coarsen(increments[:, :halo] + rim[:, :halo])
-    east = coarsen(increments[:, lon_count - halo:] + rim[:, rim.shape[1] - halo:])
-    coarse = jnp.concatenate([west, inner, east], axis=1)
+    rim = stencil_sums(*fields(rim))
+    summed = jnp.concatenate([rim[:, :1], inner, rim[:, rim.shape[1] - 1:]], axis=1)
+    coarse = lat_average(summed)
     coarse = coarse.reshape(probe_count, -1)
     all_probes = probe_count * lax.axis_size("probe")
     ident = jnp.eye(all_probes, dtype=jnp.float32)

time: 108 us -> 113 us (1.046)
  Pallas kernels: 21.8 us -> 51.1 us
  other arithmetic: 39.9 us -> 21.5 us
  local copies, waits for them, and re-layouts: 21.8 us -> 11.5 us
  waiting for transfers between devices: 0.01 us -> 5.34 us
  matrix products: 4.25 us -> 3.02 us
    pallas_call x0 -> x2, Pallas kernels: none -> 29.4 us  [stencil_sums(): pl.pallas_call(stencil_kernel, out_shape=jax.ShapeDtypeStruct((probe_coun...]
    add x16 -> x0, other arithmetic: 15.9 us -> none  [the longest x1 6.86 us: body(): inner = coarsen(increments[:, halo:lon_count - halo] + inner)]
    slice x26 -> x1, local copies, waits for them, and re-layouts: 10.4 us -> 0.99 us  [body(): rim[:, :1]]
    ppermute x1, waiting for transfers between devices: 0.01 us -> 3.82 us  [body(): from_east = lax.ppermute(east_edge, 'lon', backward)]
    min x2 -> x4, other arithmetic: 0.91 us -> 4.23 us  [the longest x2 2.65 us: stencil_sums(): jnp.minimum(east, 0.0)]
    reduce_sum x2 -> x0, other arithmetic: 2.81 us -> none  [coarsen(): sketch.reshape(probe_count, lon_count // 4, 4, level_count, lat_count)]
    ppermute x1, starting transfers between devices: 0.01 us -> 2.3 us  [body(): from_west = lax.ppermute(west_edge, 'lon', forward)]
    ppermute x1, starting transfers between devices: 9.78 us -> 7.49 us  [body(): from_east = lax.ppermute(east_edge, 'lon', backward)]
  transfers between devices with their start and end apart: 2 -> 2, of which waited for: 0 -> 2; matrix products, arithmetic and copies ran while one was open for 26% -> 4% of each run, Pallas kernels for 0% -> 13%
where the time goes in v8:
time: 113 us; the launch traced here: 112 us
  Pallas kernels  51.1 us (45%)
  other arithmetic  21.5 us (19%)
  local copies, waits for them, and re-layouts  11.5 us (10%)
  starting transfers between devices  9.79 us (9%)
  blocking collectives  8.45 us (7%)
  waiting for transfers between devices  5.34 us (5%)
  matrix products  3.02 us (3%)
    pallas_call x2, Pallas kernels, stencil_sums(): pl.pallas_call(stencil_kernel, out_shape=jax.ShapeDtypeStruct((probe_coun...  29.4 us
    pallas_call x1, Pallas kernels, butterfly_sum(): pl.pallas_call(functools.partial(exchange_kernel, count, radix), out_shap...  21.7 us
    all_gather x1, blocking collectives, body(): full_panel = lax.all_gather(coarse, 'probe', axis=0, tiled=True)  8.45 us
    ppermute x1, starting transfers between devices, body(): from_east = lax.ppermute(east_edge, 'lon', backward)  7.49 us
    another operation x3, other arithmetic, body(): lower = jnp.linalg.cholesky(gram)  6.52 us
    another operation x1, other arithmetic, body(): lax.linalg.triangular_solve(lower, ident, left_side=True, lower=True)  4.9 us
    ppermute x1, waiting for transfers between devices, body(): from_east = lax.ppermute(east_edge, 'lon', backward)  3.82 us
    slice x3, local copies, waits for them, and re-layouts, body(): part[:, lon_count - halo:]  2.87 us
  transfers between devices with their start and end apart: 2, of which 2 were waited for; matrix products, arithmetic and copies ran while one was open for 4% of the time, Pallas kernels for 13%

profile of v8, /device:TPU:8, one launch (start us, length us, event | category | flops | bytes accessed | tf_op | source)
XLA Modules:
  0.0 111.5 jit_solution(16881863641319731602)
XLA Ops:
  0.7 1.9 %minimum_bitcast_fusion = (f32[24,8,256]{2,1,0:T(8,128)}, f32[1,24,8,256]{3,2,1,0:T(8,128)S(1)}, f32[24,8,256]{2,1,0:T(8,128)}) fusion(f32[2,24,8,256]{3,2,1,0:T(8,128)} %param.4, pred[256]{0:T(512)(128)(4,1)S(1)} %iota_compare_fusion.5), kind=kLoop, calls=%fused_computation.9 | loop fusion | flops 147456 | bytes 983296 | tf_op jit(solution)/shard_map/min | solution.py:222
  2.5 0.8 fusion.24
  3.3 0.8 fusion.28
  4.1 1.3 %fusion.18 = (f32[16,4,8,256]{3,2,1,0:T(8,128)S(1)}, f32[16,4,8,256]{3,2,1,0:T(8,128)S(1)}) fusion(f32[16,24,8,256]{3,2,1,0:T(8,128)} %q_ref.1), kind=kLoop, calls=%fused_computation.48 | loop fusion | bytes 2097152 | tf_op jit(solution)/shard_map/slice | solution.py:262
  5.4 0.9 pad_maximum_fusion.2
  6.3 2.3 %collective-permute-start = (f32[19,4,8,256]{3,2,1,0:T(8,128)}, f32[19,4,8,256]{3,2,1,0:T(8,128)}, u32[]{:S(2)}, u32[]{:S(2)}) collective-permute-start(f32[19,4,8,256]{3,2,1,0:T(8,128)} %pad_maximum_fusion.2), channel_id=1, source_target_pairs={{0,4},{4,8},{8,12},{12,16},{16,20},{20,24},{24,28},{28,32},{32,36}... | collective-permute-start | bytes 1867784 | tf_op jit(solution)/shard_map/ppermute | solution.py:264
  8.6 0.9 pad_maximum_fusion.3
  9.5 7.5 %collective-permute-start.1 = (f32[19,4,8,256]{3,2,1,0:T(8,128)}, f32[19,4,8,256]{3,2,1,0:T(8,128)}, u32[]{:S(2)}, u32[]{:S(2)}) collective-permute-start(f32[19,4,8,256]{3,2,1,0:T(8,128)} %pad_maximum_fusion.3), channel_id=1, source_target_pairs={{4,0},{8,4},{12,8},{16,12},{20,16},{24,20},{28,24},{32,28},{36,32}... | collective-permute-start | bytes 1867784 | tf_op jit(solution)/shard_map/ppermute | solution.py:265
  18.4 0.8 fusion
  19.2 14.7 %shard_map.51 = f32[16,4,8,256]{3,2,1,0:T(8,128)} custom-call(f32[16,24,8,256]{3,2,1,0:T(8,128)} %q_ref.1, f32[24,8,256]{2,1,0:T(8,128)} %get-tuple-element.22.a_ref, f32[24,8,256]{2,1,0:T(8,128)} %get-tuple-element.20.b_ref, f32[24,8,256]{2,1,0:T(8,128)} %get-tuple-element.19.c_ref, f32[24,8,256]{2,1,0:T(8,128)} %get-tuple-element.18.d_ref, f32[24,8,256]{2,1,0:T(8,128)} %w_ref.1), custom_call_target="tpu_custom_call" | custom-call | flops 62914560 | bytes 4128768 | tf_op jit(solution)/shard_map/pallas_call | solution.py:229
  34.0 1.5 %collective-permute-done = f32[19,4,8,256]{3,2,1,0:T(8,128)} collective-permute-done((f32[19,4,8,256]{3,2,1,0:T(8,128)}, f32[19,4,8,256]{3,2,1,0:T(8,128)}, u32[]{:S(2)}, u32[]{:S(2)}) %collective-permute-start) | collective-permute-done | bytes 622624 | tf_op jit(solution)/shard_map/ppermute | solution.py:264
  35.6 0.8 fusion.20
  36.4 3.8 %collective-permute-done.1 = f32[19,4,8,256]{3,2,1,0:T(8,128)} collective-permute-done((f32[19,4,8,256]{3,2,1,0:T(8,128)}, f32[19,4,8,256]{3,2,1,0:T(8,128)}, u32[]{:S(2)}, u32[]{:S(2)}) %collective-permute-start.1) | collective-permute-done | bytes 622624 | tf_op jit(solution)/shard_map/ppermute | solution.py:265
  40.2 0.8 fusion.21
  41.0 0.8 minimum_bitcast_fusion.1
  41.8 0.7 maximum_bitcast_fusion.w_ref
  42.5 0.8 minimum_bitcast_fusion.2
  43.3 1.1 slice.128
  44.4 1.1 slice.131
  45.4 1.9 %pad_maximum_fusion.q_ref = f32[16,24,8,256]{3,2,1,0:T(8,128)} fusion(f32[16,4,8,256]{3,2,1,0:T(8,128)S(1)} %slice.131, f32[16,8,8,256]{3,2,1,0:T(8,128)S(1)} %get-tuple-element.9, f32[16,8,8,256]{3,2,1,0:T(8,128)S(1)} %get-tuple-element.8, f32[16,4,8,256]{3,2,1,0:T(8,128)S(1)} %slice.128), kind=kLoop, calls=%fused_computation | loop fusion | flops 2359296 | bytes 6291456 | tf_op jit(solution)/shard_map/concatenate | solution.py:274
  47.3 14.7 %shard_map.50 = f32[16,4,8,256]{3,2,1,0:T(8,128)} custom-call(f32[16,24,8,256]{3,2,1,0:T(8,128)} %pad_maximum_fusion.q_ref, f32[24,8,256]{2,1,0:T(8,128)} %get-tuple-element.34.a_ref, f32[24,8,256]{2,1,0:T(8,128)} %get-tuple-element.33.b_ref, f32[24,8,256]{2,1,0:T(8,128)} %get-tuple-element.30.c_ref, f32[24,8,256]{2,1,0:T(8,128)} %get-tuple-element.29.d_ref, ...), custom_call_target="tpu_custom_call" | custom-call | flops 62914560 | bytes 4128768 | tf_op jit(solution)/shard_map/pallas_call | solution.py:229
  62.0 1.0 fusion.22
  63.1 0.9 fusion.2
  64.2 8.5 %all_gather.3 = f32[64,3072]{1,0:T(8,128)S(1)} all-gather(f32[16,3072]{1,0:T(8,128)S(1)} %reshape_reshape.3), channel_id=1, replica_groups=mesh['lon'=64,'probe'=4] {'probe'}, dimensions={0}, use_global_device_ids=true | all-gather | bytes 983040 | tf_op jit(solution)/shard_map/all_gather | solution.py:286
  72.6 1.4 %fusion.29.block_ref = f32[64,64]{1,0:T(8,128)} fusion(f32[64,3072]{1,0:T(8,128)S(1)} %all_gather.3), kind=kOutput, calls=%fused_computation.59 | convolution fusion | flops 150994944 | bytes 802816 | tf_op jit(solution)/shard_map/dot_general | solution.py:287
  74.0 21.7 %shard_map.52 = f32[64,64]{1,0:T(8,128)} custom-call(f32[64,64]{1,0:T(8,128)} %fusion.29.block_ref), custom_call_target="tpu_custom_call" | custom-call | tf_op jit(solution)/shard_map/pallas_call | solution.py:71
  95.7 0.8 copy.9
  96.6 0.8 fusion.11
  97.3 5.8 %cholesky.17 = f32[64,64]{1,0:T(8,128)S(1)} custom-call(f32[64,64]{1,0:T(8,128)S(1)} %fusion.11), custom_call_target="Cholesky" | custom-call | tf_op jit(solution)/shard_map/jit(cholesky)/cholesky | solution.py:294
  104.5 4.9 %custom-call.6 = f32[1,64,64]{1,2,0:T(8,128)S(1)} custom-call(f32[1,64,64]{2,1,0:T(8,128)S(1)} %get-tuple-element.40), custom_call_target="InvertDiagBlocksLowerTriangular" | custom-call | tf_op jit(solution)/shard_map/triangular_solve | solution.py:295
  110.1 0.7 copy.15
  110.8 0.7 copy.11
  (30 shorter events, 3.8 us)
Async XLA Ops:
  0.6 17.1 %copy-start.3 = (f32[24,8,256]{2,1,0:T(8,128)S(1)}, f32[24,8,256]{2,1,0:T(8,128)}, u32[]{:S(2)}) copy-start(f32[24,8,256]{2,1,0:T(8,128)} %w_ref.1) | copy-start | bytes 589828
  0.7 17.7 %copy-start.2 = (f32[2,24,8,256]{3,2,1,0:T(8,128)S(1)}, f32[2,24,8,256]{3,2,1,0:T(8,128)}, u32[]{:S(2)}) copy-start(f32[2,24,8,256]{3,2,1,0:T(8,128)} %param.4) | copy-start | bytes 1179652
  6.3 29.2 %collective-permute-start = (f32[19,4,8,256]{3,2,1,0:T(8,128)}, f32[19,4,8,256]{3,2,1,0:T(8,128)}, u32[]{:S(2)}, u32[]{:S(2)}) collective-permute-start(f32[19,4,8,256]{3,2,1,0:T(8,128)} %pad_maximum_fusion.2), channel_id=1, source_target_pairs={{0,4},{4,8},{8,12},{12,16},{16,20},{20,24},{24,28},{28,32},{32,36}... | collective-permute-start | bytes 1867784 | tf_op jit(solution)/shard_map/ppermute | solution.py:264
  9.5 24.4 %copy-start = (f32[16,24,8,256]{3,2,1,0:T(8,128)S(1)}, f32[16,24,8,256]{3,2,1,0:T(8,128)}, u32[]{:S(2)}) copy-start(f32[16,24,8,256]{3,2,1,0:T(8,128)} %q_ref.1) | copy-start | bytes 9437188
  9.5 30.7 %collective-permute-start.1 = (f32[19,4,8,256]{3,2,1,0:T(8,128)}, f32[19,4,8,256]{3,2,1,0:T(8,128)}, u32[]{:S(2)}, u32[]{:S(2)}) collective-permute-start(f32[19,4,8,256]{3,2,1,0:T(8,128)} %pad_maximum_fusion.3), channel_id=1, source_target_pairs={{4,0},{8,4},{12,8},{16,12},{20,16},{24,20},{28,24},{32,28},{36,32}... | collective-permute-start | bytes 1867784 | tf_op jit(solution)/shard_map/ppermute | solution.py:265
  33.8 7.1 %copy-start.4 = (f32[1,8,8,256]{3,2,1,0:T(8,128)S(1)}, f32[1,8,8,256]{3,2,1,0:T(8,128)}, u32[]{:S(2)}) copy-start(f32[1,8,8,256]{3,2,1,0:T(8,128)} %get-tuple-element.31) | copy-start | bytes 196612
  33.8 7.2 %copy-start.5 = (f32[1,8,8,256]{3,2,1,0:T(8,128)S(1)}, f32[1,8,8,256]{3,2,1,0:T(8,128)}, u32[]{:S(2)}) copy-start(f32[1,8,8,256]{3,2,1,0:T(8,128)} %get-tuple-element.32) | copy-start | bytes 196612
  33.8 7.9 %copy-start.6 = (f32[1,8,8,256]{3,2,1,0:T(8,128)S(1)}, f32[1,8,8,256]{3,2,1,0:T(8,128)}, u32[]{:S(2)}) copy-start(f32[1,8,8,256]{3,2,1,0:T(8,128)} %get-tuple-element.27) | copy-start | bytes 196612
  33.9 7.9 %copy-start.7 = (f32[1,8,8,256]{3,2,1,0:T(8,128)S(1)}, f32[1,8,8,256]{3,2,1,0:T(8,128)}, u32[]{:S(2)}) copy-start(f32[1,8,8,256]{3,2,1,0:T(8,128)} %get-tuple-element.28) | copy-start | bytes 196612
  47.3 15.7 %copy-start.1 = (f32[16,4,8,256]{3,2,1,0:T(8,128)S(1)}, f32[16,4,8,256]{3,2,1,0:T(8,128)}, u32[]{:S(2)}) copy-start(f32[16,4,8,256]{3,2,1,0:T(8,128)} %shard_map.51) | copy-start | bytes 1572868

commit v9 on v8

--- a/solution.py
+++ b/solution.py
@@ -166,20 +166,10 @@
     return coarse.reshape(probe_count, lon_count // 4, level_count, lat_count // 4)
 
 
-def lat_below(x, lanes):
-    rolled = pltpu.roll(x, 1, x.ndim - 1)
-    return jnp.where(lanes > 0, rolled, 0.0)
-
-
-def lat_above(x, lanes):
-    rolled = pltpu.roll(x, x.shape[-1] - 1, x.ndim - 1)
-    return jnp.where(lanes < x.shape[-1] - 1, rolled, 0.0)
-
-
-def stencil_kernel(q_ref, a_ref, b_ref, c_ref, d_ref, w_ref, o_ref):
+def stencil_kernel(q_ref, a_ref, b_ref, c_ref, d_ref, w_ref, n_ref, k_ref, o_ref):
     span = q_ref.shape[1]
+    lat = q_ref.shape[-1]
     field = q_ref[0]
-    lanes = lax.broadcasted_iota(jnp.int32, field.shape[1:], 1)[None]
     state = field
     for step in range(2):
         lo, hi = step, span - step
@@ -189,24 +179,23 @@
         north_d = d_ref[lo + 1:hi - 1]
         flux_w = east_a[1:] * state[:-1] + east_b[1:] * state[1:]
         inner = state[1:-1]
-        flux_s = north_c * lat_below(inner, lanes) + north_d * inner
-        flux_n = lat_above(flux_s, lanes)
+        flux_s = north_c * pltpu.roll(inner, 1, 2) + north_d * inner
+        flux_n = pltpu.roll(flux_s, lat - 1, 2)
         state = inner - (flux_w[1:] - flux_w[:-1]) - (flux_n - flux_s)
     state = w_ref[2:span - 2] * state
     for step in range(2, 4):
         lo, hi = step, span - step
         west_b = b_ref[lo + 1:hi - 1]
         east_a = a_ref[lo + 2:hi]
-        north_c = c_ref[lo + 1:hi - 1]
         north_d = d_ref[lo + 1:hi - 1]
-        north_up = lat_above(north_c, lanes)
+        north_up = n_ref[lo + 1:hi - 1]
         inner = state[1:-1]
         state = (
-            inner * (1.0 - east_a + west_b - north_up + north_d)
+            inner * k_ref[lo + 1:hi - 1]
             - west_b * state[:-2]
             + east_a * state[2:]
-            - north_d * lat_below(inner, lanes)
-            + north_up * lat_above(inner, lanes)
+            - north_d * pltpu.roll(inner, 1, 2)
+            + north_up * pltpu.roll(inner, lat - 1, 2)
         )
     sketch = field[4:span - 4] + state
     groups = sketch.shape[0] // 4
@@ -217,23 +206,24 @@
 def stencil_sums(slab, east, north, weight):
     probe_count, span, level_count, lat_count = slab.shape
     groups = (span - 8) // 4
-    winds = (
-        jnp.maximum(east, 0.0),
-        jnp.minimum(east, 0.0),
-        jnp.maximum(north, 0.0),
-        jnp.minimum(north, 0.0),
-        weight,
-    )
+    east_a = jnp.maximum(east, 0.0)
+    east_b = jnp.minimum(east, 0.0)
+    north_c = jnp.maximum(north, 0.0)
+    north_d = jnp.minimum(north, 0.0)
+    north_up = above(north_c)
+    next_a = jnp.concatenate([east_a[1:], jnp.zeros_like(east_a[:1])], axis=0)
+    centre = 1.0 - next_a + east_b - north_up + north_d
+    winds = (east_a, east_b, north_c, north_d, weight, north_up, centre)
     full = pl.BlockSpec((span, level_count, lat_count), lambda i: (0, 0, 0))
     elements = probe_count * span * level_count * lat_count
     return pl.pallas_call(
         stencil_kernel,
         out_shape=jax.ShapeDtypeStruct((probe_count, groups, level_count, lat_count), slab.dtype),
         grid=(probe_count,),
-        in_specs=[pl.BlockSpec((1, span, level_count, lat_count), lambda i: (i, 0, 0, 0))] + [full] * 5,
+        in_specs=[pl.BlockSpec((1, span, level_count, lat_count), lambda i: (i, 0, 0, 0))] + [full] * 7,
         out_specs=pl.BlockSpec((1, groups, level_count, lat_count), lambda i: (i, 0, 0, 0)),
         cost_estimate=pl.CostEstimate(
-            flops=80 * elements, transcendentals=0, bytes_accessed=4 * elements + 20 * span * level_count * lat_count
+            flops=50 * elements, transcendentals=0, bytes_accessed=4 * elements + 28 * span * level_count * lat_count
         ),
     )(slab, *winds)
 

time: 113 us -> 115 us (1.018)
  waiting for transfers between devices: 5.34 us -> 1.37 us
  Pallas kernels: 51.1 us -> 53.3 us
  other arithmetic: 21.5 us -> 23.5 us
    ppermute x1, waiting for transfers between devices: 3.82 us -> 0.01 us  [body(): from_east = lax.ppermute(east_edge, 'lon', backward)]
    min x4 -> x1, other arithmetic: 4.23 us -> 0.71 us  [stencil_sums(): north_d = jnp.minimum(north, 0.0)]
    add x0 -> x2, other arithmetic: none -> 2.83 us  [stencil_sums(): centre = 1.0 - next_a + east_b - north_up + north_d]
    max x0 -> x3, other arithmetic: none -> 2.67 us  [the longest x2 2.65 us: stencil_sums(): east_a = jnp.maximum(east, 0.0)]
    ppermute x1, starting transfers between devices: 2.3 us -> 0.01 us  [body(): from_west = lax.ppermute(west_edge, 'lon', forward)]
    ppermute x1, starting transfers between devices: 7.49 us -> 9.78 us  [body(): from_east = lax.ppermute(east_edge, 'lon', backward)]
    pallas_call x1, Pallas kernels: 21.7 us -> 23.7 us  [butterfly_sum(): pl.pallas_call(functools.partial(exchange_kernel, count, radix), out_shap...]
    slice x0 -> x4, local copies, waits for them, and re-layouts: none -> 1.61 us  [the longest x2 0.91 us: above(): field[..., 1:]]
  transfers between devices with their start and end apart: 2 -> 2, of which waited for: 2 -> 1; matrix products, arithmetic and copies ran while one was open for 4% -> 5% of each run, Pallas kernels for 13% -> 13%
where the time goes in v9:
time: 115 us; the launch traced here: 113 us
  Pallas kernels  53.3 us (46%)
  other arithmetic  23.5 us (20%)
  local copies, waits for them, and re-layouts  12.6 us (11%)
  starting transfers between devices  9.79 us (9%)
  blocking collectives  8.45 us (7%)
  matrix products  3.02 us (3%)
  waiting for transfers between devices  1.37 us (1%)
    pallas_call x2, Pallas kernels, stencil_sums(): pl.pallas_call(stencil_kernel, out_shape=jax.ShapeDtypeStruct((probe_coun...  29.6 us
    pallas_call x1, Pallas kernels, butterfly_sum(): pl.pallas_call(functools.partial(exchange_kernel, count, radix), out_shap...  23.7 us
    ppermute x1, starting transfers between devices, body(): from_east = lax.ppermute(east_edge, 'lon', backward)  9.78 us
    all_gather x1, blocking collectives, body(): full_panel = lax.all_gather(coarse, 'probe', axis=0, tiled=True)  8.45 us
    another operation x3, other arithmetic, body(): lower = jnp.linalg.cholesky(gram)  6.52 us
    another operation x1, other arithmetic, body(): lax.linalg.triangular_solve(lower, ident, left_side=True, lower=True)  4.89 us
    slice x3, local copies, waits for them, and re-layouts, body(): part[:, lon_count - halo:]  2.93 us
    add x2, other arithmetic, stencil_sums(): centre = 1.0 - next_a + east_b - north_up + north_d  2.83 us
  transfers between devices with their start and end apart: 2, of which 1 were waited for; matrix products, arithmetic and copies ran while one was open for 5% of the time, Pallas kernels for 13%

profile of v9, /device:TPU:8, one launch (start us, length us, event | category | flops | bytes accessed | tf_op | source)
XLA Modules:
  0.0 112.9 jit_solution(9575688697535827769)
XLA Ops:
  0.7 0.8 fusion.32
  1.5 1.8 %slice_maximum_fusion = (f32[1,24,8,256]{3,2,1,0:T(8,128)S(1)}, f32[24,8,256]{2,1,0:T(8,128)}, f32[24,8,256]{2,1,0:T(8,128)}, f32[1,24,8,256]{3,2,1,0:T(8,128)S(1)}) fusion(f32[2,24,8,256]{3,2,1,0:T(8,128)} %param.4, pred[256]{0:T(512)(128)(4,1)S(1)} %iota_compare_fusion.5), kind=kLoop, calls=%fused_computation.19 | loop fusion | flops 147456 | bytes 1179904 | tf_op jit(solution)/shard_map/max | solution.py:209
  3.3 0.8 fusion.28
  4.1 1.3 %fusion.22 = (f32[16,4,8,256]{3,2,1,0:T(8,128)S(1)}, f32[16,4,8,256]{3,2,1,0:T(8,128)S(1)}) fusion(f32[16,24,8,256]{3,2,1,0:T(8,128)} %q_ref.1), kind=kLoop, calls=%fused_computation.54 | loop fusion | bytes 2097152 | tf_op jit(solution)/shard_map/slice | solution.py:252
  5.4 0.9 pad_maximum_fusion.3
  6.3 9.8 %collective-permute-start.1 = (f32[19,4,8,256]{3,2,1,0:T(8,128)}, f32[19,4,8,256]{3,2,1,0:T(8,128)}, u32[]{:S(2)}, u32[]{:S(2)}) collective-permute-start(f32[19,4,8,256]{3,2,1,0:T(8,128)} %pad_maximum_fusion.3), channel_id=1, source_target_pairs={{4,0},{8,4},{12,8},{16,12},{20,16},{24,20},{28,24},{32,28},{36,32}... | collective-permute-start | bytes 1867784 | tf_op jit(solution)/shard_map/ppermute | solution.py:255
  16.1 0.9 pad_maximum_fusion.2
  17.0 0.8 fusion.27
  17.8 0.8 slice.169
  19.3 2.0 %subtract_add_fusion = (f32[24,8,256]{2,1,0:T(8,128)}, f32[24,8,256]{2,1,0:T(8,128)}, f32[24,8,256]{2,1,0:T(8,128)}) fusion(f32[23,8,256]{2,1,0:T(8,128)} %slice_bitcast_fusion, f32[24,8,255]{2,1,0:T(8,128)} %slice.169, f32[2,24,8,256]{3,2,1,0:T(8,128)S(1)} %copy-done.1, pred[256]{0:T(512)(128)(4,1)S(1)} %iota_compare_fusion.5), kind=kLoop, calls=%fused_computation.9 | loop fusion | flops 344064 | bytes 1367552 | tf_op jit(solution)/shard_map/add | solution.py:215
  21.3 14.8 %shard_map.51 = f32[16,4,8,256]{3,2,1,0:T(8,128)} custom-call(f32[16,24,8,256]{3,2,1,0:T(8,128)} %q_ref.1, f32[24,8,256]{2,1,0:T(8,128)} %get-tuple-element.21.a_ref, f32[24,8,256]{2,1,0:T(8,128)} %get-tuple-element.22.b_ref, f32[24,8,256]{2,1,0:T(8,128)} %copy-done.3, f32[24,8,256]{2,1,0:T(8,128)} %get-tuple-element.7.d_ref, f32[24,8,256]{2,1,0:T(8,128)} %w_ref.1, ...), custom_call_target="tpu_custom_call" | custom-call | flops 39321600 | bytes 4521984 | tf_op jit(solution)/shard_map/pallas_call | solution.py:219
  36.4 0.8 fusion.25
  37.2 1.4 %collective-permute-done = f32[19,4,8,256]{3,2,1,0:T(8,128)} collective-permute-done((f32[19,4,8,256]{3,2,1,0:T(8,128)}, f32[19,4,8,256]{3,2,1,0:T(8,128)}, u32[]{:S(2)}, u32[]{:S(2)}) %collective-permute-start) | collective-permute-done | bytes 622624 | tf_op jit(solution)/shard_map/ppermute | solution.py:254
  38.5 0.8 fusion.24
  39.3 0.7 minimum_bitcast_fusion.1
  40.2 0.8 fusion.4
  41.0 0.8 subtract_add_fusion.1
  41.8 0.7 maximum_bitcast_fusion.w_ref
  42.5 1.1 slice.155
  43.6 1.1 slice.152
  44.7 1.8 %pad_maximum_fusion.q_ref = f32[16,24,8,256]{3,2,1,0:T(8,128)} fusion(f32[16,4,8,256]{3,2,1,0:T(8,128)S(1)} %slice.155, f32[16,8,8,256]{3,2,1,0:T(8,128)S(1)} %get-tuple-element.11, f32[16,8,8,256]{3,2,1,0:T(8,128)S(1)} %get-tuple-element.10, f32[16,4,8,256]{3,2,1,0:T(8,128)S(1)} %slice.152), kind=kLoop, calls=%fused_computation | loop fusion | flops 2359296 | bytes 6291456 | tf_op jit(solution)/shard_map/concatenate | solution.py:264
  46.5 14.8 %shard_map.50 = f32[16,4,8,256]{3,2,1,0:T(8,128)} custom-call(f32[16,24,8,256]{3,2,1,0:T(8,128)} %pad_maximum_fusion.q_ref, f32[24,8,256]{2,1,0:T(8,128)} %get-tuple-element.32.a_ref, f32[24,8,256]{2,1,0:T(8,128)} %get-tuple-element.33.b_ref, f32[24,8,256]{2,1,0:T(8,128)} %copy-done.4, f32[24,8,256]{2,1,0:T(8,128)} %get-tuple-element.36.d_ref, ...), custom_call_target="tpu_custom_call" | custom-call | flops 39321600 | bytes 4521984 | tf_op jit(solution)/shard_map/pallas_call | solution.py:219
  61.4 1.0 fusion.26
  62.4 0.9 fusion.2
  63.5 8.5 %all_gather.3 = f32[64,3072]{1,0:T(8,128)S(1)} all-gather(f32[16,3072]{1,0:T(8,128)S(1)} %reshape_reshape.3), channel_id=1, replica_groups=mesh['lon'=64,'probe'=4] {'probe'}, dimensions={0}, use_global_device_ids=true | all-gather | bytes 983040 | tf_op jit(solution)/shard_map/all_gather | solution.py:276
  71.9 1.4 %fusion.33.block_ref = f32[64,64]{1,0:T(8,128)} fusion(f32[64,3072]{1,0:T(8,128)S(1)} %all_gather.3), kind=kOutput, calls=%fused_computation.65 | convolution fusion | flops 150994944 | bytes 802816 | tf_op jit(solution)/shard_map/dot_general | solution.py:277
  73.3 23.7 %shard_map.52 = f32[64,64]{1,0:T(8,128)} custom-call(f32[64,64]{1,0:T(8,128)} %fusion.33.block_ref), custom_call_target="tpu_custom_call" | custom-call | tf_op jit(solution)/shard_map/pallas_call | solution.py:71
  97.1 0.8 copy.9
  97.9 0.8 fusion.12
  98.7 5.8 %cholesky.17 = f32[64,64]{1,0:T(8,128)S(1)} custom-call(f32[64,64]{1,0:T(8,128)S(1)} %fusion.12), custom_call_target="Cholesky" | custom-call | tf_op jit(solution)/shard_map/jit(cholesky)/cholesky | solution.py:284
  105.9 0.7 copy.11
  106.6 4.9 %custom-call.6 = f32[1,64,64]{1,2,0:T(8,128)S(1)} custom-call(f32[1,64,64]{2,1,0:T(8,128)S(1)} %get-tuple-element.45), custom_call_target="InvertDiagBlocksLowerTriangular" | custom-call | tf_op jit(solution)/shard_map/triangular_solve | solution.py:285
  (39 shorter events, 4.0 us)
Async XLA Ops:
  0.6 16.4 %copy-start.1 = (f32[2,24,8,256]{3,2,1,0:T(8,128)S(1)}, f32[2,24,8,256]{3,2,1,0:T(8,128)}, u32[]{:S(2)}) copy-start(f32[2,24,8,256]{3,2,1,0:T(8,128)} %param.4) | copy-start | bytes 1179652
  6.3 30.0 %collective-permute-start.1 = (f32[19,4,8,256]{3,2,1,0:T(8,128)}, f32[19,4,8,256]{3,2,1,0:T(8,128)}, u32[]{:S(2)}, u32[]{:S(2)}) collective-permute-start(f32[19,4,8,256]{3,2,1,0:T(8,128)} %pad_maximum_fusion.3), channel_id=1, source_target_pairs={{4,0},{8,4},{12,8},{16,12},{20,16},{24,20},{28,24},{32,28},{36,32}... | collective-permute-start | bytes 1867784 | tf_op jit(solution)/shard_map/ppermute | solution.py:255
  17.0 21.5 %collective-permute-start = (f32[19,4,8,256]{3,2,1,0:T(8,128)}, f32[19,4,8,256]{3,2,1,0:T(8,128)}, u32[]{:S(2)}, u32[]{:S(2)}) collective-permute-start(f32[19,4,8,256]{3,2,1,0:T(8,128)} %pad_maximum_fusion.2), channel_id=1, source_target_pairs={{0,4},{4,8},{8,12},{12,16},{16,20},{20,24},{24,28},{28,32},{32,36}... | collective-permute-start | bytes 1867784 | tf_op jit(solution)/shard_map/ppermute | solution.py:254
  17.0 2.3 %copy-start.3 = (f32[24,8,256]{2,1,0:T(8,128)}, f32[24,8,256]{2,1,0:T(8,128)S(1)}, u32[]{:S(2)}) copy-start(f32[24,8,256]{2,1,0:T(8,128)S(1)} %fusion.1.c_ref) | copy-start | bytes 589828
  19.3 16.9 %copy-start = (f32[16,24,8,256]{3,2,1,0:T(8,128)S(1)}, f32[16,24,8,256]{3,2,1,0:T(8,128)}, u32[]{:S(2)}) copy-start(f32[16,24,8,256]{3,2,1,0:T(8,128)} %q_ref.1) | copy-start | bytes 9437188
  21.3 14.8 %copy-start.5 = (f32[24,8,256]{2,1,0:T(8,128)S(1)}, f32[24,8,256]{2,1,0:T(8,128)}, u32[]{:S(2)}) copy-start(f32[24,8,256]{2,1,0:T(8,128)} %w_ref.1) | copy-start | bytes 589828
  36.1 3.2 %copy-start.8 = (f32[1,8,8,256]{3,2,1,0:T(8,128)S(1)}, f32[1,8,8,256]{3,2,1,0:T(8,128)}, u32[]{:S(2)}) copy-start(f32[1,8,8,256]{3,2,1,0:T(8,128)} %get-tuple-element.48) | copy-start | bytes 196612
  36.1 3.2 %copy-start.9 = (f32[1,8,8,256]{3,2,1,0:T(8,128)S(1)}, f32[1,8,8,256]{3,2,1,0:T(8,128)}, u32[]{:S(2)}) copy-start(f32[1,8,8,256]{3,2,1,0:T(8,128)} %get-tuple-element.49) | copy-start | bytes 196612
  36.1 4.0 %copy-start.6 = (f32[1,8,8,256]{3,2,1,0:T(8,128)S(1)}, f32[1,8,8,256]{3,2,1,0:T(8,128)}, u32[]{:S(2)}) copy-start(f32[1,8,8,256]{3,2,1,0:T(8,128)} %get-tuple-element.24) | copy-start | bytes 196612
  36.2 4.0 %copy-start.7 = (f32[1,8,8,256]{3,2,1,0:T(8,128)S(1)}, f32[1,8,8,256]{3,2,1,0:T(8,128)}, u32[]{:S(2)}) copy-start(f32[1,8,8,256]{3,2,1,0:T(8,128)} %get-tuple-element.25) | copy-start | bytes 196612
  40.1 6.5 %copy-start.4 = (f32[24,8,256]{2,1,0:T(8,128)}, f32[24,8,256]{2,1,0:T(8,128)S(1)}, u32[]{:S(2)}) copy-start(f32[24,8,256]{2,1,0:T(8,128)S(1)} %get-tuple-element.37.c_ref) | copy-start | bytes 589828
  46.5 15.8 %copy-start.2 = (f32[16,4,8,256]{3,2,1,0:T(8,128)S(1)}, f32[16,4,8,256]{3,2,1,0:T(8,128)}, u32[]{:S(2)}) copy-start(f32[16,4,8,256]{3,2,1,0:T(8,128)} %shard_map.51) | copy-start | bytes 1572868

commit v10 on v7

--- a/solution.py
+++ b/solution.py
@@ -56,7 +56,7 @@
     out_ref[...] = current[len(rounds)]
 
 
-def butterfly_sum(block, axis, radix=4):
+def butterfly_sum(block, axis, radix=8):
     count = lax.axis_size(axis)
     if count & (count - 1) or count < 2:
         return lax.psum(block, axis)

time: 108 us -> 110 us (1.019)
  the two profiles are of different devices: /device:TPU:8 before, /device:TPU:1 now
where the time goes in v10:
time: 110 us
  other arithmetic  39.9 us (36%)
  Pallas kernels  22.2 us (20%)
  local copies, waits for them, and re-layouts  21.8 us (20%)
  starting transfers between devices  11.2 us (10%)
  blocking collectives  8.94 us (8%)
  matrix products  4.24 us (4%)
  between operations  1.27 us (1%)
    pallas_call x1, Pallas kernels, butterfly_sum(): pl.pallas_call(functools.partial(exchange_kernel, count, radix), out_shap...  22.2 us
    ppermute x1, starting transfers between devices, body(): from_east = lax.ppermute(east_edge, 'lon', backward)  11.2 us
    all_gather x1, blocking collectives, body(): full_panel = lax.all_gather(coarse, 'probe', axis=0, tiled=True)  8.94 us
    add x1, other arithmetic, body(): inner = coarsen(increments[:, halo:lon_count - halo] + inner)  6.86 us
    another operation x3, other arithmetic, body(): lower = jnp.linalg.cholesky(gram)  6.52 us
    slice x8, local copies, waits for them, and re-layouts, below(): field[..., :-1]  6.21 us
    another operation x1, other arithmetic, body(): lax.linalg.triangular_solve(lower, ident, left_side=True, lower=True)  4.9 us
    slice x6, local copies, waits for them, and re-layouts, above(): field[..., 1:]  3.93 us
  transfers between devices with their start and end apart: 2, of which 0 were waited for; matrix products, arithmetic and copies ran while one was open for 26% of the time, Pallas kernels for 0%

profile of v10, /device:TPU:1, one launch (start us, length us, event | category | flops | bytes accessed | tf_op | source)
XLA Modules:
  0.0 109.6 jit_solution(306962623486856262)
XLA Ops:
  0.6 0.8 fusion.83
  1.4 1.0 fusion.78
  2.5 0.8 fusion.80
  3.3 1.5 %fusion.70 = (f32[16,4,8,256]{3,2,1,0:T(8,128)S(1)}, f32[16,4,8,256]{3,2,1,0:T(8,128)S(1)}) fusion(f32[16,24,8,256]{3,2,1,0:T(8,128)} %param.3), kind=kLoop, calls=%fused_computation.168 | loop fusion | bytes 2097152 | tf_op jit(solution)/shard_map/slice | solution.py:176
  4.8 0.9 pad_maximum_fusion.2
  5.7 11.2 %collective-permute-start.1 = (f32[19,4,8,256]{3,2,1,0:T(8,128)}, f32[19,4,8,256]{3,2,1,0:T(8,128)}, u32[]{:S(2)}, u32[]{:S(2)}) collective-permute-start(f32[19,4,8,256]{3,2,1,0:T(8,128)} %pad_maximum_fusion.2), channel_id=1, source_target_pairs={{4,0},{8,4},{12,8},{16,12},{20,16},{24,20},{28,24},{32,28},{36,32}... | collective-permute-start | bytes 1867784 | tf_op jit(solution)/shard_map/ppermute | solution.py:179
  17.0 0.9 pad_maximum_fusion.1
  21.0 0.9 multiply_add_fusion.1
  21.9 0.8 slice.640
  26.6 0.8 fusion.72
  27.7 1.2 %fusion.15 = f32[16,18,8,256]{3,2,1,0:T(8,128)S(1)} fusion(f32[16,20,8,256]{3,2,1,0:T(8,128)S(1)} %fusion.9, f32[16,18,8,255]{3,2,1,0:T(8,128)S(1)} %get-tuple-element.13, f32[16,18,8,255]{3,2,1,0:T(8,128)S(1)} %get-tuple-element.12, f32[18,8,256]{2,1,0:T(8,128)S(1)} %get-tuple-element.70, f32[18,8,256]{2,1,0:T(8,128)S(1)} %get-tuple-element.35, ...), kind=kLoop, calls=%fused_computation.32 | loop fusion | flops 5308416 | bytes 14874624 | tf_op jit(solution)/shard_map/add | solution.py:136
  29.0 2.8 %fusion.74 = (f32[16,16,8,255]{3,2,1,0:T(8,128)}, f32[16,16,8,255]{3,2,1,0:T(8,128)}) fusion(f32[16,18,8,256]{3,2,1,0:T(8,128)S(1)} %fusion.15), kind=kLoop, calls=%fused_computation.172 | loop fusion | bytes 8355840 | tf_op jit(solution)/shard_map/slice | solution.py:106
  33.3 6.9 %fusion.24 = f32[16,16,8,256]{3,2,1,0:T(8,128)} fusion(f32[16,18,8,256]{3,2,1,0:T(8,128)} %copy-done.1, f32[16,16,8,255]{3,2,1,0:T(8,128)} %get-tuple-element.17, f32[16,16,8,255]{3,2,1,0:T(8,128)} %get-tuple-element.16, f32[16,24,8,256]{3,2,1,0:T(8,128)S(1)} %copy-done, f32[16,8,256]{2,1,0:T(8,128)} %get-tuple-element.75, ...), kind=kLoop, calls=%fused_computation.47 | loop fusion | flops 5242880 | bytes 15319040 | tf_op jit(solution)/shard_map/add | solution.py:187
  40.2 2.6 %reduce_sum.28 = f32[16,4,8,256]{3,2,1,0:T(8,128)} reduce(f32[16,4,4,8,256]{4,3,2,1,0:T(8,128)} %bitcast.114, f32[]{:T(128)} %constant.79.clone.1), dimensions={2}, to_apply=%region_1.2 | reduce | flops 393216 | bytes 2621444 | tf_op jit(solution)/shard_map/reduce_sum | solution.py:156
  42.8 1.6 %fusion.41 = f32[16,4,8,64]{3,2,1,0:T(8,128)S(1)} fusion(f32[16,4,8,256]{3,2,1,0:T(8,128)} %reduce_sum.28, s32[256]{0:T(256)S(1)} %get-tuple-element.82, s32[256]{0:T(256)S(1)} %get-tuple-element.83, pred[256]{0:T(512)(128)(4,1)S(1)} %compare_and_fusion), kind=kOutput, calls=%fused_computation.122 | convolution fusion | flops 100712448 | bytes 657664 | tf_op jit(solution)/shard_map/dot_general | solution.py:160
  44.4 0.9 maximum_minimum_fusion
  45.5 0.8 fusion.77
  46.3 0.8 fusion.76
  47.3 1.1 slice.587
  48.4 1.1 slice.586
  50.3 0.8 multiply_add_fusion.2
  51.1 0.8 slice.603
  56.0 0.8 fusion.73
  57.1 1.2 %fusion.19 = f32[16,18,8,256]{3,2,1,0:T(8,128)S(1)} fusion(f32[16,20,8,256]{3,2,1,0:T(8,128)S(1)} %fusion.12, f32[16,18,8,255]{3,2,1,0:T(8,128)S(1)} %get-tuple-element.15, f32[16,18,8,255]{3,2,1,0:T(8,128)S(1)} %get-tuple-element.14, f32[18,8,256]{2,1,0:T(8,128)S(1)} %get-tuple-element.74, f32[18,8,256]{2,1,0:T(8,128)S(1)} %get-tuple-element.46, ...), kind=kLoop, calls=%fused_computation.39 | loop fusion | flops 5308416 | bytes 14874624 | tf_op jit(solution)/shard_map/add | solution.py:136
  59.2 1.1 %fusion.28 = f32[16,16,8,256]{3,2,1,0:T(8,128)S(1)} fusion(f32[16,18,8,256]{3,2,1,0:T(8,128)S(1)} %fusion.19, f32[16,16,8,255]{3,2,1,0:T(8,128)S(1)} %get-tuple-element.19, f32[16,16,8,255]{3,2,1,0:T(8,128)S(1)} %get-tuple-element.18, f32[16,8,256]{2,1,0:T(8,128)S(1)} %get-tuple-element.77, f32[16,8,256]{2,1,0:T(8,128)S(1)} %maximum_minimum_fusion, ...), kind=kLoop, calls=%fused_computation.54 | loop fusion | flops 4718592 | bytes 13221888 | tf_op jit(solution)/shard_map/add | solution.py:136
  61.3 8.9 %all_gather.3 = f32[64,3072]{1,0:T(8,128)S(1)} all-gather(f32[16,3072]{1,0:T(8,128)S(1)} %reshape.159), channel_id=1, replica_groups=mesh['lon'=64,'probe'=4] {'probe'}, dimensions={0}, use_global_device_ids=true | all-gather | bytes 983040 | tf_op jit(solution)/shard_map/all_gather | solution.py:202
  70.2 1.4 %fusion.84.block_ref = f32[64,64]{1,0:T(8,128)} fusion(f32[64,3072]{1,0:T(8,128)S(1)} %all_gather.3), kind=kOutput, calls=%fused_computation.182 | convolution fusion | flops 150994944 | bytes 802816 | tf_op jit(solution)/shard_map/dot_general | solution.py:203
  71.6 22.2 %shard_map.50 = f32[64,64]{1,0:T(8,128)} custom-call(f32[64,64]{1,0:T(8,128)} %fusion.84.block_ref), custom_call_target="tpu_custom_call" | custom-call | tf_op jit(solution)/shard_map/pallas_call | solution.py:71
  93.8 0.8 copy.10
  94.7 0.8 fusion.44
  95.4 5.8 %cholesky.17 = f32[64,64]{1,0:T(8,128)S(1)} custom-call(f32[64,64]{1,0:T(8,128)S(1)} %fusion.44), custom_call_target="Cholesky" | custom-call | tf_op jit(solution)/shard_map/jit(cholesky)/cholesky | solution.py:210
  102.6 4.9 %custom-call.6 = f32[1,64,64]{1,2,0:T(8,128)S(1)} custom-call(f32[1,64,64]{2,1,0:T(8,128)S(1)} %get-tuple-element.79), custom_call_target="InvertDiagBlocksLowerTriangular" | custom-call | tf_op jit(solution)/shard_map/triangular_solve | solution.py:211
  (96 shorter events, 19.3 us)
Async XLA Ops:
  2.5 15.4 %copy-start.4 = (f32[2,24,8,256]{3,2,1,0:T(8,128)S(1)}, f32[2,24,8,256]{3,2,1,0:T(8,128)}, u32[]{:S(2)}) copy-start(f32[2,24,8,256]{3,2,1,0:T(8,128)} %param.4) | copy-start | bytes 1179652
  3.3 15.8 %copy-start = (f32[16,24,8,256]{3,2,1,0:T(8,128)S(1)}, f32[16,24,8,256]{3,2,1,0:T(8,128)}, u32[]{:S(2)}) copy-start(f32[16,24,8,256]{3,2,1,0:T(8,128)} %param.3) | copy-start | bytes 9437188
  5.7 39.7 %collective-permute-start.1 = (f32[19,4,8,256]{3,2,1,0:T(8,128)}, f32[19,4,8,256]{3,2,1,0:T(8,128)}, u32[]{:S(2)}, u32[]{:S(2)}) collective-permute-start(f32[19,4,8,256]{3,2,1,0:T(8,128)} %pad_maximum_fusion.2), channel_id=1, source_target_pairs={{4,0},{8,4},{12,8},{16,12},{20,16},{24,20},{28,24},{32,28},{36,32}... | collective-permute-start | bytes 1867784 | tf_op jit(solution)/shard_map/ppermute | solution.py:179
  17.8 28.4 %collective-permute-start = (f32[19,4,8,256]{3,2,1,0:T(8,128)}, f32[19,4,8,256]{3,2,1,0:T(8,128)}, u32[]{:S(2)}, u32[]{:S(2)}) collective-permute-start(f32[19,4,8,256]{3,2,1,0:T(8,128)} %pad_maximum_fusion.1), channel_id=1, source_target_pairs={{0,4},{4,8},{8,12},{12,16},{16,20},{20,24},{24,28},{28,32},{32,36}... | collective-permute-start | bytes 1867784 | tf_op jit(solution)/shard_map/ppermute | solution.py:178
  19.2 0.9 copy-start.6
  19.4 2.5 %copy-start.2 = (f32[24,8,256]{2,1,0:T(8,128)}, f32[24,8,256]{2,1,0:T(8,128)S(1)}, u32[]{:S(2)}) copy-start(f32[24,8,256]{2,1,0:T(8,128)S(1)} %bitcast_select_fusion) | copy-start | bytes 589828
  26.6 0.9 slice-start
  26.6 1.0 copy-start.3
  28.9 2.8 %copy-start.1 = (f32[16,18,8,256]{3,2,1,0:T(8,128)}, f32[16,18,8,256]{3,2,1,0:T(8,128)S(1)}, u32[]{:S(2)}) copy-start(f32[16,18,8,256]{3,2,1,0:T(8,128)S(1)} %fusion.15) | copy-start | bytes 7077892
  29.0 2.8 %slice-start.1 = ((f32[24,8,256]{2,1,0:T(8,128)}), f32[16,8,256]{2,1,0:T(8,128)S(1)}, s32[]{:S(2)}) async-start(f32[24,8,256]{2,1,0:T(8,128)} %copy-done.2), calls=%async_computation.1 | async-start | bytes 262144 | tf_op jit(solution)/shard_map/slice | solution.py:128
  44.4 2.7 %copy-start.8 = (f32[1,8,8,256]{3,2,1,0:T(8,128)S(1)}, f32[1,8,8,256]{3,2,1,0:T(8,128)}, u32[]{:S(2)}) copy-start(f32[1,8,8,256]{3,2,1,0:T(8,128)} %get-tuple-element.29) | copy-start | bytes 196612
  47.1 2.4 %copy-start.5 = (f32[1,24,8,256]{3,2,1,0:T(8,128)}, f32[1,24,8,256]{3,2,1,0:T(8,128)S(1)}, u32[]{:S(2)}) copy-start(f32[1,24,8,256]{3,2,1,0:T(8,128)S(1)} %pad_maximum_fusion.4) | copy-start | bytes 589828
  51.1 0.9 slice-start.2
  58.3 0.9 copy-start.7

commit v11 on v7

--- a/solution.py
+++ b/solution.py
@@ -142,12 +142,34 @@
 
 
 def four_steps(state, east, north, weight):
-    span = state.shape[1]
+    a = jnp.maximum(east, 0.0)
+    b = jnp.minimum(east, 0.0)
+    c = jnp.maximum(north, 0.0)
+    d = jnp.minimum(north, 0.0)
+    a_east = jnp.roll(a, -1, axis=0)
+    b_east = jnp.roll(b, -1, axis=0)
+    c_north = above(c)
+    d_north = above(d)
+    centre = 1.0 - a_east + b - c_north + d
     for step in range(2):
-        state = forward_core(state, east[step:span - step], north[step:span - step])
-    state = weight[2:span - 2] * state
-    for step in range(2, 4):
-        state = adjoint_core(state, east[step:span - step], north[step:span - step])
+        west_val = jnp.roll(state, 1, axis=1)
+        east_val = jnp.roll(state, -1, axis=1)
+        flux_w = a * west_val + b * state
+        flux_e = a_east * state + b_east * east_val
+        flux_s = c * below(state) + d * state
+        flux_n = c_north * state + d_north * above(state)
+        state = state - (flux_e - flux_w) - (flux_n - flux_s)
+    state = weight * state
+    for step in range(2):
+        west_val = jnp.roll(state, 1, axis=1)
+        east_val = jnp.roll(state, -1, axis=1)
+        state = (
+            state * centre
+            - b * west_val
+            + a_east * east_val
+            - d * below(state)
+            + c_north * above(state)
+        )
     return state
 
 
@@ -184,7 +206,7 @@
         return parts[0], parts[1][0], parts[2][0], parts[3][0]
 
     inner = four_steps(*fields(pack))
-    inner = coarsen(increments[:, halo:lon_count - halo] + inner)
+    inner = coarsen(increments[:, halo:lon_count - halo] + inner[:, halo:lon_count - halo])
     rim = [
         jnp.concatenate(
             [from_west[lo:hi], part[:, :2 * halo], part[:, lon_count - 2 * halo:], from_east[lo:hi]],
@@ -193,8 +215,8 @@
         for part, (lo, hi) in zip(pack, bounds)
     ]
     rim = four_steps(*fields(rim))
-    west = coarsen(increments[:, :halo] + rim[:, :halo])
-    east = coarsen(increments[:, lon_count - halo:] + rim[:, rim.shape[1] - halo:])
+    west = coarsen(increments[:, :halo] + rim[:, halo:2 * halo])
+    east = coarsen(increments[:, lon_count - halo:] + rim[:, 4 * halo:5 * halo])
     coarse = jnp.concatenate([west, inner, east], axis=1)
     coarse = coarse.reshape(probe_count, -1)
     all_probes = probe_count * lax.axis_size("probe")

time: 108 us -> 113 us (1.046)
  local copies, waits for them, and re-layouts: 21.8 us -> 26.5 us
    add x16 -> x6, other arithmetic: 15.9 us -> 9.18 us  [the longest x3 6.3 us: four_steps(): state * centre - b * west_val + a_east * east_val - d * below(state)]
    slice x15 -> x31, local copies, waits for them, and re-layouts: 3.33 us -> 9.28 us  [the longest x10 3.49 us: four_steps(): west_val = jnp.roll(state, 1, axis=1)]
    sub x2, other arithmetic: 1.51 us -> 6.38 us  [four_steps(): state = state - (flux_e - flux_w) - (flux_n - flux_s)]
    mul x5 -> x4, other arithmetic: 1.56 us -> 5.31 us  [the longest x3 5.29 us: four_steps(): state = weight * state]
    ppermute x1, starting transfers between devices: 0.01 us -> 2.3 us  [body(): from_west = lax.ppermute(west_edge, 'lon', forward)]
    ppermute x1, starting transfers between devices: 9.78 us -> 7.49 us  [body(): from_east = lax.ppermute(east_edge, 'lon', backward)]
    slice x9 -> x0, other arithmetic: 1.93 us -> none  [the longest x1 1.05 us: body(): winds[0][None]]
    slice x8 -> x4, local copies, waits for them, and re-layouts: 6.21 us -> 4.55 us  [below(): field[..., :-1]]
  transfers between devices with their start and end apart: 2 -> 2, of which waited for: 0 -> 0; matrix products, arithmetic and copies ran while one was open for 26% -> 22% of each run, Pallas kernels for 0% -> 0%
where the time goes in v11:
time: 113 us
  other arithmetic  40.2 us (36%)
  local copies, waits for them, and re-layouts  26.5 us (23%)
  Pallas kernels  22 us (19%)
  starting transfers between devices  9.79 us (9%)
  blocking collectives  8.72 us (8%)
  matrix products  4.24 us (4%)
  between operations  1.33 us (1%)
    pallas_call x1, Pallas kernels, butterfly_sum(): pl.pallas_call(functools.partial(exchange_kernel, count, radix), out_shap...  22 us
    all_gather x1, blocking collectives, body(): full_panel = lax.all_gather(coarse, 'probe', axis=0, tiled=True)  8.72 us
    ppermute x1, starting transfers between devices, body(): from_east = lax.ppermute(east_edge, 'lon', backward)  7.49 us
    another operation x3, other arithmetic, body(): lower = jnp.linalg.cholesky(gram)  6.52 us
    sub x2, other arithmetic, four_steps(): state = state - (flux_e - flux_w) - (flux_n - flux_s)  6.38 us
    add x3, other arithmetic, four_steps(): state * centre - b * west_val + a_east * east_val - d * below(state)  6.3 us
    mul x3, other arithmetic, four_steps(): state = weight * state  5.29 us
    another operation x1, other arithmetic, body(): lax.linalg.triangular_solve(lower, ident, left_side=True, lower=True)  4.9 us
  transfers between devices with their start and end apart: 2, of which 0 were waited for; matrix products, arithmetic and copies ran while one was open for 22% of the time, Pallas kernels for 0%

profile of v11, /device:TPU:8, one launch (start us, length us, event | category | flops | bytes accessed | tf_op | source)
XLA Modules:
  0.0 112.7 jit_solution(9320557905683900705)
XLA Ops:
  1.4 1.2 %slice_maximum_fusion.1 = (f32[1,24,8,256]{3,2,1,0:T(8,128)S(1)}, f32[24,8,256]{2,1,0:T(8,128)S(1)}, f32[24,8,256]{2,1,0:T(8,128)S(1)}, f32[1,24,8,256]{3,2,1,0:...) fusion(f32[2,24,8,256]{3,2,1,0:T(8,128)} %param.4, pred[256]{0:T(512)(128)(4,1)S(1)} %iota_compare_fusion.7), kind=kLoop, calls=%fused_computation.95 | loop fusion | flops 196608 | bytes 1573120 | tf_op jit(solution)/shard_map/max | solution.py:145
  2.6 0.9 fusion.110
  3.6 1.4 %fusion.106 = (f32[16,4,8,256]{3,2,1,0:T(8,128)S(1)}, f32[16,4,8,256]{3,2,1,0:T(8,128)S(1)}) fusion(f32[16,24,8,256]{3,2,1,0:T(8,128)} %param.3), kind=kLoop, calls=%fused_computation.188 | loop fusion | bytes 2097152 | tf_op jit(solution)/shard_map/slice | solution.py:218
  5.9 2.3 %collective-permute-start = (f32[19,4,8,256]{3,2,1,0:T(8,128)}, f32[19,4,8,256]{3,2,1,0:T(8,128)}, u32[]{:S(2)}, u32[]{:S(2)}) collective-permute-start(f32[19,4,8,256]{3,2,1,0:T(8,128)} %pad_maximum_fusion.3), channel_id=1, source_target_pairs={{0,4},{4,8},{8,12},{12,16},{16,20},{20,24},{24,28},{28,32},{32,36}... | collective-permute-start | bytes 1867784 | tf_op jit(solution)/shard_map/ppermute | solution.py:200
  9.1 7.5 %collective-permute-start.1 = (f32[19,4,8,256]{3,2,1,0:T(8,128)}, f32[19,4,8,256]{3,2,1,0:T(8,128)}, u32[]{:S(2)}, u32[]{:S(2)}) collective-permute-start(f32[19,4,8,256]{3,2,1,0:T(8,128)} %pad_maximum_fusion.4), channel_id=1, source_target_pairs={{4,0},{8,4},{12,8},{16,12},{20,16},{24,20},{28,24},{32,28},{36,32}... | collective-permute-start | bytes 1867784 | tf_op jit(solution)/shard_map/ppermute | solution.py:201
  18.4 1.1 fusion.91
  20.0 2.7 %fusion.22 = f32[16,24,8,256]{3,2,1,0:T(8,128)S(1)} fusion(f32[16,24,8,256]{3,2,1,0:T(8,128)S(1)} %copy-done, f32[16,1,8,256]{3,2,1,0:T(8,128)S(1)} %get-tuple-element.33, f32[16,23,8,256]{3,2,1,0:T(8,128)S(1)} %get-tuple-element.35, f32[16,23,8,256]{3,2,1,0:T(8,128)S(1)} %get-tuple-element.34, f32[16,1,8,256]{3,2,1,0:T(8,128)S(1)} %get-tuple-element.32, ...), kind=kLoop, calls=%fused_computation.32 | loop fusion | flops 14155776 | bytes 20422656 | tf_op jit(solution)/shard_map/sub | solution.py:161
  23.2 1.2 %fusion.88 = (f32[16,24,8,255]{3,2,1,0:T(8,128)S(1)}, f32[16,24,8,255]{3,2,1,0:T(8,128)S(1)}) fusion(f32[16,24,8,256]{3,2,1,0:T(8,128)S(1)} %fusion.22), kind=kLoop, calls=%fused_computation.170 | loop fusion | bytes 12533760 | tf_op jit(solution)/shard_map/slice | solution.py:110
  24.4 2.7 %fusion.28 = f32[16,24,8,256]{3,2,1,0:T(8,128)S(1)} fusion(f32[16,24,8,256]{3,2,1,0:T(8,128)S(1)} %fusion.22, f32[16,1,8,256]{3,2,1,0:T(8,128)S(1)} %get-tuple-element.27, f32[16,23,8,256]{3,2,1,0:T(8,128)S(1)} %get-tuple-element.29, f32[16,23,8,256]{3,2,1,0:T(8,128)S(1)} %get-tuple-element.28, f32[16,1,8,256]{3,2,1,0:T(8,128)S(1)} %get-tuple-element.26, ...), kind=kLoop, calls=%fused_computation.40 | loop fusion | flops 14942208 | bytes 20619264 | tf_op jit(solution)/shard_map/mul | solution.py:162
  27.6 1.1 fusion.85
  28.7 2.0 %fusion.33 = f32[16,24,8,256]{3,2,1,0:T(8,128)S(1)} fusion(f32[16,23,8,256]{3,2,1,0:T(8,128)S(1)} %get-tuple-element.21, f32[16,1,8,256]{3,2,1,0:T(8,128)S(1)} %get-tuple-element.23, f32[16,1,8,256]{3,2,1,0:T(8,128)S(1)} %get-tuple-element.22, f32[16,23,8,256]{3,2,1,0:T(8,128)S(1)} %get-tuple-element.20, f32[16,24,8,255]{3,2,1,0:T(8,128)S(1)} %get-tuple-element.19, ...), kind=kLoop, calls=%fused_computation.47 | loop fusion | flops 8650752 | bytes 19832832 | tf_op jit(solution)/shard_map/add | solution.py:167
  30.7 1.2 %fusion.84 = (f32[16,24,8,255]{3,2,1,0:T(8,128)S(1)}, f32[16,24,8,255]{3,2,1,0:T(8,128)S(1)}) fusion(f32[16,24,8,256]{3,2,1,0:T(8,128)S(1)} %fusion.33), kind=kLoop, calls=%fused_computation.166 | loop fusion | bytes 12533760 | tf_op jit(solution)/shard_map/slice | solution.py:106
  32.6 2.8 %fusion.35 = f32[16,16,8,256]{3,2,1,0:T(8,128)} fusion(f32[16,24,8,255]{3,2,1,0:T(8,128)S(1)} %get-tuple-element.17, f32[16,24,8,255]{3,2,1,0:T(8,128)S(1)} %get-tuple-element.16, f32[16,1,8,256]{3,2,1,0:T(8,128)S(1)} %get-tuple-element.13, f32[16,23,8,256]{3,2,1,0:T(8,128)S(1)} %get-tuple-element.15, f32[16,24,8,256]{3,2,1,0:T(8,128)S(1)} %fusion.33, ...), kind=kLoop, calls=%fused_computation.51 | loop fusion | flops 6291456 | bytes 19505152 | tf_op jit(solution)/shard_map/add | solution.py:209
  35.3 2.6 %reduce_sum.28 = f32[16,4,8,256]{3,2,1,0:T(8,128)} reduce(f32[16,4,4,8,256]{4,3,2,1,0:T(8,128)} %bitcast.98, f32[]{:T(128)} %constant.70.clone.1), dimensions={2}, to_apply=%region_1.2 | reduce | flops 393216 | bytes 2621444 | tf_op jit(solution)/shard_map/reduce_sum | solution.py:178
  38.0 1.6 %fusion.51 = f32[16,4,8,64]{3,2,1,0:T(8,128)S(1)} fusion(f32[16,4,8,256]{3,2,1,0:T(8,128)} %reduce_sum.28, s32[256]{0:T(256)S(1)} %get-tuple-element.120, s32[256]{0:T(256)S(1)} %get-tuple-element.121, pred[256]{0:T(512)(128)(4,1)S(1)} %compare_and_fusion), kind=kOutput, calls=%fused_computation.106 | convolution fusion | flops 100712448 | bytes 657664 | tf_op jit(solution)/shard_map/dot_general | solution.py:182
  39.8 1.1 slice.427
  40.9 1.1 slice.426
  42.9 1.1 fusion.103
  46.2 0.9 slice.435
  47.2 0.9 slice.436
  48.1 3.7 %fusion.3 = f32[16,24,8,256]{3,2,1,0:T(8,128)S(1)} fusion(f32[16,1,8,256]{3,2,1,0:T(8,128)S(1)} %slice.435, f32[16,23,8,256]{3,2,1,0:T(8,128)S(1)} %get-tuple-element.57, f32[16,23,8,256]{3,2,1,0:T(8,128)S(1)} %get-tuple-element.56, f32[16,1,8,256]{3,2,1,0:T(8,128)S(1)} %slice.436, f32[16,24,8,255]{3,2,1,0:T(8,128)S(1)} %get-tuple-element.55, ...), kind=kLoop, calls=%fused_computation.5 | loop fusion | flops 16515072 | bytes 20422656 | tf_op jit(solution)/shard_map/sub | solution.py:161
  52.4 1.2 %fusion.100 = (f32[16,24,8,255]{3,2,1,0:T(8,128)S(1)}, f32[16,24,8,255]{3,2,1,0:T(8,128)S(1)}) fusion(f32[16,24,8,256]{3,2,1,0:T(8,128)S(1)} %fusion.3), kind=kLoop, calls=%fused_computation.182 | loop fusion | bytes 12533760 | tf_op jit(solution)/shard_map/slice | solution.py:110
  53.6 2.6 %fusion.9 = f32[16,24,8,256]{3,2,1,0:T(8,128)S(1)} fusion(f32[16,24,8,256]{3,2,1,0:T(8,128)S(1)} %fusion.3, f32[16,1,8,256]{3,2,1,0:T(8,128)S(1)} %get-tuple-element.51, f32[16,23,8,256]{3,2,1,0:T(8,128)S(1)} %get-tuple-element.53, f32[16,23,8,256]{3,2,1,0:T(8,128)S(1)} %get-tuple-element.52, f32[16,1,8,256]{3,2,1,0:T(8,128)S(1)} %get-tuple-element.50, ...), kind=kLoop, calls=%fused_computation.13 | loop fusion | flops 14942208 | bytes 20619264 | tf_op jit(solution)/shard_map/mul | solution.py:162
  56.7 1.2 %fusion.97 = (f32[16,24,8,255]{3,2,1,0:T(8,128)S(1)}, f32[16,24,8,255]{3,2,1,0:T(8,128)S(1)}) fusion(f32[16,24,8,256]{3,2,1,0:T(8,128)S(1)} %fusion.9), kind=kLoop, calls=%fused_computation.179 | loop fusion | bytes 12533760 | tf_op jit(solution)/shard_map/slice | solution.py:106
  57.9 2.2 %fusion.14 = f32[16,24,8,256]{3,2,1,0:T(8,128)S(1)} fusion(f32[16,23,8,256]{3,2,1,0:T(8,128)S(1)} %get-tuple-element.45, f32[16,1,8,256]{3,2,1,0:T(8,128)S(1)} %get-tuple-element.47, f32[16,1,8,256]{3,2,1,0:T(8,128)S(1)} %get-tuple-element.46, f32[16,23,8,256]{3,2,1,0:T(8,128)S(1)} %get-tuple-element.44, f32[16,24,8,255]{3,2,1,0:T(8,128)S(1)} %get-tuple-element.43, ...), kind=kLoop, calls=%fused_computation.20 | loop fusion | flops 8650752 | bytes 19832832 | tf_op jit(solution)/shard_map/add | solution.py:167
  60.7 1.1 fusion.94
  61.8 2.1 %fusion.18 = f32[16,24,8,256]{3,2,1,0:T(8,128)S(1)} fusion(f32[16,23,8,256]{3,2,1,0:T(8,128)S(1)} %get-tuple-element.39, f32[16,1,8,256]{3,2,1,0:T(8,128)S(1)} %get-tuple-element.41, f32[16,1,8,256]{3,2,1,0:T(8,128)S(1)} %get-tuple-element.40, f32[16,23,8,256]{3,2,1,0:T(8,128)S(1)} %get-tuple-element.38, f32[16,24,8,255]{3,2,1,0:T(8,128)S(1)} %get-tuple-element.37, ...), kind=kLoop, calls=%fused_computation.26 | loop fusion | flops 8650752 | bytes 19832832 | tf_op jit(solution)/shard_map/add | solution.py:167
  64.8 8.7 %all_gather.3 = f32[64,3072]{1,0:T(8,128)S(1)} all-gather(f32[16,3072]{1,0:T(8,128)S(1)} %reshape.162), channel_id=1, replica_groups=mesh['lon'=64,'probe'=4] {'probe'}, dimensions={0}, use_global_device_ids=true | all-gather | bytes 983040 | tf_op jit(solution)/shard_map/all_gather | solution.py:224
  73.6 1.4 %fusion.115.block_ref = f32[64,64]{1,0:T(8,128)} fusion(f32[64,3072]{1,0:T(8,128)S(1)} %all_gather.3), kind=kOutput, calls=%fused_computation.197 | convolution fusion | flops 150994944 | bytes 802816 | tf_op jit(solution)/shard_map/dot_general | solution.py:225
  74.9 22.0 %shard_map.50 = f32[64,64]{1,0:T(8,128)} custom-call(f32[64,64]{1,0:T(8,128)} %fusion.115.block_ref), custom_call_target="tpu_custom_call" | custom-call | tf_op jit(solution)/shard_map/pallas_call | solution.py:71
  98.5 5.8 %cholesky.17 = f32[64,64]{1,0:T(8,128)S(1)} custom-call(f32[64,64]{1,0:T(8,128)S(1)} %fusion.54), custom_call_target="Cholesky" | custom-call | tf_op jit(solution)/shard_map/jit(cholesky)/cholesky | solution.py:232
  105.7 4.9 %custom-call.6 = f32[1,64,64]{1,2,0:T(8,128)S(1)} custom-call(f32[1,64,64]{2,1,0:T(8,128)S(1)} %get-tuple-element.109), custom_call_target="InvertDiagBlocksLowerTriangular" | custom-call | tf_op jit(solution)/shard_map/triangular_solve | solution.py:233
  (85 shorter events, 17.2 us)
Async XLA Ops:
  1.4 15.1 %copy-start.1 = (f32[2,24,8,256]{3,2,1,0:T(8,128)S(1)}, f32[2,24,8,256]{3,2,1,0:T(8,128)}, u32[]{:S(2)}) copy-start(f32[2,24,8,256]{3,2,1,0:T(8,128)} %param.4) | copy-start | bytes 1179652
  2.6 14.7 %copy-start.2 = (f32[24,8,256]{2,1,0:T(8,128)S(1)}, f32[24,8,256]{2,1,0:T(8,128)}, u32[]{:S(2)}) copy-start(f32[24,8,256]{2,1,0:T(8,128)} %param.5) | copy-start | bytes 589828
  2.6 15.4 %copy-start = (f32[16,24,8,256]{3,2,1,0:T(8,128)S(1)}, f32[16,24,8,256]{3,2,1,0:T(8,128)}, u32[]{:S(2)}) copy-start(f32[16,24,8,256]{3,2,1,0:T(8,128)} %param.3) | copy-start | bytes 9437188
  5.9 35.1 %collective-permute-start = (f32[19,4,8,256]{3,2,1,0:T(8,128)}, f32[19,4,8,256]{3,2,1,0:T(8,128)}, u32[]{:S(2)}, u32[]{:S(2)}) collective-permute-start(f32[19,4,8,256]{3,2,1,0:T(8,128)} %pad_maximum_fusion.3), channel_id=1, source_target_pairs={{0,4},{4,8},{8,12},{12,16},{16,20},{20,24},{24,28},{28,32},{32,36}... | collective-permute-start | bytes 1867784 | tf_op jit(solution)/shard_map/ppermute | solution.py:200
  9.1 30.7 %collective-permute-start.1 = (f32[19,4,8,256]{3,2,1,0:T(8,128)}, f32[19,4,8,256]{3,2,1,0:T(8,128)}, u32[]{:S(2)}, u32[]{:S(2)}) collective-permute-start(f32[19,4,8,256]{3,2,1,0:T(8,128)} %pad_maximum_fusion.4), channel_id=1, source_target_pairs={{4,0},{8,4},{12,8},{16,12},{20,16},{24,20},{28,24},{32,28},{36,32}... | collective-permute-start | bytes 1867784 | tf_op jit(solution)/shard_map/ppermute | solution.py:201
  44.0 2.2 %copy-start.3 = (f32[8,8,256]{2,1,0:T(8,128)S(1)}, f32[8,8,256]{2,1,0:T(8,128)}, u32[]{:S(2)}) copy-start(f32[8,8,256]{2,1,0:T(8,128)} %get-tuple-element.117) | copy-start | bytes 196612
  44.0 2.2 %copy-start.4 = (f32[8,8,256]{2,1,0:T(8,128)S(1)}, f32[8,8,256]{2,1,0:T(8,128)}, u32[]{:S(2)}) copy-start(f32[8,8,256]{2,1,0:T(8,128)} %get-tuple-element.118) | copy-start | bytes 196612
  52.3 1.2 %copy-start.5 = (f32[1,8,8,256]{3,2,1,0:T(8,128)S(1)}, f32[1,8,8,256]{3,2,1,0:T(8,128)}, u32[]{:S(2)}) copy-start(f32[1,8,8,256]{3,2,1,0:T(8,128)} %get-tuple-element.90) | copy-start | bytes 196612
  52.3 1.2 %copy-start.6 = (f32[1,8,8,256]{3,2,1,0:T(8,128)S(1)}, f32[1,8,8,256]{3,2,1,0:T(8,128)}, u32[]{:S(2)}) copy-start(f32[1,8,8,256]{3,2,1,0:T(8,128)} %get-tuple-element.91) | copy-start | bytes 196612

commit v12 on v11

--- a/solution.py
+++ b/solution.py
@@ -54,6 +54,52 @@
         current[step + 1] = terms[0]
         slot += width - 1
     out_ref[...] = current[len(rounds)]
+
+
+def halo_kernel(west_ref, east_ref, from_west_ref, from_east_ref, held, send_sem, recv_sem):
+    count = lax.axis_size("lon")
+    me = lax.axis_index("lon")
+    right = lax.rem(me + 1, count)
+    left = lax.rem(me + count - 1, count)
+
+    barrier = pltpu.get_barrier_semaphore()
+    for neighbour in (left, right):
+        pl.semaphore_signal(barrier, inc=1, device_id={"lon": neighbour}, device_id_type=MESH)
+    pl.semaphore_wait(barrier, 2)
+
+    copies = []
+    for slot, (source, target) in enumerate(((west_ref, right), (east_ref, left))):
+        copy = pltpu.make_async_remote_copy(
+            src_ref=source,
+            dst_ref=held.at[slot],
+            send_sem=send_sem.at[slot],
+            recv_sem=recv_sem.at[slot],
+            device_id={"lon": target},
+            device_id_type=MESH,
+        )
+        copy.start()
+        copies.append(copy)
+    for copy in copies:
+        copy.wait()
+    from_west_ref[...] = held[0]
+    from_east_ref[...] = held[1]
+
+
+def exchange_halos(west_edge, east_edge):
+    vmem = pl.BlockSpec(memory_space=pltpu.VMEM)
+    edge = jax.ShapeDtypeStruct(west_edge.shape, west_edge.dtype)
+    return pl.pallas_call(
+        halo_kernel,
+        out_shape=(edge, edge),
+        in_specs=[vmem, vmem],
+        out_specs=(vmem, vmem),
+        scratch_shapes=[
+            pltpu.VMEM((2,) + west_edge.shape, west_edge.dtype),
+            pltpu.SemaphoreType.DMA((2,)),
+            pltpu.SemaphoreType.DMA((2,)),
+        ],
+        compiler_params=pltpu.CompilerParams(collective_id=1, has_side_effects=True),
+    )(west_edge, east_edge)
 
 
 def butterfly_sum(block, axis, radix=4):
@@ -192,32 +238,17 @@
     probe_count, lon_count, level_count, lat_count = increments.shape
     halo = 4
     pack = (increments, winds[0][None], lat_mask(winds[1])[None], obs_weight[None])
-    count = lax.axis_size("lon")
-    forward = [(i, (i + 1) % count) for i in range(count)]
-    backward = [((i + 1) % count, i) for i in range(count)]
     west_edge = jnp.concatenate([part[:, lon_count - halo:] for part in pack], axis=0)
     east_edge = jnp.concatenate([part[:, :halo] for part in pack], axis=0)
-    from_west = lax.ppermute(west_edge, "lon", forward)
-    from_east = lax.ppermute(east_edge, "lon", backward)
+    from_west, from_east = exchange_halos(west_edge, east_edge)
     bounds = ((0, probe_count), (probe_count, probe_count + 1),
               (probe_count + 1, probe_count + 2), (probe_count + 2, probe_count + 3))
-
-    def fields(parts):
-        return parts[0], parts[1][0], parts[2][0], parts[3][0]
-
-    inner = four_steps(*fields(pack))
-    inner = coarsen(increments[:, halo:lon_count - halo] + inner[:, halo:lon_count - halo])
-    rim = [
-        jnp.concatenate(
-            [from_west[lo:hi], part[:, :2 * halo], part[:, lon_count - 2 * halo:], from_east[lo:hi]],
-            axis=1,
-        )
+    wide = [
+        jnp.concatenate([from_west[lo:hi], part, from_east[lo:hi]], axis=1)
         for part, (lo, hi) in zip(pack, bounds)
     ]
-    rim = four_steps(*fields(rim))
-    west = coarsen(increments[:, :halo] + rim[:, halo:2 * halo])
-    east = coarsen(increments[:, lon_count - halo:] + rim[:, 4 * halo:5 * halo])
-    coarse = jnp.concatenate([west, inner, east], axis=1)
+    state = four_steps(wide[0], wide[1][0], wide[2][0], wide[3][0])
+    coarse = coarsen(increments + state[:, halo:halo + lon_count])
     coarse = coarse.reshape(probe_count, -1)
     all_probes = probe_count * lax.axis_size("probe")
     ident = jnp.eye(all_probes, dtype=jnp.float32)

time: 113 us -> 145 us (1.28)
  Pallas kernels: 22 us -> 58.1 us
  starting transfers between devices: 9.79 us -> 0 us
  local copies, waits for them, and re-layouts: 26.5 us -> 33.4 us
    pallas_call x0 -> x1, Pallas kernels: none -> 34 us  [exchange_halos(): pl.pallas_call(halo_kernel, out_shape=(edge, edge), in_specs=[vmem, vmem]...]
    ppermute x2 -> x0, starting transfers between devices: 9.79 us -> none  [the longest x1 7.49 us: body(): from_east = lax.ppermute(east_edge, 'lon', backward)]
    slice x10 -> x6, local copies, waits for them, and re-layouts: 3.49 us -> 11.5 us  [four_steps(): west_val = jnp.roll(state, 1, axis=1)]
    slice x9 -> x5, local copies, waits for them, and re-layouts: 3.05 us -> 0.07 us  [body(): coarse = coarsen(increments + state[:, halo:halo + lon_count])]
    add x1, other arithmetic: 2.77 us -> 5.31 us  [body(): coarse = coarsen(increments + state[:, halo:halo + lon_count])]
    slice x7 -> x3, local copies, waits for them, and re-layouts: 2.55 us -> 4.66 us  [four_steps(): east_val = jnp.roll(state, -1, axis=1)]
    pallas_call x1, Pallas kernels: 22 us -> 24.1 us  [butterfly_sum(): pl.pallas_call(functools.partial(exchange_kernel, count, radix), out_shap...]
    slice x0 -> x1, other arithmetic: none -> 1.75 us  [body(): winds[0][None]]
  transfers between devices with their start and end apart: 2 -> 0, of which waited for: 0 -> 0; matrix products, arithmetic and copies ran while one was open for 22% -> 0% of each run, Pallas kernels for 0% -> 0%
where the time goes in v12:
time: 145 us
  Pallas kernels  58.1 us (40%)
  other arithmetic  41.6 us (29%)
  local copies, waits for them, and re-layouts  33.4 us (23%)
  blocking collectives  7.56 us (5%)
  matrix products  3.01 us (2%)
    pallas_call x1, Pallas kernels, exchange_halos(): pl.pallas_call(halo_kernel, out_shape=(edge, edge), in_specs=[vmem, vmem]...  34 us
    pallas_call x1, Pallas kernels, butterfly_sum(): pl.pallas_call(functools.partial(exchange_kernel, count, radix), out_shap...  24.1 us
    slice x6, local copies, waits for them, and re-layouts, four_steps(): west_val = jnp.roll(state, 1, axis=1)  11.5 us
    all_gather x1, blocking collectives, body(): full_panel = lax.all_gather(coarse, 'probe', axis=0, tiled=True)  7.56 us
    another operation x3, other arithmetic, body(): lower = jnp.linalg.cholesky(gram)  6.52 us
    sub x1, other arithmetic, four_steps(): state = state - (flux_e - flux_w) - (flux_n - flux_s)  6.27 us
    mul x2, other arithmetic, four_steps(): state = weight * state  5.59 us
    add x1, other arithmetic, body(): coarse = coarsen(increments + state[:, halo:halo + lon_count])  5.31 us

profile of v12, /device:TPU:8, one launch (start us, length us, event | category | flops | bytes accessed | tf_op | source)
XLA Modules:
  0.0 144.7 jit_solution(2946956809586397680)
XLA Ops:
  1.4 1.7 %fusion.60 = (f32[1,24,8,256]{3,2,1,0:T(8,128)S(1)}, f32[24,8,256]{2,1,0:T(8,128)}, f32[1,24,8,256]{3,2,1,0:T(8,128)S(1)}) fusion(f32[2,24,8,256]{3,2,1,0:T(8,128)} %param.4, pred[256]{0:T(512)(128)(4,1)S(1)} %iota_compare_fusion.5), kind=kLoop, calls=%fused_computation.110 | loop fusion | flops 49152 | bytes 983296 | tf_op jit(solution)/shard_map/slice | solution.py:240
  3.2 0.9 fusion.61
  4.1 1.3 fusion.57
  5.4 1.1 pad_maximum_fusion.3
  6.6 34.0 %shard_map.50 = (f32[19,4,8,256]{3,2,1,0:T(8,128)}, f32[19,4,8,256]{3,2,1,0:T(8,128)}) custom-call(f32[19,4,8,256]{3,2,1,0:T(8,128)} %get-tuple-element.66.west_ref, f32[19,4,8,256]{3,2,1,0:T(8,128)} %get-tuple-element.67.east_ref), custom_call_target="tpu_custom_call" | custom-call | tf_op jit(solution)/shard_map/pallas_call | solution.py:91
  40.6 0.9 slice.206
  41.5 1.1 slice.193
  42.6 1.1 slice.192
  44.0 3.7 %fusion.56 = (f32[16,31,8,256]{3,2,1,0:T(8,128)}, f32[16,31,8,256]{3,2,1,0:T(8,128)}) fusion(f32[16,32,8,256]{3,2,1,0:T(8,128)S(1)} %pad_maximum_fusion), kind=kLoop, calls=%fused_computation.106 | loop fusion | bytes 16252928 | tf_op jit(solution)/shard_map/jit(_roll_static)/slice | solution.py:201
  47.7 1.6 %slice.207 = f32[16,1,8,256]{3,2,1,0:T(8,128)} slice(f32[19,4,8,256]{3,2,1,0:T(8,128)} %get-tuple-element.5), slice={[0:16], [3:4], [0:8], [0:256]} | slice | bytes 262144 | tf_op jit(solution)/shard_map/jit(_roll_static)/slice | solution.py:201
  49.3 1.6 %fusion.55 = (f32[16,32,8,255]{3,2,1,0:T(8,128)S(1)}, f32[16,32,8,255]{3,2,1,0:T(8,128)S(1)}) fusion(f32[16,32,8,256]{3,2,1,0:T(8,128)S(1)} %pad_maximum_fusion), kind=kLoop, calls=%fused_computation.105 | loop fusion | bytes 16711680 | tf_op jit(solution)/shard_map/slice | solution.py:156
  50.9 1.5 %fusion.59 = (f32[1,4,8,256]{3,2,1,0:T(8,128)}, f32[4,8,256]{2,1,0:T(8,128)S(1)}, f32[4,8,256]{2,1,0:T(8,128)S(1)}, f32[1,4,8,256]{3,2,1,0:T(8,128)S(1)}, f32[1,4,8,256]{3,2,1,0:T(8,128)S(1)}) fusion(f32[19,4,8,256]{3,2,1,0:T(8,128)} %get-tuple-element.5), kind=kLoop, calls=%fused_computation.109 | loop fusion | bytes 262144 | tf_op jit(solution)/shard_map/slice | solution.py:247
  52.3 1.4 fusion.58
  54.2 0.8 fusion.23
  55.2 6.3 %fusion.3 = f32[16,32,8,256]{3,2,1,0:T(8,128)S(1)} fusion(f32[16,1,8,256]{3,2,1,0:T(8,128)S(1)} %slice.206, f32[16,31,8,256]{3,2,1,0:T(8,128)} %get-tuple-element.31, f32[16,31,8,256]{3,2,1,0:T(8,128)} %get-tuple-element.30, f32[16,1,8,256]{3,2,1,0:T(8,128)} %slice.207, f32[16,32,8,255]{3,2,1,0:T(8,128)S(1)} %get-tuple-element.29, ...), kind=kLoop, calls=%fused_computation.5 | loop fusion | flops 20971520 | bytes 27230208 | tf_op jit(solution)/shard_map/sub | solution.py:207
  61.5 3.7 %fusion.54 = (f32[16,31,8,256]{3,2,1,0:T(8,128)}, f32[16,31,8,256]{3,2,1,0:T(8,128)}) fusion(f32[16,32,8,256]{3,2,1,0:T(8,128)S(1)} %fusion.3), kind=kLoop, calls=%fused_computation.104 | loop fusion | bytes 16252928 | tf_op jit(solution)/shard_map/jit(_roll_static)/slice | solution.py:201
  65.3 1.6 %fusion.52 = (f32[16,32,8,255]{3,2,1,0:T(8,128)S(1)}, f32[16,32,8,255]{3,2,1,0:T(8,128)S(1)}) fusion(f32[16,32,8,256]{3,2,1,0:T(8,128)S(1)} %fusion.3), kind=kLoop, calls=%fused_computation.102 | loop fusion | bytes 16711680 | tf_op jit(solution)/shard_map/slice | solution.py:156
  66.9 5.6 %fusion.9 = f32[16,32,8,256]{3,2,1,0:T(8,128)S(1)} fusion(f32[16,32,8,256]{3,2,1,0:T(8,128)S(1)} %fusion.3, f32[16,1,8,256]{3,2,1,0:T(8,128)S(1)} %get-tuple-element.25, f32[16,31,8,256]{3,2,1,0:T(8,128)} %get-tuple-element.27, f32[16,31,8,256]{3,2,1,0:T(8,128)} %get-tuple-element.26, f32[16,1,8,256]{3,2,1,0:T(8,128)S(1)} %get-tuple-element.24, ...), kind=kLoop, calls=%fused_computation.13 | loop fusion | flops 19922944 | bytes 27492352 | tf_op jit(solution)/shard_map/mul | solution.py:208
  72.5 3.7 %fusion.50 = (f32[16,31,8,256]{3,2,1,0:T(8,128)}, f32[16,31,8,256]{3,2,1,0:T(8,128)}) fusion(f32[16,32,8,256]{3,2,1,0:T(8,128)S(1)} %fusion.9), kind=kLoop, calls=%fused_computation.100 | loop fusion | bytes 16252928 | tf_op jit(solution)/shard_map/jit(_roll_static)/slice | solution.py:211
  76.3 1.6 %fusion.49 = (f32[16,32,8,255]{3,2,1,0:T(8,128)S(1)}, f32[16,32,8,255]{3,2,1,0:T(8,128)S(1)}) fusion(f32[16,32,8,256]{3,2,1,0:T(8,128)S(1)} %fusion.9), kind=kLoop, calls=%fused_computation.99 | loop fusion | bytes 16711680 | tf_op jit(solution)/shard_map/slice | solution.py:152
  77.9 5.1 %fusion.14 = f32[16,32,8,256]{3,2,1,0:T(8,128)S(1)} fusion(f32[16,31,8,256]{3,2,1,0:T(8,128)} %get-tuple-element.19, f32[16,1,8,256]{3,2,1,0:T(8,128)S(1)} %get-tuple-element.21, f32[16,1,8,256]{3,2,1,0:T(8,128)S(1)} %get-tuple-element.20, f32[16,31,8,256]{3,2,1,0:T(8,128)} %get-tuple-element.18, f32[16,32,8,255]{3,2,1,0:T(8,128)S(1)} %get-tuple-element.17, ...), kind=kLoop, calls=%fused_computation.20 | loop fusion | flops 11534336 | bytes 26443776 | tf_op jit(solution)/shard_map/add | solution.py:213
  83.0 1.6 %fusion.48 = (f32[16,32,8,255]{3,2,1,0:T(8,128)S(1)}, f32[16,32,8,255]{3,2,1,0:T(8,128)S(1)}) fusion(f32[16,32,8,256]{3,2,1,0:T(8,128)S(1)} %fusion.14), kind=kLoop, calls=%fused_computation.98 | loop fusion | bytes 16711680 | tf_op jit(solution)/shard_map/slice | solution.py:152
  84.6 2.5 %fusion.47 = (f32[16,31,8,256]{3,2,1,0:T(8,128)S(1)}, f32[16,31,8,256]{3,2,1,0:T(8,128)}) fusion(f32[16,32,8,256]{3,2,1,0:T(8,128)S(1)} %fusion.14), kind=kLoop, calls=%fused_computation.97 | loop fusion | bytes 16252928 | tf_op jit(solution)/shard_map/jit(_roll_static)/slice | solution.py:210
  87.2 5.3 %fusion.16 = f32[16,24,8,256]{3,2,1,0:T(8,128)} fusion(f32[16,24,8,256]{3,2,1,0:T(8,128)S(1)} %copy-done, f32[16,32,8,255]{3,2,1,0:T(8,128)S(1)} %get-tuple-element.15, f32[16,32,8,255]{3,2,1,0:T(8,128)S(1)} %get-tuple-element.14, f32[16,1,8,256]{3,2,1,0:T(8,128)S(1)} %get-tuple-element.11, f32[16,31,8,256]{3,2,1,0:T(8,128)} %get-tuple-element.13, ...), kind=kLoop, calls=%fused_computation.24 | loop fusion | flops 9437184 | bytes 27164672 | tf_op jit(solution)/shard_map/add | solution.py:251
  92.5 2.3 %reduce_sum.9 = f32[16,6,8,256]{3,2,1,0:T(8,128)S(1)} reduce(f32[16,6,4,8,256]{4,3,2,1,0:T(8,128)} %bitcast.55, f32[]{:T(128)} %constant.67.clone.1), dimensions={2}, to_apply=%region_0.1 | reduce | flops 589824 | bytes 3932164 | tf_op jit(solution)/shard_map/reduce_sum | solution.py:224
  94.8 0.9 fusion.30
  95.9 7.6 %all_gather.3 = f32[64,3072]{1,0:T(8,128)S(1)} all-gather(f32[16,3072]{1,0:T(8,128)S(1)} %reshape_reshape.3), channel_id=1, replica_groups=mesh['lon'=64,'probe'=4] {'probe'}, dimensions={0}, use_global_device_ids=true | all-gather | bytes 983040 | tf_op jit(solution)/shard_map/all_gather | solution.py:255
  103.5 1.4 fusion.64.block_ref
  104.8 24.1 %shard_map.51 = f32[64,64]{1,0:T(8,128)} custom-call(f32[64,64]{1,0:T(8,128)} %fusion.64.block_ref), custom_call_target="tpu_custom_call" | custom-call | tf_op jit(solution)/shard_map/pallas_call | solution.py:117
  128.9 0.8 copy.9
  130.5 5.8 %cholesky.17 = f32[64,64]{1,0:T(8,128)S(1)} custom-call(f32[64,64]{1,0:T(8,128)S(1)} %fusion.39), custom_call_target="Cholesky" | custom-call | tf_op jit(solution)/shard_map/jit(cholesky)/cholesky | solution.py:263
  137.7 4.9 %custom-call.6 = f32[1,64,64]{1,2,0:T(8,128)S(1)} custom-call(f32[1,64,64]{2,1,0:T(8,128)S(1)} %get-tuple-element.65), custom_call_target="InvertDiagBlocksLowerTriangular" | custom-call | tf_op jit(solution)/shard_map/triangular_solve | solution.py:264
  (64 shorter events, 6.2 us)
Async XLA Ops:
  3.2 40.5 %copy-start = (f32[16,24,8,256]{3,2,1,0:T(8,128)S(1)}, f32[16,24,8,256]{3,2,1,0:T(8,128)}, u32[]{:S(2)}) copy-start(f32[16,24,8,256]{3,2,1,0:T(8,128)} %param.3) | copy-start | bytes 9437188
  50.9 4.2 %copy-start.10 = (f32[24,8,256]{2,1,0:T(8,128)S(1)}, f32[24,8,256]{2,1,0:T(8,128)}, u32[]{:S(2)}) copy-start(f32[24,8,256]{2,1,0:T(8,128)} %get-tuple-element.45) | copy-start | bytes 589828
  53.8 7.7 %copy-start.1 = (f32[32,8,256]{2,1,0:T(8,128)}, f32[32,8,256]{2,1,0:T(8,128)S(1)}, u32[]{:S(2)}) copy-start(f32[32,8,256]{2,1,0:T(8,128)S(1)} %get-tuple-element.58) | copy-start | bytes 786436
  54.0 7.5 %copy-start.3 = (f32[32,8,256]{2,1,0:T(8,128)}, f32[32,8,256]{2,1,0:T(8,128)S(1)}, u32[]{:S(2)}) copy-start(f32[32,8,256]{2,1,0:T(8,128)S(1)} %concatenate.124) | copy-start | bytes 786436
  54.1 0.9 copy-start.7
  55.2 6.3 %copy-start.5 = (f32[32,8,256]{2,1,0:T(8,128)}, f32[32,8,256]{2,1,0:T(8,128)S(1)}, u32[]{:S(2)}) copy-start(f32[32,8,256]{2,1,0:T(8,128)S(1)} %pad_maximum_fusion.7) | copy-start | bytes 786436
  65.2 1.6 %copy-start.11 = (f32[24,8,256]{2,1,0:T(8,128)S(1)}, f32[24,8,256]{2,1,0:T(8,128)}, u32[]{:S(2)}) copy-start(f32[24,8,256]{2,1,0:T(8,128)} %param.5) | copy-start | bytes 589828
  65.2 1.6 %copy-start.12 = (f32[1,4,8,256]{3,2,1,0:T(8,128)S(1)}, f32[1,4,8,256]{3,2,1,0:T(8,128)}, u32[]{:S(2)}) copy-start(f32[1,4,8,256]{3,2,1,0:T(8,128)} %get-tuple-element.39) | copy-start | bytes 98308
  65.2 1.6 %copy-start.13 = (f32[1,4,8,256]{3,2,1,0:T(8,128)S(1)}, f32[1,4,8,256]{3,2,1,0:T(8,128)}, u32[]{:S(2)}) copy-start(f32[1,4,8,256]{3,2,1,0:T(8,128)} %get-tuple-element.34) | copy-start | bytes 98308
  65.2 1.7 %copy-start.2 = (f32[32,8,256]{2,1,0:T(8,128)S(1)}, f32[32,8,256]{2,1,0:T(8,128)}, u32[]{:S(2)}) copy-start(f32[32,8,256]{2,1,0:T(8,128)} %copy-done.1) | copy-start | bytes 786436
  65.2 1.7 %copy-start.4 = (f32[32,8,256]{2,1,0:T(8,128)S(1)}, f32[32,8,256]{2,1,0:T(8,128)}, u32[]{:S(2)}) copy-start(f32[32,8,256]{2,1,0:T(8,128)} %copy-done.3) | copy-start | bytes 786436
  65.2 1.7 %copy-start.6 = (f32[32,8,256]{2,1,0:T(8,128)S(1)}, f32[32,8,256]{2,1,0:T(8,128)}, u32[]{:S(2)}) copy-start(f32[32,8,256]{2,1,0:T(8,128)} %copy-done.5) | copy-start | bytes 786436
  76.3 1.6 %copy-start.9 = (f32[32,8,256]{2,1,0:T(8,128)S(1)}, f32[32,8,256]{2,1,0:T(8,128)}, u32[]{:S(2)}) copy-start(f32[32,8,256]{2,1,0:T(8,128)} %get-tuple-element.49) | copy-start | bytes 786436
  84.6 2.5 %copy-start.8 = (f32[32,8,255]{2,1,0:T(8,128)S(1)}, f32[32,8,255]{2,1,0:T(8,128)}, u32[]{:S(2)}) copy-start(f32[32,8,255]{2,1,0:T(8,128)} %copy-done.7) | copy-start | bytes 783364

commit v13 on v7

--- a/solution.py
+++ b/solution.py
@@ -110,28 +110,33 @@
     return jnp.concatenate([field[..., 1:], jnp.zeros_like(field[..., :1])], axis=-1)
 
 
+def lon(x, start, stop):
+    first, last, _ = slice(start, stop).indices(x.shape[-3])
+    return lax.slice_in_dim(x, first, last, axis=x.ndim - 3)
+
+
 def forward_core(widened, east, north):
     a_pos = jnp.maximum(east, 0.0)
     b_neg = jnp.minimum(east, 0.0)
-    c_pos = jnp.maximum(north[1:-1], 0.0)
-    d_neg = jnp.minimum(north[1:-1], 0.0)
-    flux_w = a_pos[1:] * widened[:, :-1] + b_neg[1:] * widened[:, 1:]
-    inner = widened[:, 1:-1]
+    c_pos = jnp.maximum(lon(north, 1, -1), 0.0)
+    d_neg = jnp.minimum(lon(north, 1, -1), 0.0)
+    flux_w = lon(a_pos, 1, None) * lon(widened, 0, -1) + lon(b_neg, 1, None) * lon(widened, 1, None)
+    inner = lon(widened, 1, -1)
     flux_s = c_pos * below(inner) + d_neg * inner
     flux_n = above(flux_s)
-    return inner - (flux_w[:, 1:] - flux_w[:, :-1]) - (flux_n - flux_s)
+    return inner - (lon(flux_w, 1, None) - lon(flux_w, 0, -1)) - (flux_n - flux_s)
 
 
 def adjoint_core(widened, east, north):
     a_pos = jnp.maximum(east, 0.0)
-    b_neg = jnp.minimum(east, 0.0)[1:-1]
-    c_pos = jnp.maximum(north[1:-1], 0.0)
-    d_neg = jnp.minimum(north[1:-1], 0.0)
-    a_east = a_pos[2:]
+    b_neg = lon(jnp.minimum(east, 0.0), 1, -1)
+    c_pos = jnp.maximum(lon(north, 1, -1), 0.0)
+    d_neg = jnp.minimum(lon(north, 1, -1), 0.0)
+    a_east = lon(a_pos, 2, None)
     c_north = above(c_pos)
-    inner = widened[:, 1:-1]
-    west_val = widened[:, :-2]
-    east_val = widened[:, 2:]
+    inner = lon(widened, 1, -1)
+    west_val = lon(widened, 0, -2)
+    east_val = lon(widened, 2, None)
     return (
         inner * (1.0 - a_east + b_neg - c_north + d_neg)
         - b_neg * west_val
@@ -142,12 +147,12 @@
 
 
 def four_steps(state, east, north, weight):
-    span = state.shape[1]
+    span = state.shape[-3]
     for step in range(2):
-        state = forward_core(state, east[step:span - step], north[step:span - step])
-    state = weight[2:span - 2] * state
+        state = forward_core(state, lon(east, step, span - step), lon(north, step, span - step))
+    state = lon(weight, 2, span - 2) * state
     for step in range(2, 4):
-        state = adjoint_core(state, east[step:span - step], north[step:span - step])
+        state = adjoint_core(state, lon(east, step, span - step), lon(north, step, span - step))
     return state
 
 
@@ -185,16 +190,16 @@
 
     inner = four_steps(*fields(pack))
     inner = coarsen(increments[:, halo:lon_count - halo] + inner)
-    rim = [
-        jnp.concatenate(
-            [from_west[lo:hi], part[:, :2 * halo], part[:, lon_count - 2 * halo:], from_east[lo:hi]],
-            axis=1,
-        )
+    sides = [
+        jnp.stack([
+            jnp.concatenate([from_west[lo:hi], part[:, :2 * halo]], axis=1),
+            jnp.concatenate([part[:, lon_count - 2 * halo:], from_east[lo:hi]], axis=1),
+        ])
         for part, (lo, hi) in zip(pack, bounds)
     ]
-    rim = four_steps(*fields(rim))
-    west = coarsen(increments[:, :halo] + rim[:, :halo])
-    east = coarsen(increments[:, lon_count - halo:] + rim[:, rim.shape[1] - halo:])
+    rim = four_steps(sides[0], sides[1], sides[2], sides[3])
+    west = coarsen(increments[:, :halo] + rim[0])
+    east = coarsen(increments[:, lon_count - halo:] + rim[1])
     coarse = jnp.concatenate([west, inner, east], axis=1)
     coarse = coarse.reshape(probe_count, -1)
     all_probes = probe_count * lax.axis_size("probe")

time: 108 us -> 103 us (0.954)
  Pallas kernels: 21.8 us -> 20 us
  local copies, waits for them, and re-layouts: 21.8 us -> 20 us
  other arithmetic: 39.9 us -> 38.5 us
    ppermute x1, starting transfers between devices: 0.01 us -> 2.3 us  [body(): from_west = lax.ppermute(west_edge, 'lon', forward)]
    ppermute x1, starting transfers between devices: 9.78 us -> 7.49 us  [body(): from_east = lax.ppermute(east_edge, 'lon', backward)]
    pallas_call x1, Pallas kernels: 21.8 us -> 20 us  [butterfly_sum(): pl.pallas_call(functools.partial(exchange_kernel, count, radix), out_shap...]
    slice x3, local copies, waits for them, and re-layouts: 0.78 us -> 1.96 us  [body(): part[:, :2 * halo]]
    slice x8 -> x7, local copies, waits for them, and re-layouts: 6.21 us -> 5.09 us  [below(): field[..., :-1]]
    slice x6 -> x4, local copies, waits for them, and re-layouts: 3.93 us -> 2.89 us  [above(): field[..., 1:]]
    slice x15 -> x12, local copies, waits for them, and re-layouts: 3.33 us -> 3.33 us  [the longest x2 1.62 us: body(): east_edge = jnp.concatenate([part[:, :halo] for part in pack], axis=0)]
where the time goes in v13:
time: 103 us; the launch traced here: 102 us
  other arithmetic  38.5 us (37%)
  local copies, waits for them, and re-layouts  20 us (19%)
  Pallas kernels  20 us (19%)
  starting transfers between devices  9.79 us (10%)
  blocking collectives  8.46 us (8%)
  matrix products  4.28 us (4%)
  between operations  1.28 us (1%)
    pallas_call x1, Pallas kernels, butterfly_sum(): pl.pallas_call(functools.partial(exchange_kernel, count, radix), out_shap...  20 us
    all_gather x1, blocking collectives, body(): full_panel = lax.all_gather(coarse, 'probe', axis=0, tiled=True)  8.46 us
    ppermute x1, starting transfers between devices, body(): from_east = lax.ppermute(east_edge, 'lon', backward)  7.49 us
    add x1, other arithmetic, body(): inner = coarsen(increments[:, halo:lon_count - halo] + inner)  6.8 us
    another operation x3, other arithmetic, body(): lower = jnp.linalg.cholesky(gram)  6.52 us
    slice x7, local copies, waits for them, and re-layouts, below(): field[..., :-1]  5.09 us
    another operation x1, other arithmetic, body(): lax.linalg.triangular_solve(lower, ident, left_side=True, lower=True)  4.9 us
    add x4, other arithmetic, forward_core(): flux_s = c_pos * below(inner) + d_neg * inner  3.3 us
  transfers between devices with their start and end apart: 2, of which 0 were waited for; matrix products, arithmetic and copies ran while one was open for 26% of the time, Pallas kernels for 0%

profile of v13, /device:TPU:8, one launch (start us, length us, event | category | flops | bytes accessed | tf_op | source)
XLA Modules:
  0.0 102.3 jit_solution(3199751198672971689)
XLA Ops:
  0.6 0.8 fusion.104
  1.4 1.0 %fusion.98 = (f32[1,24,8,256]{3,2,1,0:T(8,128)S(1)}, f32[1,24,8,256]{3,2,1,0:T(8,128)S(1)}) fusion(f32[2,24,8,256]{3,2,1,0:T(8,128)} %param.4, pred[256]{0:T(512)(128)(4,1)S(1)} %iota_compare_fusion.8), kind=kLoop, calls=%fused_computation.215 | loop fusion | flops 49152 | bytes 786688 | tf_op jit(solution)/shard_map/slice | solution.py:177
  2.5 0.8 fusion.100
  3.4 1.5 %fusion.91 = (f32[16,4,8,256]{3,2,1,0:T(8,128)S(1)}, f32[16,4,8,256]{3,2,1,0:T(8,128)S(1)}) fusion(f32[16,24,8,256]{3,2,1,0:T(8,128)} %param.3), kind=kLoop, calls=%fused_computation.208 | loop fusion | bytes 2097152 | tf_op jit(solution)/shard_map/slice | solution.py:201
  4.8 0.9 pad_maximum_fusion
  5.7 2.3 %collective-permute-start = (f32[19,4,8,256]{3,2,1,0:T(8,128)}, f32[19,4,8,256]{3,2,1,0:T(8,128)}, u32[]{:S(2)}, u32[]{:S(2)}) collective-permute-start(f32[19,4,8,256]{3,2,1,0:T(8,128)} %pad_maximum_fusion), channel_id=1, source_target_pairs={{0,4},{4,8},{8,12},{12,16},{16,20},{20,24},{24,28},{28,32},{32,36}... | collective-permute-start | bytes 1867784 | tf_op jit(solution)/shard_map/ppermute | solution.py:183
  8.0 0.9 pad_maximum_fusion.1
  8.9 7.5 %collective-permute-start.1 = (f32[19,4,8,256]{3,2,1,0:T(8,128)}, f32[19,4,8,256]{3,2,1,0:T(8,128)}, u32[]{:S(2)}, u32[]{:S(2)}) collective-permute-start(f32[19,4,8,256]{3,2,1,0:T(8,128)} %pad_maximum_fusion.1), channel_id=1, source_target_pairs={{4,0},{8,4},{12,8},{16,12},{20,16},{24,20},{28,24},{32,28},{36,32}... | collective-permute-start | bytes 1867784 | tf_op jit(solution)/shard_map/ppermute | solution.py:184
  18.8 0.9 multiply_add_fusion.1
  19.7 0.8 slice.609
  20.9 0.8 fusion.6
  21.9 0.8 multiply_add_fusion.2
  24.5 0.8 fusion.92
  25.6 1.2 %fusion.18 = f32[16,18,8,256]{3,2,1,0:T(8,128)S(1)} fusion(f32[16,20,8,256]{3,2,1,0:T(8,128)S(1)} %fusion.11, f32[16,18,8,255]{3,2,1,0:T(8,128)S(1)} %get-tuple-element.15, f32[16,18,8,255]{3,2,1,0:T(8,128)S(1)} %get-tuple-element.14, f32[18,8,256]{2,1,0:T(8,128)S(1)} %get-tuple-element.70, f32[18,8,256]{2,1,0:T(8,128)S(1)} %get-tuple-element.37, ...), kind=kLoop, calls=%fused_computation.35 | loop fusion | flops 5308416 | bytes 14874624 | tf_op jit(solution)/shard_map/add | solution.py:141
  26.8 2.7 %fusion.93 = (f32[16,16,8,255]{3,2,1,0:T(8,128)}, f32[16,16,8,255]{3,2,1,0:T(8,128)}) fusion(f32[16,18,8,256]{3,2,1,0:T(8,128)S(1)} %fusion.18), kind=kLoop, calls=%fused_computation.210 | loop fusion | bytes 8355840 | tf_op jit(solution)/shard_map/slice | solution.py:106
  30.4 6.8 %fusion.24 = f32[16,16,8,256]{3,2,1,0:T(8,128)} fusion(f32[16,18,8,256]{3,2,1,0:T(8,128)} %copy-done.1, f32[16,16,8,255]{3,2,1,0:T(8,128)} %get-tuple-element.17, f32[16,16,8,255]{3,2,1,0:T(8,128)} %get-tuple-element.16, f32[16,24,8,256]{3,2,1,0:T(8,128)S(1)} %copy-done, f32[16,8,256]{2,1,0:T(8,128)S(1)} %get-tuple-element.71, ...), kind=kLoop, calls=%fused_computation.46 | loop fusion | flops 5242880 | bytes 15319040 | tf_op jit(solution)/shard_map/add | solution.py:192
  37.2 2.6 %reduce_sum.28 = f32[16,4,8,256]{3,2,1,0:T(8,128)} reduce(f32[16,4,4,8,256]{4,3,2,1,0:T(8,128)} %bitcast.132, f32[]{:T(128)} %constant.92.clone.1), dimensions={2}, to_apply=%region_1.2 | reduce | flops 393216 | bytes 2621444 | tf_op jit(solution)/shard_map/reduce_sum | solution.py:161
  39.8 1.7 %fusion.54 = f32[16,4,8,64]{3,2,1,0:T(8,128)S(1)} fusion(f32[16,4,8,256]{3,2,1,0:T(8,128)} %reduce_sum.28, s32[256]{0:T(256)S(1)} %get-tuple-element.81, s32[256]{0:T(256)S(1)} %get-tuple-element.82, pred[256]{0:T(512)(128)(4,1)S(1)} %compare_and_fusion), kind=kOutput, calls=%fused_computation.152 | convolution fusion | flops 100712448 | bytes 657664 | tf_op jit(solution)/shard_map/dot_general | solution.py:165
  41.7 0.8 fusion.97
  42.5 0.8 fusion.96
  43.6 1.1 %slice.546 = f32[16,4,8,256]{3,2,1,0:T(8,128)S(1)} slice(f32[19,4,8,256]{3,2,1,0:T(8,128)} %collective-permute-done), slice={[0:16], [0:4], [0:8], [0:256]} | slice | bytes 1048576 | tf_op jit(solution)/shard_map/slice | solution.py:195
  44.8 1.1 %slice.547 = f32[16,4,8,256]{3,2,1,0:T(8,128)S(1)} slice(f32[19,4,8,256]{3,2,1,0:T(8,128)} %collective-permute-done.1), slice={[0:16], [0:4], [0:8], [0:256]} | slice | bytes 1048576 | tf_op jit(solution)/shard_map/slice | solution.py:196
  46.1 1.0 fusion.13
  48.2 1.6 %fusion.15 = f32[2,16,10,8,256]{4,3,2,1,0:T(8,128)S(1)} fusion(f32[2,16,11,8,256]{4,3,2,1,0:T(8,128)S(1)} %fusion.2, f32[2,16,10,8,255]{4,3,2,1,0:T(8,128)S(1)} %slice.568, f32[1,16,12,8,256]{4,3,2,1,0:T(8,128)S(1)} %maximum_bitcast_fusion.1, f32[1,16,12,8,256]{4,3,2,1,0:T(8,128)S(1)} %maximum_bitcast_fusion, f32[2,10,8,256]{3,2,1,0:T(8,128)S(1)} %get-tuple-element.53, ...), kind=kLoop, calls=%fused_computation.30 | loop fusion | flops 8519680 | bytes 13948928 | tf_op jit(solution)/shard_map/sub | solution.py:127
  53.6 1.0 fusion.31
  56.7 8.5 %all_gather.3 = f32[64,3072]{1,0:T(8,128)S(1)} all-gather(f32[16,3072]{1,0:T(8,128)S(1)} %reshape.165), channel_id=1, replica_groups=mesh['lon'=64,'probe'=4] {'probe'}, dimensions={0}, use_global_device_ids=true | all-gather | bytes 983040 | tf_op jit(solution)/shard_map/all_gather | solution.py:207
  65.2 1.4 %fusion.105.block_ref = f32[64,64]{1,0:T(8,128)} fusion(f32[64,3072]{1,0:T(8,128)S(1)} %all_gather.3), kind=kOutput, calls=%fused_computation.222 | convolution fusion | flops 150994944 | bytes 802816 | tf_op jit(solution)/shard_map/dot_general | solution.py:208
  66.5 20.0 %shard_map.50 = f32[64,64]{1,0:T(8,128)} custom-call(f32[64,64]{1,0:T(8,128)} %fusion.105.block_ref), custom_call_target="tpu_custom_call" | custom-call | tf_op jit(solution)/shard_map/pallas_call | solution.py:71
  86.5 0.8 copy.10
  87.4 0.8 fusion.60
  88.1 5.8 %cholesky.17 = f32[64,64]{1,0:T(8,128)S(1)} custom-call(f32[64,64]{1,0:T(8,128)S(1)} %fusion.60), custom_call_target="Cholesky" | custom-call | tf_op jit(solution)/shard_map/jit(cholesky)/cholesky | solution.py:215
  95.3 4.9 %custom-call.6 = f32[1,64,64]{1,2,0:T(8,128)S(1)} custom-call(f32[1,64,64]{2,1,0:T(8,128)S(1)} %get-tuple-element.78), custom_call_target="InvertDiagBlocksLowerTriangular" | custom-call | tf_op jit(solution)/shard_map/triangular_solve | solution.py:216
  (100 shorter events, 16.7 us)
Async XLA Ops:
  2.5 13.9 %copy-start.4 = (f32[2,24,8,256]{3,2,1,0:T(8,128)S(1)}, f32[2,24,8,256]{3,2,1,0:T(8,128)}, u32[]{:S(2)}) copy-start(f32[2,24,8,256]{3,2,1,0:T(8,128)} %param.4) | copy-start | bytes 1179652
  3.3 14.4 %copy-start.5 = (f32[24,8,256]{2,1,0:T(8,128)S(1)}, f32[24,8,256]{2,1,0:T(8,128)}, u32[]{:S(2)}) copy-start(f32[24,8,256]{2,1,0:T(8,128)} %param.5) | copy-start | bytes 589828
  3.3 15.0 %copy-start = (f32[16,24,8,256]{3,2,1,0:T(8,128)S(1)}, f32[16,24,8,256]{3,2,1,0:T(8,128)}, u32[]{:S(2)}) copy-start(f32[16,24,8,256]{3,2,1,0:T(8,128)} %param.3) | copy-start | bytes 9437188
  5.7 36.8 %collective-permute-start = (f32[19,4,8,256]{3,2,1,0:T(8,128)}, f32[19,4,8,256]{3,2,1,0:T(8,128)}, u32[]{:S(2)}, u32[]{:S(2)}) collective-permute-start(f32[19,4,8,256]{3,2,1,0:T(8,128)} %pad_maximum_fusion), channel_id=1, source_target_pairs={{0,4},{4,8},{8,12},{12,16},{16,20},{20,24},{24,28},{28,32},{32,36}... | collective-permute-start | bytes 1867784 | tf_op jit(solution)/shard_map/ppermute | solution.py:183
  8.9 32.7 %collective-permute-start.1 = (f32[19,4,8,256]{3,2,1,0:T(8,128)}, f32[19,4,8,256]{3,2,1,0:T(8,128)}, u32[]{:S(2)}, u32[]{:S(2)}) collective-permute-start(f32[19,4,8,256]{3,2,1,0:T(8,128)} %pad_maximum_fusion.1), channel_id=1, source_target_pairs={{4,0},{8,4},{12,8},{16,12},{20,16},{24,20},{28,24},{32,28},{36,32}... | collective-permute-start | bytes 1867784 | tf_op jit(solution)/shard_map/ppermute | solution.py:184
  18.6 1.1 %copy-start.2 = (f32[24,8,256]{2,1,0:T(8,128)}, f32[24,8,256]{2,1,0:T(8,128)S(1)}, u32[]{:S(2)}) copy-start(f32[24,8,256]{2,1,0:T(8,128)S(1)} %bitcast_select_fusion) | copy-start | bytes 589828
  24.4 0.9 slice-start
  24.5 1.0 %copy-start.3 = (f32[24,8,256]{2,1,0:T(8,128)S(1)}, f32[24,8,256]{2,1,0:T(8,128)}, u32[]{:S(2)}) copy-start(f32[24,8,256]{2,1,0:T(8,128)} %copy-done.2) | copy-start | bytes 589828
  26.8 2.8 %copy-start.1 = (f32[16,18,8,256]{3,2,1,0:T(8,128)}, f32[16,18,8,256]{3,2,1,0:T(8,128)S(1)}, u32[]{:S(2)}) copy-start(f32[16,18,8,256]{3,2,1,0:T(8,128)S(1)} %fusion.18) | copy-start | bytes 7077892
  26.8 2.8 %slice-start.1 = ((f32[24,8,256]{2,1,0:T(8,128)}), f32[16,8,256]{2,1,0:T(8,128)S(1)}, s32[]{:S(2)}) async-start(f32[24,8,256]{2,1,0:T(8,128)} %copy-done.2), calls=%async_computation.1 | async-start | bytes 262144 | tf_op jit(solution)/shard_map/slice | solution.py:115
  39.8 2.6 %copy-start.11 = (f32[1,8,8,256]{3,2,1,0:T(8,128)S(1)}, f32[1,8,8,256]{3,2,1,0:T(8,128)}, u32[]{:S(2)}) copy-start(f32[1,8,8,256]{3,2,1,0:T(8,128)} %get-tuple-element.31) | copy-start | bytes 196612
  39.8 3.5 %copy-start.10 = (f32[1,8,8,256]{3,2,1,0:T(8,128)S(1)}, f32[1,8,8,256]{3,2,1,0:T(8,128)}, u32[]{:S(2)}) copy-start(f32[1,8,8,256]{3,2,1,0:T(8,128)} %get-tuple-element.30) | copy-start | bytes 196612
  41.5 1.9 %copy-start.9 = (f32[1,8,8,256]{3,2,1,0:T(8,128)S(1)}, f32[1,8,8,256]{3,2,1,0:T(8,128)}, u32[]{:S(2)}) copy-start(f32[1,8,8,256]{3,2,1,0:T(8,128)} %get-tuple-element.55) | copy-start | bytes 196612
  41.5 1.9 %copy-start.8 = (f32[1,8,8,256]{3,2,1,0:T(8,128)S(1)}, f32[1,8,8,256]{3,2,1,0:T(8,128)}, u32[]{:S(2)}) copy-start(f32[1,8,8,256]{3,2,1,0:T(8,128)} %get-tuple-element.54) | copy-start | bytes 196612
  51.3 0.8 copy-start.7
  51.3 0.9 copy-start.6

commit v14 on v9

--- a/solution.py
+++ b/solution.py
@@ -110,28 +110,33 @@
     return jnp.concatenate([field[..., 1:], jnp.zeros_like(field[..., :1])], axis=-1)
 
 
+def lon(x, start, stop):
+    first, last, _ = slice(start, stop).indices(x.shape[-3])
+    return lax.slice_in_dim(x, first, last, axis=x.ndim - 3)
+
+
 def forward_core(widened, east, north):
     a_pos = jnp.maximum(east, 0.0)
     b_neg = jnp.minimum(east, 0.0)
-    c_pos = jnp.maximum(north[1:-1], 0.0)
-    d_neg = jnp.minimum(north[1:-1], 0.0)
-    flux_w = a_pos[1:] * widened[:, :-1] + b_neg[1:] * widened[:, 1:]
-    inner = widened[:, 1:-1]
+    c_pos = jnp.maximum(lon(north, 1, -1), 0.0)
+    d_neg = jnp.minimum(lon(north, 1, -1), 0.0)
+    flux_w = lon(a_pos, 1, None) * lon(widened, 0, -1) + lon(b_neg, 1, None) * lon(widened, 1, None)
+    inner = lon(widened, 1, -1)
     flux_s = c_pos * below(inner) + d_neg * inner
     flux_n = above(flux_s)
-    return inner - (flux_w[:, 1:] - flux_w[:, :-1]) - (flux_n - flux_s)
+    return inner - (lon(flux_w, 1, None) - lon(flux_w, 0, -1)) - (flux_n - flux_s)
 
 
 def adjoint_core(widened, east, north):
     a_pos = jnp.maximum(east, 0.0)
-    b_neg = jnp.minimum(east, 0.0)[1:-1]
-    c_pos = jnp.maximum(north[1:-1], 0.0)
-    d_neg = jnp.minimum(north[1:-1], 0.0)
-    a_east = a_pos[2:]
+    b_neg = lon(jnp.minimum(east, 0.0), 1, -1)
+    c_pos = jnp.maximum(lon(north, 1, -1), 0.0)
+    d_neg = jnp.minimum(lon(north, 1, -1), 0.0)
+    a_east = lon(a_pos, 2, None)
     c_north = above(c_pos)
-    inner = widened[:, 1:-1]
-    west_val = widened[:, :-2]
-    east_val = widened[:, 2:]
+    inner = lon(widened, 1, -1)
+    west_val = lon(widened, 0, -2)
+    east_val = lon(widened, 2, None)
     return (
         inner * (1.0 - a_east + b_neg - c_north + d_neg)
         - b_neg * west_val
@@ -142,12 +147,12 @@
 
 
 def four_steps(state, east, north, weight):
-    span = state.shape[1]
+    span = state.shape[-3]
     for step in range(2):
-        state = forward_core(state, east[step:span - step], north[step:span - step])
-    state = weight[2:span - 2] * state
+        state = forward_core(state, lon(east, step, span - step), lon(north, step, span - step))
+    state = lon(weight, 2, span - 2) * state
     for step in range(2, 4):
-        state = adjoint_core(state, east[step:span - step], north[step:span - step])
+        state = adjoint_core(state, lon(east, step, span - step), lon(north, step, span - step))
     return state
 
 
@@ -259,17 +264,18 @@
     def fields(parts):
         return parts[0], parts[1][0], parts[2][0], parts[3][0]
 
-    inner = stencil_sums(*fields(pack))
-    rim = [
-        jnp.concatenate(
-            [from_west[lo:hi], part[:, :2 * halo], part[:, lon_count - 2 * halo:], from_east[lo:hi]],
-            axis=1,
-        )
+    inner = lat_average(stencil_sums(*fields(pack)))
+    sides = [
+        jnp.stack([
+            jnp.concatenate([from_west[lo:hi], part[:, :2 * halo]], axis=1),
+            jnp.concatenate([part[:, lon_count - 2 * halo:], from_east[lo:hi]], axis=1),
+        ])
         for part, (lo, hi) in zip(pack, bounds)
     ]
-    rim = stencil_sums(*fields(rim))
-    summed = jnp.concatenate([rim[:, :1], inner, rim[:, rim.shape[1] - 1:]], axis=1)
-    coarse = lat_average(summed)
+    rim = four_steps(sides[0], sides[1], sides[2], sides[3])
+    west = coarsen(increments[:, :halo] + rim[0])
+    east = coarsen(increments[:, lon_count - halo:] + rim[1])
+    coarse = jnp.concatenate([west, inner, east], axis=1)
     coarse = coarse.reshape(probe_count, -1)
     all_probes = probe_count * lax.axis_size("probe")
     ident = jnp.eye(all_probes, dtype=jnp.float32)

time: 115 us -> 102 us (0.89); the launches traced: 113 us -> 101 us
  Pallas kernels: 53.3 us -> 36.6 us
  waiting for transfers between devices: 1.37 us -> 3.25 us
  matrix products: 3.02 us -> 4.25 us
    pallas_call x2 -> x1, Pallas kernels: 29.6 us -> 14.9 us  [stencil_sums(): pl.pallas_call(stencil_kernel, out_shape=jax.ShapeDtypeStruct((probe_coun...]
    add x0 -> x6, other arithmetic: none -> 3.78 us  [the longest x2 1.61 us: forward_core(): flux_s = c_pos * below(inner) + d_neg * inner]
    ppermute x1, waiting for transfers between devices: 0.01 us -> 3.25 us  [body(): from_east = lax.ppermute(east_edge, 'lon', backward)]
    ppermute x1, starting transfers between devices: 0.01 us -> 2.3 us  [body(): from_west = lax.ppermute(west_edge, 'lon', forward)]
    ppermute x1, starting transfers between devices: 9.78 us -> 7.49 us  [body(): from_east = lax.ppermute(east_edge, 'lon', backward)]
    pallas_call x1, Pallas kernels: 23.7 us -> 21.7 us  [butterfly_sum(): pl.pallas_call(functools.partial(exchange_kernel, count, radix), out_shap...]
    add x2 -> x1, other arithmetic: 2.83 us -> 0.85 us  [stencil_sums(): centre = 1.0 - next_a + east_b - north_up + north_d]
    concatenate x2 -> x1, other arithmetic: 1.91 us -> 0.03 us  [body(): coarse = jnp.concatenate([west, inner, east], axis=1)]
  transfers between devices with their start and end apart: 2 -> 2, of which waited for: 1 -> 1; matrix products, arithmetic and copies ran while one was open for 5% -> 6% of each run, Pallas kernels for 13% -> 15%
where the time goes in v14:
time: 102 us; the launch traced here: 101 us
  Pallas kernels  36.6 us (36%)
  other arithmetic  24.5 us (24%)
  local copies, waits for them, and re-layouts  13.1 us (13%)
  starting transfers between devices  9.79 us (10%)
  blocking collectives  8.64 us (8%)
  matrix products  4.25 us (4%)
  waiting for transfers between devices  3.25 us (3%)
  between operations  1.09 us (1%)
    pallas_call x1, Pallas kernels, butterfly_sum(): pl.pallas_call(functools.partial(exchange_kernel, count, radix), out_shap...  21.7 us
    pallas_call x1, Pallas kernels, stencil_sums(): pl.pallas_call(stencil_kernel, out_shape=jax.ShapeDtypeStruct((probe_coun...  14.9 us
    all_gather x1, blocking collectives, body(): full_panel = lax.all_gather(coarse, 'probe', axis=0, tiled=True)  8.64 us
    ppermute x1, starting transfers between devices, body(): from_east = lax.ppermute(east_edge, 'lon', backward)  7.49 us
    another operation x3, other arithmetic, body(): lower = jnp.linalg.cholesky(gram)  6.52 us
    another operation x1, other arithmetic, body(): lax.linalg.triangular_solve(lower, ident, left_side=True, lower=True)  4.9 us
    ppermute x1, waiting for transfers between devices, body(): from_east = lax.ppermute(east_edge, 'lon', backward)  3.25 us
    ppermute x1, starting transfers between devices, body(): from_west = lax.ppermute(west_edge, 'lon', forward)  2.3 us
  transfers between devices with their start and end apart: 2, of which 1 were waited for; matrix products, arithmetic and copies ran while one was open for 6% of the time, Pallas kernels for 15%

profile of v14, /device:TPU:8, one launch (start us, length us, event | category | flops | bytes accessed | tf_op | source)
XLA Modules:
  0.0 101.2 jit_solution(4033999627837326253)
XLA Ops:
  0.6 1.8 %slice_maximum_fusion = (f32[1,24,8,256]{3,2,1,0:T(8,128)S(1)}, f32[24,8,256]{2,1,0:T(8,128)}, f32[24,8,256]{2,1,0:T(8,128)}, f32[1,24,8,256]{3,2,1,0:T(8,128)S(1)}) fusion(f32[2,24,8,256]{3,2,1,0:T(8,128)} %param.4, pred[256]{0:T(512)(128)(4,1)S(1)} %iota_compare_fusion.8), kind=kLoop, calls=%fused_computation.73 | loop fusion | flops 147456 | bytes 1179904 | tf_op jit(solution)/shard_map/max | solution.py:214
  2.5 0.8 fusion.82
  3.3 0.8 fusion.86
  4.1 1.4 %fusion.76 = (f32[16,4,8,256]{3,2,1,0:T(8,128)S(1)}, f32[16,4,8,256]{3,2,1,0:T(8,128)S(1)}) fusion(f32[16,24,8,256]{3,2,1,0:T(8,128)} %q_ref.1), kind=kLoop, calls=%fused_computation.165 | loop fusion | bytes 2097152 | tf_op jit(solution)/shard_map/slice | solution.py:276
  5.4 0.9 pad_maximum_fusion
  6.3 2.3 %collective-permute-start = (f32[19,4,8,256]{3,2,1,0:T(8,128)}, f32[19,4,8,256]{3,2,1,0:T(8,128)}, u32[]{:S(2)}, u32[]{:S(2)}) collective-permute-start(f32[19,4,8,256]{3,2,1,0:T(8,128)} %pad_maximum_fusion), channel_id=1, source_target_pairs={{0,4},{4,8},{8,12},{12,16},{16,20},{20,24},{24,28},{28,32},{32,36}... | collective-permute-start | bytes 1867784 | tf_op jit(solution)/shard_map/ppermute | solution.py:259
  8.6 0.9 pad_maximum_fusion.1
  9.6 7.5 %collective-permute-start.1 = (f32[19,4,8,256]{3,2,1,0:T(8,128)}, f32[19,4,8,256]{3,2,1,0:T(8,128)}, u32[]{:S(2)}, u32[]{:S(2)}) collective-permute-start(f32[19,4,8,256]{3,2,1,0:T(8,128)} %pad_maximum_fusion.1), channel_id=1, source_target_pairs={{4,0},{8,4},{12,8},{16,12},{20,16},{24,20},{28,24},{32,28},{36,32}... | collective-permute-start | bytes 1867784 | tf_op jit(solution)/shard_map/ppermute | solution.py:260
  17.0 0.7 fusion.84
  18.5 0.9 subtract_add_fusion
  19.4 14.9 %shard_map.50 = f32[16,4,8,256]{3,2,1,0:T(8,128)} custom-call(f32[16,24,8,256]{3,2,1,0:T(8,128)} %q_ref.1, f32[24,8,256]{2,1,0:T(8,128)} %get-tuple-element.27.a_ref, f32[24,8,256]{2,1,0:T(8,128)} %get-tuple-element.28.b_ref, f32[24,8,256]{2,1,0:T(8,128)} %copy-done.2, f32[24,8,256]{2,1,0:T(8,128)} %get-tuple-element.9.d_ref, f32[24,8,256]{2,1,0:T(8,128)} %w_ref.1, ...), custom_call_target="tpu_custom_call" | custom-call | flops 39321600 | bytes 4521984 | tf_op jit(solution)/shard_map/pallas_call | solution.py:224
  34.3 1.6 %fusion.37 = f32[16,4,8,64]{3,2,1,0:T(8,128)S(1)} fusion(f32[16,4,8,256]{3,2,1,0:T(8,128)} %shard_map.50, s32[256]{0:T(256)S(1)} %get-tuple-element.64, s32[256]{0:T(256)S(1)} %get-tuple-element.65, pred[256]{0:T(512)(128)(4,1)S(1)} %compare_and_fusion), kind=kOutput, calls=%fused_computation.109 | convolution fusion | flops 100712448 | bytes 657664 | tf_op jit(solution)/shard_map/dot_general | solution.py:241
  36.1 0.8 fusion.79
  37.0 3.2 %collective-permute-done.1 = f32[19,4,8,256]{3,2,1,0:T(8,128)} collective-permute-done((f32[19,4,8,256]{3,2,1,0:T(8,128)}, f32[19,4,8,256]{3,2,1,0:T(8,128)}, u32[]{:S(2)}, u32[]{:S(2)}) %collective-permute-start.1) | collective-permute-done | bytes 622624 | tf_op jit(solution)/shard_map/ppermute | solution.py:260
  40.2 0.8 fusion.80
  41.3 1.1 %slice.333 = f32[16,4,8,256]{3,2,1,0:T(8,128)S(1)} slice(f32[19,4,8,256]{3,2,1,0:T(8,128)} %collective-permute-done.1), slice={[0:16], [0:4], [0:8], [0:256]} | slice | bytes 1048576 | tf_op jit(solution)/shard_map/slice | solution.py:271
  42.5 1.1 %slice.332 = f32[16,4,8,256]{3,2,1,0:T(8,128)S(1)} slice(f32[19,4,8,256]{3,2,1,0:T(8,128)} %collective-permute-done), slice={[0:16], [0:4], [0:8], [0:256]} | slice | bytes 1048576 | tf_op jit(solution)/shard_map/slice | solution.py:270
  43.8 0.9 fusion.7
  44.6 0.7 slice.354
  45.7 1.6 %fusion.9 = f32[2,16,10,8,256]{4,3,2,1,0:T(8,128)S(1)} fusion(f32[2,16,11,8,256]{4,3,2,1,0:T(8,128)S(1)} %fusion.2, f32[2,16,10,8,255]{4,3,2,1,0:T(8,128)S(1)} %slice.354, f32[1,16,12,8,256]{4,3,2,1,0:T(8,128)S(1)} %maximum_bitcast_fusion.1, f32[1,16,12,8,256]{4,3,2,1,0:T(8,128)S(1)} %maximum_bitcast_fusion, f32[2,10,8,256]{3,2,1,0:T(8,128)S(1)} %get-tuple-element.44, ...), kind=kLoop, calls=%fused_computation.18 | loop fusion | flops 8519680 | bytes 13948928 | tf_op jit(solution)/shard_map/sub | solution.py:127
  47.6 0.7 multiply_add_fusion
  49.3 0.7 fusion.13
  50.7 0.9 fusion.16
  53.6 8.6 %all_gather.3 = f32[64,3072]{1,0:T(8,128)S(1)} all-gather(f32[16,3072]{1,0:T(8,128)S(1)} %reshape.120), channel_id=1, replica_groups=mesh['lon'=64,'probe'=4] {'probe'}, dimensions={0}, use_global_device_ids=true | all-gather | bytes 983040 | tf_op jit(solution)/shard_map/all_gather | solution.py:282
  62.3 1.4 %fusion.87.block_ref = f32[64,64]{1,0:T(8,128)} fusion(f32[64,3072]{1,0:T(8,128)S(1)} %all_gather.3), kind=kOutput, calls=%fused_computation.176 | convolution fusion | flops 150994944 | bytes 802816 | tf_op jit(solution)/shard_map/dot_general | solution.py:283
  63.7 21.7 %shard_map.51 = f32[64,64]{1,0:T(8,128)} custom-call(f32[64,64]{1,0:T(8,128)} %fusion.87.block_ref), custom_call_target="tpu_custom_call" | custom-call | tf_op jit(solution)/shard_map/pallas_call | solution.py:71
  85.4 0.8 copy.10
  86.2 0.8 fusion.43
  87.0 5.8 %cholesky.17 = f32[64,64]{1,0:T(8,128)S(1)} custom-call(f32[64,64]{1,0:T(8,128)S(1)} %fusion.43), custom_call_target="Cholesky" | custom-call | tf_op jit(solution)/shard_map/jit(cholesky)/cholesky | solution.py:290
  94.2 4.9 %custom-call.6 = f32[1,64,64]{1,2,0:T(8,128)S(1)} custom-call(f32[1,64,64]{2,1,0:T(8,128)S(1)} %get-tuple-element.61), custom_call_target="InvertDiagBlocksLowerTriangular" | custom-call | tf_op jit(solution)/shard_map/triangular_solve | solution.py:291
  99.8 0.7 copy.16
  100.5 0.7 copy.12
  (61 shorter events, 7.6 us)
Async XLA Ops:
  4.1 13.7 %copy-start.1 = (f32[2,24,8,256]{3,2,1,0:T(8,128)S(1)}, f32[2,24,8,256]{3,2,1,0:T(8,128)}, u32[]{:S(2)}) copy-start(f32[2,24,8,256]{3,2,1,0:T(8,128)} %param.4) | copy-start | bytes 1179652
  4.1 14.3 %copy-start.3 = (f32[24,8,256]{2,1,0:T(8,128)S(1)}, f32[24,8,256]{2,1,0:T(8,128)}, u32[]{:S(2)}) copy-start(f32[24,8,256]{2,1,0:T(8,128)} %w_ref.1) | copy-start | bytes 589828
  6.3 29.8 %collective-permute-start = (f32[19,4,8,256]{3,2,1,0:T(8,128)}, f32[19,4,8,256]{3,2,1,0:T(8,128)}, u32[]{:S(2)}, u32[]{:S(2)}) collective-permute-start(f32[19,4,8,256]{3,2,1,0:T(8,128)} %pad_maximum_fusion), channel_id=1, source_target_pairs={{0,4},{4,8},{8,12},{12,16},{16,20},{20,24},{24,28},{28,32},{32,36}... | collective-permute-start | bytes 1867784 | tf_op jit(solution)/shard_map/ppermute | solution.py:259
  9.6 30.7 %collective-permute-start.1 = (f32[19,4,8,256]{3,2,1,0:T(8,128)}, f32[19,4,8,256]{3,2,1,0:T(8,128)}, u32[]{:S(2)}, u32[]{:S(2)}) collective-permute-start(f32[19,4,8,256]{3,2,1,0:T(8,128)} %pad_maximum_fusion.1), channel_id=1, source_target_pairs={{4,0},{8,4},{12,8},{16,12},{20,16},{24,20},{28,24},{32,28},{36,32}... | collective-permute-start | bytes 1867784 | tf_op jit(solution)/shard_map/ppermute | solution.py:260
  18.4 1.0 copy-start.2
  19.4 16.5 %copy-start = (f32[16,24,8,256]{3,2,1,0:T(8,128)S(1)}, f32[16,24,8,256]{3,2,1,0:T(8,128)}, u32[]{:S(2)}) copy-start(f32[16,24,8,256]{3,2,1,0:T(8,128)} %q_ref.1) | copy-start | bytes 9437188
  35.9 1.0 copy-start.6
  36.0 5.0 %copy-start.5 = (f32[1,8,8,256]{3,2,1,0:T(8,128)S(1)}, f32[1,8,8,256]{3,2,1,0:T(8,128)}, u32[]{:S(2)}) copy-start(f32[1,8,8,256]{3,2,1,0:T(8,128)} %get-tuple-element.46) | copy-start | bytes 196612
  36.0 5.1 %copy-start.4 = (f32[1,8,8,256]{3,2,1,0:T(8,128)S(1)}, f32[1,8,8,256]{3,2,1,0:T(8,128)}, u32[]{:S(2)}) copy-start(f32[1,8,8,256]{3,2,1,0:T(8,128)} %get-tuple-element.30) | copy-start | bytes 196612

commit v15 on v14

--- a/solution.py
+++ b/solution.py
@@ -250,7 +250,7 @@
 def body(increments, winds, obs_weight):
     probe_count, lon_count, level_count, lat_count = increments.shape
     halo = 4
-    pack = (increments, winds[0][None], lat_mask(winds[1])[None], obs_weight[None])
+    pack = (increments, winds[0][None], winds[1][None], obs_weight[None])
     count = lax.axis_size("lon")
     forward = [(i, (i + 1) % count) for i in range(count)]
     backward = [((i + 1) % count, i) for i in range(count)]
@@ -262,7 +262,7 @@
               (probe_count + 1, probe_count + 2), (probe_count + 2, probe_count + 3))
 
     def fields(parts):
-        return parts[0], parts[1][0], parts[2][0], parts[3][0]
+        return parts[0], parts[1][0], lat_mask(parts[2][0]), parts[3][0]
 
     inner = lat_average(stencil_sums(*fields(pack)))
     sides = [
@@ -272,7 +272,7 @@
         ])
         for part, (lo, hi) in zip(pack, bounds)
     ]
-    rim = four_steps(sides[0], sides[1], sides[2], sides[3])
+    rim = four_steps(sides[0], sides[1], lat_mask(sides[2]), sides[3])
     west = coarsen(increments[:, :halo] + rim[0])
     east = coarsen(increments[:, lon_count - halo:] + rim[1])
     coarse = jnp.concatenate([west, inner, east], axis=1)

time: 102 us -> 103 us (level)
  waiting for transfers between devices: 3.25 us -> 0.77 us
  Pallas kernels: 36.6 us -> 38.6 us
  local copies, waits for them, and re-layouts: 13.1 us -> 14.7 us
  other arithmetic: 24.5 us -> 23.4 us
    ppermute x1, waiting for transfers between devices: 3.25 us -> 0.01 us  [body(): from_east = lax.ppermute(east_edge, 'lon', backward)]
    ppermute x1, starting transfers between devices: 2.3 us -> 0.01 us  [body(): from_west = lax.ppermute(west_edge, 'lon', forward)]
    ppermute x1, starting transfers between devices: 7.49 us -> 9.78 us  [body(): from_east = lax.ppermute(east_edge, 'lon', backward)]
    pallas_call x1, Pallas kernels: 21.7 us -> 23.7 us  [butterfly_sum(): pl.pallas_call(functools.partial(exchange_kernel, count, radix), out_shap...]
    max x1, other arithmetic: 1.84 us -> 0.78 us  [stencil_sums(): east_a = jnp.maximum(east, 0.0)]
  transfers between devices with their start and end apart: 2 -> 2, of which waited for: 1 -> 1; matrix products, arithmetic and copies ran while one was open for 6% -> 7% of each run, Pallas kernels for 15% -> 15%
where the time goes in v15:
time: 103 us; the launch traced here: 101 us
  Pallas kernels  38.6 us (37%)
  other arithmetic  23.4 us (23%)
  local copies, waits for them, and re-layouts  14.7 us (14%)
  starting transfers between devices  9.79 us (10%)
  blocking collectives  8.64 us (8%)
  matrix products  4.25 us (4%)
  between operations  1.1 us (1%)
    pallas_call x1, Pallas kernels, butterfly_sum(): pl.pallas_call(functools.partial(exchange_kernel, count, radix), out_shap...  23.7 us
    pallas_call x1, Pallas kernels, stencil_sums(): pl.pallas_call(stencil_kernel, out_shape=jax.ShapeDtypeStruct((probe_coun...  14.9 us
    ppermute x1, starting transfers between devices, body(): from_east = lax.ppermute(east_edge, 'lon', backward)  9.78 us
    all_gather x1, blocking collectives, body(): full_panel = lax.all_gather(coarse, 'probe', axis=0, tiled=True)  8.64 us
    another operation x3, other arithmetic, body(): lower = jnp.linalg.cholesky(gram)  6.52 us
    another operation x1, other arithmetic, body(): lax.linalg.triangular_solve(lower, ident, left_side=True, lower=True)  4.9 us
  transfers between devices with their start and end apart: 2, of which 1 were waited for; matrix products, arithmetic and copies ran while one was open for 7% of the time, Pallas kernels for 15%

profile of v15, /device:TPU:8, one launch (start us, length us, event | category | flops | bytes accessed | tf_op | source)
XLA Modules:
  0.0 101.2 jit_solution(12532279848337189788)
XLA Ops:
  0.6 0.8 fusion.79
  1.4 1.4 %fusion.71 = (f32[16,4,8,256]{3,2,1,0:T(8,128)S(1)}, f32[16,4,8,256]{3,2,1,0:T(8,128)S(1)}) fusion(f32[16,24,8,256]{3,2,1,0:T(8,128)} %q_ref.1), kind=kLoop, calls=%fused_computation.155 | loop fusion | bytes 2097152 | tf_op jit(solution)/shard_map/slice | solution.py:276
  2.8 0.9 fusion.77
  3.7 0.9 pad_maximum_fusion.1
  4.6 9.8 %collective-permute-start.1 = (f32[19,4,8,256]{3,2,1,0:T(8,128)}, f32[19,4,8,256]{3,2,1,0:T(8,128)}, u32[]{:S(2)}, u32[]{:S(2)}) collective-permute-start(f32[19,4,8,256]{3,2,1,0:T(8,128)} %pad_maximum_fusion.1), channel_id=1, source_target_pairs={{4,0},{8,4},{12,8},{16,12},{20,16},{24,20},{28,24},{32,28},{36,32}... | collective-permute-start | bytes 1867784 | tf_op jit(solution)/shard_map/ppermute | solution.py:260
  14.4 0.9 pad_maximum_fusion
  15.3 0.7 fusion.76
  16.0 0.7 fusion.78
  16.6 0.8 slice_maximum_fusion
  17.6 0.8 subtract_add_fusion
  18.4 14.9 %shard_map.50 = f32[16,4,8,256]{3,2,1,0:T(8,128)} custom-call(f32[16,24,8,256]{3,2,1,0:T(8,128)} %q_ref.1, f32[24,8,256]{2,1,0:T(8,128)} %get-tuple-element.25.a_ref, f32[24,8,256]{2,1,0:T(8,128)} %get-tuple-element.26.b_ref, f32[24,8,256]{2,1,0:T(8,128)} %copy-done.4, f32[24,8,256]{2,1,0:T(8,128)} %get-tuple-element.9.d_ref, f32[24,8,256]{2,1,0:T(8,128)} %w_ref.1, ...), custom_call_target="tpu_custom_call" | custom-call | flops 39321600 | bytes 4521984 | tf_op jit(solution)/shard_map/pallas_call | solution.py:224
  33.3 1.6 %fusion.34 = f32[16,4,8,64]{3,2,1,0:T(8,128)S(1)} fusion(f32[16,4,8,256]{3,2,1,0:T(8,128)} %shard_map.50, s32[256]{0:T(256)S(1)} %get-tuple-element.62, s32[256]{0:T(256)S(1)} %get-tuple-element.63, pred[256]{0:T(512)(128)(4,1)S(1)} %compare_and_fusion), kind=kOutput, calls=%fused_computation.100 | convolution fusion | flops 100712448 | bytes 657664 | tf_op jit(solution)/shard_map/dot_general | solution.py:241
  35.2 0.8 fusion.75
  36.0 0.8 collective-permute-done
  36.8 0.8 fusion.74
  37.8 1.1 %slice.330 = f32[16,4,8,256]{3,2,1,0:T(8,128)S(1)} slice(f32[19,4,8,256]{3,2,1,0:T(8,128)} %collective-permute-done), slice={[0:16], [0:4], [0:8], [0:256]} | slice | bytes 1048576 | tf_op jit(solution)/shard_map/slice | solution.py:270
  39.0 1.1 %slice.331 = f32[16,4,8,256]{3,2,1,0:T(8,128)S(1)} slice(f32[19,4,8,256]{3,2,1,0:T(8,128)} %collective-permute-done.1), slice={[0:16], [0:4], [0:8], [0:256]} | slice | bytes 1048576 | tf_op jit(solution)/shard_map/slice | solution.py:271
  40.2 0.8 fusion.7
  41.1 0.7 slice.349
  42.2 1.6 %fusion.9 = f32[2,16,10,8,256]{4,3,2,1,0:T(8,128)S(1)} fusion(f32[2,16,11,8,256]{4,3,2,1,0:T(8,128)S(1)} %fusion.2, f32[2,16,10,8,255]{4,3,2,1,0:T(8,128)S(1)} %slice.349, f32[1,16,12,8,256]{4,3,2,1,0:T(8,128)S(1)} %maximum_bitcast_fusion.1, f32[1,16,12,8,256]{4,3,2,1,0:T(8,128)S(1)} %maximum_bitcast_fusion, f32[2,10,8,256]{3,2,1,0:T(8,128)S(1)} %get-tuple-element.45, ...), kind=kLoop, calls=%fused_computation.18 | loop fusion | flops 8519680 | bytes 13948928 | tf_op jit(solution)/shard_map/sub | solution.py:127
  46.2 0.7 fusion.13
  48.0 1.0 %fusion.16 = f32[2,16,6,8,256]{4,3,2,1,0:T(8,128)S(1)} fusion(f32[2,16,8,8,256]{4,3,2,1,0:T(8,128)S(1)} %fusion.13, f32[2,16,6,8,255]{4,3,2,1,0:T(8,128)S(1)} %get-tuple-element.15, f32[2,16,6,8,255]{4,3,2,1,0:T(8,128)S(1)} %get-tuple-element.14, f32[2,6,8,256]{3,2,1,0:T(8,128)S(1)} %get-tuple-element.54, f32[2,6,8,256]{3,2,1,0:T(8,128)S(1)} %get-tuple-element.39, ...), kind=kLoop, calls=%fused_computation.30 | loop fusion | flops 3538944 | bytes 9916416 | tf_op jit(solution)/shard_map/add | solution.py:141
  50.0 0.7 fusion.20
  51.6 8.6 %all_gather.3 = f32[64,3072]{1,0:T(8,128)S(1)} all-gather(f32[16,3072]{1,0:T(8,128)S(1)} %reshape.156), channel_id=1, replica_groups=mesh['lon'=64,'probe'=4] {'probe'}, dimensions={0}, use_global_device_ids=true | all-gather | bytes 983040 | tf_op jit(solution)/shard_map/all_gather | solution.py:282
  60.3 1.4 %fusion.80.block_ref = f32[64,64]{1,0:T(8,128)} fusion(f32[64,3072]{1,0:T(8,128)S(1)} %all_gather.3), kind=kOutput, calls=%fused_computation.164 | convolution fusion | flops 150994944 | bytes 802816 | tf_op jit(solution)/shard_map/dot_general | solution.py:283
  61.6 23.7 %shard_map.51 = f32[64,64]{1,0:T(8,128)} custom-call(f32[64,64]{1,0:T(8,128)} %fusion.80.block_ref), custom_call_target="tpu_custom_call" | custom-call | tf_op jit(solution)/shard_map/pallas_call | solution.py:71
  85.4 0.8 copy.10
  86.2 0.8 fusion.40
  87.0 5.8 %cholesky.17 = f32[64,64]{1,0:T(8,128)S(1)} custom-call(f32[64,64]{1,0:T(8,128)S(1)} %fusion.40), custom_call_target="Cholesky" | custom-call | tf_op jit(solution)/shard_map/jit(cholesky)/cholesky | solution.py:290
  94.2 4.9 %custom-call.6 = f32[1,64,64]{1,2,0:T(8,128)S(1)} custom-call(f32[1,64,64]{2,1,0:T(8,128)S(1)} %get-tuple-element.57), custom_call_target="InvertDiagBlocksLowerTriangular" | custom-call | tf_op jit(solution)/shard_map/triangular_solve | solution.py:291
  99.8 0.7 copy.16
  100.5 0.7 copy.12
  (72 shorter events, 8.3 us)
Async XLA Ops:
  1.4 13.8 %copy-start.1 = (f32[2,24,8,256]{3,2,1,0:T(8,128)S(1)}, f32[2,24,8,256]{3,2,1,0:T(8,128)}, u32[]{:S(2)}) copy-start(f32[2,24,8,256]{3,2,1,0:T(8,128)} %param.4) | copy-start | bytes 1179652
  1.4 14.6 %copy-start.5 = (f32[24,8,256]{2,1,0:T(8,128)S(1)}, f32[24,8,256]{2,1,0:T(8,128)}, u32[]{:S(2)}) copy-start(f32[24,8,256]{2,1,0:T(8,128)} %w_ref.1) | copy-start | bytes 589828
  4.6 30.6 %collective-permute-start.1 = (f32[19,4,8,256]{3,2,1,0:T(8,128)}, f32[19,4,8,256]{3,2,1,0:T(8,128)}, u32[]{:S(2)}, u32[]{:S(2)}) collective-permute-start(f32[19,4,8,256]{3,2,1,0:T(8,128)} %pad_maximum_fusion.1), channel_id=1, source_target_pairs={{4,0},{8,4},{12,8},{16,12},{20,16},{24,20},{28,24},{32,28},{36,32}... | collective-permute-start | bytes 1867784 | tf_op jit(solution)/shard_map/ppermute | solution.py:260
  15.3 21.5 %collective-permute-start = (f32[19,4,8,256]{3,2,1,0:T(8,128)}, f32[19,4,8,256]{3,2,1,0:T(8,128)}, u32[]{:S(2)}, u32[]{:S(2)}) collective-permute-start(f32[19,4,8,256]{3,2,1,0:T(8,128)} %pad_maximum_fusion), channel_id=1, source_target_pairs={{0,4},{4,8},{8,12},{12,16},{16,20},{20,24},{24,28},{28,32},{32,36}... | collective-permute-start | bytes 1867784 | tf_op jit(solution)/shard_map/ppermute | solution.py:259
  17.4 1.0 copy-start.4
  18.4 16.5 %copy-start = (f32[16,24,8,256]{3,2,1,0:T(8,128)S(1)}, f32[16,24,8,256]{3,2,1,0:T(8,128)}, u32[]{:S(2)}) copy-start(f32[16,24,8,256]{3,2,1,0:T(8,128)} %q_ref.1) | copy-start | bytes 9437188
  35.0 1.0 copy-start.10
  35.0 1.0 copy-start.11
  35.0 2.6 %copy-start.8 = (f32[1,8,8,256]{3,2,1,0:T(8,128)S(1)}, f32[1,8,8,256]{3,2,1,0:T(8,128)}, u32[]{:S(2)}) copy-start(f32[1,8,8,256]{3,2,1,0:T(8,128)} %get-tuple-element.27) | copy-start | bytes 196612
  35.0 2.6 %copy-start.9 = (f32[1,8,8,256]{3,2,1,0:T(8,128)S(1)}, f32[1,8,8,256]{3,2,1,0:T(8,128)}, u32[]{:S(2)}) copy-start(f32[1,8,8,256]{3,2,1,0:T(8,128)} %get-tuple-element.30) | copy-start | bytes 196612
  37.6 1.4 %copy-start.2 = (f32[2,1,12,8,256]{4,3,2,1,0:T(8,128)}, f32[2,1,12,8,256]{4,3,2,1,0:T(8,128)S(1)}, u32[]{:S(2)}) copy-start(f32[2,1,12,8,256]{4,3,2,1,0:T(8,128)S(1)} %maximum_select_fusion) | copy-start | bytes 589828
  45.3 0.8 copy-start.7
  45.3 0.9 copy-start.6
  46.9 0.9 slice-start
  46.9 1.0 copy-start.3
  49.0 0.8 slice-start.1

commit v16 on v14

--- a/solution.py
+++ b/solution.py
@@ -287,7 +287,7 @@
         preferred_element_type=jnp.float32,
     )
     gram = butterfly_sum(local_gram, "lon")
-    lower = jnp.linalg.cholesky(gram)
+    lower = lax.linalg.cholesky(gram, symmetrize_input=False)
     inverse = lax.linalg.triangular_solve(lower, ident, left_side=True, lower=True)
     own_rows = lax.dynamic_slice_in_dim(
         inverse, lax.axis_index("probe") * probe_count, probe_count, 0

time: 102 us -> 102 us (level)
  no operation moved by 1% of the time
where the time goes in v16:
time: 102 us; the launch traced here: 101 us
  Pallas kernels  36.6 us (36%)
  other arithmetic  24.3 us (24%)
  local copies, waits for them, and re-layouts  13.5 us (13%)
  starting transfers between devices  9.79 us (10%)
  blocking collectives  8.63 us (8%)
  matrix products  4.25 us (4%)
  waiting for transfers between devices  2.59 us (3%)
  between operations  1.09 us (1%)
    pallas_call x1, Pallas kernels, butterfly_sum(): pl.pallas_call(functools.partial(exchange_kernel, count, radix), out_shap...  21.7 us
    pallas_call x1, Pallas kernels, stencil_sums(): pl.pallas_call(stencil_kernel, out_shape=jax.ShapeDtypeStruct((probe_coun...  14.9 us
    all_gather x1, blocking collectives, body(): full_panel = lax.all_gather(coarse, 'probe', axis=0, tiled=True)  8.63 us
    ppermute x1, starting transfers between devices, body(): from_east = lax.ppermute(east_edge, 'lon', backward)  7.49 us
    another operation x3, other arithmetic, body(): lower = lax.linalg.cholesky(gram, symmetrize_input=False)  7.27 us
    another operation x1, other arithmetic, body(): lax.linalg.triangular_solve(lower, ident, left_side=True, lower=True)  4.9 us
    ppermute x1, waiting for transfers between devices, body(): from_east = lax.ppermute(east_edge, 'lon', backward)  2.59 us
    ppermute x1, starting transfers between devices, body(): from_west = lax.ppermute(west_edge, 'lon', forward)  2.3 us
  transfers between devices with their start and end apart: 2, of which 1 were waited for; matrix products, arithmetic and copies ran while one was open for 6% of the time, Pallas kernels for 15%

profile of v16, /device:TPU:8, one launch (start us, length us, event | category | flops | bytes accessed | tf_op | source)
XLA Modules:
  0.0 100.8 jit_solution(17340846352119541693)
XLA Ops:
  0.6 1.8 %slice_maximum_fusion = (f32[1,24,8,256]{3,2,1,0:T(8,128)S(1)}, f32[24,8,256]{2,1,0:T(8,128)}, f32[24,8,256]{2,1,0:T(8,128)}, f32[1,24,8,256]{3,2,1,0:T(8,128)S(1)}) fusion(f32[2,24,8,256]{3,2,1,0:T(8,128)} %param.4, pred[256]{0:T(512)(128)(4,1)S(1)} %iota_compare_fusion.8), kind=kLoop, calls=%fused_computation.73 | loop fusion | flops 147456 | bytes 1179904 | tf_op jit(solution)/shard_map/max | solution.py:214
  2.5 0.8 fusion.81
  3.3 0.8 fusion.85
  4.1 1.4 %fusion.75 = (f32[16,4,8,256]{3,2,1,0:T(8,128)S(1)}, f32[16,4,8,256]{3,2,1,0:T(8,128)S(1)}) fusion(f32[16,24,8,256]{3,2,1,0:T(8,128)} %q_ref.1), kind=kLoop, calls=%fused_computation.163 | loop fusion | bytes 2097152 | tf_op jit(solution)/shard_map/slice | solution.py:276
  5.4 0.9 pad_maximum_fusion
  6.3 2.3 %collective-permute-start = (f32[19,4,8,256]{3,2,1,0:T(8,128)}, f32[19,4,8,256]{3,2,1,0:T(8,128)}, u32[]{:S(2)}, u32[]{:S(2)}) collective-permute-start(f32[19,4,8,256]{3,2,1,0:T(8,128)} %pad_maximum_fusion), channel_id=1, source_target_pairs={{0,4},{4,8},{8,12},{12,16},{16,20},{20,24},{24,28},{28,32},{32,36}... | collective-permute-start | bytes 1867784 | tf_op jit(solution)/shard_map/ppermute | solution.py:259
  8.6 0.9 pad_maximum_fusion.1
  9.5 7.5 %collective-permute-start.1 = (f32[19,4,8,256]{3,2,1,0:T(8,128)}, f32[19,4,8,256]{3,2,1,0:T(8,128)}, u32[]{:S(2)}, u32[]{:S(2)}) collective-permute-start(f32[19,4,8,256]{3,2,1,0:T(8,128)} %pad_maximum_fusion.1), channel_id=1, source_target_pairs={{4,0},{8,4},{12,8},{16,12},{20,16},{24,20},{28,24},{32,28},{36,32}... | collective-permute-start | bytes 1867784 | tf_op jit(solution)/shard_map/ppermute | solution.py:260
  17.0 0.7 fusion.83
  17.7 0.7 fusion.80
  18.3 0.7 fusion.82
  19.2 0.8 subtract_add_fusion
  20.0 14.9 %shard_map.50 = f32[16,4,8,256]{3,2,1,0:T(8,128)} custom-call(f32[16,24,8,256]{3,2,1,0:T(8,128)} %q_ref.1, f32[24,8,256]{2,1,0:T(8,128)} %get-tuple-element.27.a_ref, f32[24,8,256]{2,1,0:T(8,128)} %get-tuple-element.28.b_ref, f32[24,8,256]{2,1,0:T(8,128)} %copy-done.2, f32[24,8,256]{2,1,0:T(8,128)} %get-tuple-element.9.d_ref, f32[24,8,256]{2,1,0:T(8,128)} %w_ref.1, ...), custom_call_target="tpu_custom_call" | custom-call | flops 39321600 | bytes 4521984 | tf_op jit(solution)/shard_map/pallas_call | solution.py:224
  34.9 1.6 %fusion.37 = f32[16,4,8,64]{3,2,1,0:T(8,128)S(1)} fusion(f32[16,4,8,256]{3,2,1,0:T(8,128)} %shard_map.50, s32[256]{0:T(256)S(1)} %get-tuple-element.64, s32[256]{0:T(256)S(1)} %get-tuple-element.65, pred[256]{0:T(512)(128)(4,1)S(1)} %compare_and_fusion), kind=kOutput, calls=%fused_computation.109 | convolution fusion | flops 100712448 | bytes 657664 | tf_op jit(solution)/shard_map/dot_general | solution.py:241
  36.8 0.8 fusion.78
  37.6 2.6 %collective-permute-done.1 = f32[19,4,8,256]{3,2,1,0:T(8,128)} collective-permute-done((f32[19,4,8,256]{3,2,1,0:T(8,128)}, f32[19,4,8,256]{3,2,1,0:T(8,128)}, u32[]{:S(2)}, u32[]{:S(2)}) %collective-permute-start.1) | collective-permute-done | bytes 622624 | tf_op jit(solution)/shard_map/ppermute | solution.py:260
  40.2 0.8 fusion.79
  41.3 1.1 %slice.331 = f32[16,4,8,256]{3,2,1,0:T(8,128)S(1)} slice(f32[19,4,8,256]{3,2,1,0:T(8,128)} %collective-permute-done.1), slice={[0:16], [0:4], [0:8], [0:256]} | slice | bytes 1048576 | tf_op jit(solution)/shard_map/slice | solution.py:271
  42.5 1.1 %slice.330 = f32[16,4,8,256]{3,2,1,0:T(8,128)S(1)} slice(f32[19,4,8,256]{3,2,1,0:T(8,128)} %collective-permute-done), slice={[0:16], [0:4], [0:8], [0:256]} | slice | bytes 1048576 | tf_op jit(solution)/shard_map/slice | solution.py:270
  43.7 0.9 fusion.7
  44.6 0.7 slice.352
  45.7 1.6 %fusion.9 = f32[2,16,10,8,256]{4,3,2,1,0:T(8,128)S(1)} fusion(f32[2,16,11,8,256]{4,3,2,1,0:T(8,128)S(1)} %fusion.2, f32[2,16,10,8,255]{4,3,2,1,0:T(8,128)S(1)} %slice.352, f32[1,16,12,8,256]{4,3,2,1,0:T(8,128)S(1)} %maximum_bitcast_fusion.1, f32[1,16,12,8,256]{4,3,2,1,0:T(8,128)S(1)} %maximum_bitcast_fusion, f32[2,10,8,256]{3,2,1,0:T(8,128)S(1)} %get-tuple-element.44, ...), kind=kLoop, calls=%fused_computation.18 | loop fusion | flops 8519680 | bytes 13948928 | tf_op jit(solution)/shard_map/sub | solution.py:127
  49.7 0.7 fusion.13
  51.2 0.9 fusion.16
  54.1 8.6 %all_gather.3 = f32[64,3072]{1,0:T(8,128)S(1)} all-gather(f32[16,3072]{1,0:T(8,128)S(1)} %reshape.119), channel_id=1, replica_groups=mesh['lon'=64,'probe'=4] {'probe'}, dimensions={0}, use_global_device_ids=true | all-gather | bytes 983040 | tf_op jit(solution)/shard_map/all_gather | solution.py:282
  62.7 1.4 %fusion.86.block_ref = f32[64,64]{1,0:T(8,128)} fusion(f32[64,3072]{1,0:T(8,128)S(1)} %all_gather.3), kind=kOutput, calls=%fused_computation.174 | convolution fusion | flops 150994944 | bytes 802816 | tf_op jit(solution)/shard_map/dot_general | solution.py:283
  64.1 21.7 %shard_map.51 = f32[64,64]{1,0:T(8,128)} custom-call(f32[64,64]{1,0:T(8,128)} %fusion.86.block_ref), custom_call_target="tpu_custom_call" | custom-call | tf_op jit(solution)/shard_map/pallas_call | solution.py:71
  85.8 6.6 %cholesky.17 = f32[64,64]{1,0:T(8,128)S(1)} custom-call(f32[64,64]{1,0:T(8,128)} %shard_map.51), custom_call_target="Cholesky" | custom-call | tf_op jit(solution)/shard_map/cholesky | solution.py:290
  93.1 0.7 fusion.58
  93.8 4.9 %custom-call.5 = f32[1,64,64]{1,2,0:T(8,128)S(1)} custom-call(f32[1,64,64]{2,1,0:T(8,128)S(1)} %get-tuple-element.61), custom_call_target="InvertDiagBlocksLowerTriangular" | custom-call | tf_op jit(solution)/shard_map/triangular_solve | solution.py:291
  99.4 0.7 copy.14
  100.1 0.7 copy.10
  (65 shorter events, 7.5 us)
Async XLA Ops:
  4.1 13.6 %copy-start.1 = (f32[2,24,8,256]{3,2,1,0:T(8,128)S(1)}, f32[2,24,8,256]{3,2,1,0:T(8,128)}, u32[]{:S(2)}) copy-start(f32[2,24,8,256]{3,2,1,0:T(8,128)} %param.4) | copy-start | bytes 1179652
  4.1 14.3 %copy-start.3 = (f32[24,8,256]{2,1,0:T(8,128)S(1)}, f32[24,8,256]{2,1,0:T(8,128)}, u32[]{:S(2)}) copy-start(f32[24,8,256]{2,1,0:T(8,128)} %w_ref.1) | copy-start | bytes 589828
  6.3 30.4 %collective-permute-start = (f32[19,4,8,256]{3,2,1,0:T(8,128)}, f32[19,4,8,256]{3,2,1,0:T(8,128)}, u32[]{:S(2)}, u32[]{:S(2)}) collective-permute-start(f32[19,4,8,256]{3,2,1,0:T(8,128)} %pad_maximum_fusion), channel_id=1, source_target_pairs={{0,4},{4,8},{8,12},{12,16},{16,20},{20,24},{24,28},{28,32},{32,36}... | collective-permute-start | bytes 1867784 | tf_op jit(solution)/shard_map/ppermute | solution.py:259
  9.5 30.7 %collective-permute-start.1 = (f32[19,4,8,256]{3,2,1,0:T(8,128)}, f32[19,4,8,256]{3,2,1,0:T(8,128)}, u32[]{:S(2)}, u32[]{:S(2)}) collective-permute-start(f32[19,4,8,256]{3,2,1,0:T(8,128)} %pad_maximum_fusion.1), channel_id=1, source_target_pairs={{4,0},{8,4},{12,8},{16,12},{20,16},{24,20},{28,24},{32,28},{36,32}... | collective-permute-start | bytes 1867784 | tf_op jit(solution)/shard_map/ppermute | solution.py:260
  19.0 1.0 copy-start.2
  20.0 16.5 %copy-start = (f32[16,24,8,256]{3,2,1,0:T(8,128)S(1)}, f32[16,24,8,256]{3,2,1,0:T(8,128)}, u32[]{:S(2)}) copy-start(f32[16,24,8,256]{3,2,1,0:T(8,128)} %q_ref.1) | copy-start | bytes 9437188
  36.6 1.0 copy-start.9
  36.6 4.4 %copy-start.8 = (f32[1,8,8,256]{3,2,1,0:T(8,128)S(1)}, f32[1,8,8,256]{3,2,1,0:T(8,128)}, u32[]{:S(2)}) copy-start(f32[1,8,8,256]{3,2,1,0:T(8,128)} %get-tuple-element.46) | copy-start | bytes 196612
  36.6 4.5 %copy-start.7 = (f32[1,8,8,256]{3,2,1,0:T(8,128)S(1)}, f32[1,8,8,256]{3,2,1,0:T(8,128)}, u32[]{:S(2)}) copy-start(f32[1,8,8,256]{3,2,1,0:T(8,128)} %get-tuple-element.30) | copy-start | bytes 196612
  36.6 4.5 %copy-start.6 = (f32[1,8,8,256]{3,2,1,0:T(8,128)S(1)}, f32[1,8,8,256]{3,2,1,0:T(8,128)}, u32[]{:S(2)}) copy-start(f32[1,8,8,256]{3,2,1,0:T(8,128)} %get-tuple-element.31) | copy-start | bytes 196612
  48.8 0.8 copy-start.5
  48.9 0.9 copy-start.4

commit v17 on v16

--- a/solution.py
+++ b/solution.py
@@ -292,10 +292,14 @@
     own_rows = lax.dynamic_slice_in_dim(
         inverse, lax.axis_index("probe") * probe_count, probe_count, 0
     )
-    basis = jnp.dot(
-        own_rows, full_panel, precision=lax.Precision.HIGHEST, preferred_element_type=jnp.float32
-    )
-    return (basis.reshape(probe_count, lon_count // 4, -1), lower.T)
+    basis = lax.dot_general(
+        own_rows,
+        full_panel.reshape(all_probes, lon_count // 4, -1),
+        (((1,), (0,)), ((), ())),
+        precision=lax.Precision.HIGHEST,
+        preferred_element_type=jnp.float32,
+    )
+    return (basis, lower.T)
 
 
 def solution(mesh):

time: 102 us -> 102 us (level)
  no operation moved by 1% of the time
where the time goes in v17:
time: 102 us; the launch traced here: 101 us
  Pallas kernels  36.6 us (36%)
  other arithmetic  24.3 us (24%)
  local copies, waits for them, and re-layouts  12.8 us (13%)
  starting transfers between devices  9.79 us (10%)
  blocking collectives  8.63 us (8%)
  matrix products  4.93 us (5%)
  waiting for transfers between devices  2.59 us (3%)
  between operations  1.08 us (1%)
    pallas_call x1, Pallas kernels, butterfly_sum(): pl.pallas_call(functools.partial(exchange_kernel, count, radix), out_shap...  21.7 us
    pallas_call x1, Pallas kernels, stencil_sums(): pl.pallas_call(stencil_kernel, out_shape=jax.ShapeDtypeStruct((probe_coun...  14.9 us
    all_gather x1, blocking collectives, body(): full_panel = lax.all_gather(coarse, 'probe', axis=0, tiled=True)  8.63 us
    ppermute x1, starting transfers between devices, body(): from_east = lax.ppermute(east_edge, 'lon', backward)  7.49 us
    another operation x3, other arithmetic, body(): lower = lax.linalg.cholesky(gram, symmetrize_input=False)  7.27 us
    another operation x1, other arithmetic, body(): lax.linalg.triangular_solve(lower, ident, left_side=True, lower=True)  4.9 us
    ppermute x1, waiting for transfers between devices, body(): from_east = lax.ppermute(east_edge, 'lon', backward)  2.59 us
    ppermute x1, starting transfers between devices, body(): from_west = lax.ppermute(west_edge, 'lon', forward)  2.3 us
  transfers between devices with their start and end apart: 2, of which 1 were waited for; matrix products, arithmetic and copies ran while one was open for 6% of the time, Pallas kernels for 15%

profile of v17, /device:TPU:8, one launch (start us, length us, event | category | flops | bytes accessed | tf_op | source)
XLA Modules:
  0.0 100.8 jit_solution(1042550931468734483)
XLA Ops:
  0.6 1.8 %slice_maximum_fusion = (f32[1,24,8,256]{3,2,1,0:T(8,128)S(1)}, f32[24,8,256]{2,1,0:T(8,128)}, f32[24,8,256]{2,1,0:T(8,128)}, f32[1,24,8,256]{3,2,1,0:T(8,128)S(1)}) fusion(f32[2,24,8,256]{3,2,1,0:T(8,128)} %param.4, pred[256]{0:T(512)(128)(4,1)S(1)} %iota_compare_fusion.8), kind=kLoop, calls=%fused_computation.75 | loop fusion | flops 147456 | bytes 1179904 | tf_op jit(solution)/shard_map/max | solution.py:214
  2.5 0.8 fusion.84
  3.3 0.8 fusion.88
  4.1 1.4 %fusion.78 = (f32[16,4,8,256]{3,2,1,0:T(8,128)S(1)}, f32[16,4,8,256]{3,2,1,0:T(8,128)S(1)}) fusion(f32[16,24,8,256]{3,2,1,0:T(8,128)} %q_ref.1), kind=kLoop, calls=%fused_computation.165 | loop fusion | bytes 2097152 | tf_op jit(solution)/shard_map/slice | solution.py:276
  5.4 0.9 pad_maximum_fusion
  6.3 2.3 %collective-permute-start = (f32[19,4,8,256]{3,2,1,0:T(8,128)}, f32[19,4,8,256]{3,2,1,0:T(8,128)}, u32[]{:S(2)}, u32[]{:S(2)}) collective-permute-start(f32[19,4,8,256]{3,2,1,0:T(8,128)} %pad_maximum_fusion), channel_id=1, source_target_pairs={{0,4},{4,8},{8,12},{12,16},{16,20},{20,24},{24,28},{28,32},{32,36}... | collective-permute-start | bytes 1867784 | tf_op jit(solution)/shard_map/ppermute | solution.py:259
  8.6 0.9 pad_maximum_fusion.1
  9.5 7.5 %collective-permute-start.1 = (f32[19,4,8,256]{3,2,1,0:T(8,128)}, f32[19,4,8,256]{3,2,1,0:T(8,128)}, u32[]{:S(2)}, u32[]{:S(2)}) collective-permute-start(f32[19,4,8,256]{3,2,1,0:T(8,128)} %pad_maximum_fusion.1), channel_id=1, source_target_pairs={{4,0},{8,4},{12,8},{16,12},{20,16},{24,20},{28,24},{32,28},{36,32}... | collective-permute-start | bytes 1867784 | tf_op jit(solution)/shard_map/ppermute | solution.py:260
  17.0 0.7 fusion.86
  17.7 0.7 fusion.83
  18.3 0.7 fusion.85
  19.2 0.8 subtract_add_fusion
  20.0 14.9 %shard_map.50 = f32[16,4,8,256]{3,2,1,0:T(8,128)} custom-call(f32[16,24,8,256]{3,2,1,0:T(8,128)} %q_ref.1, f32[24,8,256]{2,1,0:T(8,128)} %get-tuple-element.27.a_ref, f32[24,8,256]{2,1,0:T(8,128)} %get-tuple-element.28.b_ref, f32[24,8,256]{2,1,0:T(8,128)} %copy-done.2, f32[24,8,256]{2,1,0:T(8,128)} %get-tuple-element.9.d_ref, f32[24,8,256]{2,1,0:T(8,128)} %w_ref.1, ...), custom_call_target="tpu_custom_call" | custom-call | flops 39321600 | bytes 4521984 | tf_op jit(solution)/shard_map/pallas_call | solution.py:224
  34.9 1.6 %fusion.40 = f32[16,4,8,64]{3,2,1,0:T(8,128)S(1)} fusion(f32[16,4,8,256]{3,2,1,0:T(8,128)} %shard_map.50, s32[256]{0:T(256)S(1)} %get-tuple-element.64, s32[256]{0:T(256)S(1)} %get-tuple-element.65, pred[256]{0:T(512)(128)(4,1)S(1)} %compare_and_fusion), kind=kOutput, calls=%fused_computation.111 | convolution fusion | flops 100712448 | bytes 657664 | tf_op jit(solution)/shard_map/dot_general | solution.py:241
  36.8 0.8 fusion.81
  37.6 2.6 %collective-permute-done.1 = f32[19,4,8,256]{3,2,1,0:T(8,128)} collective-permute-done((f32[19,4,8,256]{3,2,1,0:T(8,128)}, f32[19,4,8,256]{3,2,1,0:T(8,128)}, u32[]{:S(2)}, u32[]{:S(2)}) %collective-permute-start.1) | collective-permute-done | bytes 622624 | tf_op jit(solution)/shard_map/ppermute | solution.py:260
  40.2 0.8 fusion.82
  41.3 1.1 %slice.331 = f32[16,4,8,256]{3,2,1,0:T(8,128)S(1)} slice(f32[19,4,8,256]{3,2,1,0:T(8,128)} %collective-permute-done.1), slice={[0:16], [0:4], [0:8], [0:256]} | slice | bytes 1048576 | tf_op jit(solution)/shard_map/slice | solution.py:271
  42.5 1.1 %slice.330 = f32[16,4,8,256]{3,2,1,0:T(8,128)S(1)} slice(f32[19,4,8,256]{3,2,1,0:T(8,128)} %collective-permute-done), slice={[0:16], [0:4], [0:8], [0:256]} | slice | bytes 1048576 | tf_op jit(solution)/shard_map/slice | solution.py:270
  43.7 0.9 fusion.7
  44.6 0.7 slice.352
  45.7 1.6 %fusion.9 = f32[2,16,10,8,256]{4,3,2,1,0:T(8,128)S(1)} fusion(f32[2,16,11,8,256]{4,3,2,1,0:T(8,128)S(1)} %fusion.2, f32[2,16,10,8,255]{4,3,2,1,0:T(8,128)S(1)} %slice.352, f32[1,16,12,8,256]{4,3,2,1,0:T(8,128)S(1)} %maximum_bitcast_fusion.1, f32[1,16,12,8,256]{4,3,2,1,0:T(8,128)S(1)} %maximum_bitcast_fusion, f32[2,10,8,256]{3,2,1,0:T(8,128)S(1)} %get-tuple-element.44, ...), kind=kLoop, calls=%fused_computation.18 | loop fusion | flops 8519680 | bytes 13948928 | tf_op jit(solution)/shard_map/sub | solution.py:127
  49.7 0.7 fusion.13
  51.2 0.9 fusion.16
  54.1 8.6 %all_gather.3 = f32[64,3072]{1,0:T(8,128)S(1)} all-gather(f32[16,3072]{1,0:T(8,128)S(1)} %reshape.119), channel_id=1, replica_groups=mesh['lon'=64,'probe'=4] {'probe'}, dimensions={0}, use_global_device_ids=true | all-gather | bytes 983040 | tf_op jit(solution)/shard_map/all_gather | solution.py:282
  62.7 1.4 %fusion.89.block_ref = f32[64,64]{1,0:T(8,128)} fusion(f32[64,3072]{1,0:T(8,128)S(1)} %all_gather.3), kind=kOutput, calls=%fused_computation.176 | convolution fusion | flops 150994944 | bytes 802816 | tf_op jit(solution)/shard_map/dot_general | solution.py:283
  64.1 21.7 %shard_map.51 = f32[64,64]{1,0:T(8,128)} custom-call(f32[64,64]{1,0:T(8,128)} %fusion.89.block_ref), custom_call_target="tpu_custom_call" | custom-call | tf_op jit(solution)/shard_map/pallas_call | solution.py:71
  85.8 6.6 %cholesky.17 = f32[64,64]{1,0:T(8,128)S(1)} custom-call(f32[64,64]{1,0:T(8,128)} %shard_map.51), custom_call_target="Cholesky" | custom-call | tf_op jit(solution)/shard_map/cholesky | solution.py:290
  93.1 0.7 fusion.61
  93.8 4.9 %custom-call.5 = f32[1,64,64]{1,2,0:T(8,128)S(1)} custom-call(f32[1,64,64]{2,1,0:T(8,128)S(1)} %get-tuple-element.61), custom_call_target="InvertDiagBlocksLowerTriangular" | custom-call | tf_op jit(solution)/shard_map/triangular_solve | solution.py:291
  98.9 0.7 copy.9
  99.6 1.2 %fusion.22 = f32[16,6,512]{2,0,1:T(8,128)} fusion(f32[8,6,8,512]{3,2,1,0:T(8,128)S(1)} %bitcast.118, f32[64,64]{1,0:T(8,128)S(1)} %fusion.44, s32[]{:T(128)S(6)} %select_n.39), kind=kOutput, calls=%fused_computation.45 | convolution fusion | flops 37748736 | bytes 991236 | tf_op jit(solution)/shard_map/dot_general | solution.py:295
  (64 shorter events, 7.0 us)
Async XLA Ops:
  4.1 13.6 %copy-start.1 = (f32[2,24,8,256]{3,2,1,0:T(8,128)S(1)}, f32[2,24,8,256]{3,2,1,0:T(8,128)}, u32[]{:S(2)}) copy-start(f32[2,24,8,256]{3,2,1,0:T(8,128)} %param.4) | copy-start | bytes 1179652
  4.1 14.3 %copy-start.3 = (f32[24,8,256]{2,1,0:T(8,128)S(1)}, f32[24,8,256]{2,1,0:T(8,128)}, u32[]{:S(2)}) copy-start(f32[24,8,256]{2,1,0:T(8,128)} %w_ref.1) | copy-start | bytes 589828
  6.3 30.4 %collective-permute-start = (f32[19,4,8,256]{3,2,1,0:T(8,128)}, f32[19,4,8,256]{3,2,1,0:T(8,128)}, u32[]{:S(2)}, u32[]{:S(2)}) collective-permute-start(f32[19,4,8,256]{3,2,1,0:T(8,128)} %pad_maximum_fusion), channel_id=1, source_target_pairs={{0,4},{4,8},{8,12},{12,16},{16,20},{20,24},{24,28},{28,32},{32,36}... | collective-permute-start | bytes 1867784 | tf_op jit(solution)/shard_map/ppermute | solution.py:259
  9.5 30.7 %collective-permute-start.1 = (f32[19,4,8,256]{3,2,1,0:T(8,128)}, f32[19,4,8,256]{3,2,1,0:T(8,128)}, u32[]{:S(2)}, u32[]{:S(2)}) collective-permute-start(f32[19,4,8,256]{3,2,1,0:T(8,128)} %pad_maximum_fusion.1), channel_id=1, source_target_pairs={{4,0},{8,4},{12,8},{16,12},{20,16},{24,20},{28,24},{32,28},{36,32}... | collective-permute-start | bytes 1867784 | tf_op jit(solution)/shard_map/ppermute | solution.py:260
  19.0 1.0 copy-start.2
  20.0 16.5 %copy-start = (f32[16,24,8,256]{3,2,1,0:T(8,128)S(1)}, f32[16,24,8,256]{3,2,1,0:T(8,128)}, u32[]{:S(2)}) copy-start(f32[16,24,8,256]{3,2,1,0:T(8,128)} %q_ref.1) | copy-start | bytes 9437188
  36.6 1.0 copy-start.9
  36.6 4.4 %copy-start.8 = (f32[1,8,8,256]{3,2,1,0:T(8,128)S(1)}, f32[1,8,8,256]{3,2,1,0:T(8,128)}, u32[]{:S(2)}) copy-start(f32[1,8,8,256]{3,2,1,0:T(8,128)} %get-tuple-element.46) | copy-start | bytes 196612
  36.6 4.5 %copy-start.7 = (f32[1,8,8,256]{3,2,1,0:T(8,128)S(1)}, f32[1,8,8,256]{3,2,1,0:T(8,128)}, u32[]{:S(2)}) copy-start(f32[1,8,8,256]{3,2,1,0:T(8,128)} %get-tuple-element.30) | copy-start | bytes 196612
  36.6 4.5 %copy-start.6 = (f32[1,8,8,256]{3,2,1,0:T(8,128)S(1)}, f32[1,8,8,256]{3,2,1,0:T(8,128)}, u32[]{:S(2)}) copy-start(f32[1,8,8,256]{3,2,1,0:T(8,128)} %get-tuple-element.31) | copy-start | bytes 196612
  48.8 0.8 copy-start.5
  48.9 0.9 copy-start.4

commit v18 on v16

--- a/solution.py
+++ b/solution.py
@@ -254,12 +254,29 @@
     count = lax.axis_size("lon")
     forward = [(i, (i + 1) % count) for i in range(count)]
     backward = [((i + 1) % count, i) for i in range(count)]
-    west_edge = jnp.concatenate([part[:, lon_count - halo:] for part in pack], axis=0)
-    east_edge = jnp.concatenate([part[:, :halo] for part in pack], axis=0)
+    west_width = (halo, halo - 1, halo - 1, halo - 2)
+    east_width = (halo, halo, halo - 1, halo - 2)
+    west_edge = jnp.concatenate(
+        [part[:, lon_count - width:].reshape((-1,) + part.shape[2:])
+         for part, width in zip(pack, west_width)], axis=0)
+    east_edge = jnp.concatenate(
+        [part[:, :width].reshape((-1,) + part.shape[2:])
+         for part, width in zip(pack, east_width)], axis=0)
     from_west = lax.ppermute(west_edge, "lon", forward)
     from_east = lax.ppermute(east_edge, "lon", backward)
-    bounds = ((0, probe_count), (probe_count, probe_count + 1),
-              (probe_count + 1, probe_count + 2), (probe_count + 2, probe_count + 3))
+
+    def unpack(flat, widths, west_side):
+        parts, row = [], 0
+        for part, width in zip(pack, widths):
+            rows = part.shape[0] * width
+            piece = flat[row:row + rows].reshape((part.shape[0], width) + part.shape[2:])
+            fill = jnp.zeros((part.shape[0], halo - width) + part.shape[2:], part.dtype)
+            parts.append(jnp.concatenate([fill, piece] if west_side else [piece, fill], axis=1))
+            row += rows
+        return parts
+
+    west_parts = unpack(from_west, west_width, True)
+    east_parts = unpack(from_east, east_width, False)
 
     def fields(parts):
         return parts[0], parts[1][0], parts[2][0], parts[3][0]
@@ -267,10 +284,10 @@
     inner = lat_average(stencil_sums(*fields(pack)))
     sides = [
         jnp.stack([
-            jnp.concatenate([from_west[lo:hi], part[:, :2 * halo]], axis=1),
-            jnp.concatenate([part[:, lon_count - 2 * halo:], from_east[lo:hi]], axis=1),
+            jnp.concatenate([west_part, part[:, :2 * halo]], axis=1),
+            jnp.concatenate([part[:, lon_count - 2 * halo:], east_part], axis=1),
         ])
-        for part, (lo, hi) in zip(pack, bounds)
+        for part, west_part, east_part in zip(pack, west_parts, east_parts)
     ]
     rim = four_steps(sides[0], sides[1], sides[2], sides[3])
     west = coarsen(increments[:, :halo] + rim[0])

time: 102 us -> 102 us (level)
  waiting for transfers between devices: 2.59 us -> 0.08 us
  Pallas kernels: 36.6 us -> 38.5 us
    reshape x0 -> x9, local copies, waits for them, and re-layouts: none -> 5.24 us  [the longest x5 3.7 us: unpack(): flat[row:row + rows].reshape((part.shape[0], width) + part.shape[2:])]
    slice x6 -> x2, local copies, waits for them, and re-layouts: 5.32 us -> 2.18 us  [unpack(): flat[row:row + rows].reshape((part.shape[0], width) + part.shape[2:])]
    ppermute x1, waiting for transfers between devices: 2.59 us -> 0.08 us  [body(): from_east = lax.ppermute(east_edge, 'lon', backward)]
    pallas_call x1, Pallas kernels: 21.7 us -> 23.6 us  [butterfly_sum(): pl.pallas_call(functools.partial(exchange_kernel, count, radix), out_shap...]
  transfers between devices with their start and end apart: 2 -> 2, of which waited for: 1 -> 1; matrix products, arithmetic and copies ran while one was open for 6% -> 8% of each run, Pallas kernels for 15% -> 15%
where the time goes in v18:
time: 102 us; the launch traced here: 101 us
  Pallas kernels  38.5 us (38%)
  other arithmetic  24.4 us (24%)
  local copies, waits for them, and re-layouts  14.4 us (14%)
  starting transfers between devices  9.79 us (10%)
  blocking collectives  8.63 us (8%)
  matrix products  4.25 us (4%)
  between operations  1.04 us (1%)
    pallas_call x1, Pallas kernels, butterfly_sum(): pl.pallas_call(functools.partial(exchange_kernel, count, radix), out_shap...  23.6 us
    pallas_call x1, Pallas kernels, stencil_sums(): pl.pallas_call(stencil_kernel, out_shape=jax.ShapeDtypeStruct((probe_coun...  14.9 us
    all_gather x1, blocking collectives, body(): full_panel = lax.all_gather(coarse, 'probe', axis=0, tiled=True)  8.63 us
    ppermute x1, starting transfers between devices, body(): from_east = lax.ppermute(east_edge, 'lon', backward)  7.49 us
    another operation x3, other arithmetic, body(): lower = lax.linalg.cholesky(gram, symmetrize_input=False)  7.27 us
    another operation x1, other arithmetic, body(): lax.linalg.triangular_solve(lower, ident, left_side=True, lower=True)  4.89 us
    reshape x5, local copies, waits for them, and re-layouts, unpack(): flat[row:row + rows].reshape((part.shape[0], width) + part.shape[2:])  3.7 us
    ppermute x1, starting transfers between devices, body(): from_west = lax.ppermute(west_edge, 'lon', forward)  2.3 us
  transfers between devices with their start and end apart: 2, of which 1 were waited for; matrix products, arithmetic and copies ran while one was open for 8% of the time, Pallas kernels for 15%

profile of v18, /device:TPU:8, one launch (start us, length us, event | category | flops | bytes accessed | tf_op | source)
XLA Modules:
  0.0 101.1 jit_solution(6048064765162983912)
XLA Ops:
  0.7 0.8 slice_bitcast_fusion.10
  1.4 0.7 slice_bitcast_fusion.12
  2.2 1.8 %slice_maximum_fusion = (f32[1,24,8,256]{3,2,1,0:T(8,128)S(1)}, f32[24,8,256]{2,1,0:T(8,128)}, f32[24,8,256]{2,1,0:T(8,128)}, f32[1,24,8,256]{3,2,1,0:T(8,128)S(1)}) fusion(f32[2,24,8,256]{3,2,1,0:T(8,128)} %param.4, pred[256]{0:T(512)(128)(4,1)S(1)} %iota_compare_fusion.8), kind=kLoop, calls=%fused_computation.73 | loop fusion | flops 147456 | bytes 1179904 | tf_op jit(solution)/shard_map/max | solution.py:214
  4.0 1.3 %fusion.79 = (f32[16,4,8,256]{3,2,1,0:T(8,128)S(1)}, f32[16,4,8,256]{3,2,1,0:T(8,128)S(1)}) fusion(f32[16,24,8,256]{3,2,1,0:T(8,128)} %q_ref.1), kind=kLoop, calls=%fused_computation.179 | loop fusion | bytes 2097152 | tf_op jit(solution)/shard_map/slice | solution.py:293
  5.4 0.9 pad_maximum_fusion.1
  6.2 2.3 %collective-permute-start = (f32[72,8,256]{2,1,0:T(8,128)}, f32[72,8,256]{2,1,0:T(8,128)}, u32[]{:S(2)}, u32[]{:S(2)}) collective-permute-start(f32[72,8,256]{2,1,0:T(8,128)} %pad_maximum_fusion.1), channel_id=1, source_target_pairs={{0,4},{4,8},{8,12},{12,16},{16,20},{20,24},{24,28},{28,32},{32,36}... | collective-permute-start | bytes 1769480 | tf_op jit(solution)/shard_map/ppermute | solution.py:265
  8.5 0.9 pad_maximum_fusion
  9.4 7.5 %collective-permute-start.1 = (f32[73,8,256]{2,1,0:T(8,128)}, f32[73,8,256]{2,1,0:T(8,128)}, u32[]{:S(2)}, u32[]{:S(2)}) collective-permute-start(f32[73,8,256]{2,1,0:T(8,128)} %pad_maximum_fusion), channel_id=1, source_target_pairs={{4,0},{8,4},{12,8},{16,12},{20,16},{24,20},{28,24},{32,28},{36,32}... | collective-permute-start | bytes 1794056 | tf_op jit(solution)/shard_map/ppermute | solution.py:266
  17.6 0.7 fusion.84
  18.4 0.9 subtract_add_fusion
  19.3 14.9 %shard_map.50 = f32[16,4,8,256]{3,2,1,0:T(8,128)} custom-call(f32[16,24,8,256]{3,2,1,0:T(8,128)} %q_ref.1, f32[24,8,256]{2,1,0:T(8,128)} %get-tuple-element.23.a_ref, f32[24,8,256]{2,1,0:T(8,128)} %get-tuple-element.24.b_ref, f32[24,8,256]{2,1,0:T(8,128)} %copy-done.2, f32[24,8,256]{2,1,0:T(8,128)} %get-tuple-element.9.d_ref, f32[24,8,256]{2,1,0:T(8,128)} %w_ref.1, ...), custom_call_target="tpu_custom_call" | custom-call | flops 39321600 | bytes 4521984 | tf_op jit(solution)/shard_map/pallas_call | solution.py:224
  34.2 1.6 %fusion.41 = f32[16,4,8,64]{3,2,1,0:T(8,128)S(1)} fusion(f32[16,4,8,256]{3,2,1,0:T(8,128)} %shard_map.50, s32[256]{0:T(256)S(1)} %get-tuple-element.62, s32[256]{0:T(256)S(1)} %get-tuple-element.63, pred[256]{0:T(512)(128)(4,1)S(1)} %compare_and_fusion), kind=kOutput, calls=%fused_computation.113 | convolution fusion | flops 100712448 | bytes 657664 | tf_op jit(solution)/shard_map/dot_general | solution.py:241
  36.0 1.1 %slice.330 = f32[64,8,256]{2,1,0:T(8,128)S(1)} slice(f32[72,8,256]{2,1,0:T(8,128)} %collective-permute-done), slice={[0:64], [0:8], [0:256]} | slice | bytes 1048576 | tf_op jit(solution)/shard_map/slice | solution.py:272
  37.3 0.7 slice_bitcast_fusion.13
  38.0 0.8 slice_bitcast_fusion.6
  38.8 0.7 slice_bitcast_fusion.5
  39.6 0.8 slice_bitcast_fusion.3
  40.8 1.1 %slice.331 = f32[64,8,256]{2,1,0:T(8,128)S(1)} slice(f32[73,8,256]{2,1,0:T(8,128)} %collective-permute-done.1), slice={[0:64], [0:8], [0:256]} | slice | bytes 1048576 | tf_op jit(solution)/shard_map/slice | solution.py:272
  42.0 0.8 fusion.7
  42.8 0.7 slice.352
  43.9 1.6 %fusion.9 = f32[2,16,10,8,256]{4,3,2,1,0:T(8,128)S(1)} fusion(f32[2,16,11,8,256]{4,3,2,1,0:T(8,128)S(1)} %fusion.2, f32[2,16,10,8,255]{4,3,2,1,0:T(8,128)S(1)} %slice.352, f32[1,16,12,8,256]{4,3,2,1,0:T(8,128)S(1)} %maximum_bitcast_fusion.1, f32[1,16,12,8,256]{4,3,2,1,0:T(8,128)S(1)} %maximum_bitcast_fusion, f32[2,10,8,256]{3,2,1,0:T(8,128)S(1)} %get-tuple-element.38, ...), kind=kLoop, calls=%fused_computation.18 | loop fusion | flops 8519680 | bytes 13948928 | tf_op jit(solution)/shard_map/sub | solution.py:127
  47.0 0.7 slice_bitcast_fusion.11
  48.1 0.7 fusion.13
  49.5 1.0 %fusion.16 = f32[2,16,6,8,256]{4,3,2,1,0:T(8,128)S(1)} fusion(f32[2,16,8,8,256]{4,3,2,1,0:T(8,128)S(1)} %fusion.13, f32[2,16,6,8,255]{4,3,2,1,0:T(8,128)S(1)} %get-tuple-element.17, f32[2,16,6,8,255]{4,3,2,1,0:T(8,128)S(1)} %get-tuple-element.16, f32[2,6,8,256]{3,2,1,0:T(8,128)S(1)} %get-tuple-element.52, f32[2,6,8,256]{3,2,1,0:T(8,128)S(1)} %get-tuple-element.10, ...), kind=kLoop, calls=%fused_computation.30 | loop fusion | flops 3538944 | bytes 9916416 | tf_op jit(solution)/shard_map/add | solution.py:141
  50.8 0.7 fusion.20
  52.5 8.6 %all_gather.3 = f32[64,3072]{1,0:T(8,128)S(1)} all-gather(f32[16,3072]{1,0:T(8,128)S(1)} %reshape.183), channel_id=1, replica_groups=mesh['lon'=64,'probe'=4] {'probe'}, dimensions={0}, use_global_device_ids=true | all-gather | bytes 983040 | tf_op jit(solution)/shard_map/all_gather | solution.py:299
  61.1 1.4 %fusion.85.block_ref = f32[64,64]{1,0:T(8,128)} fusion(f32[64,3072]{1,0:T(8,128)S(1)} %all_gather.3), kind=kOutput, calls=%fused_computation.185 | convolution fusion | flops 150994944 | bytes 802816 | tf_op jit(solution)/shard_map/dot_general | solution.py:300
  62.5 23.6 %shard_map.51 = f32[64,64]{1,0:T(8,128)} custom-call(f32[64,64]{1,0:T(8,128)} %fusion.85.block_ref), custom_call_target="tpu_custom_call" | custom-call | tf_op jit(solution)/shard_map/pallas_call | solution.py:71
  86.1 6.6 %cholesky.17 = f32[64,64]{1,0:T(8,128)S(1)} custom-call(f32[64,64]{1,0:T(8,128)} %shard_map.51), custom_call_target="Cholesky" | custom-call | tf_op jit(solution)/shard_map/cholesky | solution.py:307
  94.0 0.7 copy.10
  94.7 4.9 %custom-call.5 = f32[1,64,64]{1,2,0:T(8,128)S(1)} custom-call(f32[1,64,64]{2,1,0:T(8,128)S(1)} %get-tuple-element.55), custom_call_target="InvertDiagBlocksLowerTriangular" | custom-call | tf_op jit(solution)/shard_map/triangular_solve | solution.py:308
  100.4 0.7 copy.14
  (62 shorter events, 7.7 us)
Async XLA Ops:
  0.6 7.9 %copy-start.1 = (f32[2,24,8,256]{3,2,1,0:T(8,128)S(1)}, f32[2,24,8,256]{3,2,1,0:T(8,128)}, u32[]{:S(2)}) copy-start(f32[2,24,8,256]{3,2,1,0:T(8,128)} %param.4) | copy-start | bytes 1179652
  4.0 12.9 %copy-start.3 = (f32[24,8,256]{2,1,0:T(8,128)S(1)}, f32[24,8,256]{2,1,0:T(8,128)}, u32[]{:S(2)}) copy-start(f32[24,8,256]{2,1,0:T(8,128)} %w_ref.1) | copy-start | bytes 589828
  6.2 29.8 %collective-permute-start = (f32[72,8,256]{2,1,0:T(8,128)}, f32[72,8,256]{2,1,0:T(8,128)}, u32[]{:S(2)}, u32[]{:S(2)}) collective-permute-start(f32[72,8,256]{2,1,0:T(8,128)} %pad_maximum_fusion.1), channel_id=1, source_target_pairs={{0,4},{4,8},{8,12},{12,16},{16,20},{20,24},{24,28},{28,32},{32,36}... | collective-permute-start | bytes 1769480 | tf_op jit(solution)/shard_map/ppermute | solution.py:265
  9.4 29.4 %collective-permute-start.1 = (f32[73,8,256]{2,1,0:T(8,128)}, f32[73,8,256]{2,1,0:T(8,128)}, u32[]{:S(2)}, u32[]{:S(2)}) collective-permute-start(f32[73,8,256]{2,1,0:T(8,128)} %pad_maximum_fusion), channel_id=1, source_target_pairs={{4,0},{8,4},{12,8},{16,12},{20,16},{24,20},{28,24},{32,28},{36,32}... | collective-permute-start | bytes 1794056 | tf_op jit(solution)/shard_map/ppermute | solution.py:266
  17.6 1.7 %copy-start.2 = (f32[24,8,256]{2,1,0:T(8,128)}, f32[24,8,256]{2,1,0:T(8,128)S(1)}, u32[]{:S(2)}) copy-start(f32[24,8,256]{2,1,0:T(8,128)S(1)} %fusion.27.c_ref) | copy-start | bytes 589828
  19.3 16.5 %copy-start = (f32[16,24,8,256]{3,2,1,0:T(8,128)S(1)}, f32[16,24,8,256]{3,2,1,0:T(8,128)}, u32[]{:S(2)}) copy-start(f32[16,24,8,256]{3,2,1,0:T(8,128)} %q_ref.1) | copy-start | bytes 9437188
  36.0 4.3 %copy-start.4 = (f32[1,8,8,256]{3,2,1,0:T(8,128)S(1)}, f32[1,8,8,256]{3,2,1,0:T(8,128)}, u32[]{:S(2)}) copy-start(f32[1,8,8,256]{3,2,1,0:T(8,128)} %get-tuple-element.40) | copy-start | bytes 196612
  46.4 1.4 %copy-start.5 = (f32[1,8,8,256]{3,2,1,0:T(8,128)S(1)}, f32[1,8,8,256]{3,2,1,0:T(8,128)}, u32[]{:S(2)}) copy-start(f32[1,8,8,256]{3,2,1,0:T(8,128)} %get-tuple-element.33) | copy-start | bytes 196612
  46.4 1.3 %copy-start.6 = (f32[1,8,8,256]{3,2,1,0:T(8,128)S(1)}, f32[1,8,8,256]{3,2,1,0:T(8,128)}, u32[]{:S(2)}) copy-start(f32[1,8,8,256]{3,2,1,0:T(8,128)} %get-tuple-element.34) | copy-start | bytes 196612

commit v19 on v16

--- a/solution.py
+++ b/solution.py
@@ -209,26 +209,27 @@
 
 
 def stencil_sums(slab, east, north, weight):
-    probe_count, span, level_count, lat_count = slab.shape
+    rows, span, level_count, lat_count = slab.shape
+    per_run = rows // east.shape[0]
     groups = (span - 8) // 4
     east_a = jnp.maximum(east, 0.0)
     east_b = jnp.minimum(east, 0.0)
     north_c = jnp.maximum(north, 0.0)
     north_d = jnp.minimum(north, 0.0)
     north_up = above(north_c)
-    next_a = jnp.concatenate([east_a[1:], jnp.zeros_like(east_a[:1])], axis=0)
+    next_a = jnp.concatenate([east_a[:, 1:], jnp.zeros_like(east_a[:, :1])], axis=1)
     centre = 1.0 - next_a + east_b - north_up + north_d
     winds = (east_a, east_b, north_c, north_d, weight, north_up, centre)
-    full = pl.BlockSpec((span, level_count, lat_count), lambda i: (0, 0, 0))
-    elements = probe_count * span * level_count * lat_count
+    full = pl.BlockSpec((None, span, level_count, lat_count), lambda i: (i // per_run, 0, 0, 0))
+    elements = rows * span * level_count * lat_count
     return pl.pallas_call(
         stencil_kernel,
-        out_shape=jax.ShapeDtypeStruct((probe_count, groups, level_count, lat_count), slab.dtype),
-        grid=(probe_count,),
+        out_shape=jax.ShapeDtypeStruct((rows, groups, level_count, lat_count), slab.dtype),
+        grid=(rows,),
         in_specs=[pl.BlockSpec((1, span, level_count, lat_count), lambda i: (i, 0, 0, 0))] + [full] * 7,
         out_specs=pl.BlockSpec((1, groups, level_count, lat_count), lambda i: (i, 0, 0, 0)),
         cost_estimate=pl.CostEstimate(
-            flops=50 * elements, transcendentals=0, bytes_accessed=4 * elements + 28 * span * level_count * lat_count
+            flops=50 * elements, transcendentals=0, bytes_accessed=4 * elements + 28 * east.size
         ),
     )(slab, *winds)
 
@@ -264,7 +265,7 @@
     def fields(parts):
         return parts[0], parts[1][0], parts[2][0], parts[3][0]
 
-    inner = lat_average(stencil_sums(*fields(pack)))
+    inner = lat_average(stencil_sums(pack[0], pack[1], pack[2], pack[3]))
     sides = [
         jnp.stack([
             jnp.concatenate([from_west[lo:hi], part[:, :2 * halo]], axis=1),
@@ -272,9 +273,12 @@
         ])
         for part, (lo, hi) in zip(pack, bounds)
     ]
-    rim = four_steps(sides[0], sides[1], sides[2], sides[3])
-    west = coarsen(increments[:, :halo] + rim[0])
-    east = coarsen(increments[:, lon_count - halo:] + rim[1])
+    rim = stencil_sums(
+        sides[0].reshape((-1,) + sides[0].shape[2:]),
+        sides[1][:, 0], sides[2][:, 0], sides[3][:, 0],
+    )
+    rim = lat_average(rim)
+    west, east = rim[:probe_count], rim[probe_count:]
     coarse = jnp.concatenate([west, inner, east], axis=1)
     coarse = coarse.reshape(probe_count, -1)
     all_probes = probe_count * lax.axis_size("probe")

time: 102 us -> 124 us (1.22)
  the two profiles are of different devices: /device:TPU:8 before, /device:TPU:16 now
where the time goes in v19:
time: 124 us; the launch traced here: 122 us
  Pallas kernels  64.1 us (52%)
  other arithmetic  22.5 us (18%)
  local copies, waits for them, and re-layouts  10.8 us (9%)
  blocking collectives  8.39 us (7%)
  waiting for transfers between devices  5.77 us (5%)
  matrix products  5.04 us (4%)
  starting transfers between devices  4.43 us (4%)
    pallas_call x2, Pallas kernels, stencil_sums(): pl.pallas_call(stencil_kernel, out_shape=jax.ShapeDtypeStruct((rows, grou...  39.1 us
    pallas_call x1, Pallas kernels, butterfly_sum(): pl.pallas_call(functools.partial(exchange_kernel, count, radix), out_shap...  25 us
    all_gather x1, blocking collectives, body(): full_panel = lax.all_gather(coarse, 'probe', axis=0, tiled=True)  8.39 us
    another operation x3, other arithmetic, body(): lower = lax.linalg.cholesky(gram, symmetrize_input=False)  7.27 us
    ppermute x1, waiting for transfers between devices, body(): from_west = lax.ppermute(west_edge, 'lon', forward)  5.76 us
    another operation x1, other arithmetic, body(): lax.linalg.triangular_solve(lower, ident, left_side=True, lower=True)  4.89 us
    dot_general x2, matrix products, lat_average(): jnp.dot(summed.reshape(-1, lat_count), average, precision=lax.Precision.H...  2.94 us
    slice x3, local copies, waits for them, and re-layouts, body(): part[:, lon_count - halo:]  2.93 us
  transfers between devices with their start and end apart: 2, of which 1 were waited for; matrix products, arithmetic and copies ran while one was open for 5% of the time, Pallas kernels for 12%

profile of v19, /device:TPU:16, one launch (start us, length us, event | category | flops | bytes accessed | tf_op | source)
XLA Modules:
  0.0 122.0 jit_solution(1559104046439892025)
XLA Ops:
  0.6 0.8 fusion.35
  1.4 1.7 %broadcast_minimum_fusion = (f32[1,24,8,256]{3,2,1,0:T(8,128)}, f32[1,24,8,256]{3,2,1,0:T(8,128)S(1)}, f32[1,24,8,256]{3,2,1,0:T(8,128)S(1)}) fusion(f32[2,24,8,256]{3,2,1,0:T(8,128)} %param.4, pred[256]{0:T(512)(128)(4,1)S(1)} %iota_compare_fusion.6), kind=kLoop, calls=%fused_computation.29 | loop fusion | flops 147456 | bytes 983296 | tf_op jit(solution)/shard_map/min | solution.py:218
  3.2 0.8 fusion.31
  4.0 1.3 %fusion.26 = (f32[16,4,8,256]{3,2,1,0:T(8,128)S(1)}, f32[16,4,8,256]{3,2,1,0:T(8,128)S(1)}) fusion(f32[16,24,8,256]{3,2,1,0:T(8,128)} %q_ref.1), kind=kLoop, calls=%fused_computation.67 | loop fusion | bytes 2097152 | tf_op jit(solution)/shard_map/slice | solution.py:258
  5.4 0.9 pad_maximum_fusion.2
  6.2 2.1 %collective-permute-start.1 = (f32[19,4,8,256]{3,2,1,0:T(8,128)}, f32[19,4,8,256]{3,2,1,0:T(8,128)}, u32[]{:S(2)}, u32[]{:S(2)}) collective-permute-start(f32[19,4,8,256]{3,2,1,0:T(8,128)} %pad_maximum_fusion.2), channel_id=1, source_target_pairs={{4,0},{8,4},{12,8},{16,12},{20,16},{24,20},{28,24},{32,28},{36,32}... | collective-permute-start | bytes 1867784 | tf_op jit(solution)/shard_map/ppermute | solution.py:261
  8.3 0.9 pad_maximum_fusion.1
  9.2 2.4 %collective-permute-start = (f32[19,4,8,256]{3,2,1,0:T(8,128)}, f32[19,4,8,256]{3,2,1,0:T(8,128)}, u32[]{:S(2)}, u32[]{:S(2)}) collective-permute-start(f32[19,4,8,256]{3,2,1,0:T(8,128)} %pad_maximum_fusion.1), channel_id=1, source_target_pairs={{0,4},{4,8},{8,12},{12,16},{16,20},{20,24},{24,28},{28,32},{32,36}... | collective-permute-start | bytes 1867784 | tf_op jit(solution)/shard_map/ppermute | solution.py:260
  12.2 0.7 fusion.30
  12.9 0.7 fusion.33
  13.7 0.8 subtract_add_fusion
  14.6 15.0 %shard_map.51 = f32[16,4,8,256]{3,2,1,0:T(8,128)} custom-call(f32[16,24,8,256]{3,2,1,0:T(8,128)} %q_ref.1, f32[1,24,8,256]{3,2,1,0:T(8,128)} %copy-done.3, f32[1,24,8,256]{3,2,1,0:T(8,128)} %get-tuple-element.19.b_ref, f32[1,24,8,256]{3,2,1,0:T(8,128)} %copy-done.2, f32[1,24,8,256]{3,2,1,0:T(8,128)} %get-tuple-element.6.d_ref, f32[1,24,8,256]{3,2,1,0:T(8,128)} %bitcast.75, ...), custom_call_target="tpu_custom_call" | custom-call | flops 39321600 | bytes 4521984 | tf_op jit(solution)/shard_map/pallas_call | solution.py:225
  29.6 1.6 %fusion.5 = f32[16,4,8,64]{3,2,1,0:T(8,128)S(1)} fusion(f32[16,4,8,256]{3,2,1,0:T(8,128)} %shard_map.51, s32[256]{0:T(256)S(1)} %get-tuple-element.44, s32[256]{0:T(256)S(1)} %get-tuple-element.45, pred[256]{0:T(512)(128)(4,1)S(1)} %compare_and_fusion), kind=kOutput, calls=%fused_computation.33 | convolution fusion | flops 100712448 | bytes 657664 | tf_op jit(solution)/shard_map/dot_general | solution.py:242
  31.4 0.8 fusion.29
  32.3 5.8 %collective-permute-done = f32[19,4,8,256]{3,2,1,0:T(8,128)} collective-permute-done((f32[19,4,8,256]{3,2,1,0:T(8,128)}, f32[19,4,8,256]{3,2,1,0:T(8,128)}, u32[]{:S(2)}, u32[]{:S(2)}) %collective-permute-start) | collective-permute-done | bytes 622624 | tf_op jit(solution)/shard_map/ppermute | solution.py:260
  38.1 0.8 fusion.28
  38.9 0.7 fusion.2.d_ref
  39.8 0.7 minimum_bitcast_fusion
  40.6 0.7 maximum_bitcast_fusion.2.w_ref
  41.3 0.8 subtract_add_fusion.1
  42.1 1.1 slice.150
  43.3 1.1 slice.153
  44.5 2.0 %pad_maximum_fusion = f32[2,16,12,8,256]{4,3,2,1,0:T(8,128)} fusion(f32[1,16,12,8,256]{4,3,2,1,0:T(8,128)S(1)} %maximum_bitcast_fusion.1, f32[1,16,12,8,256]{4,3,2,1,0:T(8,128)S(1)} %maximum_bitcast_fusion), kind=kLoop, calls=%fused_computation | loop fusion | flops 786432 | bytes 6291456 | tf_op jit(solution)/shard_map/stack | solution.py:270
  46.5 24.0 %shard_map.50 = f32[32,1,8,256]{3,2,1,0:T(8,128)} custom-call(f32[32,12,8,256]{3,2,1,0:T(8,128)} %bitcast.73, f32[2,12,8,256]{3,2,1,0:T(8,128)} %copy-done.4, f32[2,12,8,256]{3,2,1,0:T(8,128)} %get-tuple-element.32.b_ref, f32[2,12,8,256]{3,2,1,0:T(8,128)} %copy-done.1, f32[2,12,8,256]{3,2,1,0:T(8,128)} %fusion.2.d_ref, ...), custom_call_target="tpu_custom_call" | custom-call | flops 39321600 | bytes 4521984 | tf_op jit(solution)/shard_map/pallas_call | solution.py:225
  70.5 1.3 %fusion = f32[256,64]{0,1:T(8,128)S(1)} fusion(f32[32,1,8,256]{3,2,1,0:T(8,128)} %shard_map.50, s32[256]{0:T(256)S(1)} %get-tuple-element.44, s32[256]{0:T(256)S(1)} %get-tuple-element.45, pred[256]{0:T(512)(128)(4,1)S(1)} %compare_and_fusion), kind=kOutput, calls=%fused_computation.6 | convolution fusion | flops 50380800 | bytes 329984 | tf_op jit(solution)/shard_map/dot_general | solution.py:242
  72.3 8.4 %all_gather.3 = f32[64,3072]{1,0:T(8,128)S(1)} all-gather(f32[16,3072]{1,0:T(8,128)S(1)} %reshape.43), channel_id=1, replica_groups=mesh['lon'=64,'probe'=4] {'probe'}, dimensions={0}, use_global_device_ids=true | all-gather | bytes 983040 | tf_op jit(solution)/shard_map/all_gather | solution.py:286
  80.7 1.4 %fusion.37.block_ref = f32[64,64]{1,0:T(8,128)} fusion(f32[64,3072]{1,0:T(8,128)S(1)} %all_gather.3), kind=kOutput, calls=%fused_computation.78 | convolution fusion | flops 150994944 | bytes 802816 | tf_op jit(solution)/shard_map/dot_general | solution.py:287
  82.0 25.0 %shard_map.52 = f32[64,64]{1,0:T(8,128)} custom-call(f32[64,64]{1,0:T(8,128)} %fusion.37.block_ref), custom_call_target="tpu_custom_call" | custom-call | tf_op jit(solution)/shard_map/pallas_call | solution.py:71
  107.0 6.6 %cholesky.17 = f32[64,64]{1,0:T(8,128)S(1)} custom-call(f32[64,64]{1,0:T(8,128)} %shard_map.52), custom_call_target="Cholesky" | custom-call | tf_op jit(solution)/shard_map/cholesky | solution.py:294
  115.0 0.7 copy.18
  115.7 4.9 %custom-call.5 = f32[1,64,64]{1,2,0:T(8,128)S(1)} custom-call(f32[1,64,64]{2,1,0:T(8,128)S(1)} %get-tuple-element.41), custom_call_target="InvertDiagBlocksLowerTriangular" | custom-call | tf_op jit(solution)/shard_map/triangular_solve | solution.py:295
  121.3 0.7 copy.22
  (56 shorter events, 3.8 us)
Async XLA Ops:
  3.2 10.4 %copy-start.3 = (f32[1,24,8,256]{3,2,1,0:T(8,128)}, f32[1,24,8,256]{3,2,1,0:T(8,128)S(1)}, u32[]{:S(2)}) copy-start(f32[1,24,8,256]{3,2,1,0:T(8,128)S(1)} %get-tuple-element.20.a_ref) | copy-start | bytes 589828
  5.3 6.3 %copy-start.6 = (f32[24,8,256]{2,1,0:T(8,128)S(1)}, f32[24,8,256]{2,1,0:T(8,128)}, u32[]{:S(2)}) copy-start(f32[24,8,256]{2,1,0:T(8,128)} %param.5) | copy-start | bytes 589828
  5.3 6.9 %copy-start.5 = (f32[2,24,8,256]{3,2,1,0:T(8,128)S(1)}, f32[2,24,8,256]{3,2,1,0:T(8,128)}, u32[]{:S(2)}) copy-start(f32[2,24,8,256]{3,2,1,0:T(8,128)} %param.4) | copy-start | bytes 1179652
  6.2 25.2 %collective-permute-start.1 = (f32[19,4,8,256]{3,2,1,0:T(8,128)}, f32[19,4,8,256]{3,2,1,0:T(8,128)}, u32[]{:S(2)}, u32[]{:S(2)}) collective-permute-start(f32[19,4,8,256]{3,2,1,0:T(8,128)} %pad_maximum_fusion.2), channel_id=1, source_target_pairs={{4,0},{8,4},{12,8},{16,12},{20,16},{24,20},{28,24},{32,28},{36,32}... | collective-permute-start | bytes 1867784 | tf_op jit(solution)/shard_map/ppermute | solution.py:261
  9.2 28.8 %collective-permute-start = (f32[19,4,8,256]{3,2,1,0:T(8,128)}, f32[19,4,8,256]{3,2,1,0:T(8,128)}, u32[]{:S(2)}, u32[]{:S(2)}) collective-permute-start(f32[19,4,8,256]{3,2,1,0:T(8,128)} %pad_maximum_fusion.1), channel_id=1, source_target_pairs={{0,4},{4,8},{8,12},{12,16},{16,20},{20,24},{24,28},{28,32},{32,36}... | collective-permute-start | bytes 1867784 | tf_op jit(solution)/shard_map/ppermute | solution.py:260
  13.6 1.0 copy-start.2
  14.6 16.7 %copy-start = (f32[16,24,8,256]{3,2,1,0:T(8,128)S(1)}, f32[16,24,8,256]{3,2,1,0:T(8,128)}, u32[]{:S(2)}) copy-start(f32[16,24,8,256]{3,2,1,0:T(8,128)} %q_ref.1) | copy-start | bytes 9437188
  31.2 1.0 copy-start.12
  31.3 7.6 %copy-start.11 = (f32[1,8,8,256]{3,2,1,0:T(8,128)S(1)}, f32[1,8,8,256]{3,2,1,0:T(8,128)}, u32[]{:S(2)}) copy-start(f32[1,8,8,256]{3,2,1,0:T(8,128)} %get-tuple-element.30) | copy-start | bytes 196612
  31.4 8.4 %copy-start.10 = (f32[1,8,8,256]{3,2,1,0:T(8,128)S(1)}, f32[1,8,8,256]{3,2,1,0:T(8,128)}, u32[]{:S(2)}) copy-start(f32[1,8,8,256]{3,2,1,0:T(8,128)} %get-tuple-element.22) | copy-start | bytes 196612
  31.4 8.4 %copy-start.9 = (f32[1,8,8,256]{3,2,1,0:T(8,128)S(1)}, f32[1,8,8,256]{3,2,1,0:T(8,128)}, u32[]{:S(2)}) copy-start(f32[1,8,8,256]{3,2,1,0:T(8,128)} %get-tuple-element.21) | copy-start | bytes 196612
  32.3 8.3 %copy-start.8 = (f32[1,8,8,256]{3,2,1,0:T(8,128)S(1)}, f32[1,8,8,256]{3,2,1,0:T(8,128)}, u32[]{:S(2)}) copy-start(f32[1,8,8,256]{3,2,1,0:T(8,128)} %get-tuple-element.29) | copy-start | bytes 196612
  32.3 8.3 %copy-start.7 = (f32[1,8,8,256]{3,2,1,0:T(8,128)S(1)}, f32[1,8,8,256]{3,2,1,0:T(8,128)}, u32[]{:S(2)}) copy-start(f32[1,8,8,256]{3,2,1,0:T(8,128)} %get-tuple-element.28) | copy-start | bytes 196612
  38.9 3.2 %copy-start.1 = (f32[2,12,8,256]{3,2,1,0:T(8,128)}, f32[2,12,8,256]{3,2,1,0:T(8,128)S(1)}, u32[]{:S(2)}) copy-start(f32[2,12,8,256]{3,2,1,0:T(8,128)S(1)} %fusion.3.c_ref) | copy-start | bytes 589828
  40.6 2.7 %copy-start.4 = (f32[2,12,8,256]{3,2,1,0:T(8,128)}, f32[2,12,8,256]{3,2,1,0:T(8,128)S(1)}, u32[]{:S(2)}) copy-start(f32[2,12,8,256]{3,2,1,0:T(8,128)S(1)} %get-tuple-element.33.a_ref) | copy-start | bytes 589828

commit v20 on v19

--- a/solution.py
+++ b/solution.py
@@ -172,9 +172,14 @@
 
 
 def stencil_kernel(q_ref, a_ref, b_ref, c_ref, d_ref, w_ref, n_ref, k_ref, o_ref):
+    for row in range(q_ref.shape[0]):
+        stencil_row(row, q_ref, a_ref, b_ref, c_ref, d_ref, w_ref, n_ref, k_ref, o_ref)
+
+
+def stencil_row(row, q_ref, a_ref, b_ref, c_ref, d_ref, w_ref, n_ref, k_ref, o_ref):
     span = q_ref.shape[1]
     lat = q_ref.shape[-1]
-    field = q_ref[0]
+    field = q_ref[row]
     state = field
     for step in range(2):
         lo, hi = step, span - step
@@ -205,7 +210,7 @@
     sketch = field[4:span - 4] + state
     groups = sketch.shape[0] // 4
     for g in range(groups):
-        o_ref[0, g] = ((sketch[4 * g] + sketch[4 * g + 1]) + sketch[4 * g + 2]) + sketch[4 * g + 3]
+        o_ref[row, g] = ((sketch[4 * g] + sketch[4 * g + 1]) + sketch[4 * g + 2]) + sketch[4 * g + 3]
 
 
 def stencil_sums(slab, east, north, weight):
@@ -220,14 +225,18 @@
     next_a = jnp.concatenate([east_a[:, 1:], jnp.zeros_like(east_a[:, :1])], axis=1)
     centre = 1.0 - next_a + east_b - north_up + north_d
     winds = (east_a, east_b, north_c, north_d, weight, north_up, centre)
-    full = pl.BlockSpec((None, span, level_count, lat_count), lambda i: (i // per_run, 0, 0, 0))
+    block = 4 if per_run % 4 == 0 else 1
+    full = pl.BlockSpec(
+        (None, span, level_count, lat_count), lambda i: (i * block // per_run, 0, 0, 0)
+    )
     elements = rows * span * level_count * lat_count
     return pl.pallas_call(
         stencil_kernel,
         out_shape=jax.ShapeDtypeStruct((rows, groups, level_count, lat_count), slab.dtype),
-        grid=(rows,),
-        in_specs=[pl.BlockSpec((1, span, level_count, lat_count), lambda i: (i, 0, 0, 0))] + [full] * 7,
-        out_specs=pl.BlockSpec((1, groups, level_count, lat_count), lambda i: (i, 0, 0, 0)),
+        grid=(rows // block,),
+        in_specs=[pl.BlockSpec((block, span, level_count, lat_count), lambda i: (i, 0, 0, 0))]
+        + [full] * 7,
+        out_specs=pl.BlockSpec((block, groups, level_count, lat_count), lambda i: (i, 0, 0, 0)),
         cost_estimate=pl.CostEstimate(
             flops=50 * elements, transcendentals=0, bytes_accessed=4 * elements + 28 * east.size
         ),

time: 124 us -> 108 us (0.87)
  the two profiles are of different devices: /device:TPU:16 before, /device:TPU:8 now
where the time goes in v20:
time: 108 us; the launch traced here: 107 us
  Pallas kernels  45.3 us (42%)
  other arithmetic  22.5 us (21%)
  local copies, waits for them, and re-layouts  10.8 us (10%)
  starting transfers between devices  9.79 us (9%)
  blocking collectives  8.45 us (8%)
  matrix products  5.04 us (5%)
  waiting for transfers between devices  3.81 us (4%)
    pallas_call x1, Pallas kernels, butterfly_sum(): pl.pallas_call(functools.partial(exchange_kernel, count, radix), out_shap...  23.7 us
    pallas_call x2, Pallas kernels, stencil_sums(): pl.pallas_call(stencil_kernel, out_shape=jax.ShapeDtypeStruct((rows, grou...  21.5 us
    ppermute x1, starting transfers between devices, body(): from_east = lax.ppermute(east_edge, 'lon', backward)  9.78 us
    all_gather x1, blocking collectives, body(): full_panel = lax.all_gather(coarse, 'probe', axis=0, tiled=True)  8.45 us
    another operation x3, other arithmetic, body(): lower = lax.linalg.cholesky(gram, symmetrize_input=False)  7.27 us
    another operation x1, other arithmetic, body(): lax.linalg.triangular_solve(lower, ident, left_side=True, lower=True)  4.89 us
    ppermute x1, waiting for transfers between devices, body(): from_west = lax.ppermute(west_edge, 'lon', forward)  3.81 us
    dot_general x2, matrix products, lat_average(): jnp.dot(summed.reshape(-1, lat_count), average, precision=lax.Precision.H...  2.94 us
  transfers between devices with their start and end apart: 2, of which 1 were waited for; matrix products, arithmetic and copies ran while one was open for 6% of the time, Pallas kernels for 11%

profile of v20, /device:TPU:8, one launch (start us, length us, event | category | flops | bytes accessed | tf_op | source)
XLA Modules:
  0.0 106.7 jit_solution(7478454663416946756)
XLA Ops:
  0.6 0.8 fusion.35
  1.4 1.7 %broadcast_minimum_fusion = (f32[1,24,8,256]{3,2,1,0:T(8,128)}, f32[1,24,8,256]{3,2,1,0:T(8,128)S(1)}, f32[1,24,8,256]{3,2,1,0:T(8,128)S(1)}) fusion(f32[2,24,8,256]{3,2,1,0:T(8,128)} %param.4, pred[256]{0:T(512)(128)(4,1)S(1)} %iota_compare_fusion.6), kind=kLoop, calls=%fused_computation.29 | loop fusion | flops 147456 | bytes 983296 | tf_op jit(solution)/shard_map/min | solution.py:223
  3.2 0.8 fusion.31
  4.0 1.3 %fusion.26 = (f32[16,4,8,256]{3,2,1,0:T(8,128)S(1)}, f32[16,4,8,256]{3,2,1,0:T(8,128)S(1)}) fusion(f32[16,24,8,256]{3,2,1,0:T(8,128)} %q_ref.1), kind=kLoop, calls=%fused_computation.67 | loop fusion | bytes 2097152 | tf_op jit(solution)/shard_map/slice | solution.py:267
  5.4 0.9 pad_maximum_fusion.2
  6.2 9.8 %collective-permute-start.1 = (f32[19,4,8,256]{3,2,1,0:T(8,128)}, f32[19,4,8,256]{3,2,1,0:T(8,128)}, u32[]{:S(2)}, u32[]{:S(2)}) collective-permute-start(f32[19,4,8,256]{3,2,1,0:T(8,128)} %pad_maximum_fusion.2), channel_id=1, source_target_pairs={{4,0},{8,4},{12,8},{16,12},{20,16},{24,20},{28,24},{32,28},{36,32}... | collective-permute-start | bytes 1867784 | tf_op jit(solution)/shard_map/ppermute | solution.py:270
  16.0 0.9 pad_maximum_fusion.1
  17.6 0.7 fusion.30
  18.3 0.7 fusion.33
  19.1 0.8 subtract_add_fusion
  19.9 12.0 %shard_map.51 = f32[16,4,8,256]{3,2,1,0:T(8,128)} custom-call(f32[16,24,8,256]{3,2,1,0:T(8,128)} %q_ref.1, f32[1,24,8,256]{3,2,1,0:T(8,128)} %copy-done.3, f32[1,24,8,256]{3,2,1,0:T(8,128)} %get-tuple-element.19.b_ref, f32[1,24,8,256]{3,2,1,0:T(8,128)} %copy-done.2, f32[1,24,8,256]{3,2,1,0:T(8,128)} %get-tuple-element.6.d_ref, f32[1,24,8,256]{3,2,1,0:T(8,128)} %bitcast.75, ...), custom_call_target="tpu_custom_call" | custom-call | flops 39321600 | bytes 4521984 | tf_op jit(solution)/shard_map/pallas_call | solution.py:233
  32.0 1.6 %fusion.5 = f32[16,4,8,64]{3,2,1,0:T(8,128)S(1)} fusion(f32[16,4,8,256]{3,2,1,0:T(8,128)} %shard_map.51, s32[256]{0:T(256)S(1)} %get-tuple-element.44, s32[256]{0:T(256)S(1)} %get-tuple-element.45, pred[256]{0:T(512)(128)(4,1)S(1)} %compare_and_fusion), kind=kOutput, calls=%fused_computation.33 | convolution fusion | flops 100712448 | bytes 657664 | tf_op jit(solution)/shard_map/dot_general | solution.py:251
  33.8 0.8 fusion.29
  34.7 3.8 %collective-permute-done = f32[19,4,8,256]{3,2,1,0:T(8,128)} collective-permute-done((f32[19,4,8,256]{3,2,1,0:T(8,128)}, f32[19,4,8,256]{3,2,1,0:T(8,128)}, u32[]{:S(2)}, u32[]{:S(2)}) %collective-permute-start) | collective-permute-done | bytes 622624 | tf_op jit(solution)/shard_map/ppermute | solution.py:269
  38.5 0.8 fusion.28
  39.3 0.7 fusion.2.d_ref
  40.2 0.7 minimum_bitcast_fusion
  41.0 0.7 maximum_bitcast_fusion.2.w_ref
  41.7 0.8 subtract_add_fusion.1
  42.5 1.1 %slice.150 = f32[16,4,8,256]{3,2,1,0:T(8,128)S(1)} slice(f32[19,4,8,256]{3,2,1,0:T(8,128)} %collective-permute-done), slice={[0:16], [0:4], [0:8], [0:256]} | slice | bytes 1048576 | tf_op jit(solution)/shard_map/slice | solution.py:280
  43.7 1.1 %slice.153 = f32[16,4,8,256]{3,2,1,0:T(8,128)S(1)} slice(f32[19,4,8,256]{3,2,1,0:T(8,128)} %collective-permute-done.1), slice={[0:16], [0:4], [0:8], [0:256]} | slice | bytes 1048576 | tf_op jit(solution)/shard_map/slice | solution.py:281
  44.9 2.0 %pad_maximum_fusion = f32[2,16,12,8,256]{4,3,2,1,0:T(8,128)} fusion(f32[1,16,12,8,256]{4,3,2,1,0:T(8,128)S(1)} %maximum_bitcast_fusion.1, f32[1,16,12,8,256]{4,3,2,1,0:T(8,128)S(1)} %maximum_bitcast_fusion), kind=kLoop, calls=%fused_computation | loop fusion | flops 786432 | bytes 6291456 | tf_op jit(solution)/shard_map/stack | solution.py:279
  46.9 9.5 %shard_map.50 = f32[32,1,8,256]{3,2,1,0:T(8,128)} custom-call(f32[32,12,8,256]{3,2,1,0:T(8,128)} %bitcast.73, f32[2,12,8,256]{3,2,1,0:T(8,128)} %copy-done.4, f32[2,12,8,256]{3,2,1,0:T(8,128)} %get-tuple-element.32.b_ref, f32[2,12,8,256]{3,2,1,0:T(8,128)} %copy-done.1, f32[2,12,8,256]{3,2,1,0:T(8,128)} %fusion.2.d_ref, ...), custom_call_target="tpu_custom_call" | custom-call | flops 39321600 | bytes 4521984 | tf_op jit(solution)/shard_map/pallas_call | solution.py:233
  56.4 1.3 %fusion = f32[256,64]{0,1:T(8,128)S(1)} fusion(f32[32,1,8,256]{3,2,1,0:T(8,128)} %shard_map.50, s32[256]{0:T(256)S(1)} %get-tuple-element.44, s32[256]{0:T(256)S(1)} %get-tuple-element.45, pred[256]{0:T(512)(128)(4,1)S(1)} %compare_and_fusion), kind=kOutput, calls=%fused_computation.6 | convolution fusion | flops 50380800 | bytes 329984 | tf_op jit(solution)/shard_map/dot_general | solution.py:251
  58.1 8.5 %all_gather.3 = f32[64,3072]{1,0:T(8,128)S(1)} all-gather(f32[16,3072]{1,0:T(8,128)S(1)} %reshape.43), channel_id=1, replica_groups=mesh['lon'=64,'probe'=4] {'probe'}, dimensions={0}, use_global_device_ids=true | all-gather | bytes 983040 | tf_op jit(solution)/shard_map/all_gather | solution.py:295
  66.6 1.4 %fusion.37.block_ref = f32[64,64]{1,0:T(8,128)} fusion(f32[64,3072]{1,0:T(8,128)S(1)} %all_gather.3), kind=kOutput, calls=%fused_computation.78 | convolution fusion | flops 150994944 | bytes 802816 | tf_op jit(solution)/shard_map/dot_general | solution.py:296
  68.0 23.7 %shard_map.52 = f32[64,64]{1,0:T(8,128)} custom-call(f32[64,64]{1,0:T(8,128)} %fusion.37.block_ref), custom_call_target="tpu_custom_call" | custom-call | tf_op jit(solution)/shard_map/pallas_call | solution.py:71
  91.7 6.6 %cholesky.17 = f32[64,64]{1,0:T(8,128)S(1)} custom-call(f32[64,64]{1,0:T(8,128)} %shard_map.52), custom_call_target="Cholesky" | custom-call | tf_op jit(solution)/shard_map/cholesky | solution.py:303
  99.0 0.7 fusion.18
  99.7 0.7 copy.18
  100.4 4.9 %custom-call.5 = f32[1,64,64]{1,2,0:T(8,128)S(1)} custom-call(f32[1,64,64]{2,1,0:T(8,128)S(1)} %get-tuple-element.41), custom_call_target="InvertDiagBlocksLowerTriangular" | custom-call | tf_op jit(solution)/shard_map/triangular_solve | solution.py:304
  106.0 0.7 copy.22
  (56 shorter events, 3.2 us)
Async XLA Ops:
  3.2 15.8 %copy-start.3 = (f32[1,24,8,256]{3,2,1,0:T(8,128)}, f32[1,24,8,256]{3,2,1,0:T(8,128)S(1)}, u32[]{:S(2)}) copy-start(f32[1,24,8,256]{3,2,1,0:T(8,128)S(1)} %get-tuple-element.20.a_ref) | copy-start | bytes 589828
  5.3 11.6 %copy-start.6 = (f32[24,8,256]{2,1,0:T(8,128)S(1)}, f32[24,8,256]{2,1,0:T(8,128)}, u32[]{:S(2)}) copy-start(f32[24,8,256]{2,1,0:T(8,128)} %param.5) | copy-start | bytes 589828
  5.3 12.3 %copy-start.5 = (f32[2,24,8,256]{3,2,1,0:T(8,128)S(1)}, f32[2,24,8,256]{3,2,1,0:T(8,128)}, u32[]{:S(2)}) copy-start(f32[2,24,8,256]{3,2,1,0:T(8,128)} %param.4) | copy-start | bytes 1179652
  6.2 27.5 %collective-permute-start.1 = (f32[19,4,8,256]{3,2,1,0:T(8,128)}, f32[19,4,8,256]{3,2,1,0:T(8,128)}, u32[]{:S(2)}, u32[]{:S(2)}) collective-permute-start(f32[19,4,8,256]{3,2,1,0:T(8,128)} %pad_maximum_fusion.2), channel_id=1, source_target_pairs={{4,0},{8,4},{12,8},{16,12},{20,16},{24,20},{28,24},{32,28},{36,32}... | collective-permute-start | bytes 1867784 | tf_op jit(solution)/shard_map/ppermute | solution.py:270
  16.9 21.5 %collective-permute-start = (f32[19,4,8,256]{3,2,1,0:T(8,128)}, f32[19,4,8,256]{3,2,1,0:T(8,128)}, u32[]{:S(2)}, u32[]{:S(2)}) collective-permute-start(f32[19,4,8,256]{3,2,1,0:T(8,128)} %pad_maximum_fusion.1), channel_id=1, source_target_pairs={{0,4},{4,8},{8,12},{12,16},{16,20},{20,24},{24,28},{28,32},{32,36}... | collective-permute-start | bytes 1867784 | tf_op jit(solution)/shard_map/ppermute | solution.py:269
  18.9 1.0 copy-start.2
  19.9 13.6 %copy-start = (f32[16,24,8,256]{3,2,1,0:T(8,128)S(1)}, f32[16,24,8,256]{3,2,1,0:T(8,128)}, u32[]{:S(2)}) copy-start(f32[16,24,8,256]{3,2,1,0:T(8,128)} %q_ref.1) | copy-start | bytes 9437188
  33.6 1.0 copy-start.12
  33.6 5.7 %copy-start.11 = (f32[1,8,8,256]{3,2,1,0:T(8,128)S(1)}, f32[1,8,8,256]{3,2,1,0:T(8,128)}, u32[]{:S(2)}) copy-start(f32[1,8,8,256]{3,2,1,0:T(8,128)} %get-tuple-element.30) | copy-start | bytes 196612
  33.8 6.4 %copy-start.10 = (f32[1,8,8,256]{3,2,1,0:T(8,128)S(1)}, f32[1,8,8,256]{3,2,1,0:T(8,128)}, u32[]{:S(2)}) copy-start(f32[1,8,8,256]{3,2,1,0:T(8,128)} %get-tuple-element.22) | copy-start | bytes 196612
  33.8 6.4 %copy-start.9 = (f32[1,8,8,256]{3,2,1,0:T(8,128)S(1)}, f32[1,8,8,256]{3,2,1,0:T(8,128)}, u32[]{:S(2)}) copy-start(f32[1,8,8,256]{3,2,1,0:T(8,128)} %get-tuple-element.21) | copy-start | bytes 196612
  34.6 6.3 %copy-start.8 = (f32[1,8,8,256]{3,2,1,0:T(8,128)S(1)}, f32[1,8,8,256]{3,2,1,0:T(8,128)}, u32[]{:S(2)}) copy-start(f32[1,8,8,256]{3,2,1,0:T(8,128)} %get-tuple-element.29) | copy-start | bytes 196612
  34.6 6.3 %copy-start.7 = (f32[1,8,8,256]{3,2,1,0:T(8,128)S(1)}, f32[1,8,8,256]{3,2,1,0:T(8,128)}, u32[]{:S(2)}) copy-start(f32[1,8,8,256]{3,2,1,0:T(8,128)} %get-tuple-element.28) | copy-start | bytes 196612
  39.3 3.2 %copy-start.1 = (f32[2,12,8,256]{3,2,1,0:T(8,128)}, f32[2,12,8,256]{3,2,1,0:T(8,128)S(1)}, u32[]{:S(2)}) copy-start(f32[2,12,8,256]{3,2,1,0:T(8,128)S(1)} %fusion.3.c_ref) | copy-start | bytes 589828
  40.9 2.7 %copy-start.4 = (f32[2,12,8,256]{3,2,1,0:T(8,128)}, f32[2,12,8,256]{3,2,1,0:T(8,128)S(1)}, u32[]{:S(2)}) copy-start(f32[2,12,8,256]{3,2,1,0:T(8,128)S(1)} %get-tuple-element.33.a_ref) | copy-start | bytes 589828

commit v21 on v16

--- a/solution.py
+++ b/solution.py
@@ -56,7 +56,7 @@
     out_ref[...] = current[len(rounds)]
 
 
-def butterfly_sum(block, axis, radix=4):
+def butterfly_sum(block, axis, radix=8):
     count = lax.axis_size(axis)
     if count & (count - 1) or count < 2:
         return lax.psum(block, axis)

time: 102 us -> 104 us (1.020)
  Pallas kernels: 36.6 us -> 38.8 us
    pallas_call x1, Pallas kernels: 21.7 us -> 23.9 us  [butterfly_sum(): pl.pallas_call(functools.partial(exchange_kernel, count, radix), out_shap...]
  transfers between devices with their start and end apart: 2 -> 2, of which waited for: 1 -> 1; matrix products, arithmetic and copies ran while one was open for 6% -> 6% of each run, Pallas kernels for 15% -> 14%
where the time goes in v21:
time: 104 us; the launch traced here: 103 us
  Pallas kernels  38.8 us (37%)
  other arithmetic  24.3 us (23%)
  local copies, waits for them, and re-layouts  13.5 us (13%)
  starting transfers between devices  9.79 us (9%)
  blocking collectives  8.63 us (8%)
  matrix products  4.25 us (4%)
  waiting for transfers between devices  2.59 us (2%)
  between operations  1.09 us (1%)
    pallas_call x1, Pallas kernels, butterfly_sum(): pl.pallas_call(functools.partial(exchange_kernel, count, radix), out_shap...  23.9 us
    pallas_call x1, Pallas kernels, stencil_sums(): pl.pallas_call(stencil_kernel, out_shape=jax.ShapeDtypeStruct((probe_coun...  14.9 us
    all_gather x1, blocking collectives, body(): full_panel = lax.all_gather(coarse, 'probe', axis=0, tiled=True)  8.63 us
    ppermute x1, starting transfers between devices, body(): from_east = lax.ppermute(east_edge, 'lon', backward)  7.49 us
    another operation x3, other arithmetic, body(): lower = lax.linalg.cholesky(gram, symmetrize_input=False)  7.27 us
    another operation x1, other arithmetic, body(): lax.linalg.triangular_solve(lower, ident, left_side=True, lower=True)  4.9 us
    ppermute x1, waiting for transfers between devices, body(): from_east = lax.ppermute(east_edge, 'lon', backward)  2.59 us
    ppermute x1, starting transfers between devices, body(): from_west = lax.ppermute(west_edge, 'lon', forward)  2.3 us
  transfers between devices with their start and end apart: 2, of which 1 were waited for; matrix products, arithmetic and copies ran while one was open for 6% of the time, Pallas kernels for 14%

profile of v21, /device:TPU:8, one launch (start us, length us, event | category | flops | bytes accessed | tf_op | source)
XLA Modules:
  0.0 102.9 jit_solution(17836785300468545093)
XLA Ops:
  0.6 1.8 %slice_maximum_fusion = (f32[1,24,8,256]{3,2,1,0:T(8,128)S(1)}, f32[24,8,256]{2,1,0:T(8,128)}, f32[24,8,256]{2,1,0:T(8,128)}, f32[1,24,8,256]{3,2,1,0:T(8,128)S(1)}) fusion(f32[2,24,8,256]{3,2,1,0:T(8,128)} %param.4, pred[256]{0:T(512)(128)(4,1)S(1)} %iota_compare_fusion.8), kind=kLoop, calls=%fused_computation.73 | loop fusion | flops 147456 | bytes 1179904 | tf_op jit(solution)/shard_map/max | solution.py:214
  2.5 0.8 fusion.81
  3.3 0.8 fusion.85
  4.1 1.4 %fusion.75 = (f32[16,4,8,256]{3,2,1,0:T(8,128)S(1)}, f32[16,4,8,256]{3,2,1,0:T(8,128)S(1)}) fusion(f32[16,24,8,256]{3,2,1,0:T(8,128)} %q_ref.1), kind=kLoop, calls=%fused_computation.163 | loop fusion | bytes 2097152 | tf_op jit(solution)/shard_map/slice | solution.py:276
  5.4 0.9 pad_maximum_fusion
  6.3 2.3 %collective-permute-start = (f32[19,4,8,256]{3,2,1,0:T(8,128)}, f32[19,4,8,256]{3,2,1,0:T(8,128)}, u32[]{:S(2)}, u32[]{:S(2)}) collective-permute-start(f32[19,4,8,256]{3,2,1,0:T(8,128)} %pad_maximum_fusion), channel_id=1, source_target_pairs={{0,4},{4,8},{8,12},{12,16},{16,20},{20,24},{24,28},{28,32},{32,36}... | collective-permute-start | bytes 1867784 | tf_op jit(solution)/shard_map/ppermute | solution.py:259
  8.6 0.9 pad_maximum_fusion.1
  9.5 7.5 %collective-permute-start.1 = (f32[19,4,8,256]{3,2,1,0:T(8,128)}, f32[19,4,8,256]{3,2,1,0:T(8,128)}, u32[]{:S(2)}, u32[]{:S(2)}) collective-permute-start(f32[19,4,8,256]{3,2,1,0:T(8,128)} %pad_maximum_fusion.1), channel_id=1, source_target_pairs={{4,0},{8,4},{12,8},{16,12},{20,16},{24,20},{28,24},{32,28},{36,32}... | collective-permute-start | bytes 1867784 | tf_op jit(solution)/shard_map/ppermute | solution.py:260
  17.0 0.7 fusion.83
  17.7 0.7 fusion.80
  18.3 0.7 fusion.82
  19.2 0.8 subtract_add_fusion
  20.0 14.9 %shard_map.50 = f32[16,4,8,256]{3,2,1,0:T(8,128)} custom-call(f32[16,24,8,256]{3,2,1,0:T(8,128)} %q_ref.1, f32[24,8,256]{2,1,0:T(8,128)} %get-tuple-element.27.a_ref, f32[24,8,256]{2,1,0:T(8,128)} %get-tuple-element.28.b_ref, f32[24,8,256]{2,1,0:T(8,128)} %copy-done.2, f32[24,8,256]{2,1,0:T(8,128)} %get-tuple-element.9.d_ref, f32[24,8,256]{2,1,0:T(8,128)} %w_ref.1, ...), custom_call_target="tpu_custom_call" | custom-call | flops 39321600 | bytes 4521984 | tf_op jit(solution)/shard_map/pallas_call | solution.py:224
  34.9 1.6 %fusion.37 = f32[16,4,8,64]{3,2,1,0:T(8,128)S(1)} fusion(f32[16,4,8,256]{3,2,1,0:T(8,128)} %shard_map.50, s32[256]{0:T(256)S(1)} %get-tuple-element.64, s32[256]{0:T(256)S(1)} %get-tuple-element.65, pred[256]{0:T(512)(128)(4,1)S(1)} %compare_and_fusion), kind=kOutput, calls=%fused_computation.109 | convolution fusion | flops 100712448 | bytes 657664 | tf_op jit(solution)/shard_map/dot_general | solution.py:241
  36.8 0.8 fusion.78
  37.6 2.6 %collective-permute-done.1 = f32[19,4,8,256]{3,2,1,0:T(8,128)} collective-permute-done((f32[19,4,8,256]{3,2,1,0:T(8,128)}, f32[19,4,8,256]{3,2,1,0:T(8,128)}, u32[]{:S(2)}, u32[]{:S(2)}) %collective-permute-start.1) | collective-permute-done | bytes 622624 | tf_op jit(solution)/shard_map/ppermute | solution.py:260
  40.2 0.8 fusion.79
  41.3 1.1 %slice.331 = f32[16,4,8,256]{3,2,1,0:T(8,128)S(1)} slice(f32[19,4,8,256]{3,2,1,0:T(8,128)} %collective-permute-done.1), slice={[0:16], [0:4], [0:8], [0:256]} | slice | bytes 1048576 | tf_op jit(solution)/shard_map/slice | solution.py:271
  42.5 1.1 %slice.330 = f32[16,4,8,256]{3,2,1,0:T(8,128)S(1)} slice(f32[19,4,8,256]{3,2,1,0:T(8,128)} %collective-permute-done), slice={[0:16], [0:4], [0:8], [0:256]} | slice | bytes 1048576 | tf_op jit(solution)/shard_map/slice | solution.py:270
  43.7 0.9 fusion.7
  44.6 0.7 slice.352
  45.7 1.6 %fusion.9 = f32[2,16,10,8,256]{4,3,2,1,0:T(8,128)S(1)} fusion(f32[2,16,11,8,256]{4,3,2,1,0:T(8,128)S(1)} %fusion.2, f32[2,16,10,8,255]{4,3,2,1,0:T(8,128)S(1)} %slice.352, f32[1,16,12,8,256]{4,3,2,1,0:T(8,128)S(1)} %maximum_bitcast_fusion.1, f32[1,16,12,8,256]{4,3,2,1,0:T(8,128)S(1)} %maximum_bitcast_fusion, f32[2,10,8,256]{3,2,1,0:T(8,128)S(1)} %get-tuple-element.44, ...), kind=kLoop, calls=%fused_computation.18 | loop fusion | flops 8519680 | bytes 13948928 | tf_op jit(solution)/shard_map/sub | solution.py:127
  49.7 0.7 fusion.13
  51.2 0.9 fusion.16
  54.1 8.6 %all_gather.3 = f32[64,3072]{1,0:T(8,128)S(1)} all-gather(f32[16,3072]{1,0:T(8,128)S(1)} %reshape.119), channel_id=1, replica_groups=mesh['lon'=64,'probe'=4] {'probe'}, dimensions={0}, use_global_device_ids=true | all-gather | bytes 983040 | tf_op jit(solution)/shard_map/all_gather | solution.py:282
  62.7 1.4 %fusion.86.block_ref = f32[64,64]{1,0:T(8,128)} fusion(f32[64,3072]{1,0:T(8,128)S(1)} %all_gather.3), kind=kOutput, calls=%fused_computation.174 | convolution fusion | flops 150994944 | bytes 802816 | tf_op jit(solution)/shard_map/dot_general | solution.py:283
  64.1 23.9 %shard_map.51 = f32[64,64]{1,0:T(8,128)} custom-call(f32[64,64]{1,0:T(8,128)} %fusion.86.block_ref), custom_call_target="tpu_custom_call" | custom-call | tf_op jit(solution)/shard_map/pallas_call | solution.py:71
  88.0 6.6 %cholesky.17 = f32[64,64]{1,0:T(8,128)S(1)} custom-call(f32[64,64]{1,0:T(8,128)} %shard_map.51), custom_call_target="Cholesky" | custom-call | tf_op jit(solution)/shard_map/cholesky | solution.py:290
  95.2 0.7 fusion.58
  95.9 4.9 %custom-call.5 = f32[1,64,64]{1,2,0:T(8,128)S(1)} custom-call(f32[1,64,64]{2,1,0:T(8,128)S(1)} %get-tuple-element.61), custom_call_target="InvertDiagBlocksLowerTriangular" | custom-call | tf_op jit(solution)/shard_map/triangular_solve | solution.py:291
  101.5 0.7 copy.14
  102.2 0.7 copy.10
  (65 shorter events, 7.5 us)
Async XLA Ops:
  4.1 13.6 %copy-start.1 = (f32[2,24,8,256]{3,2,1,0:T(8,128)S(1)}, f32[2,24,8,256]{3,2,1,0:T(8,128)}, u32[]{:S(2)}) copy-start(f32[2,24,8,256]{3,2,1,0:T(8,128)} %param.4) | copy-start | bytes 1179652
  4.1 14.3 %copy-start.3 = (f32[24,8,256]{2,1,0:T(8,128)S(1)}, f32[24,8,256]{2,1,0:T(8,128)}, u32[]{:S(2)}) copy-start(f32[24,8,256]{2,1,0:T(8,128)} %w_ref.1) | copy-start | bytes 589828
  6.3 30.4 %collective-permute-start = (f32[19,4,8,256]{3,2,1,0:T(8,128)}, f32[19,4,8,256]{3,2,1,0:T(8,128)}, u32[]{:S(2)}, u32[]{:S(2)}) collective-permute-start(f32[19,4,8,256]{3,2,1,0:T(8,128)} %pad_maximum_fusion), channel_id=1, source_target_pairs={{0,4},{4,8},{8,12},{12,16},{16,20},{20,24},{24,28},{28,32},{32,36}... | collective-permute-start | bytes 1867784 | tf_op jit(solution)/shard_map/ppermute | solution.py:259
  9.5 30.7 %collective-permute-start.1 = (f32[19,4,8,256]{3,2,1,0:T(8,128)}, f32[19,4,8,256]{3,2,1,0:T(8,128)}, u32[]{:S(2)}, u32[]{:S(2)}) collective-permute-start(f32[19,4,8,256]{3,2,1,0:T(8,128)} %pad_maximum_fusion.1), channel_id=1, source_target_pairs={{4,0},{8,4},{12,8},{16,12},{20,16},{24,20},{28,24},{32,28},{36,32}... | collective-permute-start | bytes 1867784 | tf_op jit(solution)/shard_map/ppermute | solution.py:260
  19.0 1.0 copy-start.2
  20.0 16.5 %copy-start = (f32[16,24,8,256]{3,2,1,0:T(8,128)S(1)}, f32[16,24,8,256]{3,2,1,0:T(8,128)}, u32[]{:S(2)}) copy-start(f32[16,24,8,256]{3,2,1,0:T(8,128)} %q_ref.1) | copy-start | bytes 9437188
  36.6 1.0 copy-start.9
  36.6 4.4 %copy-start.8 = (f32[1,8,8,256]{3,2,1,0:T(8,128)S(1)}, f32[1,8,8,256]{3,2,1,0:T(8,128)}, u32[]{:S(2)}) copy-start(f32[1,8,8,256]{3,2,1,0:T(8,128)} %get-tuple-element.46) | copy-start | bytes 196612
  36.6 4.5 %copy-start.7 = (f32[1,8,8,256]{3,2,1,0:T(8,128)S(1)}, f32[1,8,8,256]{3,2,1,0:T(8,128)}, u32[]{:S(2)}) copy-start(f32[1,8,8,256]{3,2,1,0:T(8,128)} %get-tuple-element.30) | copy-start | bytes 196612
  36.6 4.5 %copy-start.6 = (f32[1,8,8,256]{3,2,1,0:T(8,128)S(1)}, f32[1,8,8,256]{3,2,1,0:T(8,128)}, u32[]{:S(2)}) copy-start(f32[1,8,8,256]{3,2,1,0:T(8,128)} %get-tuple-element.31) | copy-start | bytes 196612
  48.8 0.8 copy-start.5
  48.9 0.9 copy-start.4

commit v22 on v18

--- a/solution.py
+++ b/solution.py
@@ -309,10 +309,14 @@
     own_rows = lax.dynamic_slice_in_dim(
         inverse, lax.axis_index("probe") * probe_count, probe_count, 0
     )
-    basis = jnp.dot(
-        own_rows, full_panel, precision=lax.Precision.HIGHEST, preferred_element_type=jnp.float32
-    )
-    return (basis.reshape(probe_count, lon_count // 4, -1), lower.T)
+    basis = lax.dot_general(
+        own_rows,
+        full_panel.reshape(all_probes, lon_count // 4, -1),
+        (((1,), (0,)), ((), ())),
+        precision=lax.Precision.HIGHEST,
+        preferred_element_type=jnp.float32,
+    )
+    return (basis, lower.T)
 
 
 def solution(mesh):

time: 102 us -> 102 us (level)
  no operation moved by 1% of the time
where the time goes in v22:
time: 102 us; the launch traced here: 101 us
  Pallas kernels  38.5 us (38%)
  other arithmetic  24.4 us (24%)
  local copies, waits for them, and re-layouts  13.7 us (13%)
  starting transfers between devices  9.79 us (10%)
  blocking collectives  8.64 us (8%)
  matrix products  4.94 us (5%)
  between operations  1.04 us (1%)
    pallas_call x1, Pallas kernels, butterfly_sum(): pl.pallas_call(functools.partial(exchange_kernel, count, radix), out_shap...  23.6 us
    pallas_call x1, Pallas kernels, stencil_sums(): pl.pallas_call(stencil_kernel, out_shape=jax.ShapeDtypeStruct((probe_coun...  14.9 us
    all_gather x1, blocking collectives, body(): full_panel = lax.all_gather(coarse, 'probe', axis=0, tiled=True)  8.64 us
    ppermute x1, starting transfers between devices, body(): from_east = lax.ppermute(east_edge, 'lon', backward)  7.49 us
    another operation x3, other arithmetic, body(): lower = lax.linalg.cholesky(gram, symmetrize_input=False)  7.27 us
    another operation x1, other arithmetic, body(): lax.linalg.triangular_solve(lower, ident, left_side=True, lower=True)  4.89 us
    reshape x5, local copies, waits for them, and re-layouts, unpack(): flat[row:row + rows].reshape((part.shape[0], width) + part.shape[2:])  3.7 us
    ppermute x1, starting transfers between devices, body(): from_west = lax.ppermute(west_edge, 'lon', forward)  2.3 us
  transfers between devices with their start and end apart: 2, of which 1 were waited for; matrix products, arithmetic and copies ran while one was open for 8% of the time, Pallas kernels for 15%

profile of v22, /device:TPU:8, one launch (start us, length us, event | category | flops | bytes accessed | tf_op | source)
XLA Modules:
  0.0 101.0 jit_solution(5005548215562255029)
XLA Ops:
  0.7 0.8 slice_bitcast_fusion.10
  1.4 0.7 slice_bitcast_fusion.12
  2.2 1.8 %slice_maximum_fusion = (f32[1,24,8,256]{3,2,1,0:T(8,128)S(1)}, f32[24,8,256]{2,1,0:T(8,128)}, f32[24,8,256]{2,1,0:T(8,128)}, f32[1,24,8,256]{3,2,1,0:T(8,128)S(1)}) fusion(f32[2,24,8,256]{3,2,1,0:T(8,128)} %param.4, pred[256]{0:T(512)(128)(4,1)S(1)} %iota_compare_fusion.8), kind=kLoop, calls=%fused_computation.75 | loop fusion | flops 147456 | bytes 1179904 | tf_op jit(solution)/shard_map/max | solution.py:214
  4.0 1.3 %fusion.82 = (f32[16,4,8,256]{3,2,1,0:T(8,128)S(1)}, f32[16,4,8,256]{3,2,1,0:T(8,128)S(1)}) fusion(f32[16,24,8,256]{3,2,1,0:T(8,128)} %q_ref.1), kind=kLoop, calls=%fused_computation.181 | loop fusion | bytes 2097152 | tf_op jit(solution)/shard_map/slice | solution.py:293
  5.3 0.9 pad_maximum_fusion.1
  6.2 2.3 %collective-permute-start = (f32[72,8,256]{2,1,0:T(8,128)}, f32[72,8,256]{2,1,0:T(8,128)}, u32[]{:S(2)}, u32[]{:S(2)}) collective-permute-start(f32[72,8,256]{2,1,0:T(8,128)} %pad_maximum_fusion.1), channel_id=1, source_target_pairs={{0,4},{4,8},{8,12},{12,16},{16,20},{20,24},{24,28},{28,32},{32,36}... | collective-permute-start | bytes 1769480 | tf_op jit(solution)/shard_map/ppermute | solution.py:265
  8.5 0.9 pad_maximum_fusion
  9.4 7.5 %collective-permute-start.1 = (f32[73,8,256]{2,1,0:T(8,128)}, f32[73,8,256]{2,1,0:T(8,128)}, u32[]{:S(2)}, u32[]{:S(2)}) collective-permute-start(f32[73,8,256]{2,1,0:T(8,128)} %pad_maximum_fusion), channel_id=1, source_target_pairs={{4,0},{8,4},{12,8},{16,12},{20,16},{24,20},{28,24},{32,28},{36,32}... | collective-permute-start | bytes 1794056 | tf_op jit(solution)/shard_map/ppermute | solution.py:266
  17.6 0.7 fusion.87
  18.4 0.9 subtract_add_fusion
  19.3 14.9 %shard_map.50 = f32[16,4,8,256]{3,2,1,0:T(8,128)} custom-call(f32[16,24,8,256]{3,2,1,0:T(8,128)} %q_ref.1, f32[24,8,256]{2,1,0:T(8,128)} %get-tuple-element.23.a_ref, f32[24,8,256]{2,1,0:T(8,128)} %get-tuple-element.24.b_ref, f32[24,8,256]{2,1,0:T(8,128)} %copy-done.2, f32[24,8,256]{2,1,0:T(8,128)} %get-tuple-element.9.d_ref, f32[24,8,256]{2,1,0:T(8,128)} %w_ref.1, ...), custom_call_target="tpu_custom_call" | custom-call | flops 39321600 | bytes 4521984 | tf_op jit(solution)/shard_map/pallas_call | solution.py:224
  34.2 1.6 %fusion.44 = f32[16,4,8,64]{3,2,1,0:T(8,128)S(1)} fusion(f32[16,4,8,256]{3,2,1,0:T(8,128)} %shard_map.50, s32[256]{0:T(256)S(1)} %get-tuple-element.62, s32[256]{0:T(256)S(1)} %get-tuple-element.63, pred[256]{0:T(512)(128)(4,1)S(1)} %compare_and_fusion), kind=kOutput, calls=%fused_computation.115 | convolution fusion | flops 100712448 | bytes 657664 | tf_op jit(solution)/shard_map/dot_general | solution.py:241
  36.0 1.1 %slice.330 = f32[64,8,256]{2,1,0:T(8,128)S(1)} slice(f32[72,8,256]{2,1,0:T(8,128)} %collective-permute-done), slice={[0:64], [0:8], [0:256]} | slice | bytes 1048576 | tf_op jit(solution)/shard_map/slice | solution.py:272
  37.2 0.7 slice_bitcast_fusion.13
  38.0 0.8 slice_bitcast_fusion.6
  38.8 0.7 slice_bitcast_fusion.5
  39.5 0.8 slice_bitcast_fusion.3
  40.7 1.1 %slice.331 = f32[64,8,256]{2,1,0:T(8,128)S(1)} slice(f32[73,8,256]{2,1,0:T(8,128)} %collective-permute-done.1), slice={[0:64], [0:8], [0:256]} | slice | bytes 1048576 | tf_op jit(solution)/shard_map/slice | solution.py:272
  42.0 0.8 fusion.7
  42.8 0.7 slice.352
  43.9 1.6 %fusion.9 = f32[2,16,10,8,256]{4,3,2,1,0:T(8,128)S(1)} fusion(f32[2,16,11,8,256]{4,3,2,1,0:T(8,128)S(1)} %fusion.2, f32[2,16,10,8,255]{4,3,2,1,0:T(8,128)S(1)} %slice.352, f32[1,16,12,8,256]{4,3,2,1,0:T(8,128)S(1)} %maximum_bitcast_fusion.1, f32[1,16,12,8,256]{4,3,2,1,0:T(8,128)S(1)} %maximum_bitcast_fusion, f32[2,10,8,256]{3,2,1,0:T(8,128)S(1)} %get-tuple-element.38, ...), kind=kLoop, calls=%fused_computation.18 | loop fusion | flops 8519680 | bytes 13948928 | tf_op jit(solution)/shard_map/sub | solution.py:127
  47.0 0.7 slice_bitcast_fusion.11
  48.0 0.7 fusion.13
  49.4 1.0 %fusion.16 = f32[2,16,6,8,256]{4,3,2,1,0:T(8,128)S(1)} fusion(f32[2,16,8,8,256]{4,3,2,1,0:T(8,128)S(1)} %fusion.13, f32[2,16,6,8,255]{4,3,2,1,0:T(8,128)S(1)} %get-tuple-element.17, f32[2,16,6,8,255]{4,3,2,1,0:T(8,128)S(1)} %get-tuple-element.16, f32[2,6,8,256]{3,2,1,0:T(8,128)S(1)} %get-tuple-element.52, f32[2,6,8,256]{3,2,1,0:T(8,128)S(1)} %get-tuple-element.10, ...), kind=kLoop, calls=%fused_computation.30 | loop fusion | flops 3538944 | bytes 9916416 | tf_op jit(solution)/shard_map/add | solution.py:141
  50.8 0.7 fusion.20
  52.4 8.6 %all_gather.3 = f32[64,3072]{1,0:T(8,128)S(1)} all-gather(f32[16,3072]{1,0:T(8,128)S(1)} %reshape.183), channel_id=1, replica_groups=mesh['lon'=64,'probe'=4] {'probe'}, dimensions={0}, use_global_device_ids=true | all-gather | bytes 983040 | tf_op jit(solution)/shard_map/all_gather | solution.py:299
  61.1 1.4 %fusion.88.block_ref = f32[64,64]{1,0:T(8,128)} fusion(f32[64,3072]{1,0:T(8,128)S(1)} %all_gather.3), kind=kOutput, calls=%fused_computation.187 | convolution fusion | flops 150994944 | bytes 802816 | tf_op jit(solution)/shard_map/dot_general | solution.py:300
  62.4 23.6 %shard_map.51 = f32[64,64]{1,0:T(8,128)} custom-call(f32[64,64]{1,0:T(8,128)} %fusion.88.block_ref), custom_call_target="tpu_custom_call" | custom-call | tf_op jit(solution)/shard_map/pallas_call | solution.py:71
  86.0 6.6 %cholesky.17 = f32[64,64]{1,0:T(8,128)S(1)} custom-call(f32[64,64]{1,0:T(8,128)} %shard_map.51), custom_call_target="Cholesky" | custom-call | tf_op jit(solution)/shard_map/cholesky | solution.py:307
  94.0 0.7 copy.9
  94.7 4.9 %custom-call.5 = f32[1,64,64]{1,2,0:T(8,128)S(1)} custom-call(f32[1,64,64]{2,1,0:T(8,128)S(1)} %get-tuple-element.55), custom_call_target="InvertDiagBlocksLowerTriangular" | custom-call | tf_op jit(solution)/shard_map/triangular_solve | solution.py:308
  99.8 1.2 %fusion.22 = f32[16,6,512]{2,0,1:T(8,128)} fusion(f32[8,6,8,512]{3,2,1,0:T(8,128)S(1)} %bitcast.146, f32[64,64]{1,0:T(8,128)S(1)} %fusion.48, s32[]{:T(128)S(6)} %select_n.39), kind=kOutput, calls=%fused_computation.45 | convolution fusion | flops 37748736 | bytes 991236 | tf_op jit(solution)/shard_map/dot_general | solution.py:312
  (61 shorter events, 7.2 us)
Async XLA Ops:
  0.6 7.9 %copy-start.1 = (f32[2,24,8,256]{3,2,1,0:T(8,128)S(1)}, f32[2,24,8,256]{3,2,1,0:T(8,128)}, u32[]{:S(2)}) copy-start(f32[2,24,8,256]{3,2,1,0:T(8,128)} %param.4) | copy-start | bytes 1179652
  4.0 12.9 %copy-start.3 = (f32[24,8,256]{2,1,0:T(8,128)S(1)}, f32[24,8,256]{2,1,0:T(8,128)}, u32[]{:S(2)}) copy-start(f32[24,8,256]{2,1,0:T(8,128)} %w_ref.1) | copy-start | bytes 589828
  6.2 29.8 %collective-permute-start = (f32[72,8,256]{2,1,0:T(8,128)}, f32[72,8,256]{2,1,0:T(8,128)}, u32[]{:S(2)}, u32[]{:S(2)}) collective-permute-start(f32[72,8,256]{2,1,0:T(8,128)} %pad_maximum_fusion.1), channel_id=1, source_target_pairs={{0,4},{4,8},{8,12},{12,16},{16,20},{20,24},{24,28},{28,32},{32,36}... | collective-permute-start | bytes 1769480 | tf_op jit(solution)/shard_map/ppermute | solution.py:265
  9.4 29.4 %collective-permute-start.1 = (f32[73,8,256]{2,1,0:T(8,128)}, f32[73,8,256]{2,1,0:T(8,128)}, u32[]{:S(2)}, u32[]{:S(2)}) collective-permute-start(f32[73,8,256]{2,1,0:T(8,128)} %pad_maximum_fusion), channel_id=1, source_target_pairs={{4,0},{8,4},{12,8},{16,12},{20,16},{24,20},{28,24},{32,28},{36,32}... | collective-permute-start | bytes 1794056 | tf_op jit(solution)/shard_map/ppermute | solution.py:266
  17.6 1.7 %copy-start.2 = (f32[24,8,256]{2,1,0:T(8,128)}, f32[24,8,256]{2,1,0:T(8,128)S(1)}, u32[]{:S(2)}) copy-start(f32[24,8,256]{2,1,0:T(8,128)S(1)} %fusion.30.c_ref) | copy-start | bytes 589828
  19.3 16.5 %copy-start = (f32[16,24,8,256]{3,2,1,0:T(8,128)S(1)}, f32[16,24,8,256]{3,2,1,0:T(8,128)}, u32[]{:S(2)}) copy-start(f32[16,24,8,256]{3,2,1,0:T(8,128)} %q_ref.1) | copy-start | bytes 9437188
  36.0 4.3 %copy-start.4 = (f32[1,8,8,256]{3,2,1,0:T(8,128)S(1)}, f32[1,8,8,256]{3,2,1,0:T(8,128)}, u32[]{:S(2)}) copy-start(f32[1,8,8,256]{3,2,1,0:T(8,128)} %get-tuple-element.40) | copy-start | bytes 196612
  46.4 1.4 %copy-start.5 = (f32[1,8,8,256]{3,2,1,0:T(8,128)S(1)}, f32[1,8,8,256]{3,2,1,0:T(8,128)}, u32[]{:S(2)}) copy-start(f32[1,8,8,256]{3,2,1,0:T(8,128)} %get-tuple-element.33) | copy-start | bytes 196612
  46.4 1.3 %copy-start.6 = (f32[1,8,8,256]{3,2,1,0:T(8,128)S(1)}, f32[1,8,8,256]{3,2,1,0:T(8,128)}, u32[]{:S(2)}) copy-start(f32[1,8,8,256]{3,2,1,0:T(8,128)} %get-tuple-element.34) | copy-start | bytes 196612

commit v23 on v16

--- a/solution.py
+++ b/solution.py
@@ -172,9 +172,14 @@
 
 
 def stencil_kernel(q_ref, a_ref, b_ref, c_ref, d_ref, w_ref, n_ref, k_ref, o_ref):
+    for row in range(q_ref.shape[0]):
+        stencil_row(row, q_ref, a_ref, b_ref, c_ref, d_ref, w_ref, n_ref, k_ref, o_ref)
+
+
+def stencil_row(row, q_ref, a_ref, b_ref, c_ref, d_ref, w_ref, n_ref, k_ref, o_ref):
     span = q_ref.shape[1]
     lat = q_ref.shape[-1]
-    field = q_ref[0]
+    field = q_ref[row]
     state = field
     for step in range(2):
         lo, hi = step, span - step
@@ -205,7 +210,7 @@
     sketch = field[4:span - 4] + state
     groups = sketch.shape[0] // 4
     for g in range(groups):
-        o_ref[0, g] = ((sketch[4 * g] + sketch[4 * g + 1]) + sketch[4 * g + 2]) + sketch[4 * g + 3]
+        o_ref[row, g] = ((sketch[4 * g] + sketch[4 * g + 1]) + sketch[4 * g + 2]) + sketch[4 * g + 3]
 
 
 def stencil_sums(slab, east, north, weight):
@@ -219,14 +224,16 @@
     next_a = jnp.concatenate([east_a[1:], jnp.zeros_like(east_a[:1])], axis=0)
     centre = 1.0 - next_a + east_b - north_up + north_d
     winds = (east_a, east_b, north_c, north_d, weight, north_up, centre)
+    block = 4 if probe_count % 4 == 0 else 1
     full = pl.BlockSpec((span, level_count, lat_count), lambda i: (0, 0, 0))
     elements = probe_count * span * level_count * lat_count
     return pl.pallas_call(
         stencil_kernel,
         out_shape=jax.ShapeDtypeStruct((probe_count, groups, level_count, lat_count), slab.dtype),
-        grid=(probe_count,),
-        in_specs=[pl.BlockSpec((1, span, level_count, lat_count), lambda i: (i, 0, 0, 0))] + [full] * 7,
-        out_specs=pl.BlockSpec((1, groups, level_count, lat_count), lambda i: (i, 0, 0, 0)),
+        grid=(probe_count // block,),
+        in_specs=[pl.BlockSpec((block, span, level_count, lat_count), lambda i: (i, 0, 0, 0))]
+        + [full] * 7,
+        out_specs=pl.BlockSpec((block, groups, level_count, lat_count), lambda i: (i, 0, 0, 0)),
         cost_estimate=pl.CostEstimate(
             flops=50 * elements, transcendentals=0, bytes_accessed=4 * elements + 28 * span * level_count * lat_count
         ),

time: 102 us -> 102 us (level)
  Pallas kernels: 36.6 us -> 33.5 us
  waiting for transfers between devices: 2.59 us -> 5.68 us
    pallas_call x1, Pallas kernels: 14.9 us -> 11.8 us  [stencil_sums(): pl.pallas_call(stencil_kernel, out_shape=jax.ShapeDtypeStruct((probe_coun...]
    ppermute x1, waiting for transfers between devices: 0.01 us -> 1.9 us  [body(): from_west = lax.ppermute(west_edge, 'lon', forward)]
    ppermute x1, waiting for transfers between devices: 2.59 us -> 3.78 us  [body(): from_east = lax.ppermute(east_edge, 'lon', backward)]
  transfers between devices with their start and end apart: 2 -> 2, of which waited for: 1 -> 2; matrix products, arithmetic and copies ran while one was open for 6% -> 6% of each run, Pallas kernels for 15% -> 12%
where the time goes in v23:
time: 102 us; the launch traced here: 101 us
  Pallas kernels  33.5 us (33%)
  other arithmetic  24.3 us (24%)
  local copies, waits for them, and re-layouts  13.5 us (13%)
  starting transfers between devices  9.79 us (10%)
  blocking collectives  8.63 us (8%)
  waiting for transfers between devices  5.68 us (6%)
  matrix products  4.25 us (4%)
  between operations  1.08 us (1%)
    pallas_call x1, Pallas kernels, butterfly_sum(): pl.pallas_call(functools.partial(exchange_kernel, count, radix), out_shap...  21.7 us
    pallas_call x1, Pallas kernels, stencil_sums(): pl.pallas_call(stencil_kernel, out_shape=jax.ShapeDtypeStruct((probe_coun...  11.8 us
    all_gather x1, blocking collectives, body(): full_panel = lax.all_gather(coarse, 'probe', axis=0, tiled=True)  8.63 us
    ppermute x1, starting transfers between devices, body(): from_east = lax.ppermute(east_edge, 'lon', backward)  7.49 us
    another operation x3, other arithmetic, body(): lower = lax.linalg.cholesky(gram, symmetrize_input=False)  7.27 us
    another operation x1, other arithmetic, body(): lax.linalg.triangular_solve(lower, ident, left_side=True, lower=True)  4.9 us
    ppermute x1, waiting for transfers between devices, body(): from_east = lax.ppermute(east_edge, 'lon', backward)  3.78 us
    ppermute x1, starting transfers between devices, body(): from_west = lax.ppermute(west_edge, 'lon', forward)  2.3 us
  transfers between devices with their start and end apart: 2, of which 2 were waited for; matrix products, arithmetic and copies ran while one was open for 6% of the time, Pallas kernels for 12%

profile of v23, /device:TPU:8, one launch (start us, length us, event | category | flops | bytes accessed | tf_op | source)
XLA Modules:
  0.0 100.8 jit_solution(3882345276208206492)
XLA Ops:
  0.6 1.8 %slice_maximum_fusion = (f32[1,24,8,256]{3,2,1,0:T(8,128)S(1)}, f32[24,8,256]{2,1,0:T(8,128)}, f32[24,8,256]{2,1,0:T(8,128)}, f32[1,24,8,256]{3,2,1,0:T(8,128)S(1)}) fusion(f32[2,24,8,256]{3,2,1,0:T(8,128)} %param.4, pred[256]{0:T(512)(128)(4,1)S(1)} %iota_compare_fusion.8), kind=kLoop, calls=%fused_computation.73 | loop fusion | flops 147456 | bytes 1179904 | tf_op jit(solution)/shard_map/max | solution.py:219
  2.5 0.8 fusion.81
  3.3 0.8 fusion.85
  4.1 1.4 %fusion.75 = (f32[16,4,8,256]{3,2,1,0:T(8,128)S(1)}, f32[16,4,8,256]{3,2,1,0:T(8,128)S(1)}) fusion(f32[16,24,8,256]{3,2,1,0:T(8,128)} %q_ref.1), kind=kLoop, calls=%fused_computation.163 | loop fusion | bytes 2097152 | tf_op jit(solution)/shard_map/slice | solution.py:283
  5.4 0.9 pad_maximum_fusion
  6.3 2.3 %collective-permute-start = (f32[19,4,8,256]{3,2,1,0:T(8,128)}, f32[19,4,8,256]{3,2,1,0:T(8,128)}, u32[]{:S(2)}, u32[]{:S(2)}) collective-permute-start(f32[19,4,8,256]{3,2,1,0:T(8,128)} %pad_maximum_fusion), channel_id=1, source_target_pairs={{0,4},{4,8},{8,12},{12,16},{16,20},{20,24},{24,28},{28,32},{32,36}... | collective-permute-start | bytes 1867784 | tf_op jit(solution)/shard_map/ppermute | solution.py:266
  8.6 0.9 pad_maximum_fusion.1
  9.5 7.5 %collective-permute-start.1 = (f32[19,4,8,256]{3,2,1,0:T(8,128)}, f32[19,4,8,256]{3,2,1,0:T(8,128)}, u32[]{:S(2)}, u32[]{:S(2)}) collective-permute-start(f32[19,4,8,256]{3,2,1,0:T(8,128)} %pad_maximum_fusion.1), channel_id=1, source_target_pairs={{4,0},{8,4},{12,8},{16,12},{20,16},{24,20},{28,24},{32,28},{36,32}... | collective-permute-start | bytes 1867784 | tf_op jit(solution)/shard_map/ppermute | solution.py:267
  17.0 0.7 fusion.83
  17.7 0.7 fusion.80
  18.3 0.7 fusion.82
  19.2 0.8 subtract_add_fusion
  20.0 11.8 %shard_map.50 = f32[16,4,8,256]{3,2,1,0:T(8,128)} custom-call(f32[16,24,8,256]{3,2,1,0:T(8,128)} %q_ref.1, f32[24,8,256]{2,1,0:T(8,128)} %get-tuple-element.27.a_ref, f32[24,8,256]{2,1,0:T(8,128)} %get-tuple-element.28.b_ref, f32[24,8,256]{2,1,0:T(8,128)} %copy-done.2, f32[24,8,256]{2,1,0:T(8,128)} %get-tuple-element.9.d_ref, f32[24,8,256]{2,1,0:T(8,128)} %w_ref.1, ...), custom_call_target="tpu_custom_call" | custom-call | flops 39321600 | bytes 4521984 | tf_op jit(solution)/shard_map/pallas_call | solution.py:230
  31.9 1.6 %fusion.37 = f32[16,4,8,64]{3,2,1,0:T(8,128)S(1)} fusion(f32[16,4,8,256]{3,2,1,0:T(8,128)} %shard_map.50, s32[256]{0:T(256)S(1)} %get-tuple-element.64, s32[256]{0:T(256)S(1)} %get-tuple-element.65, pred[256]{0:T(512)(128)(4,1)S(1)} %compare_and_fusion), kind=kOutput, calls=%fused_computation.109 | convolution fusion | flops 100712448 | bytes 657664 | tf_op jit(solution)/shard_map/dot_general | solution.py:248
  33.7 1.9 %collective-permute-done = f32[19,4,8,256]{3,2,1,0:T(8,128)} collective-permute-done((f32[19,4,8,256]{3,2,1,0:T(8,128)}, f32[19,4,8,256]{3,2,1,0:T(8,128)}, u32[]{:S(2)}, u32[]{:S(2)}) %collective-permute-start) | collective-permute-done | bytes 622624 | tf_op jit(solution)/shard_map/ppermute | solution.py:266
  35.6 0.8 fusion.78
  36.4 3.8 %collective-permute-done.1 = f32[19,4,8,256]{3,2,1,0:T(8,128)} collective-permute-done((f32[19,4,8,256]{3,2,1,0:T(8,128)}, f32[19,4,8,256]{3,2,1,0:T(8,128)}, u32[]{:S(2)}, u32[]{:S(2)}) %collective-permute-start.1) | collective-permute-done | bytes 622624 | tf_op jit(solution)/shard_map/ppermute | solution.py:267
  40.2 0.8 fusion.79
  41.3 1.1 %slice.331 = f32[16,4,8,256]{3,2,1,0:T(8,128)S(1)} slice(f32[19,4,8,256]{3,2,1,0:T(8,128)} %collective-permute-done.1), slice={[0:16], [0:4], [0:8], [0:256]} | slice | bytes 1048576 | tf_op jit(solution)/shard_map/slice | solution.py:278
  42.5 1.1 %slice.330 = f32[16,4,8,256]{3,2,1,0:T(8,128)S(1)} slice(f32[19,4,8,256]{3,2,1,0:T(8,128)} %collective-permute-done), slice={[0:16], [0:4], [0:8], [0:256]} | slice | bytes 1048576 | tf_op jit(solution)/shard_map/slice | solution.py:277
  43.7 0.9 fusion.7
  44.6 0.7 slice.352
  45.7 1.6 %fusion.9 = f32[2,16,10,8,256]{4,3,2,1,0:T(8,128)S(1)} fusion(f32[2,16,11,8,256]{4,3,2,1,0:T(8,128)S(1)} %fusion.2, f32[2,16,10,8,255]{4,3,2,1,0:T(8,128)S(1)} %slice.352, f32[1,16,12,8,256]{4,3,2,1,0:T(8,128)S(1)} %maximum_bitcast_fusion.1, f32[1,16,12,8,256]{4,3,2,1,0:T(8,128)S(1)} %maximum_bitcast_fusion, f32[2,10,8,256]{3,2,1,0:T(8,128)S(1)} %get-tuple-element.44, ...), kind=kLoop, calls=%fused_computation.18 | loop fusion | flops 8519680 | bytes 13948928 | tf_op jit(solution)/shard_map/sub | solution.py:127
  49.7 0.7 fusion.13
  51.2 0.9 fusion.16
  54.1 8.6 %all_gather.3 = f32[64,3072]{1,0:T(8,128)S(1)} all-gather(f32[16,3072]{1,0:T(8,128)S(1)} %reshape.119), channel_id=1, replica_groups=mesh['lon'=64,'probe'=4] {'probe'}, dimensions={0}, use_global_device_ids=true | all-gather | bytes 983040 | tf_op jit(solution)/shard_map/all_gather | solution.py:289
  62.7 1.4 %fusion.86.block_ref = f32[64,64]{1,0:T(8,128)} fusion(f32[64,3072]{1,0:T(8,128)S(1)} %all_gather.3), kind=kOutput, calls=%fused_computation.174 | convolution fusion | flops 150994944 | bytes 802816 | tf_op jit(solution)/shard_map/dot_general | solution.py:290
  64.1 21.7 %shard_map.51 = f32[64,64]{1,0:T(8,128)} custom-call(f32[64,64]{1,0:T(8,128)} %fusion.86.block_ref), custom_call_target="tpu_custom_call" | custom-call | tf_op jit(solution)/shard_map/pallas_call | solution.py:71
  85.8 6.6 %cholesky.17 = f32[64,64]{1,0:T(8,128)S(1)} custom-call(f32[64,64]{1,0:T(8,128)} %shard_map.51), custom_call_target="Cholesky" | custom-call | tf_op jit(solution)/shard_map/cholesky | solution.py:297
  93.8 4.9 %custom-call.5 = f32[1,64,64]{1,2,0:T(8,128)S(1)} custom-call(f32[1,64,64]{2,1,0:T(8,128)S(1)} %get-tuple-element.61), custom_call_target="InvertDiagBlocksLowerTriangular" | custom-call | tf_op jit(solution)/shard_map/triangular_solve | solution.py:298
  99.4 0.7 copy.14
  100.1 0.7 copy.10
  (65 shorter events, 8.1 us)
Async XLA Ops:
  4.1 13.6 %copy-start.1 = (f32[2,24,8,256]{3,2,1,0:T(8,128)S(1)}, f32[2,24,8,256]{3,2,1,0:T(8,128)}, u32[]{:S(2)}) copy-start(f32[2,24,8,256]{3,2,1,0:T(8,128)} %param.4) | copy-start | bytes 1179652
  4.1 14.3 %copy-start.3 = (f32[24,8,256]{2,1,0:T(8,128)S(1)}, f32[24,8,256]{2,1,0:T(8,128)}, u32[]{:S(2)}) copy-start(f32[24,8,256]{2,1,0:T(8,128)} %w_ref.1) | copy-start | bytes 589828
  6.3 29.2 %collective-permute-start = (f32[19,4,8,256]{3,2,1,0:T(8,128)}, f32[19,4,8,256]{3,2,1,0:T(8,128)}, u32[]{:S(2)}, u32[]{:S(2)}) collective-permute-start(f32[19,4,8,256]{3,2,1,0:T(8,128)} %pad_maximum_fusion), channel_id=1, source_target_pairs={{0,4},{4,8},{8,12},{12,16},{16,20},{20,24},{24,28},{28,32},{32,36}... | collective-permute-start | bytes 1867784 | tf_op jit(solution)/shard_map/ppermute | solution.py:266
  9.5 30.7 %collective-permute-start.1 = (f32[19,4,8,256]{3,2,1,0:T(8,128)}, f32[19,4,8,256]{3,2,1,0:T(8,128)}, u32[]{:S(2)}, u32[]{:S(2)}) collective-permute-start(f32[19,4,8,256]{3,2,1,0:T(8,128)} %pad_maximum_fusion.1), channel_id=1, source_target_pairs={{4,0},{8,4},{12,8},{16,12},{20,16},{24,20},{28,24},{32,28},{36,32}... | collective-permute-start | bytes 1867784 | tf_op jit(solution)/shard_map/ppermute | solution.py:267
  19.0 1.0 copy-start.2
  20.0 13.5 %copy-start = (f32[16,24,8,256]{3,2,1,0:T(8,128)S(1)}, f32[16,24,8,256]{3,2,1,0:T(8,128)}, u32[]{:S(2)}) copy-start(f32[16,24,8,256]{3,2,1,0:T(8,128)} %q_ref.1) | copy-start | bytes 9437188
  33.5 2.9 %copy-start.9 = (f32[1,8,8,256]{3,2,1,0:T(8,128)S(1)}, f32[1,8,8,256]{3,2,1,0:T(8,128)}, u32[]{:S(2)}) copy-start(f32[1,8,8,256]{3,2,1,0:T(8,128)} %get-tuple-element.45) | copy-start | bytes 196612
  33.5 7.5 %copy-start.8 = (f32[1,8,8,256]{3,2,1,0:T(8,128)S(1)}, f32[1,8,8,256]{3,2,1,0:T(8,128)}, u32[]{:S(2)}) copy-start(f32[1,8,8,256]{3,2,1,0:T(8,128)} %get-tuple-element.46) | copy-start | bytes 196612
  33.5 7.6 %copy-start.7 = (f32[1,8,8,256]{3,2,1,0:T(8,128)S(1)}, f32[1,8,8,256]{3,2,1,0:T(8,128)}, u32[]{:S(2)}) copy-start(f32[1,8,8,256]{3,2,1,0:T(8,128)} %get-tuple-element.30) | copy-start | bytes 196612
  33.5 7.6 %copy-start.6 = (f32[1,8,8,256]{3,2,1,0:T(8,128)S(1)}, f32[1,8,8,256]{3,2,1,0:T(8,128)}, u32[]{:S(2)}) copy-start(f32[1,8,8,256]{3,2,1,0:T(8,128)} %get-tuple-element.31) | copy-start | bytes 196612
  48.8 0.8 copy-start.5
  48.9 0.9 copy-start.4

commit v24 on v23

--- a/solution.py
+++ b/solution.py
@@ -280,8 +280,9 @@
         for part, (lo, hi) in zip(pack, bounds)
     ]
     rim = four_steps(sides[0], sides[1], sides[2], sides[3])
-    west = coarsen(increments[:, :halo] + rim[0])
-    east = coarsen(increments[:, lon_count - halo:] + rim[1])
+    edges = jnp.stack([increments[:, :halo], increments[:, lon_count - halo:]]) + rim
+    edges = coarsen(edges.reshape((-1,) + edges.shape[2:]))
+    west, east = edges[:probe_count], edges[probe_count:]
     coarse = jnp.concatenate([west, inner, east], axis=1)
     coarse = coarse.reshape(probe_count, -1)
     all_probes = probe_count * lax.axis_size("probe")

time: 102 us -> 103 us (level)
  local copies, waits for them, and re-layouts: 13.5 us -> 14.9 us
    another operation x0 -> x1, local copies, waits for them, and re-layouts: none -> 2.49 us  [body(): jnp.stack([increments[:, :halo], increments[:, lon_count - halo:]]) + rim]
    slice x1 -> x3, local copies, waits for them, and re-layouts: 1.37 us -> 0.19 us  [body(): west, east = (edges[:probe_count], edges[probe_count:])]
    unnamed x21 -> x25, local copies, waits for them, and re-layouts: 1.31 us -> 2.11 us
where the time goes in v24:
time: 103 us; the launch traced here: 102 us
  Pallas kernels  33.6 us (33%)
  other arithmetic  24.2 us (23%)
  local copies, waits for them, and re-layouts  14.9 us (14%)
  starting transfers between devices  9.79 us (10%)
  blocking collectives  8.63 us (8%)
  waiting for transfers between devices  5.63 us (5%)
  matrix products  4.1 us (4%)
  between operations  1.1 us (1%)
    pallas_call x1, Pallas kernels, butterfly_sum(): pl.pallas_call(functools.partial(exchange_kernel, count, radix), out_shap...  21.7 us
    pallas_call x1, Pallas kernels, stencil_sums(): pl.pallas_call(stencil_kernel, out_shape=jax.ShapeDtypeStruct((probe_coun...  11.8 us
    all_gather x1, blocking collectives, body(): full_panel = lax.all_gather(coarse, 'probe', axis=0, tiled=True)  8.63 us
    ppermute x1, starting transfers between devices, body(): from_east = lax.ppermute(east_edge, 'lon', backward)  7.49 us
    another operation x3, other arithmetic, body(): lower = lax.linalg.cholesky(gram, symmetrize_input=False)  7.27 us
    another operation x1, other arithmetic, body(): lax.linalg.triangular_solve(lower, ident, left_side=True, lower=True)  4.9 us
    ppermute x1, waiting for transfers between devices, body(): from_east = lax.ppermute(east_edge, 'lon', backward)  3.77 us
    another operation x1, local copies, waits for them, and re-layouts, body(): jnp.stack([increments[:, :halo], increments[:, lon_count - halo:]]) + rim  2.49 us
  transfers between devices with their start and end apart: 2, of which 2 were waited for; matrix products, arithmetic and copies ran while one was open for 6% of the time, Pallas kernels for 12%

profile of v24, /device:TPU:8, one launch (start us, length us, event | category | flops | bytes accessed | tf_op | source)
XLA Modules:
  0.0 101.9 jit_solution(16186018291409667086)
XLA Ops:
  0.7 1.9 %slice_maximum_fusion = (f32[1,24,8,256]{3,2,1,0:T(8,128)S(1)}, f32[24,8,256]{2,1,0:T(8,128)}, f32[24,8,256]{2,1,0:T(8,128)}, f32[1,24,8,256]{3,2,1,0:T(8,128)S(1)}) fusion(f32[2,24,8,256]{3,2,1,0:T(8,128)} %param.4, pred[256]{0:T(512)(128)(4,1)S(1)} %iota_compare_fusion.7), kind=kLoop, calls=%fused_computation.67 | loop fusion | flops 147456 | bytes 1179904 | tf_op jit(solution)/shard_map/max | solution.py:219
  2.5 0.8 fusion.73
  3.3 2.5 %slice_bitcast_fusion.2 = (f32[1,16,4,8,256]{4,3,2,1,0:T(8,128)}, f32[1,16,4,8,256]{4,3,2,1,0:T(8,128)}, f32[16,4,8,256]{3,2,1,0:T(8,128)S(1)}, f32[16,4,8,256]{3,2,1,0:T(8,128)S(1)}) fusion(f32[16,24,8,256]{3,2,1,0:T(8,128)} %q_ref.1), kind=kLoop, calls=%fused_computation.151 | loop fusion | bytes 3145728 | tf_op jit(solution)/shard_map/stack | solution.py:283
  5.8 0.9 pad_maximum_fusion
  6.7 2.3 %collective-permute-start = (f32[19,4,8,256]{3,2,1,0:T(8,128)}, f32[19,4,8,256]{3,2,1,0:T(8,128)}, u32[]{:S(2)}, u32[]{:S(2)}) collective-permute-start(f32[19,4,8,256]{3,2,1,0:T(8,128)} %pad_maximum_fusion), channel_id=1, source_target_pairs={{0,4},{4,8},{8,12},{12,16},{16,20},{20,24},{24,28},{28,32},{32,36}... | collective-permute-start | bytes 1867784 | tf_op jit(solution)/shard_map/ppermute | solution.py:266
  9.0 0.9 pad_maximum_fusion.1
  9.9 7.5 %collective-permute-start.1 = (f32[19,4,8,256]{3,2,1,0:T(8,128)}, f32[19,4,8,256]{3,2,1,0:T(8,128)}, u32[]{:S(2)}, u32[]{:S(2)}) collective-permute-start(f32[19,4,8,256]{3,2,1,0:T(8,128)} %pad_maximum_fusion.1), channel_id=1, source_target_pairs={{4,0},{8,4},{12,8},{16,12},{20,16},{24,20},{28,24},{32,28},{36,32}... | collective-permute-start | bytes 1867784 | tf_op jit(solution)/shard_map/ppermute | solution.py:267
  17.4 0.7 fusion.75
  18.0 0.7 fusion.72
  18.7 0.7 fusion.74
  19.6 0.9 subtract_add_fusion
  20.4 11.8 %shard_map.50 = f32[16,4,8,256]{3,2,1,0:T(8,128)} custom-call(f32[16,24,8,256]{3,2,1,0:T(8,128)} %q_ref.1, f32[24,8,256]{2,1,0:T(8,128)} %get-tuple-element.27.a_ref, f32[24,8,256]{2,1,0:T(8,128)} %get-tuple-element.28.b_ref, f32[24,8,256]{2,1,0:T(8,128)} %copy-done.4, f32[24,8,256]{2,1,0:T(8,128)} %get-tuple-element.7.d_ref, f32[24,8,256]{2,1,0:T(8,128)} %w_ref.1, ...), custom_call_target="tpu_custom_call" | custom-call | flops 39321600 | bytes 4521984 | tf_op jit(solution)/shard_map/pallas_call | solution.py:230
  32.3 1.6 %fusion.37 = f32[16,4,8,64]{3,2,1,0:T(8,128)S(1)} fusion(f32[16,4,8,256]{3,2,1,0:T(8,128)} %shard_map.50, s32[256]{0:T(256)S(1)} %get-tuple-element.66, s32[256]{0:T(256)S(1)} %get-tuple-element.67, pred[256]{0:T(512)(128)(4,1)S(1)} %compare_and_fusion), kind=kOutput, calls=%fused_computation.104 | convolution fusion | flops 100712448 | bytes 657664 | tf_op jit(solution)/shard_map/dot_general | solution.py:248
  34.1 1.9 %collective-permute-done = f32[19,4,8,256]{3,2,1,0:T(8,128)} collective-permute-done((f32[19,4,8,256]{3,2,1,0:T(8,128)}, f32[19,4,8,256]{3,2,1,0:T(8,128)}, u32[]{:S(2)}, u32[]{:S(2)}) %collective-permute-start) | collective-permute-done | bytes 622624 | tf_op jit(solution)/shard_map/ppermute | solution.py:266
  35.9 0.8 fusion.70
  36.8 3.8 %collective-permute-done.1 = f32[19,4,8,256]{3,2,1,0:T(8,128)} collective-permute-done((f32[19,4,8,256]{3,2,1,0:T(8,128)}, f32[19,4,8,256]{3,2,1,0:T(8,128)}, u32[]{:S(2)}, u32[]{:S(2)}) %collective-permute-start.1) | collective-permute-done | bytes 622624 | tf_op jit(solution)/shard_map/ppermute | solution.py:267
  40.5 0.8 fusion.71
  41.7 1.1 %slice.339 = f32[16,4,8,256]{3,2,1,0:T(8,128)S(1)} slice(f32[19,4,8,256]{3,2,1,0:T(8,128)} %collective-permute-done.1), slice={[0:16], [0:4], [0:8], [0:256]} | slice | bytes 1048576 | tf_op jit(solution)/shard_map/slice | solution.py:278
  42.9 1.1 %slice.338 = f32[16,4,8,256]{3,2,1,0:T(8,128)S(1)} slice(f32[19,4,8,256]{3,2,1,0:T(8,128)} %collective-permute-done), slice={[0:16], [0:4], [0:8], [0:256]} | slice | bytes 1048576 | tf_op jit(solution)/shard_map/slice | solution.py:277
  44.1 0.9 fusion.7
  45.0 0.7 slice.360
  46.1 1.6 %fusion.9 = f32[2,16,10,8,256]{4,3,2,1,0:T(8,128)S(1)} fusion(f32[2,16,11,8,256]{4,3,2,1,0:T(8,128)S(1)} %fusion.2, f32[2,16,10,8,255]{4,3,2,1,0:T(8,128)S(1)} %slice.360, f32[1,16,12,8,256]{4,3,2,1,0:T(8,128)S(1)} %maximum_bitcast_fusion.1, f32[1,16,12,8,256]{4,3,2,1,0:T(8,128)S(1)} %maximum_bitcast_fusion, f32[2,10,8,256]{3,2,1,0:T(8,128)S(1)} %get-tuple-element.44, ...), kind=kLoop, calls=%fused_computation.18 | loop fusion | flops 8519680 | bytes 13948928 | tf_op jit(solution)/shard_map/sub | solution.py:127
  50.1 0.7 fusion.13
  51.6 0.9 fusion.16
  53.7 0.7 fusion.22
  55.2 8.6 %all_gather.3 = f32[64,3072]{1,0:T(8,128)S(1)} all-gather(f32[16,3072]{1,0:T(8,128)S(1)} %reshape.110), channel_id=1, replica_groups=mesh['lon'=64,'probe'=4] {'probe'}, dimensions={0}, use_global_device_ids=true | all-gather | bytes 983040 | tf_op jit(solution)/shard_map/all_gather | solution.py:290
  63.8 1.4 %fusion.79.block_ref = f32[64,64]{1,0:T(8,128)} fusion(f32[64,3072]{1,0:T(8,128)S(1)} %all_gather.3), kind=kOutput, calls=%fused_computation.164 | convolution fusion | flops 150994944 | bytes 802816 | tf_op jit(solution)/shard_map/dot_general | solution.py:291
  65.2 21.7 %shard_map.51 = f32[64,64]{1,0:T(8,128)} custom-call(f32[64,64]{1,0:T(8,128)} %fusion.79.block_ref), custom_call_target="tpu_custom_call" | custom-call | tf_op jit(solution)/shard_map/pallas_call | solution.py:71
  87.0 6.6 %cholesky.17 = f32[64,64]{1,0:T(8,128)S(1)} custom-call(f32[64,64]{1,0:T(8,128)} %shard_map.51), custom_call_target="Cholesky" | custom-call | tf_op jit(solution)/shard_map/cholesky | solution.py:298
  94.9 4.9 %custom-call.5 = f32[1,64,64]{1,2,0:T(8,128)S(1)} custom-call(f32[1,64,64]{2,1,0:T(8,128)S(1)} %get-tuple-element.63), custom_call_target="InvertDiagBlocksLowerTriangular" | custom-call | tf_op jit(solution)/shard_map/triangular_solve | solution.py:299
  100.5 0.7 copy.18
  101.2 0.7 copy.14
  (70 shorter events, 8.2 us)
Async XLA Ops:
  0.6 5.2 %copy-start.5 = (f32[24,8,256]{2,1,0:T(8,128)S(1)}, f32[24,8,256]{2,1,0:T(8,128)}, u32[]{:S(2)}) copy-start(f32[24,8,256]{2,1,0:T(8,128)} %w_ref.1) | copy-start | bytes 589828
  3.3 14.7 %copy-start.1 = (f32[2,24,8,256]{3,2,1,0:T(8,128)S(1)}, f32[2,24,8,256]{3,2,1,0:T(8,128)}, u32[]{:S(2)}) copy-start(f32[2,24,8,256]{3,2,1,0:T(8,128)} %param.4) | copy-start | bytes 1179652
  6.7 29.2 %collective-permute-start = (f32[19,4,8,256]{3,2,1,0:T(8,128)}, f32[19,4,8,256]{3,2,1,0:T(8,128)}, u32[]{:S(2)}, u32[]{:S(2)}) collective-permute-start(f32[19,4,8,256]{3,2,1,0:T(8,128)} %pad_maximum_fusion), channel_id=1, source_target_pairs={{0,4},{4,8},{8,12},{12,16},{16,20},{20,24},{24,28},{28,32},{32,36}... | collective-permute-start | bytes 1867784 | tf_op jit(solution)/shard_map/ppermute | solution.py:266
  9.9 30.7 %collective-permute-start.1 = (f32[19,4,8,256]{3,2,1,0:T(8,128)}, f32[19,4,8,256]{3,2,1,0:T(8,128)}, u32[]{:S(2)}, u32[]{:S(2)}) collective-permute-start(f32[19,4,8,256]{3,2,1,0:T(8,128)} %pad_maximum_fusion.1), channel_id=1, source_target_pairs={{4,0},{8,4},{12,8},{16,12},{20,16},{24,20},{28,24},{32,28},{36,32}... | collective-permute-start | bytes 1867784 | tf_op jit(solution)/shard_map/ppermute | solution.py:267
  19.4 1.0 %copy-start.4 = (f32[24,8,256]{2,1,0:T(8,128)}, f32[24,8,256]{2,1,0:T(8,128)S(1)}, u32[]{:S(2)}) copy-start(f32[24,8,256]{2,1,0:T(8,128)S(1)} %fusion.25.c_ref) | copy-start | bytes 589828
  20.4 13.5 %copy-start = (f32[16,24,8,256]{3,2,1,0:T(8,128)S(1)}, f32[16,24,8,256]{3,2,1,0:T(8,128)}, u32[]{:S(2)}) copy-start(f32[16,24,8,256]{3,2,1,0:T(8,128)} %q_ref.1) | copy-start | bytes 9437188
  33.9 2.8 %copy-start.11 = (f32[1,8,8,256]{3,2,1,0:T(8,128)S(1)}, f32[1,8,8,256]{3,2,1,0:T(8,128)}, u32[]{:S(2)}) copy-start(f32[1,8,8,256]{3,2,1,0:T(8,128)} %get-tuple-element.45) | copy-start | bytes 196612
  33.9 7.4 %copy-start.10 = (f32[1,8,8,256]{3,2,1,0:T(8,128)S(1)}, f32[1,8,8,256]{3,2,1,0:T(8,128)}, u32[]{:S(2)}) copy-start(f32[1,8,8,256]{3,2,1,0:T(8,128)} %get-tuple-element.46) | copy-start | bytes 196612
  33.9 7.5 %copy-start.9 = (f32[1,8,8,256]{3,2,1,0:T(8,128)S(1)}, f32[1,8,8,256]{3,2,1,0:T(8,128)}, u32[]{:S(2)}) copy-start(f32[1,8,8,256]{3,2,1,0:T(8,128)} %get-tuple-element.30) | copy-start | bytes 196612
  33.9 7.5 %copy-start.8 = (f32[1,8,8,256]{3,2,1,0:T(8,128)S(1)}, f32[1,8,8,256]{3,2,1,0:T(8,128)}, u32[]{:S(2)}) copy-start(f32[1,8,8,256]{3,2,1,0:T(8,128)} %get-tuple-element.31) | copy-start | bytes 196612
  49.2 0.8 copy-start.7
  49.2 0.9 copy-start.6
  52.5 1.0 %copy-start.2 = (f32[1,16,4,8,256]{4,3,2,1,0:T(8,128)S(1)}, f32[1,16,4,8,256]{4,3,2,1,0:T(8,128)}, u32[]{:S(2)}) copy-start(f32[1,16,4,8,256]{4,3,2,1,0:T(8,128)} %get-tuple-element.10) | copy-start | bytes 1572868
  52.5 1.2 %copy-start.3 = (f32[1,16,4,8,256]{4,3,2,1,0:T(8,128)S(1)}, f32[1,16,4,8,256]{4,3,2,1,0:T(8,128)}, u32[]{:S(2)}) copy-start(f32[1,16,4,8,256]{4,3,2,1,0:T(8,128)} %get-tuple-element.11) | copy-start | bytes 1572868
